TPU v7x, 32 devices: a whole 2x2x4 slice. The times are simulated.
32 devices in a mesh: row: 8 (over z, x), col: 4 (over y, core).
Axes of the slice: x: 2, y: 2, z: 4, core: 2. Of those that a mesh axis runs over, the one named last changes fastest.
Arguments:
- amplitudes: float32 [4096, 4096], P('row', 'col'), may hold values from -1 to 1, as said below
- interaction: float32 [4096, 4096], P('row', 'col'), may hold values from -9 to 9, as said below
- occ_energy: float32 [4], replicated, may hold values from -2.5 to -0.5
- vir_energy: float32 [1024], replicated, may hold values from 0.2 to 4
Outputs:
- updated: float32 [4096, 4096], P('row', 'col')
- residual: float32 [4096, 4096], P('row', 'col')
Inputs may be any that keep to these rules, and one draw needn't show every extreme that they name: amplitudes is symmetric: it equals its transpose exactly. interaction is symmetric: it equals its transpose exactly.
All inputs are finite; a program needn't handle non-finite values.
Results may differ from a plain program's by a relative error of at most 0.000057.
Values sent between devices are 32-bit elements; how exact they have to be, the bound alone decides.
No kernel may reach another device: no remote copies, remote signals or barrier semaphores. Data moves between devices by JAX's collectives and lax.ppermute only.
A program may use at most 64 MiB of HBM per device.

v0:
```python
import jax
import jax.numpy as jnp
from jax import lax
from jax.sharding import PartitionSpec as P


def swapped(block, axis, distance):
    count = lax.axis_size(axis)
    route = []
    for low in range(count):
        high = low | 1 << distance
        if high != low and high < count:
            route += [(low, high), (high, low)]
    return lax.ppermute(block, axis, route)


def from_behind(block, axis, distance):
    devices = range(lax.axis_size(axis))
    route = [(i - distance, i) for i in devices if i - distance in devices]
    return lax.ppermute(block, axis, route)


def contract(left_tile, right_tile):
    right_panel = lax.all_gather(right_tile, "row", axis=0, tiled=True)
    return jnp.dot(
        lax.all_gather(left_tile, "col", axis=1, tiled=True),
        right_panel,
        precision=lax.Precision.HIGHEST,
        preferred_element_type=jnp.float32,
    )


def diagonal_tile(tile, row_place, col_place):
    tile_rows = tile.shape[0]
    col_count = lax.axis_size("col")
    ratio = lax.axis_size("row") // col_count
    ratio_bits = ratio.bit_length() - 1
    row_bits = lax.axis_size("row").bit_length() - 1
    blocks = tile.reshape(tile_rows, ratio, tile_rows).transpose(1, 2, 0)
    for bit_index in range(row_bits):
        row_flag = row_place // 2**bit_index % 2
        if bit_index < ratio_bits:
            lower = 2**bit_index
            grouped = blocks.reshape(ratio // (2 * lower), 2, lower, tile_rows, tile_rows)
            zero_half = grouped[:, 0]
            one_half = grouped[:, 1]
            outgoing = jnp.where(row_flag == 0, one_half, zero_half)
            incoming = swapped(outgoing, "row", bit_index)
            new_zero = jnp.where(row_flag == 1, incoming, zero_half)
            new_one = jnp.where(row_flag == 0, incoming, one_half)
            blocks = jnp.stack([new_zero, new_one], axis=1).reshape(ratio, tile_rows, tile_rows)
        else:
            col_flag = col_place // 2 ** (bit_index - ratio_bits) % 2
            stride = 2**bit_index * col_count - 2 ** (bit_index - ratio_bits)
            from_above = from_behind(blocks, ("row", "col"), -stride)
            from_below = from_behind(blocks, ("row", "col"), stride)
            incoming = jnp.where(row_flag == 0, from_above, from_below)
            blocks = jnp.where(row_flag != col_flag, incoming, blocks)
    return blocks.transpose(1, 0, 2).reshape(tile_rows, ratio * tile_rows)


def local(amplitudes, interaction, occ_energy, vir_energy):
    tile_rows, tile_cols = amplitudes.shape
    row_place = lax.axis_index("row")
    col_place = lax.axis_index("col")
    product = contract(amplitudes, interaction)
    mirrored = diagonal_tile(product, row_place, col_place)
    gaps = (vir_energy[None, :] - occ_energy[:, None]).reshape(-1)
    row_gap = lax.dynamic_slice_in_dim(gaps, row_place * tile_rows, tile_rows, 0)
    col_gap = lax.dynamic_slice_in_dim(gaps, col_place * tile_cols, tile_cols, 0)
    denom = row_gap[:, None] + col_gap[None, :]
    residual = interaction + product + mirrored + denom * amplitudes
    updated = amplitudes - residual / denom
    return (updated, residual)


def solution(mesh):
    return jax.shard_map(
        local,
        mesh=mesh,
        in_specs=(P("row", "col"), P("row", "col"), P(), P()),
        out_specs=(P("row", "col"), P("row", "col")),
        check_vma=False,
    )
```

profile of v0, /device:TPU:29, one launch (start us, length us, event | category | flops | bytes accessed | tf_op | source)
XLA Modules:
  0.0 543.7 jit_solution(10985203287929512605)
XLA Ops:
  7.2 0.0 all-gather.3.cloned.1.call-start
  7.2 0.7 all-gather.3.cloned.1.call-update
  7.9 0.0 all-gather.5.cloned.1.call-start
  7.9 0.7 all-gather.5.cloned.1.call-update
  8.7 59.6 %all-gather.3.cloned.1.call-done = f32[512,4096]{1,0:T(8,128)} async-done(((f32[512,1024]{1,0:T(8,128)}), f32[512,4096]{1,0:T(8,128)}) %all-gather.3.cloned.1.call-update) | async-done | bytes 8388624 | tf_op jit(solution)/shard_map/all_gather | solution.py:26
  68.3 228.1 %all-gather.5.cloned.1.call-done = f32[4096,1024]{1,0:T(8,128)} async-done(((f32[512,1024]{1,0:T(8,128)}), f32[4096,1024]{1,0:T(8,128)}) %all-gather.5.cloned.1.call-update) | async-done | bytes 16777232 | tf_op jit(solution)/shard_map/all_gather | solution.py:24
  296.4 31.8 %fusion.5 = f32[512,1024]{1,0:T(8,128)} fusion(f32[512,4096]{1,0:T(8,128)} %all-gather.3.cloned.1.call-done, f32[4096,1024]{1,0:T(8,128)} %all-gather.5.cloned.1.call-done), kind=kOutput, calls=%fused_computation.16 | convolution fusion | flops 25769803776 | bytes 27262976 | tf_op jit(solution)/shard_map/dot_general | solution.py:25
  328.1 3.0 reshape.44
  331.2 1.1 broadcast_select_fusion.1
  332.2 0.3 collective-permute-start
  332.6 24.0 %collective-permute-done = f32[1,1,512,512]{2,1,3,0:T(1,128)} collective-permute-done((f32[1,1,512,512]{2,1,3,0:T(1,128)S(1)}, f32[1,1,512,512]{2,1,3,0:T(1,128)}, u32[]{:S(2)}, u32[]{:S(2)}) %collective-permute-start) | collective-permute-done | bytes 1048608 | tf_op jit(solution)/shard_map/ppermute | solution.py:14
  356.6 2.9 fusion.2
  359.5 3.2 maximum_bitcast_fusion
  362.7 4.0 collective-permute-start.1
  366.7 1.3 collective-permute-start.2
  368.0 0.0 copy-start.5
  368.0 0.0 copy-start.6
  368.0 43.3 %collective-permute-done.1 = f32[2,512,512]{1,0,2:T(2,128)S(1)} collective-permute-done((f32[2,512,512]{1,0,2:T(2,128)}, f32[2,512,512]{1,0,2:T(2,128)S(1)}, u32[]{:S(2)}, u32[]{:S(2)}) %collective-permute-start.1) | collective-permute-done | bytes 2097184 | tf_op jit(solution)/shard_map/ppermute | solution.py:20
  411.3 1.3 copy-done.4
  412.7 2.5 collective-permute-done.2
  415.1 4.1 select_select_fusion
  419.2 6.0 %collective-permute-start.3 = (f32[2,512,512]{1,0,2:T(2,128)S(1)}, f32[2,512,512]{1,0,2:T(2,128)}, u32[]{:S(2)}, u32[]{:S(2)}) collective-permute-start(f32[2,512,512]{1,0,2:T(2,128)S(1)} %select_select_fusion), channel_id=1, source_target_pairs={{14,0},{15,1},{16,2},{17,3},{18,4},{19,5},{20,6},{21,7},{22,8},{23... | collective-permute-start | bytes 6291464 | tf_op jit(solution)/shard_map/ppermute | solution.py:20
  425.2 1.3 collective-permute-start.4
  426.6 0.1 subtract_bitcast_fusion
  426.7 0.1 dynamic_slice.6
  426.8 41.9 %collective-permute-done.3 = f32[2,512,512]{1,0,2:T(2,128)} collective-permute-done((f32[2,512,512]{1,0,2:T(2,128)S(1)}, f32[2,512,512]{1,0,2:T(2,128)}, u32[]{:S(2)}, u32[]{:S(2)}) %collective-permute-start.3) | collective-permute-done | bytes 2097184 | tf_op jit(solution)/shard_map/ppermute | solution.py:20
  468.6 52.1 %collective-permute-done.4 = f32[2,512,512]{1,0,2:T(2,128)} collective-permute-done((f32[2,512,512]{1,0,2:T(2,128)S(1)}, f32[2,512,512]{1,0,2:T(2,128)}, u32[]{:S(2)}, u32[]{:S(2)}) %collective-permute-start.4) | collective-permute-done | bytes 2097184 | tf_op jit(solution)/shard_map/ppermute | solution.py:20
  520.7 4.4 select_bitcast_fusion
  525.0 6.2 %copy.6 = f32[512,2,512]{2,1,0:T(2,128)} copy(f32[512,2,512]{0,1,2:T(2,128)} %select_bitcast_fusion) | data formatting | bytes 4194304 | tf_op jit(solution)/shard_map/transpose | solution.py:59
  531.3 2.2 copy.7
  533.5 0.6 copy-done.2
  534.1 2.7 fusion.1
  (12 shorter events, 0.0 us)
Async XLA Ops:
  7.2 61.1 %all-gather.3.cloned.1.call-start = ((), (), s32[]{:S(2)}) async-start(), calls=%async_computation | async-start | bytes 10485760 | tf_op jit(solution)/shard_map/all_gather | solution.py:26
  7.9 288.5 %all-gather.5.cloned.1.call-start = ((), (), s32[]{:S(2)}) async-start(), calls=%async_computation.1 | async-start | bytes 18874368 | tf_op jit(solution)/shard_map/all_gather | solution.py:24
  332.2 24.3 %collective-permute-start = (f32[1,1,512,512]{2,1,3,0:T(1,128)S(1)}, f32[1,1,512,512]{2,1,3,0:T(1,128)}, u32[]{:S(2)}, u32[]{:S(2)}) collective-permute-start(f32[1,1,512,512]{2,1,3,0:T(1,128)S(1)} %broadcast_select_fusion.1), channel_id=1, source_target_pairs={{0,4},{4,0},{8,12},{12,8},{16,20},{20,16},{24,28},{28,24},{1,5},{5... | collective-permute-start | bytes 3145736 | tf_op jit(solution)/shard_map/ppermute | solution.py:14
  359.4 3.2 copy-start
  362.7 48.6 %collective-permute-start.1 = (f32[2,512,512]{1,0,2:T(2,128)}, f32[2,512,512]{1,0,2:T(2,128)S(1)}, u32[]{:S(2)}, u32[]{:S(2)}) collective-permute-start(f32[2,512,512]{1,0,2:T(2,128)} %maximum_bitcast_fusion), channel_id=1, source_target_pairs={{7,0},{8,1},{9,2},{10,3},{11,4},{12,5},{13,6},{14,7},{15,8},{16,9}... | collective-permute-start | bytes 6291464 | tf_op jit(solution)/shard_map/ppermute | solution.py:20
  366.7 48.5 %collective-permute-start.2 = (f32[2,512,512]{1,0,2:T(2,128)}, f32[2,512,512]{1,0,2:T(2,128)}, u32[]{:S(2)}, u32[]{:S(2)}) collective-permute-start(f32[2,512,512]{1,0,2:T(2,128)} %maximum_bitcast_fusion), channel_id=1, source_target_pairs={{0,7},{1,8},{2,9},{3,10},{4,11},{5,12},{6,13},{7,14},{8,15},{9,16}... | collective-permute-start | bytes 6291464 | tf_op jit(solution)/shard_map/ppermute | solution.py:20
  368.0 58.6 %copy-start.5 = (f32[1024]{0:T(1024)S(1)}, f32[1024]{0:T(1024)}, u32[]{:S(2)}) copy-start(f32[1024]{0:T(1024)} %param.7) | copy-start | bytes 12292
  368.0 58.6 %copy-start.6 = (f32[4]{0:T(128)S(1)}, f32[4]{0:T(128)}, u32[]{:S(2)}) copy-start(f32[4]{0:T(128)} %param.6) | copy-start | bytes 52
  411.3 1.3 copy-start.4
  419.2 49.4 %collective-permute-start.3 = (f32[2,512,512]{1,0,2:T(2,128)S(1)}, f32[2,512,512]{1,0,2:T(2,128)}, u32[]{:S(2)}, u32[]{:S(2)}) collective-permute-start(f32[2,512,512]{1,0,2:T(2,128)S(1)} %select_select_fusion), channel_id=1, source_target_pairs={{14,0},{15,1},{16,2},{17,3},{18,4},{19,5},{20,6},{21,7},{22,8},{23... | collective-permute-start | bytes 6291464 | tf_op jit(solution)/shard_map/ppermute | solution.py:20
  425.2 95.4 %collective-permute-start.4 = (f32[2,512,512]{1,0,2:T(2,128)S(1)}, f32[2,512,512]{1,0,2:T(2,128)}, u32[]{:S(2)}, u32[]{:S(2)}) collective-permute-start(f32[2,512,512]{1,0,2:T(2,128)S(1)} %select_select_fusion), channel_id=1, source_target_pairs={{0,14},{1,15},{2,16},{3,17},{4,18},{5,19},{6,20},{7,21},{8,22},{9,... | collective-permute-start | bytes 6291464 | tf_op jit(solution)/shard_map/ppermute | solution.py:20
  525.0 8.5 %copy-start.3 = (f32[512,1024]{1,0:T(8,128)S(1)}, f32[512,1024]{1,0:T(8,128)}, u32[]{:S(2)}) copy-start(f32[512,1024]{1,0:T(8,128)} %fusion.5) | copy-start | bytes 6291460
  531.3 2.2 copy-start.1
  531.3 2.9 copy-start.2
Sparse Core Ops, SparseCore 0:
  9.5 58.6 all-gather.2
  70.4 225.9 all-gather.4
where the time goes:
time: 544 us
  waiting for transfers between devices  453 us (83%)
  matrix products  31.8 us (6%)
  other arithmetic  18.4 us (3%)
  between operations  14.3 us (3%)
  local copies, waits for them, and re-layouts  13.5 us (2%)
  starting transfers between devices  13 us (2%)
    all_gather x1, waiting for transfers between devices, contract(): right_panel = lax.all_gather(right_tile, 'row', axis=0, tiled=True)  228 us
    ppermute x4, waiting for transfers between devices, from_behind(): return lax.ppermute(block, axis, route)  140 us
    all_gather x1, waiting for transfers between devices, contract(): lax.all_gather(left_tile, 'col', axis=1, tiled=True)  59.6 us
    dot_general x1, matrix products, contract(): jnp.dot(lax.all_gather(left_tile, 'col', axis=1, tiled=True), right_panel...  31.8 us
    ppermute x1, waiting for transfers between devices, swapped(): return lax.ppermute(block, axis, route)  24 us
    ppermute x4, starting transfers between devices, from_behind(): return lax.ppermute(block, axis, route)  12.6 us
  transfers between devices with their start and end apart: 7, of which 7 were waited for; matrix products, arithmetic and copies ran while one was open for 0% of the time, Pallas kernels for 0%

commit v1 on v0

--- a/solution.py
+++ b/solution.py
@@ -1,7 +1,15 @@
+import functools
+
 import jax
 import jax.numpy as jnp
 from jax import lax
+from jax.experimental import pallas as pl
+from jax.experimental.pallas import tpu as pltpu
 from jax.sharding import PartitionSpec as P
+
+
+CHUNKS = 4
+PAD = 8
 
 
 def swapped(block, axis, distance):
@@ -59,24 +67,468 @@
     return blocks.transpose(1, 0, 2).reshape(tile_rows, ratio * tile_rows)
 
 
-def local(amplitudes, interaction, occ_energy, vir_energy):
-    tile_rows, tile_cols = amplitudes.shape
-    row_place = lax.axis_index("row")
-    col_place = lax.axis_index("col")
+def general_sum(amplitudes, interaction):
     product = contract(amplitudes, interaction)
-    mirrored = diagonal_tile(product, row_place, col_place)
+    mirrored = diagonal_tile(product, lax.axis_index("row"), lax.axis_index("col"))
+    return product + mirrored
+
+
+def routed(block, target):
+    rows, cols = lax.axis_size("row"), lax.axis_size("col")
+    route = []
+    for r in range(rows):
+        for c in range(cols):
+            place = target(r, c)
+            if place is not None:
+                route.append((r * cols + c, place[0] * cols + place[1]))
+    return lax.ppermute(block, ("row", "col"), route)
+
+
+def is_near(r, c):
+    return r >> 2 == c >> 1
+
+
+def flipped(z, x, c):
+    return x if z < c else 1 - x
+
+
+def near_target(r, c):
+    z, x = r >> 1, r & 1
+    if not is_near(r, c):
+        return None
+    if z == c:
+        return (r ^ 1, c)
+    return (2 * c + flipped(z, x, c), z)
+
+
+def far_target(r, c):
+    z, x = r >> 1, r & 1
+    if not is_near(r, c):
+        return None
+    return (2 * c + flipped(z ^ 2, x, c), z ^ 2)
+
+
+X_PLACE, ODD, TURN_1, TURN_2, NEAR, MIDDLE, PLACE = range(7)
+VMEM = 40 * 2**20
+
+
+def params():
+    return pltpu.CompilerParams(vmem_limit_bytes=VMEM)
+
+
+def zeros(count):
+    return (0,) * count
+
+
+def call(kernel, shapes, meta, args, in_specs=None, out_specs=None, scratch=(), aliases=None):
+    if in_specs is None:
+        in_specs = [None] * len(args)
+    if out_specs is None:
+        out_specs = [None] * len(shapes)
+    whole = lambda a: pl.BlockSpec(a.shape, lambda i, m: zeros(len(a.shape)))
+    return pl.pallas_call(
+        kernel,
+        out_shape=list(shapes),
+        grid_spec=pltpu.PrefetchScalarGridSpec(
+            num_scalar_prefetch=1,
+            grid=(1,),
+            in_specs=[s or whole(a) for s, a in zip(in_specs, args)],
+            out_specs=[s or whole(a) for s, a in zip(out_specs, shapes)],
+            scratch_shapes=list(scratch),
+        ),
+        input_output_aliases=aliases or {},
+        compiler_params=params(),
+    )(meta, *args)
+
+
+def shaped(*shape):
+    return jax.ShapeDtypeStruct(shape, jnp.float32)
+
+
+def halves(value):
+    high = value.astype(jnp.bfloat16)
+    return high, (value - high.astype(jnp.float32)).astype(jnp.bfloat16)
+
+
+def left_of(t, v):
+    t_high, t_low = halves(t)
+    v_high, v_low = halves(v)
+    return jnp.concatenate([t_high, t_high, t_low, v_high, v_high, v_low], axis=0)
+
+
+def right_of(t, v):
+    t_high, t_low = halves(t)
+    v_high, v_low = halves(v)
+    return jnp.concatenate([v_high, v_low, v_high, t_high, t_low, t_high], axis=0)
+
+
+def crossed(left, right):
+    return lax.dot_general(
+        left, right, (((0,), (0,)), ((), ())), preferred_element_type=jnp.float32
+    )
+
+
+def placed(place, n, offset=0, size=None):
+    return pl.ds(pl.multiple_of(place * n + offset, 128), size or n)
+
+
+def pick_kernel(side, first, m, t_ref, v_ref, out_ref, sems):
+    n = t_ref.shape[0]
+    cols = placed(m[X_PLACE] ^ side, n, first, out_ref.shape[2])
+    copies = [
+        pltpu.make_async_copy(ref.at[:, cols], out_ref.at[i], sems.at[i])
+        for i, ref in enumerate((t_ref, v_ref))
+    ]
+    for copy in copies:
+        copy.start()
+    for copy in copies:
+        copy.wait()
+
+
+def pick(meta, t, v, side, first, count):
+    n = t.shape[0]
+    w = n // CHUNKS
+    hbm = pl.BlockSpec(memory_space=pltpu.MemorySpace.HBM)
+    return call(
+        functools.partial(pick_kernel, side, first * w),
+        [shaped(2, n, count * w)],
+        meta,
+        [t, v],
+        in_specs=[hbm, hbm],
+        scratch=[pltpu.SemaphoreType.DMA((2,))],
+    )[0]
+
+
+def middle_block(m, side, k, w, t_ref, v_ref, store):
+    n = t_ref.shape[0]
+    half = m[X_PLACE] ^ side
+    cols = placed(half, n, k * w, w)
+    left = left_of(t_ref[:, cols], v_ref[:, cols])
+    same, cross = placed(half, n), placed(1 - half, n)
+    diagonal = crossed(left, right_of(t_ref[:, same], v_ref[:, same]))
+    aside = crossed(left, right_of(t_ref[:, cross], v_ref[:, cross]))
+    line = lax.broadcasted_iota(jnp.int32, (w, n), 0) + k * w
+    lane = lax.broadcasted_iota(jnp.int32, (w, n), 1)
+    extra = jnp.sum(jnp.where(line == lane, aside, 0.0), axis=0, keepdims=True)
+    store(jnp.where(line >= lane, diagonal, aside), jnp.broadcast_to(extra, (PAD, n)))
+
+
+def next_block(m, side, k, w, at_ref, av_ref, t_ref, v_ref, store):
+    n = t_ref.shape[0]
+    cols = placed(m[X_PLACE] ^ side, n, k * w, w)
+    half = placed(m[TURN_1] ^ side, n)
+    left = left_of(at_ref[:, cols], av_ref[:, cols])
+    store(
+        crossed(left, right_of(t_ref[:, half], v_ref[:, half])), jnp.zeros((PAD, n), jnp.float32)
+    )
+
+
+def stored(out_ref, place, w):
+    def store(block, pad):
+        out_ref[place, :w, :] = block
+        out_ref[place, w:, :] = pad
+
+    return store
+
+
+def middle_kernel(side, k, w, m, t_ref, v_ref, out_ref):
+    middle_block(m, side, k, w, t_ref, v_ref, stored(out_ref, 0, w))
+
+
+def middle_part(meta, t, v, side, k):
+    n = t.shape[0]
+    w = n // CHUNKS
+    return call(
+        functools.partial(middle_kernel, side, k, w),
+        [shaped(2, w + PAD, n)],
+        meta,
+        [t, v],
+        out_specs=[pl.BlockSpec((1, w + PAD, n), lambda i, m: (0, 0, 0))],
+    )[0]
+
+
+def next_kernel(side, k, w, m, _, at_ref, av_ref, t_ref, v_ref, out_ref):
+    next_block(m, side, k, w, at_ref, av_ref, t_ref, v_ref, stored(out_ref, 0, w))
+
+
+def next_part(meta, base, at, av, t, v, side, k):
+    n = t.shape[0]
+    w = n // CHUNKS
+    return call(
+        functools.partial(next_kernel, side, k, w),
+        [shaped(*base.shape)],
+        meta,
+        [base, at, av, t, v],
+        in_specs=[pl.BlockSpec(memory_space=pl.ANY), None, None, None, None],
+        out_specs=[pl.BlockSpec((1, w + PAD, n), lambda i, m: (1, 0, 0))],
+        aliases={1: 0},
+    )[0]
+
+
+def near_kernel(side, chunks, w, m, at_ref, av_ref, t_ref, v_ref, *outs):
+    for out_ref, k in zip(outs, chunks):
+        middle_block(m, side, k, w, t_ref, v_ref, stored(out_ref, 0, w))
+        next_block(m, side, k, w, at_ref, av_ref, t_ref, v_ref, stored(out_ref, 1, w))
+
+
+def near_parts(meta, at, av, t, v, side, chunks):
+    n = t.shape[0]
+    w = n // CHUNKS
+    return call(
+        functools.partial(near_kernel, side, chunks, w),
+        [shaped(2, w + PAD, n) for _ in chunks],
+        meta,
+        [at, av, t, v],
+    )
+
+
+def far_kernel(side, m, a_ref, b_ref, t_ref, v_ref, *outs):
+    n = t_ref.shape[0]
+    w = outs[0].shape[1]
+    half = placed(m[TURN_2] ^ side, n)
+    right = right_of(t_ref[:, half], v_ref[:, half])
+    for d, ref in enumerate((a_ref, b_ref)):
+        for i, out_ref in enumerate(outs):
+            cols = slice(i * w, (i + 1) * w)
+            out_ref[d] = crossed(left_of(ref[0, :, cols], ref[1, :, cols]), right)
+
+
+def far_parts(meta, a, b, t, v, side):
+    n = t.shape[0]
+    w = n // CHUNKS
+    return call(
+        functools.partial(far_kernel, side),
+        [shaped(2, w, n)] * (a.shape[2] // w),
+        meta,
+        [a, b, t, v],
+    )
+
+
+def fold_kernel(_, keep_pass, come_pass, keep_stay, come_stay, pass_ref, stay_ref):
+    pass_ref[...] = keep_pass[0] + come_pass[0]
+    stay_ref[...] = keep_stay[0] + come_stay[0]
+
+
+def fold(meta, keep, come):
+    _, lines, n = keep.shape
+    leave = pl.BlockSpec((1, lines, n), lambda i, m: (1 - m[ODD], 0, 0))
+    stay = pl.BlockSpec((1, lines, n), lambda i, m: (m[ODD], 0, 0))
+    return call(
+        fold_kernel,
+        [shaped(lines, n)] * 2,
+        meta,
+        [keep, come, keep, come],
+        in_specs=[leave, leave, stay, stay],
+    )
+
+
+def add_kernel(_, a_ref, b_ref, out_ref):
+    out_ref[...] = a_ref[...] + b_ref[...]
+
+
+def add(meta, a, b):
+    return call(add_kernel, [shaped(*a.shape)], meta, [a, b])[0]
+
+
+def join_kernel(w, count, _, *refs):
+    out_ref = refs[2 * count]
+    extra = None
+    for k in range(count):
+        a_ref, b_ref = refs[k], refs[count + k]
+        out_ref[k * w : (k + 1) * w, :] = a_ref[:w, :] + b_ref[:w, :]
+        if a_ref.shape[0] > w:
+            pad = a_ref[w:, :] + b_ref[w:, :]
+            extra = pad if extra is None else extra + pad
+    if extra is not None:
+        refs[2 * count + 1][...] = extra
+
+
+def join(meta, parts, comes):
+    n = parts[0].shape[1]
+    w = n // CHUNKS
+    shapes = [shaped(len(parts) * w, n)]
+    if parts[0].shape[0] > w:
+        shapes.append(shaped(PAD, n))
+    return call(functools.partial(join_kernel, w, len(parts)), shapes, meta, [*parts, *comes])
+
+
+def closing(t, v, row, col, value):
+    denom = row + col
+    residual = v + value + denom * t
+    return t - residual / denom, residual
+
+
+def most_kernel(m, *refs):
+    near_own, near_back, extra_ref, *refs = refs
+    far_own, far_back = refs[:3], refs[3:5]
+    t_ref, v_ref, row_ref, col_ref, new_ref, res_ref = refs[5:]
+    n = t_ref.shape[0]
+    place = m[PLACE]
+
+    def write(first, count, half, value):
+        rows = pl.ds(first, count)
+        new_ref[rows, half], res_ref[rows, half] = closing(
+            t_ref[rows, half], v_ref[rows, half], row_ref[rows, :], col_ref[:, half], value
+        )
+
+    @pl.when(m[NEAR] == 0)
+    def _():
+        first = 0
+        for ref in far_own:
+            write(first, ref.shape[0], placed(place, n), ref[...])
+            first += ref.shape[0]
+        first = 0
+        for ref in far_back:
+            count = ref.shape[0]
+            write(0, n, placed(1 - place, n, first, count), ref[...].T)
+            first += count
+
+    @pl.when((m[NEAR] == 1) & (m[MIDDLE] == 0))
+    def _():
+        write(0, n, placed(place, n), near_own[...])
+        write(0, n, placed(1 - place, n), near_back[...].T)
+
+    @pl.when(m[MIDDLE] == 1)
+    def _():
+        line = lax.broadcasted_iota(jnp.int32, (n, n), 0)
+        lane = lax.broadcasted_iota(jnp.int32, (n, n), 1)
+        own = near_own[...]
+        write(0, n, placed(place, n), jnp.where(line >= lane, own, own.T))
+        lower = jnp.where(line > lane, near_back[...].T, extra_ref[:1, :])
+        write(0, n, placed(1 - place, n), jnp.where(line < lane, own, lower))
+
+
+def most(meta, t, *args):
+    return call(most_kernel, [shaped(*t.shape)] * 2, meta, args)
+
+
+def last_kernel(m, back_ref, new_in, res_in, t_ref, v_ref, row_ref, col_ref, new_ref, res_ref):
+    @pl.when(m[NEAR] == 1)
+    def _():
+        new_ref[...] = new_in[...]
+        res_ref[...] = res_in[...]
+
+    @pl.when(m[NEAR] == 0)
+    def _():
+        new_ref[...], res_ref[...] = closing(
+            t_ref[...], v_ref[...], row_ref[...], col_ref[...], back_ref[...].T
+        )
+
+
+def last(meta, back, new, res, t, v, row_gap, col_gap):
+    n = t.shape[0]
+    w = n // CHUNKS
+    at = lambda i, m: (0, (2 - m[PLACE]) * CHUNKS - 1)
+    block = pl.BlockSpec((n, w), at)
+    return call(
+        last_kernel,
+        [shaped(*t.shape)] * 2,
+        meta,
+        [back, new, res, t, v, row_gap, col_gap],
+        in_specs=[None, block, block, block, block, None, pl.BlockSpec((1, w), at)],
+        out_specs=[block, block],
+        aliases={2: 0, 3: 1},
+    )
+
+
+def split_update(t, v, row_gap, col_gap):
+    r = lax.axis_index("row")
+    c = lax.axis_index("col")
+    z, x = r // 2, r % 2
+    slot = lax.iota(jnp.int32, 8)
+    values = {
+        X_PLACE: x,
+        ODD: (z + c) % 2,
+        TURN_1: jnp.where(c % 2 == 1, x, 1 - x),
+        TURN_2: jnp.where(c // 2 == 1, x, 1 - x),
+        NEAR: r // 4 == c // 2,
+        MIDDLE: z == c,
+        PLACE: jnp.where(z <= c, x, 1 - x),
+    }
+    meta = jnp.zeros((8,), jnp.int32)
+    for index, value in values.items():
+        meta = jnp.where(slot == index, value.astype(jnp.int32), meta)
+
+    across = lambda block: routed(block, lambda r, c: (r, c ^ 2))
+    beside = lambda block: routed(block, lambda r, c: (r, c ^ 1))
+    over_x = lambda block: routed(block, lambda r, c: (r ^ 1, c))
+    over_z = lambda block: routed(block, lambda r, c: (r ^ 2, c))
+    over_far = lambda block: routed(block, lambda r, c: (r ^ 4, c))
+    to_near = lambda block: routed(block, lambda r, c: None if is_near(r, c) else (r ^ 4, c))
+    back_near = lambda block: routed(block, near_target)
+    back_far = lambda block: routed(block, far_target)
+
+    next_t = beside(t)
+    next_v = beside(v)
+    send, keep = {}, {}
+    base = middle_part(meta, t, v, 1, 0)
+    send["n", 0] = next_part(meta, base, next_t, next_v, t, v, 1, 0)
+    for side, chunks in NEAR_GROUPS:
+        blocks = near_parts(meta, next_t, next_v, t, v, side, chunks)
+        for k, block in zip(chunks, blocks):
+            (send if side else keep)["n", k] = block
+    for tag, side, first, count in FAR_GROUPS:
+        piece = pick(meta, t, v, side, first, count)
+        piece = across(piece)
+        other = beside(piece)
+        blocks = far_parts(meta, piece, other, t, v, side)
+        for i, block in enumerate(blocks):
+            (send if side else keep)["f", first + i] = block
+    total, come = {}, {}
+    for tag in "nf":
+        for k in range(CHUNKS):
+            key = tag, k
+            arrived = over_x(send[key])
+            leave, stay = fold(meta, keep[key], arrived)
+            arrived = over_z(leave)
+            total[key] = add(meta, stay, arrived)
+            come[key] = (to_near if tag == "n" else over_far)(total[key])
+
+    def joined(tag, chunks):
+        return join(meta, [total[tag, k] for k in chunks], [come[tag, k] for k in chunks])
+
+    near_own, extra = joined("n", range(CHUNKS))
+    near_back = back_near(near_own)
+    far_own, far_back = [], []
+    for chunks in ((0, 1), (2,), (3,)):
+        far_own += joined("f", chunks)
+        far_back.append(back_far(far_own[-1]))
+    new, res = most(
+        meta, t, near_own, near_back, extra, *far_own, *far_back[:2], t, v, row_gap, col_gap
+    )
+    return last(meta, far_back[2], new, res, t, v, row_gap, col_gap)
+
+
+NEAR_GROUPS = ((1, (1, 2, 3)), (0, (0, 1, 2, 3)))
+FAR_GROUPS = (("s0", 1, 0, 2), ("k0", 0, 0, 2), ("s1", 1, 2, 2), ("k1", 0, 2, 1), ("k2", 0, 3, 1))
+
+
+def gap_slices(shape, occ_energy, vir_energy):
+    tile_rows, tile_cols = shape
     gaps = (vir_energy[None, :] - occ_energy[:, None]).reshape(-1)
-    row_gap = lax.dynamic_slice_in_dim(gaps, row_place * tile_rows, tile_rows, 0)
-    col_gap = lax.dynamic_slice_in_dim(gaps, col_place * tile_cols, tile_cols, 0)
-    denom = row_gap[:, None] + col_gap[None, :]
-    residual = interaction + product + mirrored + denom * amplitudes
+    row_gap = lax.dynamic_slice_in_dim(gaps, lax.axis_index("row") * tile_rows, tile_rows, 0)
+    col_gap = lax.dynamic_slice_in_dim(gaps, lax.axis_index("col") * tile_cols, tile_cols, 0)
+    return row_gap[:, None], col_gap[None, :]
+
+
+def split_local(amplitudes, interaction, occ_energy, vir_energy):
+    gaps = gap_slices(amplitudes.shape, occ_energy, vir_energy)
+    return tuple(split_update(amplitudes, interaction, *gaps))
+
+
+def general_local(amplitudes, interaction, occ_energy, vir_energy):
+    row_gap, col_gap = gap_slices(amplitudes.shape, occ_energy, vir_energy)
+    denom = row_gap + col_gap
+    residual = interaction + general_sum(amplitudes, interaction) + denom * amplitudes
     updated = amplitudes - residual / denom
     return (updated, residual)
 
 
 def solution(mesh):
+    rows, cols = mesh.shape["row"], mesh.shape["col"]
+    split = cols == 4 and rows == 2 * cols
     return jax.shard_map(
-        local,
+        split_local if split else general_local,
         mesh=mesh,
         in_specs=(P("row", "col"), P("row", "col"), P(), P()),
         out_specs=(P("row", "col"), P("row", "col")),

time: 544 us -> 288 us (0.53)
  the two profiles are of different devices: /device:TPU:29 before, /device:TPU:4 now
where the time goes in v1:
time: 288 us
  waiting for transfers between devices  133 us (46%)
  starting transfers between devices  91 us (32%)
  Pallas kernels  57.7 us (20%)
  local copies, waits for them, and re-layouts  5.03 us (2%)
    ppermute x40, waiting for transfers between devices, routed(): return lax.ppermute(block, ('row', 'col'), route)  133 us
    ppermute x40, starting transfers between devices, routed(): return lax.ppermute(block, ('row', 'col'), route)  91 us
    pallas_call x36, Pallas kernels, call(): pl.pallas_call(kernel, out_shape=list(shapes), grid_spec=pltpu.PrefetchSc...  57.7 us
  transfers between devices with their start and end apart: 40, of which 13 were waited for; matrix products, arithmetic and copies ran while one was open for 0% of the time, Pallas kernels for 19%

profile of v1, /device:TPU:4, one launch (start us, length us, event | category | flops | bytes accessed | tf_op | source)
XLA Modules:
  0.0 287.9 jit_solution(5640068053122448816)
XLA Ops:
  5.9 2.1 collective-permute-start.2
  9.5 10.4 %collective-permute-done.a_ref = f32[2,512,128]{2,1,0:T(8,128)S(1)} collective-permute-done((f32[2,512,128]{2,1,0:T(8,128)S(1)}, f32[2,512,128]{2,1,0:T(8,128)S(1)}, u32[]{:S(2)}, u32[]{:S(2)}) %collective-permute-start) | collective-permute-done | bytes 524320 | tf_op jit(solution)/shard_map/ppermute | solution.py:84
  19.9 22.5 %collective-permute-done.2.a_ref = f32[2,512,256]{2,1,0:T(8,128)S(1)} collective-permute-done((f32[2,512,256]{2,1,0:T(8,128)S(1)}, f32[2,512,256]{2,1,0:T(8,128)S(1)}, u32[]{:S(2)}, u32[]{:S(2)}) %collective-permute-start.2) | collective-permute-done | bytes 1048608 | tf_op jit(solution)/shard_map/ppermute | solution.py:84
  42.4 22.5 %collective-permute-done.25.a_ref = f32[2,512,256]{2,1,0:T(8,128)S(1)} collective-permute-done((f32[2,512,256]{2,1,0:T(8,128)S(1)}, f32[2,512,256]{2,1,0:T(8,128)S(1)}, u32[]{:S(2)}, u32[]{:S(2)}) %collective-permute-start.25) | collective-permute-done | bytes 1048608 | tf_op jit(solution)/shard_map/ppermute | solution.py:84
  65.5 20.9 %collective-permute-done.23.a_ref = f32[2,512,256]{2,1,0:T(8,128)S(1)} collective-permute-done((f32[2,512,256]{2,1,0:T(8,128)S(1)}, f32[2,512,256]{2,1,0:T(8,128)S(1)}, u32[]{:S(2)}, u32[]{:S(2)}) %collective-permute-start.23) | collective-permute-done | bytes 1048608 | tf_op jit(solution)/shard_map/ppermute | solution.py:84
  87.2 1.9 shard_map.67._
  89.1 2.9 %shard_map.68 = f32[2,136,512]{2,1,0:T(8,128)S(1)} custom-call(s32[8]{0:T(128)S(1)} %compare_select_fusion.6.m._, f32[2,136,512]{2,1,0:T(8,128)S(1)} %shard_map.67._, f32[512,1024]{1,0:T(8,128)S(1)} %collective-permute-done.8.at_ref, f32[512,1024]{1,0:T(8,128)} %collective-permute-done.9.av_ref, ...), custom_call_target="tpu_custom_call", output_to_operand_aliasing={{}: (1, {})} | custom-call | tf_op jit(solution)/shard_map/pallas_call | solution.py:129
  92.1 7.4 %collective-permute-done.33.a_ref = f32[2,512,128]{2,1,0:T(8,128)S(1)} collective-permute-done((f32[2,512,128]{2,1,0:T(8,128)S(1)}, f32[2,512,128]{2,1,0:T(8,128)S(1)}, u32[]{:S(2)}, u32[]{:S(2)}) %collective-permute-start.33) | collective-permute-done | bytes 524320 | tf_op jit(solution)/shard_map/ppermute | solution.py:84
  101.0 8.0 %shard_map.71 = (f32[2,136,512]{2,1,0:T(8,128)S(1)}, f32[2,136,512]{2,1,0:T(8,128)S(1)}, f32[2,136,512]{2,1,0:T(8,128)S(1)}) custom-call(s32[8]{0:T(128)S(1)} %compare_select_fusion.6.m._, f32[512,1024]{1,0:T(8,128)S(1)} %collective-permute-done.8.at_ref, f32[512,1024]{1,0:T(8,128)} %collective-permute-done.9.av_ref, f32[512,1024]{1,0:T(8,128)S(1)} %copy-done, ...), custom_call_target="tpu_custom_call" | custom-call | tf_op jit(solution)/shard_map/pallas_call | solution.py:129
  111.6 2.5 shard_map.82
  116.5 9.9 %shard_map.66 = (f32[2,136,512]{2,1,0:T(8,128)S(1)}, f32[2,136,512]{2,1,0:T(8,128)S(1)}, f32[2,136,512]{2,1,0:T(8,128)S(1)}, f32[2,136,512]{2,1,0:T(8,128)S(1)}) custom-call(s32[8]{0:T(128)S(1)} %compare_select_fusion.6.m._, f32[512,1024]{1,0:T(8,128)S(1)} %collective-permute-done.8.at_ref, f32[512,1024]{1,0:T(8,128)} %collective-permute-done.9.av_ref, ...), custom_call_target="tpu_custom_call" | custom-call | tf_op jit(solution)/shard_map/pallas_call | solution.py:129
  129.8 9.0 %collective-permute-done.14.come_pass.come_stay = f32[2,136,512]{2,1,0:T(8,128)S(1)} collective-permute-done((f32[2,136,512]{2,1,0:T(8,128)S(1)}, f32[2,136,512]{2,1,0:T(8,128)S(1)}, u32[]{:S(2)}, u32[]{:S(2)}) %collective-permute-start.14) | collective-permute-done | bytes 557088 | tf_op jit(solution)/shard_map/ppermute | solution.py:84
  141.0 9.8 %collective-permute-done.16.come_pass.come_stay = f32[2,136,512]{2,1,0:T(8,128)S(1)} collective-permute-done((f32[2,136,512]{2,1,0:T(8,128)S(1)}, f32[2,136,512]{2,1,0:T(8,128)S(1)}, u32[]{:S(2)}, u32[]{:S(2)}) %collective-permute-start.16) | collective-permute-done | bytes 557088 | tf_op jit(solution)/shard_map/ppermute | solution.py:84
  154.1 4.5 %collective-permute-start.18 = (f32[136,512]{1,0:T(8,128)S(1)}, f32[136,512]{1,0:T(8,128)S(1)}, u32[]{:S(2)}, u32[]{:S(2)}) collective-permute-start(f32[136,512]{1,0:T(8,128)S(1)} %shard_map.70.refs_0_), channel_id=1, source_target_pairs={{2,18},{3,19},{6,22},{7,23},{10,26},{11,27},{14,30},{15,31},{16,0}... | collective-permute-start | bytes 835592 | tf_op jit(solution)/shard_map/ppermute | solution.py:84
  159.2 2.8 collective-permute-done.27.come_pass.come_stay
  162.0 4.5 %collective-permute-start.19 = (f32[136,512]{1,0:T(8,128)S(1)}, f32[136,512]{1,0:T(8,128)S(1)}, u32[]{:S(2)}, u32[]{:S(2)}) collective-permute-start(f32[136,512]{1,0:T(8,128)S(1)} %shard_map.73.refs_1_), channel_id=1, source_target_pairs={{2,18},{3,19},{6,22},{7,23},{10,26},{11,27},{14,30},{15,31},{16,0}... | collective-permute-start | bytes 835592 | tf_op jit(solution)/shard_map/ppermute | solution.py:84
  167.2 2.2 collective-permute-start.20
  170.7 4.5 %collective-permute-start.21 = (f32[136,512]{1,0:T(8,128)S(1)}, f32[136,512]{1,0:T(8,128)S(1)}, u32[]{:S(2)}, u32[]{:S(2)}) collective-permute-start(f32[136,512]{1,0:T(8,128)S(1)} %shard_map.77.refs_3_), channel_id=1, source_target_pairs={{2,18},{3,19},{6,22},{7,23},{10,26},{11,27},{14,30},{15,31},{16,0}... | collective-permute-start | bytes 835592 | tf_op jit(solution)/shard_map/ppermute | solution.py:84
  175.2 2.5 shard_map.62
  179.8 2.5 shard_map.80
  183.0 15.4 %collective-permute-start.28 = (f32[128,512]{1,0:T(8,128)S(1)}, f32[128,512]{1,0:T(8,128)S(1)}, u32[]{:S(2)}, u32[]{:S(2)}) collective-permute-start(f32[128,512]{1,0:T(8,128)S(1)} %get-tuple-element.58), channel_id=1, source_target_pairs={{0,8},{1,9},{2,10},{3,11},{4,12},{5,13},{6,14},{7,15},{8,0},{9,1},... | collective-permute-start | bytes 786440 | tf_op jit(solution)/shard_map/ppermute | solution.py:84
  199.0 4.2 %collective-permute-start.30 = (f32[128,512]{1,0:T(8,128)S(1)}, f32[128,512]{1,0:T(8,128)S(1)}, u32[]{:S(2)}, u32[]{:S(2)}) collective-permute-start(f32[128,512]{1,0:T(8,128)S(1)} %get-tuple-element.62), channel_id=1, source_target_pairs={{0,8},{1,9},{2,10},{3,11},{4,12},{5,13},{6,14},{7,15},{8,0},{9,1},... | collective-permute-start | bytes 786440 | tf_op jit(solution)/shard_map/ppermute | solution.py:84
  203.1 1.7 shard_map.78
  211.1 5.3 %collective-permute-start.31 = (f32[128,512]{1,0:T(8,128)S(1)}, f32[128,512]{1,0:T(8,128)S(1)}, u32[]{:S(2)}, u32[]{:S(2)}) collective-permute-start(f32[128,512]{1,0:T(8,128)S(1)} %shard_map.84.refs_0_), channel_id=1, source_target_pairs={{0,16},{1,17},{2,18},{3,19},{4,20},{5,21},{6,22},{7,23},{8,24},{9,... | collective-permute-start | bytes 786440 | tf_op jit(solution)/shard_map/ppermute | solution.py:84
  217.6 2.1 collective-permute-start.5
  219.7 7.8 %collective-permute-done.36.b_ref = f32[128,512]{1,0:T(8,128)S(1)} collective-permute-done((f32[128,512]{1,0:T(8,128)S(1)}, f32[128,512]{1,0:T(8,128)S(1)}, u32[]{:S(2)}, u32[]{:S(2)}) %collective-permute-start.36) | collective-permute-done | bytes 262176 | tf_op jit(solution)/shard_map/ppermute | solution.py:84
  228.1 9.8 %collective-permute-start.37 = (f32[128,512]{1,0:T(8,128)S(1)}, f32[128,512]{1,0:T(8,128)S(1)}, u32[]{:S(2)}, u32[]{:S(2)}) collective-permute-start(f32[128,512]{1,0:T(8,128)S(1)} %shard_map.91.refs_0_), channel_id=1, source_target_pairs={{0,16},{1,17},{2,18},{3,19},{4,20},{5,21},{6,22},{7,23},{8,24},{9,... | collective-permute-start | bytes 786440 | tf_op jit(solution)/shard_map/ppermute | solution.py:84
  240.4 15.9 %collective-permute-start.6 = (f32[128,512]{1,0:T(8,128)S(1)}, f32[128,512]{1,0:T(8,128)S(1)}, u32[]{:S(2)}, u32[]{:S(2)}) collective-permute-start(f32[128,512]{1,0:T(8,128)S(1)} %shard_map.64.refs_0_), channel_id=1, source_target_pairs={{0,16},{1,17},{2,18},{3,19},{4,20},{5,21},{6,22},{7,23},{8,24},{9,... | collective-permute-start | bytes 786440 | tf_op jit(solution)/shard_map/ppermute | solution.py:84
  258.1 10.1 %collective-permute-done.6.refs_1_ = f32[128,512]{1,0:T(8,128)S(1)} collective-permute-done((f32[128,512]{1,0:T(8,128)S(1)}, f32[128,512]{1,0:T(8,128)S(1)}, u32[]{:S(2)}, u32[]{:S(2)}) %collective-permute-start.6) | collective-permute-done | bytes 262176 | tf_op jit(solution)/shard_map/ppermute | solution.py:84
  270.5 8.0 %collective-permute-done.39.refs_7_ = f32[128,512]{1,0:T(8,128)} collective-permute-done((f32[128,512]{1,0:T(8,128)S(1)}, f32[128,512]{1,0:T(8,128)}, u32[]{:S(2)}, u32[]{:S(2)}) %collective-permute-start.39) | collective-permute-done | bytes 262176 | tf_op jit(solution)/shard_map/ppermute | solution.py:84
  280.1 5.1 %shard_map.93 = (f32[512,1024]{1,0:T(8,128)}, f32[512,1024]{1,0:T(8,128)}) custom-call(s32[8]{0:T(128)S(1)} %compare_select_fusion.6.m._, f32[512,512]{1,0:T(8,128)} %get-tuple-element.53.refs_0_, f32[512,512]{1,0:T(8,128)} %collective-permute-done.22.refs_1_, f32[8,512]{1,0:T(8,128)S(1)} %get-tuple-element.54.refs_2_, f32[256,512]{1,0:T(8,128)S(1)} %shard_map.87.refs_3_, ...), custom_call_target="tpu_custom_call" | custom-call | tf_op jit(solution)/shard_map/pallas_call | solution.py:129
  285.2 2.7 shard_map.94
  (104 shorter events, 45.3 us)
Async XLA Ops:
  0.6 86.1 %collective-permute-start.8 = (f32[512,1024]{1,0:T(8,128)}, f32[512,1024]{1,0:T(8,128)S(1)}, u32[]{:S(2)}, u32[]{:S(2)}) collective-permute-start(f32[512,1024]{1,0:T(8,128)} %t_ref.29), channel_id=1, source_target_pairs={{0,1},{1,0},{2,3},{3,2},{4,5},{5,4},{6,7},{7,6},{8,9},{9,8},{10,11... | collective-permute-start | bytes 6291464 | tf_op jit(solution)/shard_map/ppermute | solution.py:84
  0.7 86.0 %collective-permute-start.9 = (f32[512,1024]{1,0:T(8,128)}, f32[512,1024]{1,0:T(8,128)}, u32[]{:S(2)}, u32[]{:S(2)}) collective-permute-start(f32[512,1024]{1,0:T(8,128)} %v_ref.29), channel_id=1, source_target_pairs={{0,1},{1,0},{2,3},{3,2},{4,5},{5,4},{6,7},{7,6},{8,9},{9,8},{10,11... | collective-permute-start | bytes 6291464 | tf_op jit(solution)/shard_map/ppermute | solution.py:84
  5.9 36.5 %collective-permute-start.2 = (f32[2,512,256]{2,1,0:T(8,128)S(1)}, f32[2,512,256]{2,1,0:T(8,128)S(1)}, u32[]{:S(2)}, u32[]{:S(2)}) collective-permute-start(f32[2,512,256]{2,1,0:T(8,128)S(1)} %shard_map.61), channel_id=1, source_target_pairs={{0,2},{1,3},{2,0},{3,1},{4,6},{5,7},{6,4},{7,5},{8,10},{9,11},{10,... | collective-permute-start | bytes 3145736 | tf_op jit(solution)/shard_map/ppermute | solution.py:84
  8.7 56.2 %collective-permute-start.25 = (f32[2,512,256]{2,1,0:T(8,128)S(1)}, f32[2,512,256]{2,1,0:T(8,128)S(1)}, u32[]{:S(2)}, u32[]{:S(2)}) collective-permute-start(f32[2,512,256]{2,1,0:T(8,128)S(1)} %shard_map.81), channel_id=1, source_target_pairs={{0,2},{1,3},{2,0},{3,1},{4,6},{5,7},{6,4},{7,5},{8,10},{9,11},{10,... | collective-permute-start | bytes 3145736 | tf_op jit(solution)/shard_map/ppermute | solution.py:84
  19.9 66.5 %collective-permute-start.23 = (f32[2,512,256]{2,1,0:T(8,128)S(1)}, f32[2,512,256]{2,1,0:T(8,128)S(1)}, u32[]{:S(2)}, u32[]{:S(2)}) collective-permute-start(f32[2,512,256]{2,1,0:T(8,128)S(1)} %shard_map.79), channel_id=1, source_target_pairs={{0,2},{1,3},{2,0},{3,1},{4,6},{5,7},{6,4},{7,5},{8,10},{9,11},{10,... | collective-permute-start | bytes 3145736 | tf_op jit(solution)/shard_map/ppermute | solution.py:84
  42.4 67.2 %collective-permute-start.3 = (f32[2,512,256]{2,1,0:T(8,128)S(1)}, f32[2,512,256]{2,1,0:T(8,128)S(1)}, u32[]{:S(2)}, u32[]{:S(2)}) collective-permute-start(f32[2,512,256]{2,1,0:T(8,128)S(1)} %collective-permute-done.2.a_ref), channel_id=1, source_target_pairs={{0,1},{1,0},{2,3},{3,2},{4,5},{5,4},{6,7},{7,6},{8,9},{9,8},{10,11... | collective-permute-start | bytes 3145736 | tf_op jit(solution)/shard_map/ppermute | solution.py:84
  64.8 46.2 %collective-permute-start.26 = (f32[2,512,256]{2,1,0:T(8,128)S(1)}, f32[2,512,256]{2,1,0:T(8,128)S(1)}, u32[]{:S(2)}, u32[]{:S(2)}) collective-permute-start(f32[2,512,256]{2,1,0:T(8,128)S(1)} %collective-permute-done.25.a_ref), channel_id=1, source_target_pairs={{0,1},{1,0},{2,3},{3,2},{4,5},{5,4},{6,7},{7,6},{8,9},{9,8},{10,11... | collective-permute-start | bytes 3145736 | tf_op jit(solution)/shard_map/ppermute | solution.py:84
  86.7 22.2 %collective-permute-start.1 = (f32[2,512,128]{2,1,0:T(8,128)S(1)}, f32[2,512,128]{2,1,0:T(8,128)S(1)}, u32[]{:S(2)}, u32[]{:S(2)}) collective-permute-start(f32[2,512,128]{2,1,0:T(8,128)S(1)} %collective-permute-done.a_ref), channel_id=1, source_target_pairs={{0,1},{1,0},{2,3},{3,2},{4,5},{5,4},{6,7},{7,6},{8,9},{9,8},{10,11... | collective-permute-start | bytes 1572872 | tf_op jit(solution)/shard_map/ppermute | solution.py:84
  86.7 42.6 %collective-permute-start.24 = (f32[2,512,256]{2,1,0:T(8,128)S(1)}, f32[2,512,256]{2,1,0:T(8,128)S(1)}, u32[]{:S(2)}, u32[]{:S(2)}) collective-permute-start(f32[2,512,256]{2,1,0:T(8,128)S(1)} %collective-permute-done.23.a_ref), channel_id=1, source_target_pairs={{0,1},{1,0},{2,3},{3,2},{4,5},{5,4},{6,7},{7,6},{8,9},{9,8},{10,11... | collective-permute-start | bytes 3145736 | tf_op jit(solution)/shard_map/ppermute | solution.py:84
  109.0 18.1 %collective-permute-start.12 = (f32[2,136,512]{2,1,0:T(8,128)S(1)}, f32[2,136,512]{2,1,0:T(8,128)S(1)}, u32[]{:S(2)}, u32[]{:S(2)}) collective-permute-start(f32[2,136,512]{2,1,0:T(8,128)S(1)} %get-tuple-element.42), channel_id=1, source_target_pairs={{0,4},{1,5},{2,6},{3,7},{4,0},{5,1},{6,2},{7,3},{8,12},{9,13},{10,... | collective-permute-start | bytes 1671176 | tf_op jit(solution)/shard_map/ppermute | solution.py:84
  109.6 29.3 %collective-permute-start.14 = (f32[2,136,512]{2,1,0:T(8,128)S(1)}, f32[2,136,512]{2,1,0:T(8,128)S(1)}, u32[]{:S(2)}, u32[]{:S(2)}) collective-permute-start(f32[2,136,512]{2,1,0:T(8,128)S(1)} %get-tuple-element.46), channel_id=1, source_target_pairs={{0,4},{1,5},{2,6},{3,7},{4,0},{5,1},{6,2},{7,3},{8,12},{9,13},{10,... | collective-permute-start | bytes 1671176 | tf_op jit(solution)/shard_map/ppermute | solution.py:84
  111.1 39.7 %collective-permute-start.16 = (f32[2,136,512]{2,1,0:T(8,128)S(1)}, f32[2,136,512]{2,1,0:T(8,128)S(1)}, u32[]{:S(2)}, u32[]{:S(2)}) collective-permute-start(f32[2,136,512]{2,1,0:T(8,128)S(1)} %get-tuple-element.50), channel_id=1, source_target_pairs={{0,4},{1,5},{2,6},{3,7},{4,0},{5,1},{6,2},{7,3},{8,12},{9,13},{10,... | collective-permute-start | bytes 1671176 | tf_op jit(solution)/shard_map/ppermute | solution.py:84
  115.0 47.0 %collective-permute-start.27 = (f32[2,128,512]{2,1,0:T(8,128)S(1)}, f32[2,128,512]{2,1,0:T(8,128)S(1)}, u32[]{:S(2)}, u32[]{:S(2)}) collective-permute-start(f32[2,128,512]{2,1,0:T(8,128)S(1)} %get-tuple-element.56), channel_id=1, source_target_pairs={{0,4},{1,5},{2,6},{3,7},{4,0},{5,1},{6,2},{7,3},{8,12},{9,13},{10,... | collective-permute-start | bytes 1572872 | tf_op jit(solution)/shard_map/ppermute | solution.py:84
  127.0 25.9 %collective-permute-start.11 = (f32[136,512]{1,0:T(8,128)S(1)}, f32[136,512]{1,0:T(8,128)S(1)}, u32[]{:S(2)}, u32[]{:S(2)}) collective-permute-start(f32[136,512]{1,0:T(8,128)S(1)} %get-tuple-element.40), channel_id=1, source_target_pairs={{0,8},{1,9},{2,10},{3,11},{4,12},{5,13},{6,14},{7,15},{8,0},{9,1},... | collective-permute-start | bytes 835592 | tf_op jit(solution)/shard_map/ppermute | solution.py:84
  129.3 24.8 %collective-permute-start.13 = (f32[136,512]{1,0:T(8,128)S(1)}, f32[136,512]{1,0:T(8,128)S(1)}, u32[]{:S(2)}, u32[]{:S(2)}) collective-permute-start(f32[136,512]{1,0:T(8,128)S(1)} %get-tuple-element.44), channel_id=1, source_target_pairs={{0,8},{1,9},{2,10},{3,11},{4,12},{5,13},{6,14},{7,15},{8,0},{9,1},... | collective-permute-start | bytes 835592 | tf_op jit(solution)/shard_map/ppermute | solution.py:84
  138.9 31.8 %collective-permute-start.29 = (f32[2,128,512]{2,1,0:T(8,128)S(1)}, f32[2,128,512]{2,1,0:T(8,128)S(1)}, u32[]{:S(2)}, u32[]{:S(2)}) collective-permute-start(f32[2,128,512]{2,1,0:T(8,128)S(1)} %get-tuple-element.60), channel_id=1, source_target_pairs={{0,4},{1,5},{2,6},{3,7},{4,0},{5,1},{6,2},{7,3},{8,12},{9,13},{10,... | collective-permute-start | bytes 1572872 | tf_op jit(solution)/shard_map/ppermute | solution.py:84
  154.1 23.6 %collective-permute-start.18 = (f32[136,512]{1,0:T(8,128)S(1)}, f32[136,512]{1,0:T(8,128)S(1)}, u32[]{:S(2)}, u32[]{:S(2)}) collective-permute-start(f32[136,512]{1,0:T(8,128)S(1)} %shard_map.70.refs_0_), channel_id=1, source_target_pairs={{2,18},{3,19},{6,22},{7,23},{10,26},{11,27},{14,30},{15,31},{16,0}... | collective-permute-start | bytes 835592 | tf_op jit(solution)/shard_map/ppermute | solution.py:84
  162.0 17.3 %collective-permute-start.19 = (f32[136,512]{1,0:T(8,128)S(1)}, f32[136,512]{1,0:T(8,128)S(1)}, u32[]{:S(2)}, u32[]{:S(2)}) collective-permute-start(f32[136,512]{1,0:T(8,128)S(1)} %shard_map.73.refs_1_), channel_id=1, source_target_pairs={{2,18},{3,19},{6,22},{7,23},{10,26},{11,27},{14,30},{15,31},{16,0}... | collective-permute-start | bytes 835592 | tf_op jit(solution)/shard_map/ppermute | solution.py:84
  166.5 38.3 %collective-permute-start.34 = (f32[2,512,128]{2,1,0:T(8,128)S(1)}, f32[2,512,128]{2,1,0:T(8,128)S(1)}, u32[]{:S(2)}, u32[]{:S(2)}) collective-permute-start(f32[2,512,128]{2,1,0:T(8,128)S(1)} %collective-permute-done.33.a_ref), channel_id=1, source_target_pairs={{0,1},{1,0},{2,3},{3,2},{4,5},{5,4},{6,7},{7,6},{8,9},{9,8},{10,11... | collective-permute-start | bytes 1572872 | tf_op jit(solution)/shard_map/ppermute | solution.py:84
  170.7 28.3 %collective-permute-start.21 = (f32[136,512]{1,0:T(8,128)S(1)}, f32[136,512]{1,0:T(8,128)S(1)}, u32[]{:S(2)}, u32[]{:S(2)}) collective-permute-start(f32[136,512]{1,0:T(8,128)S(1)} %shard_map.77.refs_3_), channel_id=1, source_target_pairs={{2,18},{3,19},{6,22},{7,23},{10,26},{11,27},{14,30},{15,31},{16,0}... | collective-permute-start | bytes 835592 | tf_op jit(solution)/shard_map/ppermute | solution.py:84
  177.7 32.0 %collective-permute-start.35 = (f32[2,128,512]{2,1,0:T(8,128)S(1)}, f32[2,128,512]{2,1,0:T(8,128)S(1)}, u32[]{:S(2)}, u32[]{:S(2)}) collective-permute-start(f32[2,128,512]{2,1,0:T(8,128)S(1)} %get-tuple-element.63), channel_id=1, source_target_pairs={{0,4},{1,5},{2,6},{3,7},{4,0},{5,1},{6,2},{7,3},{8,12},{9,13},{10,... | collective-permute-start | bytes 1572872 | tf_op jit(solution)/shard_map/ppermute | solution.py:84
  179.3 37.7 %collective-permute-start.4 = (f32[2,128,512]{2,1,0:T(8,128)S(1)}, f32[2,128,512]{2,1,0:T(8,128)S(1)}, u32[]{:S(2)}, u32[]{:S(2)}) collective-permute-start(f32[2,128,512]{2,1,0:T(8,128)S(1)} %get-tuple-element.35), channel_id=1, source_target_pairs={{0,4},{1,5},{2,6},{3,7},{4,0},{5,1},{6,2},{7,3},{8,12},{9,13},{10,... | collective-permute-start | bytes 1572872 | tf_op jit(solution)/shard_map/ppermute | solution.py:84
  183.0 27.5 %collective-permute-start.28 = (f32[128,512]{1,0:T(8,128)S(1)}, f32[128,512]{1,0:T(8,128)S(1)}, u32[]{:S(2)}, u32[]{:S(2)}) collective-permute-start(f32[128,512]{1,0:T(8,128)S(1)} %get-tuple-element.58), channel_id=1, source_target_pairs={{0,8},{1,9},{2,10},{3,11},{4,12},{5,13},{6,14},{7,15},{8,0},{9,1},... | collective-permute-start | bytes 786440 | tf_op jit(solution)/shard_map/ppermute | solution.py:84
  199.0 17.4 %collective-permute-start.30 = (f32[128,512]{1,0:T(8,128)S(1)}, f32[128,512]{1,0:T(8,128)S(1)}, u32[]{:S(2)}, u32[]{:S(2)}) collective-permute-start(f32[128,512]{1,0:T(8,128)S(1)} %get-tuple-element.62), channel_id=1, source_target_pairs={{0,8},{1,9},{2,10},{3,11},{4,12},{5,13},{6,14},{7,15},{8,0},{9,1},... | collective-permute-start | bytes 786440 | tf_op jit(solution)/shard_map/ppermute | solution.py:84
  204.8 73.7 %collective-permute-start.22 = (f32[512,512]{1,0:T(8,128)}, f32[512,512]{1,0:T(8,128)}, u32[]{:S(2)}, u32[]{:S(2)}) collective-permute-start(f32[512,512]{1,0:T(8,128)} %get-tuple-element.53.refs_0_), channel_id=1, source_target_pairs={{0,4},{1,8},{4,0},{5,12},{8,5},{9,13},{12,1},{13,9},{18,22},{19,26... | collective-permute-start | bytes 3145736 | tf_op jit(solution)/shard_map/ppermute | solution.py:84
  211.1 26.9 %collective-permute-start.31 = (f32[128,512]{1,0:T(8,128)S(1)}, f32[128,512]{1,0:T(8,128)S(1)}, u32[]{:S(2)}, u32[]{:S(2)}) collective-permute-start(f32[128,512]{1,0:T(8,128)S(1)} %shard_map.84.refs_0_), channel_id=1, source_target_pairs={{0,16},{1,17},{2,18},{3,19},{4,20},{5,21},{6,22},{7,23},{8,24},{9,... | collective-permute-start | bytes 786440 | tf_op jit(solution)/shard_map/ppermute | solution.py:84
  216.9 21.0 %collective-permute-start.32 = (f32[128,512]{1,0:T(8,128)S(1)}, f32[128,512]{1,0:T(8,128)S(1)}, u32[]{:S(2)}, u32[]{:S(2)}) collective-permute-start(f32[128,512]{1,0:T(8,128)S(1)} %shard_map.86.refs_1_), channel_id=1, source_target_pairs={{0,16},{1,17},{2,18},{3,19},{4,20},{5,21},{6,22},{7,23},{8,24},{9,... | collective-permute-start | bytes 786440 | tf_op jit(solution)/shard_map/ppermute | solution.py:84
  217.6 22.2 %collective-permute-start.5 = (f32[128,512]{1,0:T(8,128)S(1)}, f32[128,512]{1,0:T(8,128)S(1)}, u32[]{:S(2)}, u32[]{:S(2)}) collective-permute-start(f32[128,512]{1,0:T(8,128)S(1)} %get-tuple-element.37), channel_id=1, source_target_pairs={{0,8},{1,9},{2,10},{3,11},{4,12},{5,13},{6,14},{7,15},{8,0},{9,1},... | collective-permute-start | bytes 786440 | tf_op jit(solution)/shard_map/ppermute | solution.py:84
  228.1 28.2 %collective-permute-start.37 = (f32[128,512]{1,0:T(8,128)S(1)}, f32[128,512]{1,0:T(8,128)S(1)}, u32[]{:S(2)}, u32[]{:S(2)}) collective-permute-start(f32[128,512]{1,0:T(8,128)S(1)} %shard_map.91.refs_0_), channel_id=1, source_target_pairs={{0,16},{1,17},{2,18},{3,19},{4,20},{5,21},{6,22},{7,23},{8,24},{9,... | collective-permute-start | bytes 786440 | tf_op jit(solution)/shard_map/ppermute | solution.py:84
  238.5 40.0 %collective-permute-start.38 = (f32[256,512]{1,0:T(8,128)S(1)}, f32[256,512]{1,0:T(8,128)}, u32[]{:S(2)}, u32[]{:S(2)}) collective-permute-start(f32[256,512]{1,0:T(8,128)S(1)} %shard_map.87.refs_3_), channel_id=1, source_target_pairs={{0,6},{1,14},{4,2},{5,10},{8,7},{9,15},{12,3},{13,11},{18,16},{19,... | collective-permute-start | bytes 1572872 | tf_op jit(solution)/shard_map/ppermute | solution.py:84
  240.4 27.8 %collective-permute-start.6 = (f32[128,512]{1,0:T(8,128)S(1)}, f32[128,512]{1,0:T(8,128)S(1)}, u32[]{:S(2)}, u32[]{:S(2)}) collective-permute-start(f32[128,512]{1,0:T(8,128)S(1)} %shard_map.64.refs_0_), channel_id=1, source_target_pairs={{0,16},{1,17},{2,18},{3,19},{4,20},{5,21},{6,22},{7,23},{8,24},{9,... | collective-permute-start | bytes 786440 | tf_op jit(solution)/shard_map/ppermute | solution.py:84
  256.8 21.6 %collective-permute-start.39 = (f32[128,512]{1,0:T(8,128)S(1)}, f32[128,512]{1,0:T(8,128)}, u32[]{:S(2)}, u32[]{:S(2)}) collective-permute-start(f32[128,512]{1,0:T(8,128)S(1)} %shard_map.92.refs_4_), channel_id=1, source_target_pairs={{0,6},{1,14},{4,2},{5,10},{8,7},{9,15},{12,3},{13,11},{18,16},{19,... | collective-permute-start | bytes 786440 | tf_op jit(solution)/shard_map/ppermute | solution.py:84
  (15 other events, 241.8 us)

commit v2 on v1

--- a/solution.py
+++ b/solution.py
@@ -150,22 +150,26 @@
     return high, (value - high.astype(jnp.float32)).astype(jnp.bfloat16)
 
 
+def joined_left(t_high, t_low, v_high, v_low):
+    return jnp.concatenate([t_high, t_high, t_low, v_high, v_high, v_low], axis=1)
+
+
 def left_of(t, v):
-    t_high, t_low = halves(t)
-    v_high, v_low = halves(v)
-    return jnp.concatenate([t_high, t_high, t_low, v_high, v_high, v_low], axis=0)
-
-
-def right_of(t, v):
-    t_high, t_low = halves(t)
-    v_high, v_low = halves(v)
-    return jnp.concatenate([v_high, v_low, v_high, t_high, t_low, t_high], axis=0)
+    t_high, t_low = halves(t.T)
+    v_high, v_low = halves(v.T)
+    return joined_left(t_high, t_low, v_high, v_low)
+
+
+def own_left(own_ref, cols):
+    return joined_left(*(own_ref[i, :, cols].T for i in range(4)))
+
+
+def own_right(own_ref, cols):
+    return jnp.concatenate([own_ref[i, :, cols] for i in (2, 3, 2, 0, 1, 0)], axis=0)
 
 
 def crossed(left, right):
-    return lax.dot_general(
-        left, right, (((0,), (0,)), ((), ())), preferred_element_type=jnp.float32
-    )
+    return jnp.dot(left, right, preferred_element_type=jnp.float32)
 
 
 def placed(place, n, offset=0, size=None):
@@ -199,108 +203,116 @@
     )[0]
 
 
-def middle_block(m, side, k, w, t_ref, v_ref, store):
-    n = t_ref.shape[0]
+def prep_kernel(_, t_ref, v_ref, own_ref):
+    own_ref[0], own_ref[1] = halves(t_ref[...])
+    own_ref[2], own_ref[3] = halves(v_ref[...])
+
+
+def prep(meta, t, v):
+    return call(prep_kernel, [jax.ShapeDtypeStruct((4, *t.shape), jnp.bfloat16)], meta, [t, v])[0]
+
+
+def middle_block(m, side, chunks, own_ref, outs):
+    n = own_ref.shape[1]
+    w = n // CHUNKS
     half = m[X_PLACE] ^ side
-    cols = placed(half, n, k * w, w)
-    left = left_of(t_ref[:, cols], v_ref[:, cols])
-    same, cross = placed(half, n), placed(1 - half, n)
-    diagonal = crossed(left, right_of(t_ref[:, same], v_ref[:, same]))
-    aside = crossed(left, right_of(t_ref[:, cross], v_ref[:, cross]))
-    line = lax.broadcasted_iota(jnp.int32, (w, n), 0) + k * w
+    left = own_left(own_ref, placed(half, n, chunks[0] * w, len(chunks) * w))
+    diagonal = crossed(left, own_right(own_ref, placed(half, n)))
+    aside = crossed(left, own_right(own_ref, placed(1 - half, n)))
     lane = lax.broadcasted_iota(jnp.int32, (w, n), 1)
-    extra = jnp.sum(jnp.where(line == lane, aside, 0.0), axis=0, keepdims=True)
-    store(jnp.where(line >= lane, diagonal, aside), jnp.broadcast_to(extra, (PAD, n)))
-
-
-def next_block(m, side, k, w, at_ref, av_ref, t_ref, v_ref, store):
-    n = t_ref.shape[0]
-    cols = placed(m[X_PLACE] ^ side, n, k * w, w)
-    half = placed(m[TURN_1] ^ side, n)
-    left = left_of(at_ref[:, cols], av_ref[:, cols])
-    store(
-        crossed(left, right_of(t_ref[:, half], v_ref[:, half])), jnp.zeros((PAD, n), jnp.float32)
-    )
-
-
-def stored(out_ref, place, w):
-    def store(block, pad):
-        out_ref[place, :w, :] = block
-        out_ref[place, w:, :] = pad
-
-    return store
-
-
-def middle_kernel(side, k, w, m, t_ref, v_ref, out_ref):
-    middle_block(m, side, k, w, t_ref, v_ref, stored(out_ref, 0, w))
-
-
-def middle_part(meta, t, v, side, k):
-    n = t.shape[0]
-    w = n // CHUNKS
-    return call(
-        functools.partial(middle_kernel, side, k, w),
+    for i, (k, out_ref) in enumerate(zip(chunks, outs)):
+        line = lax.broadcasted_iota(jnp.int32, (w, n), 0) + k * w
+        rows = slice(i * w, (i + 1) * w)
+        out_ref[0, :w, :] = jnp.where(line >= lane, diagonal[rows], aside[rows])
+        extra = jnp.sum(jnp.where(line == lane, aside[rows], 0.0), axis=0, keepdims=True)
+        out_ref[0, w:, :] = jnp.broadcast_to(extra, (PAD, n))
+
+
+def middle_kernel(side, k, m, own_ref, out_ref):
+    middle_block(m, side, (k,), own_ref, [out_ref])
+
+
+def middle_part(meta, own, side, k):
+    n = own.shape[1]
+    w = n // CHUNKS
+    return call(
+        functools.partial(middle_kernel, side, k),
         [shaped(2, w + PAD, n)],
         meta,
-        [t, v],
+        [own],
         out_specs=[pl.BlockSpec((1, w + PAD, n), lambda i, m: (0, 0, 0))],
     )[0]
 
 
-def next_kernel(side, k, w, m, _, at_ref, av_ref, t_ref, v_ref, out_ref):
-    next_block(m, side, k, w, at_ref, av_ref, t_ref, v_ref, stored(out_ref, 0, w))
-
-
-def next_part(meta, base, at, av, t, v, side, k):
-    n = t.shape[0]
-    w = n // CHUNKS
-    return call(
-        functools.partial(next_kernel, side, k, w),
+def next_part(meta, base, at, av, own, side, k):
+    n = own.shape[1]
+    w = n // CHUNKS
+    block = pl.BlockSpec((n, w), lambda i, m: (0, (m[X_PLACE] ^ side) * CHUNKS + k))
+    return call(
+        functools.partial(next_kernel_blocked, side),
         [shaped(*base.shape)],
         meta,
-        [base, at, av, t, v],
-        in_specs=[pl.BlockSpec(memory_space=pl.ANY), None, None, None, None],
+        [base, at, av, own],
+        in_specs=[pl.BlockSpec(memory_space=pl.ANY), block, block, None],
         out_specs=[pl.BlockSpec((1, w + PAD, n), lambda i, m: (1, 0, 0))],
         aliases={1: 0},
     )[0]
 
 
-def near_kernel(side, chunks, w, m, at_ref, av_ref, t_ref, v_ref, *outs):
-    for out_ref, k in zip(outs, chunks):
-        middle_block(m, side, k, w, t_ref, v_ref, stored(out_ref, 0, w))
-        next_block(m, side, k, w, at_ref, av_ref, t_ref, v_ref, stored(out_ref, 1, w))
-
-
-def near_parts(meta, at, av, t, v, side, chunks):
-    n = t.shape[0]
-    w = n // CHUNKS
-    return call(
-        functools.partial(near_kernel, side, chunks, w),
+def next_kernel_blocked(side, m, _, at_ref, av_ref, own_ref, out_ref):
+    n = own_ref.shape[1]
+    w = at_ref.shape[1]
+    right = own_right(own_ref, placed(m[TURN_1] ^ side, n))
+    out_ref[0, :w, :] = crossed(left_of(at_ref[...], av_ref[...]), right)
+    out_ref[0, w:, :] = jnp.zeros((PAD, n), jnp.float32)
+
+
+def near_parts(meta, at, av, own, side, chunks):
+    n = own.shape[1]
+    w = n // CHUNKS
+    half = pl.BlockSpec((n, n), lambda i, m: (0, m[X_PLACE] ^ side))
+    return call(
+        functools.partial(near_half_kernel, side, chunks),
         [shaped(2, w + PAD, n) for _ in chunks],
         meta,
-        [at, av, t, v],
+        [at, av, own],
+        in_specs=[half, half, None],
     )
 
 
-def far_kernel(side, m, a_ref, b_ref, t_ref, v_ref, *outs):
-    n = t_ref.shape[0]
+def near_half_kernel(side, chunks, m, at_ref, av_ref, own_ref, *outs):
+    n = own_ref.shape[1]
+    w = n // CHUNKS
+    middle_block(m, side, chunks, own_ref, outs)
+    cols = slice(chunks[0] * w, (chunks[-1] + 1) * w)
+    right = own_right(own_ref, placed(m[TURN_1] ^ side, n))
+    block = crossed(left_of(at_ref[:, cols], av_ref[:, cols]), right)
+    for i, out_ref in enumerate(outs):
+        out_ref[1, :w, :] = block[i * w : (i + 1) * w]
+        out_ref[1, w:, :] = jnp.zeros((PAD, n), jnp.float32)
+
+
+def far_kernel(side, m, a_ref, b_ref, own_ref, *outs):
+    n = own_ref.shape[1]
     w = outs[0].shape[1]
-    half = placed(m[TURN_2] ^ side, n)
-    right = right_of(t_ref[:, half], v_ref[:, half])
-    for d, ref in enumerate((a_ref, b_ref)):
+    count = len(outs)
+    right = own_right(own_ref, placed(m[TURN_2] ^ side, n))
+    left = jnp.concatenate([left_of(ref[0], ref[1]) for ref in (a_ref, b_ref)], axis=0)
+    block = crossed(left, right)
+    for d in range(2):
         for i, out_ref in enumerate(outs):
-            cols = slice(i * w, (i + 1) * w)
-            out_ref[d] = crossed(left_of(ref[0, :, cols], ref[1, :, cols]), right)
-
-
-def far_parts(meta, a, b, t, v, side):
-    n = t.shape[0]
+            first = (d * count + i) * w
+            out_ref[d] = block[first : first + w]
+
+
+def far_parts(meta, a, b, own, side):
+    n = own.shape[1]
     w = n // CHUNKS
     return call(
         functools.partial(far_kernel, side),
         [shaped(2, w, n)] * (a.shape[2] // w),
         meta,
-        [a, b, t, v],
+        [a, b, own],
     )
 
 
@@ -359,50 +371,43 @@
 
 
 def most_kernel(m, *refs):
-    near_own, near_back, extra_ref, *refs = refs
-    far_own, far_back = refs[:3], refs[3:5]
+    near_own, near_back, extra_ref, far_own, far_back = refs[:5]
     t_ref, v_ref, row_ref, col_ref, new_ref, res_ref = refs[5:]
     n = t_ref.shape[0]
     place = m[PLACE]
 
-    def write(first, count, half, value):
-        rows = pl.ds(first, count)
+    def write(count, half, value):
+        rows = pl.ds(0, count)
         new_ref[rows, half], res_ref[rows, half] = closing(
             t_ref[rows, half], v_ref[rows, half], row_ref[rows, :], col_ref[:, half], value
         )
 
     @pl.when(m[NEAR] == 0)
     def _():
-        first = 0
-        for ref in far_own:
-            write(first, ref.shape[0], placed(place, n), ref[...])
-            first += ref.shape[0]
-        first = 0
-        for ref in far_back:
-            count = ref.shape[0]
-            write(0, n, placed(1 - place, n, first, count), ref[...].T)
-            first += count
+        count = far_own.shape[0]
+        write(count, placed(place, n), far_own[...])
+        write(n, placed(1 - place, n, 0, count), far_back[...].T)
 
     @pl.when((m[NEAR] == 1) & (m[MIDDLE] == 0))
     def _():
-        write(0, n, placed(place, n), near_own[...])
-        write(0, n, placed(1 - place, n), near_back[...].T)
+        write(n, placed(place, n), near_own[...])
+        write(n, placed(1 - place, n), near_back[...].T)
 
     @pl.when(m[MIDDLE] == 1)
     def _():
         line = lax.broadcasted_iota(jnp.int32, (n, n), 0)
         lane = lax.broadcasted_iota(jnp.int32, (n, n), 1)
         own = near_own[...]
-        write(0, n, placed(place, n), jnp.where(line >= lane, own, own.T))
+        write(n, placed(place, n), jnp.where(line >= lane, own, own.T))
         lower = jnp.where(line > lane, near_back[...].T, extra_ref[:1, :])
-        write(0, n, placed(1 - place, n), jnp.where(line < lane, own, lower))
+        write(n, placed(1 - place, n), jnp.where(line < lane, own, lower))
 
 
 def most(meta, t, *args):
     return call(most_kernel, [shaped(*t.shape)] * 2, meta, args)
 
 
-def last_kernel(m, back_ref, new_in, res_in, t_ref, v_ref, row_ref, col_ref, new_ref, res_ref):
+def late_kernel(turned, m, value_ref, new_in, res_in, t_ref, v_ref, row_ref, col_ref, new_ref, res_ref):
     @pl.when(m[NEAR] == 1)
     def _():
         new_ref[...] = new_in[...]
@@ -410,22 +415,29 @@
 
     @pl.when(m[NEAR] == 0)
     def _():
+        value = value_ref[...].T if turned else value_ref[...]
         new_ref[...], res_ref[...] = closing(
-            t_ref[...], v_ref[...], row_ref[...], col_ref[...], back_ref[...].T
+            t_ref[...], v_ref[...], row_ref[...], col_ref[...], value
         )
 
 
-def last(meta, back, new, res, t, v, row_gap, col_gap):
-    n = t.shape[0]
-    w = n // CHUNKS
-    at = lambda i, m: (0, (2 - m[PLACE]) * CHUNKS - 1)
-    block = pl.BlockSpec((n, w), at)
-    return call(
-        last_kernel,
+def late(meta, turned, chunk, value, new, res, t, v, row_gap, col_gap):
+    w, n = value.shape
+    if turned:
+        at = lambda i, m: (0, (1 - m[PLACE]) * CHUNKS + chunk)
+        block = pl.BlockSpec((n, w), at)
+        row, col = None, pl.BlockSpec((1, w), at)
+    else:
+        at = lambda i, m: (chunk, m[PLACE])
+        block = pl.BlockSpec((w, n), at)
+        row = pl.BlockSpec((w, 1), lambda i, m: (chunk, 0))
+        col = pl.BlockSpec((1, n), lambda i, m: (0, m[PLACE]))
+    return call(
+        functools.partial(late_kernel, turned),
         [shaped(*t.shape)] * 2,
         meta,
-        [back, new, res, t, v, row_gap, col_gap],
-        in_specs=[None, block, block, block, block, None, pl.BlockSpec((1, w), at)],
+        [value, new, res, t, v, row_gap, col_gap],
+        in_specs=[None, block, block, block, block, row, col],
         out_specs=[block, block],
         aliases={2: 0, 3: 1},
     )
@@ -460,18 +472,19 @@
 
     next_t = beside(t)
     next_v = beside(v)
+    own = prep(meta, t, v)
     send, keep = {}, {}
-    base = middle_part(meta, t, v, 1, 0)
-    send["n", 0] = next_part(meta, base, next_t, next_v, t, v, 1, 0)
+    base = middle_part(meta, own, 1, 0)
+    send["n", 0] = next_part(meta, base, next_t, next_v, own, 1, 0)
     for side, chunks in NEAR_GROUPS:
-        blocks = near_parts(meta, next_t, next_v, t, v, side, chunks)
+        blocks = near_parts(meta, next_t, next_v, own, side, chunks)
         for k, block in zip(chunks, blocks):
             (send if side else keep)["n", k] = block
     for tag, side, first, count in FAR_GROUPS:
         piece = pick(meta, t, v, side, first, count)
         piece = across(piece)
         other = beside(piece)
-        blocks = far_parts(meta, piece, other, t, v, side)
+        blocks = far_parts(meta, piece, other, own, side)
         for i, block in enumerate(blocks):
             (send if side else keep)["f", first + i] = block
     total, come = {}, {}
@@ -493,13 +506,15 @@
     for chunks in ((0, 1), (2,), (3,)):
         far_own += joined("f", chunks)
         far_back.append(back_far(far_own[-1]))
-    new, res = most(
-        meta, t, near_own, near_back, extra, *far_own, *far_back[:2], t, v, row_gap, col_gap
-    )
-    return last(meta, far_back[2], new, res, t, v, row_gap, col_gap)
-
-
-NEAR_GROUPS = ((1, (1, 2, 3)), (0, (0, 1, 2, 3)))
+    fixed = (t, v, row_gap, col_gap)
+    pair = most(meta, t, near_own, near_back, extra, far_own[0], far_back[0], *fixed)
+    for i in (1, 2):
+        pair = late(meta, False, i + 1, far_own[i], *pair, *fixed)
+        pair = late(meta, True, i + 1, far_back[i], *pair, *fixed)
+    return pair
+
+
+NEAR_GROUPS = ((1, (1, 2, 3)), (0, (0,)), (0, (1, 2, 3)))
 FAR_GROUPS = (("s0", 1, 0, 2), ("k0", 0, 0, 2), ("s1", 1, 2, 2), ("k1", 0, 2, 1), ("k2", 0, 3, 1))
 
 

time: 288 us -> 284 us (0.986)
  the two profiles are of different devices: /device:TPU:4 before, /device:TPU:29 now
where the time goes in v2:
time: 284 us; the launch traced here: 279 us
  waiting for transfers between devices  159 us (56%)
  Pallas kernels  61.3 us (22%)
  starting transfers between devices  53.2 us (19%)
  local copies, waits for them, and re-layouts  5.02 us (2%)
    ppermute x40, waiting for transfers between devices, routed(): return lax.ppermute(block, ('row', 'col'), route)  159 us
    pallas_call x41, Pallas kernels, call(): pl.pallas_call(kernel, out_shape=list(shapes), grid_spec=pltpu.PrefetchSc...  61.3 us
    ppermute x40, starting transfers between devices, routed(): return lax.ppermute(block, ('row', 'col'), route)  53.2 us
  transfers between devices with their start and end apart: 40, of which 18 were waited for; matrix products, arithmetic and copies ran while one was open for 0% of the time, Pallas kernels for 21%

profile of v2, /device:TPU:29, one launch (start us, length us, event | category | flops | bytes accessed | tf_op | source)
XLA Modules:
  0.0 279.4 jit_solution(11758394296502373907)
XLA Ops:
  9.4 20.3 %collective-permute-done.2.a_ref = f32[2,512,256]{2,1,0:T(8,128)S(1)} collective-permute-done((f32[2,512,256]{2,1,0:T(8,128)S(1)}, f32[2,512,256]{2,1,0:T(8,128)S(1)}, u32[]{:S(2)}, u32[]{:S(2)}) %collective-permute-start.2) | collective-permute-done | bytes 1048608 | tf_op jit(solution)/shard_map/ppermute | solution.py:84
  30.0 2.5 collective-permute-start.3
  39.3 24.1 %collective-permute-done.a_ref = f32[2,512,128]{2,1,0:T(8,128)S(1)} collective-permute-done((f32[2,512,128]{2,1,0:T(8,128)S(1)}, f32[2,512,128]{2,1,0:T(8,128)S(1)}, u32[]{:S(2)}, u32[]{:S(2)}) %collective-permute-start) | collective-permute-done | bytes 524320 | tf_op jit(solution)/shard_map/ppermute | solution.py:84
  64.6 2.5 collective-permute-start.32
  67.1 5.7 %shard_map.78 = (f32[2,136,512]{2,1,0:T(8,128)S(1)}, f32[2,136,512]{2,1,0:T(8,128)S(1)}, f32[2,136,512]{2,1,0:T(8,128)S(1)}) custom-call(s32[8]{0:T(128)S(1)} %compare_select_fusion.6.m._, f32[512,1024]{1,0:T(8,128)S(1)} %collective-permute-done.14.at_ref, f32[512,1024]{1,0:T(8,128)} %collective-permute-done.15.av_ref, ...), custom_call_target="tpu_custom_call" | custom-call | tf_op jit(solution)/shard_map/pallas_call | solution.py:129
  72.8 24.3 %collective-permute-done.8.a_ref = f32[2,512,128]{2,1,0:T(8,128)S(1)} collective-permute-done((f32[2,512,128]{2,1,0:T(8,128)S(1)}, f32[2,512,128]{2,1,0:T(8,128)S(1)}, u32[]{:S(2)}, u32[]{:S(2)}) %collective-permute-start.8) | collective-permute-done | bytes 524320 | tf_op jit(solution)/shard_map/ppermute | solution.py:84
  102.0 3.2 %shard_map.72.keep_pass.keep_stay = f32[2,136,512]{2,1,0:T(8,128)S(1)} custom-call(s32[8]{0:T(128)S(1)} %compare_select_fusion.6.m._, f32[512,1024]{1,0:T(8,128)S(1)} %collective-permute-done.14.at_ref, f32[512,1024]{1,0:T(8,128)} %collective-permute-done.15.av_ref, bf16[4,512,1024]{2,1,0:T(8,128)(2,1)S(1)} %shard_map.60.own_ref), custom_call_target="tpu_custom_call" | custom-call | tf_op jit(solution)/shard_map/pallas_call | solution.py:129
  105.2 5.7 %shard_map.77 = (f32[2,136,512]{2,1,0:T(8,128)S(1)}, f32[2,136,512]{2,1,0:T(8,128)S(1)}, f32[2,136,512]{2,1,0:T(8,128)S(1)}) custom-call(s32[8]{0:T(128)S(1)} %compare_select_fusion.6.m._, f32[512,1024]{1,0:T(8,128)S(1)} %collective-permute-done.14.at_ref, f32[512,1024]{1,0:T(8,128)} %collective-permute-done.15.av_ref, ...), custom_call_target="tpu_custom_call" | custom-call | tf_op jit(solution)/shard_map/pallas_call | solution.py:129
  113.8 2.4 shard_map.89
  116.2 5.8 %collective-permute-done.20.come_pass.come_stay = f32[2,136,512]{2,1,0:T(8,128)S(1)} collective-permute-done((f32[2,136,512]{2,1,0:T(8,128)S(1)}, f32[2,136,512]{2,1,0:T(8,128)S(1)}, u32[]{:S(2)}, u32[]{:S(2)}) %collective-permute-start.20) | collective-permute-done | bytes 557088 | tf_op jit(solution)/shard_map/ppermute | solution.py:84
  123.2 10.7 %collective-permute-done.22.come_pass.come_stay = f32[2,136,512]{2,1,0:T(8,128)S(1)} collective-permute-done((f32[2,136,512]{2,1,0:T(8,128)S(1)}, f32[2,136,512]{2,1,0:T(8,128)S(1)}, u32[]{:S(2)}, u32[]{:S(2)}) %collective-permute-start.22) | collective-permute-done | bytes 557088 | tf_op jit(solution)/shard_map/ppermute | solution.py:84
  143.4 4.3 %collective-permute-done.23.b_ref = f32[136,512]{1,0:T(8,128)S(1)} collective-permute-done((f32[136,512]{1,0:T(8,128)S(1)}, f32[136,512]{1,0:T(8,128)S(1)}, u32[]{:S(2)}, u32[]{:S(2)}) %collective-permute-start.23) | collective-permute-done | bytes 278560 | tf_op jit(solution)/shard_map/ppermute | solution.py:84
  150.8 2.4 shard_map.87
  153.8 2.6 collective-permute-done.35.come_pass.come_stay
  156.6 2.4 shard_map.63
  159.6 2.3 collective-permute-done.34.b_ref
  161.9 7.1 %collective-permute-start.9 = (f32[2,512,128]{2,1,0:T(8,128)S(1)}, f32[2,512,128]{2,1,0:T(8,128)S(1)}, u32[]{:S(2)}, u32[]{:S(2)}) collective-permute-start(f32[2,512,128]{2,1,0:T(8,128)S(1)} %collective-permute-done.8.a_ref), channel_id=1, source_target_pairs={{0,1},{1,0},{2,3},{3,2},{4,5},{5,4},{6,7},{7,6},{8,9},{9,8},{10,11... | collective-permute-start | bytes 1572872 | tf_op jit(solution)/shard_map/ppermute | solution.py:84
  169.3 8.4 %collective-permute-done.25.refs_5_ = f32[136,512]{1,0:T(8,128)S(1)} collective-permute-done((f32[136,512]{1,0:T(8,128)S(1)}, f32[136,512]{1,0:T(8,128)S(1)}, u32[]{:S(2)}, u32[]{:S(2)}) %collective-permute-start.25) | collective-permute-done | bytes 278560 | tf_op jit(solution)/shard_map/ppermute | solution.py:84
  177.6 6.0 %collective-permute-done.26.refs_6_ = f32[136,512]{1,0:T(8,128)S(1)} collective-permute-done((f32[136,512]{1,0:T(8,128)S(1)}, f32[136,512]{1,0:T(8,128)S(1)}, u32[]{:S(2)}, u32[]{:S(2)}) %collective-permute-start.26) | collective-permute-done | bytes 278560 | tf_op jit(solution)/shard_map/ppermute | solution.py:84
  183.6 6.4 %collective-permute-start.1 = (f32[2,512,128]{2,1,0:T(8,128)S(1)}, f32[2,512,128]{2,1,0:T(8,128)S(1)}, u32[]{:S(2)}, u32[]{:S(2)}) collective-permute-start(f32[2,512,128]{2,1,0:T(8,128)S(1)} %collective-permute-done.a_ref), channel_id=1, source_target_pairs={{0,1},{1,0},{2,3},{3,2},{4,5},{5,4},{6,7},{7,6},{8,9},{9,8},{10,11... | collective-permute-start | bytes 1572872 | tf_op jit(solution)/shard_map/ppermute | solution.py:84
  192.0 6.1 %collective-permute-done.36.b_ref = f32[128,512]{1,0:T(8,128)S(1)} collective-permute-done((f32[128,512]{1,0:T(8,128)S(1)}, f32[128,512]{1,0:T(8,128)S(1)}, u32[]{:S(2)}, u32[]{:S(2)}) %collective-permute-start.36) | collective-permute-done | bytes 262176 | tf_op jit(solution)/shard_map/ppermute | solution.py:84
  201.5 2.3 collective-permute-start.38
  210.0 11.7 %collective-permute-done.37.refs_2_ = f32[128,512]{1,0:T(8,128)S(1)} collective-permute-done((f32[128,512]{1,0:T(8,128)S(1)}, f32[128,512]{1,0:T(8,128)S(1)}, u32[]{:S(2)}, u32[]{:S(2)}) %collective-permute-start.37) | collective-permute-done | bytes 262176 | tf_op jit(solution)/shard_map/ppermute | solution.py:84
  221.7 5.6 %collective-permute-done.38.refs_3_ = f32[128,512]{1,0:T(8,128)S(1)} collective-permute-done((f32[128,512]{1,0:T(8,128)S(1)}, f32[128,512]{1,0:T(8,128)S(1)}, u32[]{:S(2)}, u32[]{:S(2)}) %collective-permute-start.38) | collective-permute-done | bytes 262176 | tf_op jit(solution)/shard_map/ppermute | solution.py:84
  230.1 3.8 %collective-permute-done.11.b_ref = f32[128,512]{1,0:T(8,128)S(1)} collective-permute-done((f32[128,512]{1,0:T(8,128)S(1)}, f32[128,512]{1,0:T(8,128)S(1)}, u32[]{:S(2)}, u32[]{:S(2)}) %collective-permute-start.11) | collective-permute-done | bytes 262176 | tf_op jit(solution)/shard_map/ppermute | solution.py:84
  237.5 16.8 %collective-permute-done.12.refs_1_ = f32[128,512]{1,0:T(8,128)S(1)} collective-permute-done((f32[128,512]{1,0:T(8,128)S(1)}, f32[128,512]{1,0:T(8,128)S(1)}, u32[]{:S(2)}, u32[]{:S(2)}) %collective-permute-start.12) | collective-permute-done | bytes 262176 | tf_op jit(solution)/shard_map/ppermute | solution.py:84
  256.9 2.9 %collective-permute-done.6.refs_1_ = f32[128,512]{1,0:T(8,128)S(1)} collective-permute-done((f32[128,512]{1,0:T(8,128)S(1)}, f32[128,512]{1,0:T(8,128)S(1)}, u32[]{:S(2)}, u32[]{:S(2)}) %collective-permute-start.6) | collective-permute-done | bytes 262176 | tf_op jit(solution)/shard_map/ppermute | solution.py:84
  264.3 5.3 %shard_map.95 = (f32[512,1024]{1,0:T(8,128)}, f32[512,1024]{1,0:T(8,128)}) custom-call(s32[8]{0:T(128)S(1)} %compare_select_fusion.6.m._, f32[512,512]{1,0:T(8,128)} %get-tuple-element.60.refs_0_, f32[512,512]{1,0:T(8,128)} %collective-permute-done.28.refs_1_, f32[8,512]{1,0:T(8,128)S(1)} %get-tuple-element.61.refs_2_, f32[256,512]{1,0:T(8,128)S(1)} %shard_map.94.refs_3_, ...), custom_call_target="tpu_custom_call" | custom-call | tf_op jit(solution)/shard_map/pallas_call | solution.py:129
  269.6 2.4 shard_map.96
  272.1 2.5 shard_map.97
  274.5 2.4 shard_map.98
  277.0 2.5 shard_map.99
  (107 shorter events, 65.0 us)
Async XLA Ops:
  0.6 29.3 %collective-permute-start.14 = (f32[512,1024]{1,0:T(8,128)}, f32[512,1024]{1,0:T(8,128)S(1)}, u32[]{:S(2)}, u32[]{:S(2)}) collective-permute-start(f32[512,1024]{1,0:T(8,128)} %t_ref.19), channel_id=1, source_target_pairs={{0,1},{1,0},{2,3},{3,2},{4,5},{5,4},{6,7},{7,6},{8,9},{9,8},{10,11... | collective-permute-start | bytes 6291464 | tf_op jit(solution)/shard_map/ppermute | solution.py:84
  1.4 31.7 %collective-permute-start.15 = (f32[512,1024]{1,0:T(8,128)}, f32[512,1024]{1,0:T(8,128)}, u32[]{:S(2)}, u32[]{:S(2)}) collective-permute-start(f32[512,1024]{1,0:T(8,128)} %v_ref.19), channel_id=1, source_target_pairs={{0,1},{1,0},{2,3},{3,2},{4,5},{5,4},{6,7},{7,6},{8,9},{9,8},{10,11... | collective-permute-start | bytes 6291464 | tf_op jit(solution)/shard_map/ppermute | solution.py:84
  5.4 24.4 %collective-permute-start.2 = (f32[2,512,256]{2,1,0:T(8,128)S(1)}, f32[2,512,256]{2,1,0:T(8,128)S(1)}, u32[]{:S(2)}, u32[]{:S(2)}) collective-permute-start(f32[2,512,256]{2,1,0:T(8,128)S(1)} %shard_map.62), channel_id=1, source_target_pairs={{0,2},{1,3},{2,0},{3,1},{4,6},{5,7},{6,4},{7,5},{8,10},{9,11},{10,... | collective-permute-start | bytes 3145736 | tf_op jit(solution)/shard_map/ppermute | solution.py:84
  6.4 58.2 %collective-permute-start.31 = (f32[2,512,256]{2,1,0:T(8,128)S(1)}, f32[2,512,256]{2,1,0:T(8,128)S(1)}, u32[]{:S(2)}, u32[]{:S(2)}) collective-permute-start(f32[2,512,256]{2,1,0:T(8,128)S(1)} %shard_map.88), channel_id=1, source_target_pairs={{0,2},{1,3},{2,0},{3,1},{4,6},{5,7},{6,4},{7,5},{8,10},{9,11},{10,... | collective-permute-start | bytes 3145736 | tf_op jit(solution)/shard_map/ppermute | solution.py:84
  8.4 55.1 %collective-permute-start = (f32[2,512,128]{2,1,0:T(8,128)S(1)}, f32[2,512,128]{2,1,0:T(8,128)S(1)}, u32[]{:S(2)}, u32[]{:S(2)}) collective-permute-start(f32[2,512,128]{2,1,0:T(8,128)S(1)} %shard_map.59), channel_id=1, source_target_pairs={{0,2},{1,3},{2,0},{3,1},{4,6},{5,7},{6,4},{7,5},{8,10},{9,11},{10,... | collective-permute-start | bytes 1572872 | tf_op jit(solution)/shard_map/ppermute | solution.py:84
  29.7 68.6 %collective-permute-start.29 = (f32[2,512,256]{2,1,0:T(8,128)S(1)}, f32[2,512,256]{2,1,0:T(8,128)S(1)}, u32[]{:S(2)}, u32[]{:S(2)}) collective-permute-start(f32[2,512,256]{2,1,0:T(8,128)S(1)} %shard_map.86), channel_id=1, source_target_pairs={{0,2},{1,3},{2,0},{3,1},{4,6},{5,7},{6,4},{7,5},{8,10},{9,11},{10,... | collective-permute-start | bytes 3145736 | tf_op jit(solution)/shard_map/ppermute | solution.py:84
  30.0 68.7 %collective-permute-start.3 = (f32[2,512,256]{2,1,0:T(8,128)S(1)}, f32[2,512,256]{2,1,0:T(8,128)S(1)}, u32[]{:S(2)}, u32[]{:S(2)}) collective-permute-start(f32[2,512,256]{2,1,0:T(8,128)S(1)} %collective-permute-done.2.a_ref), channel_id=1, source_target_pairs={{0,1},{1,0},{2,3},{3,2},{4,5},{5,4},{6,7},{7,6},{8,9},{9,8},{10,11... | collective-permute-start | bytes 3145736 | tf_op jit(solution)/shard_map/ppermute | solution.py:84
  33.1 64.1 %collective-permute-start.8 = (f32[2,512,128]{2,1,0:T(8,128)S(1)}, f32[2,512,128]{2,1,0:T(8,128)S(1)}, u32[]{:S(2)}, u32[]{:S(2)}) collective-permute-start(f32[2,512,128]{2,1,0:T(8,128)S(1)} %shard_map.67), channel_id=1, source_target_pairs={{0,2},{1,3},{2,0},{3,1},{4,6},{5,7},{6,4},{7,5},{8,10},{9,11},{10,... | collective-permute-start | bytes 1572872 | tf_op jit(solution)/shard_map/ppermute | solution.py:84
  63.4 36.4 %collective-permute-start.16 = (f32[2,136,512]{2,1,0:T(8,128)S(1)}, f32[2,136,512]{2,1,0:T(8,128)S(1)}, u32[]{:S(2)}, u32[]{:S(2)}) collective-permute-start(f32[2,136,512]{2,1,0:T(8,128)S(1)} %shard_map.74), channel_id=1, source_target_pairs={{0,4},{1,5},{2,6},{3,7},{4,0},{5,1},{6,2},{7,3},{8,12},{9,13},{10,... | collective-permute-start | bytes 1671176 | tf_op jit(solution)/shard_map/ppermute | solution.py:84
  64.6 47.8 %collective-permute-start.32 = (f32[2,512,256]{2,1,0:T(8,128)S(1)}, f32[2,512,256]{2,1,0:T(8,128)S(1)}, u32[]{:S(2)}, u32[]{:S(2)}) collective-permute-start(f32[2,512,256]{2,1,0:T(8,128)S(1)} %collective-permute-done.31.a_ref), channel_id=1, source_target_pairs={{0,1},{1,0},{2,3},{3,2},{4,5},{5,4},{6,7},{7,6},{8,9},{9,8},{10,11... | collective-permute-start | bytes 3145736 | tf_op jit(solution)/shard_map/ppermute | solution.py:84
  98.4 23.6 %collective-permute-start.20 = (f32[2,136,512]{2,1,0:T(8,128)S(1)}, f32[2,136,512]{2,1,0:T(8,128)S(1)}, u32[]{:S(2)}, u32[]{:S(2)}) collective-permute-start(f32[2,136,512]{2,1,0:T(8,128)S(1)} %get-tuple-element.53), channel_id=1, source_target_pairs={{0,4},{1,5},{2,6},{3,7},{4,0},{5,1},{6,2},{7,3},{8,12},{9,13},{10,... | collective-permute-start | bytes 1671176 | tf_op jit(solution)/shard_map/ppermute | solution.py:84
  98.6 35.3 %collective-permute-start.22 = (f32[2,136,512]{2,1,0:T(8,128)S(1)}, f32[2,136,512]{2,1,0:T(8,128)S(1)}, u32[]{:S(2)}, u32[]{:S(2)}) collective-permute-start(f32[2,136,512]{2,1,0:T(8,128)S(1)} %get-tuple-element.57), channel_id=1, source_target_pairs={{0,4},{1,5},{2,6},{3,7},{4,0},{5,1},{6,2},{7,3},{8,12},{9,13},{10,... | collective-permute-start | bytes 1671176 | tf_op jit(solution)/shard_map/ppermute | solution.py:84
  99.8 39.5 %collective-permute-start.30 = (f32[2,512,256]{2,1,0:T(8,128)S(1)}, f32[2,512,256]{2,1,0:T(8,128)S(1)}, u32[]{:S(2)}, u32[]{:S(2)}) collective-permute-start(f32[2,512,256]{2,1,0:T(8,128)S(1)} %collective-permute-done.29.a_ref), channel_id=1, source_target_pairs={{0,1},{1,0},{2,3},{3,2},{4,5},{5,4},{6,7},{7,6},{8,9},{9,8},{10,11... | collective-permute-start | bytes 3145736 | tf_op jit(solution)/shard_map/ppermute | solution.py:84
  111.6 24.2 %collective-permute-start.17 = (f32[136,512]{1,0:T(8,128)S(1)}, f32[136,512]{1,0:T(8,128)S(1)}, u32[]{:S(2)}, u32[]{:S(2)}) collective-permute-start(f32[136,512]{1,0:T(8,128)S(1)} %get-tuple-element.47), channel_id=1, source_target_pairs={{0,8},{1,9},{2,10},{3,11},{4,12},{5,13},{6,14},{7,15},{8,0},{9,1},... | collective-permute-start | bytes 835592 | tf_op jit(solution)/shard_map/ppermute | solution.py:84
  112.4 24.2 %collective-permute-start.19 = (f32[136,512]{1,0:T(8,128)S(1)}, f32[136,512]{1,0:T(8,128)S(1)}, u32[]{:S(2)}, u32[]{:S(2)}) collective-permute-start(f32[136,512]{1,0:T(8,128)S(1)} %get-tuple-element.51), channel_id=1, source_target_pairs={{0,8},{1,9},{2,10},{3,11},{4,12},{5,13},{6,14},{7,15},{8,0},{9,1},... | collective-permute-start | bytes 835592 | tf_op jit(solution)/shard_map/ppermute | solution.py:84
  122.0 27.5 %collective-permute-start.33 = (f32[2,128,512]{2,1,0:T(8,128)S(1)}, f32[2,128,512]{2,1,0:T(8,128)S(1)}, u32[]{:S(2)}, u32[]{:S(2)}) collective-permute-start(f32[2,128,512]{2,1,0:T(8,128)S(1)} %get-tuple-element.63), channel_id=1, source_target_pairs={{0,4},{1,5},{2,6},{3,7},{4,0},{5,1},{6,2},{7,3},{8,12},{9,13},{10,... | collective-permute-start | bytes 1572872 | tf_op jit(solution)/shard_map/ppermute | solution.py:84
  133.9 22.5 %collective-permute-start.35 = (f32[2,128,512]{2,1,0:T(8,128)S(1)}, f32[2,128,512]{2,1,0:T(8,128)S(1)}, u32[]{:S(2)}, u32[]{:S(2)}) collective-permute-start(f32[2,128,512]{2,1,0:T(8,128)S(1)} %get-tuple-element.67), channel_id=1, source_target_pairs={{0,4},{1,5},{2,6},{3,7},{4,0},{5,1},{6,2},{7,3},{8,12},{9,13},{10,... | collective-permute-start | bytes 1572872 | tf_op jit(solution)/shard_map/ppermute | solution.py:84
  139.3 29.7 %collective-permute-start.24 = (f32[136,512]{1,0:T(8,128)S(1)}, f32[136,512]{1,0:T(8,128)S(1)}, u32[]{:S(2)}, u32[]{:S(2)}) collective-permute-start(f32[136,512]{1,0:T(8,128)S(1)} %shard_map.76.refs_0_), channel_id=1, source_target_pairs={{2,18},{3,19},{6,22},{7,23},{10,26},{11,27},{14,30},{15,31},{16,0}... | collective-permute-start | bytes 835592 | tf_op jit(solution)/shard_map/ppermute | solution.py:84
  141.5 36.1 %collective-permute-start.25 = (f32[136,512]{1,0:T(8,128)S(1)}, f32[136,512]{1,0:T(8,128)S(1)}, u32[]{:S(2)}, u32[]{:S(2)}) collective-permute-start(f32[136,512]{1,0:T(8,128)S(1)} %shard_map.80.refs_1_), channel_id=1, source_target_pairs={{2,18},{3,19},{6,22},{7,23},{10,26},{11,27},{14,30},{15,31},{16,0}... | collective-permute-start | bytes 835592 | tf_op jit(solution)/shard_map/ppermute | solution.py:84
  147.6 36.0 %collective-permute-start.26 = (f32[136,512]{1,0:T(8,128)S(1)}, f32[136,512]{1,0:T(8,128)S(1)}, u32[]{:S(2)}, u32[]{:S(2)}) collective-permute-start(f32[136,512]{1,0:T(8,128)S(1)} %shard_map.82.refs_2_), channel_id=1, source_target_pairs={{2,18},{3,19},{6,22},{7,23},{10,26},{11,27},{14,30},{15,31},{16,0}... | collective-permute-start | bytes 835592 | tf_op jit(solution)/shard_map/ppermute | solution.py:84
  149.5 40.6 %collective-permute-start.27 = (f32[136,512]{1,0:T(8,128)S(1)}, f32[136,512]{1,0:T(8,128)S(1)}, u32[]{:S(2)}, u32[]{:S(2)}) collective-permute-start(f32[136,512]{1,0:T(8,128)S(1)} %shard_map.84.refs_3_), channel_id=1, source_target_pairs={{2,18},{3,19},{6,22},{7,23},{10,26},{11,27},{14,30},{15,31},{16,0}... | collective-permute-start | bytes 835592 | tf_op jit(solution)/shard_map/ppermute | solution.py:84
  161.9 39.5 %collective-permute-start.9 = (f32[2,512,128]{2,1,0:T(8,128)S(1)}, f32[2,512,128]{2,1,0:T(8,128)S(1)}, u32[]{:S(2)}, u32[]{:S(2)}) collective-permute-start(f32[2,512,128]{2,1,0:T(8,128)S(1)} %collective-permute-done.8.a_ref), channel_id=1, source_target_pairs={{0,1},{1,0},{2,3},{3,2},{4,5},{5,4},{6,7},{7,6},{8,9},{9,8},{10,11... | collective-permute-start | bytes 1572872 | tf_op jit(solution)/shard_map/ppermute | solution.py:84
  169.0 32.5 %collective-permute-start.10 = (f32[2,128,512]{2,1,0:T(8,128)S(1)}, f32[2,128,512]{2,1,0:T(8,128)S(1)}, u32[]{:S(2)}, u32[]{:S(2)}) collective-permute-start(f32[2,128,512]{2,1,0:T(8,128)S(1)} %get-tuple-element.43), channel_id=1, source_target_pairs={{0,4},{1,5},{2,6},{3,7},{4,0},{5,1},{6,2},{7,3},{8,12},{9,13},{10,... | collective-permute-start | bytes 1572872 | tf_op jit(solution)/shard_map/ppermute | solution.py:84
  177.6 20.4 %collective-permute-start.36 = (f32[128,512]{1,0:T(8,128)S(1)}, f32[128,512]{1,0:T(8,128)S(1)}, u32[]{:S(2)}, u32[]{:S(2)}) collective-permute-start(f32[128,512]{1,0:T(8,128)S(1)} %get-tuple-element.69), channel_id=1, source_target_pairs={{0,8},{1,9},{2,10},{3,11},{4,12},{5,13},{6,14},{7,15},{8,0},{9,1},... | collective-permute-start | bytes 786440 | tf_op jit(solution)/shard_map/ppermute | solution.py:84
  183.6 22.4 %collective-permute-start.1 = (f32[2,512,128]{2,1,0:T(8,128)S(1)}, f32[2,512,128]{2,1,0:T(8,128)S(1)}, u32[]{:S(2)}, u32[]{:S(2)}) collective-permute-start(f32[2,512,128]{2,1,0:T(8,128)S(1)} %collective-permute-done.a_ref), channel_id=1, source_target_pairs={{0,1},{1,0},{2,3},{3,2},{4,5},{5,4},{6,7},{7,6},{8,9},{9,8},{10,11... | collective-permute-start | bytes 1572872 | tf_op jit(solution)/shard_map/ppermute | solution.py:84
  198.1 64.6 %collective-permute-start.28 = (f32[512,512]{1,0:T(8,128)}, f32[512,512]{1,0:T(8,128)}, u32[]{:S(2)}, u32[]{:S(2)}) collective-permute-start(f32[512,512]{1,0:T(8,128)} %get-tuple-element.60.refs_0_), channel_id=1, source_target_pairs={{0,4},{1,8},{4,0},{5,12},{8,5},{9,13},{12,1},{13,9},{18,22},{19,26... | collective-permute-start | bytes 3145736 | tf_op jit(solution)/shard_map/ppermute | solution.py:84
  201.4 20.3 %collective-permute-start.37 = (f32[128,512]{1,0:T(8,128)S(1)}, f32[128,512]{1,0:T(8,128)S(1)}, u32[]{:S(2)}, u32[]{:S(2)}) collective-permute-start(f32[128,512]{1,0:T(8,128)S(1)} %shard_map.91.refs_0_), channel_id=1, source_target_pairs={{0,16},{1,17},{2,18},{3,19},{4,20},{5,21},{6,22},{7,23},{8,24},{9,... | collective-permute-start | bytes 786440 | tf_op jit(solution)/shard_map/ppermute | solution.py:84
  201.5 25.8 %collective-permute-start.38 = (f32[128,512]{1,0:T(8,128)S(1)}, f32[128,512]{1,0:T(8,128)S(1)}, u32[]{:S(2)}, u32[]{:S(2)}) collective-permute-start(f32[128,512]{1,0:T(8,128)S(1)} %shard_map.93.refs_1_), channel_id=1, source_target_pairs={{0,16},{1,17},{2,18},{3,19},{4,20},{5,21},{6,22},{7,23},{8,24},{9,... | collective-permute-start | bytes 786440 | tf_op jit(solution)/shard_map/ppermute | solution.py:84
  206.0 27.8 %collective-permute-start.11 = (f32[128,512]{1,0:T(8,128)S(1)}, f32[128,512]{1,0:T(8,128)S(1)}, u32[]{:S(2)}, u32[]{:S(2)}) collective-permute-start(f32[128,512]{1,0:T(8,128)S(1)} %get-tuple-element.45), channel_id=1, source_target_pairs={{0,8},{1,9},{2,10},{3,11},{4,12},{5,13},{6,14},{7,15},{8,0},{9,1},... | collective-permute-start | bytes 786440 | tf_op jit(solution)/shard_map/ppermute | solution.py:84
  209.9 26.8 %collective-permute-start.5 = (f32[128,512]{1,0:T(8,128)S(1)}, f32[128,512]{1,0:T(8,128)S(1)}, u32[]{:S(2)}, u32[]{:S(2)}) collective-permute-start(f32[128,512]{1,0:T(8,128)S(1)} %get-tuple-element.42), channel_id=1, source_target_pairs={{0,8},{1,9},{2,10},{3,11},{4,12},{5,13},{6,14},{7,15},{8,0},{9,1},... | collective-permute-start | bytes 786440 | tf_op jit(solution)/shard_map/ppermute | solution.py:84
  227.9 34.8 %collective-permute-start.39 = (f32[256,512]{1,0:T(8,128)S(1)}, f32[256,512]{1,0:T(8,128)}, u32[]{:S(2)}, u32[]{:S(2)}) collective-permute-start(f32[256,512]{1,0:T(8,128)S(1)} %shard_map.94.refs_3_), channel_id=1, source_target_pairs={{0,6},{1,14},{4,2},{5,10},{8,7},{9,15},{12,3},{13,11},{18,16},{19,... | collective-permute-start | bytes 1572872 | tf_op jit(solution)/shard_map/ppermute | solution.py:84
  237.2 22.5 %collective-permute-start.6 = (f32[128,512]{1,0:T(8,128)S(1)}, f32[128,512]{1,0:T(8,128)S(1)}, u32[]{:S(2)}, u32[]{:S(2)}) collective-permute-start(f32[128,512]{1,0:T(8,128)S(1)} %shard_map.65.refs_0_), channel_id=1, source_target_pairs={{0,16},{1,17},{2,18},{3,19},{4,20},{5,21},{6,22},{7,23},{8,24},{9,... | collective-permute-start | bytes 786440 | tf_op jit(solution)/shard_map/ppermute | solution.py:84
  (14 other events, 254.1 us)

commit v3 on v2

--- a/solution.py
+++ b/solution.py
@@ -371,74 +371,88 @@
 
 
 def most_kernel(m, *refs):
-    near_own, near_back, extra_ref, far_own, far_back = refs[:5]
-    t_ref, v_ref, row_ref, col_ref, new_ref, res_ref = refs[5:]
+    near_own, near_back, extra_ref = refs[:3]
+    far_own, far_back = refs[3:5], refs[5:7]
+    t_ref, v_ref, row_ref, col_ref, new_ref, res_ref = refs[7:]
     n = t_ref.shape[0]
     place = m[PLACE]
 
-    def write(count, half, value):
-        rows = pl.ds(0, count)
+    def write(first, count, half, value):
+        rows = pl.ds(first, count)
         new_ref[rows, half], res_ref[rows, half] = closing(
             t_ref[rows, half], v_ref[rows, half], row_ref[rows, :], col_ref[:, half], value
         )
 
     @pl.when(m[NEAR] == 0)
     def _():
-        count = far_own.shape[0]
-        write(count, placed(place, n), far_own[...])
-        write(n, placed(1 - place, n, 0, count), far_back[...].T)
+        first = 0
+        for own_ref, back_ref in zip(far_own, far_back):
+            count = own_ref.shape[0]
+            write(first, count, placed(place, n), own_ref[...])
+            write(0, n, placed(1 - place, n, first, count), back_ref[...].T)
+            first += count
 
     @pl.when((m[NEAR] == 1) & (m[MIDDLE] == 0))
     def _():
-        write(n, placed(place, n), near_own[...])
-        write(n, placed(1 - place, n), near_back[...].T)
+        write(0, n, placed(place, n), near_own[...])
+        write(0, n, placed(1 - place, n), near_back[...].T)
 
     @pl.when(m[MIDDLE] == 1)
     def _():
         line = lax.broadcasted_iota(jnp.int32, (n, n), 0)
         lane = lax.broadcasted_iota(jnp.int32, (n, n), 1)
         own = near_own[...]
-        write(n, placed(place, n), jnp.where(line >= lane, own, own.T))
+        write(0, n, placed(place, n), jnp.where(line >= lane, own, own.T))
         lower = jnp.where(line > lane, near_back[...].T, extra_ref[:1, :])
-        write(n, placed(1 - place, n), jnp.where(line < lane, own, lower))
+        write(0, n, placed(1 - place, n), jnp.where(line < lane, own, lower))
 
 
 def most(meta, t, *args):
     return call(most_kernel, [shaped(*t.shape)] * 2, meta, args)
 
 
-def late_kernel(turned, m, value_ref, new_in, res_in, t_ref, v_ref, row_ref, col_ref, new_ref, res_ref):
-    @pl.when(m[NEAR] == 1)
-    def _():
-        new_ref[...] = new_in[...]
-        res_ref[...] = res_in[...]
+def late_kernel(turned, m, value_ref, _, __, t_ref, v_ref, row_ref, col_ref, new_ref, res_ref, new, res, sems):
+    n, w = max(value_ref.shape), min(value_ref.shape)
 
     @pl.when(m[NEAR] == 0)
     def _():
         value = value_ref[...].T if turned else value_ref[...]
-        new_ref[...], res_ref[...] = closing(
+        new[...], res[...] = closing(
             t_ref[...], v_ref[...], row_ref[...], col_ref[...], value
         )
-
-
-def late(meta, turned, chunk, value, new, res, t, v, row_gap, col_gap):
+        if turned:
+            rows, cols = pl.ds(0, n), placed(1 - m[PLACE], n, n - w, w)
+        else:
+            rows, cols = pl.ds(n - w, w), placed(m[PLACE], n)
+        copies = [
+            pltpu.make_async_copy(source, target.at[rows, cols], sems.at[i])
+            for i, (source, target) in enumerate(((new, new_ref), (res, res_ref)))
+        ]
+        for copy in copies:
+            copy.start()
+        for copy in copies:
+            copy.wait()
+
+
+def late(meta, turned, value, new, res, t, v, row_gap, col_gap):
     w, n = value.shape
     if turned:
-        at = lambda i, m: (0, (1 - m[PLACE]) * CHUNKS + chunk)
+        at = lambda i, m: (0, (2 - m[PLACE]) * CHUNKS - 1)
         block = pl.BlockSpec((n, w), at)
         row, col = None, pl.BlockSpec((1, w), at)
     else:
-        at = lambda i, m: (chunk, m[PLACE])
-        block = pl.BlockSpec((w, n), at)
-        row = pl.BlockSpec((w, 1), lambda i, m: (chunk, 0))
+        block = pl.BlockSpec((w, n), lambda i, m: (CHUNKS - 1, m[PLACE]))
+        row = pl.BlockSpec((w, 1), lambda i, m: (CHUNKS - 1, 0))
         col = pl.BlockSpec((1, n), lambda i, m: (0, m[PLACE]))
+    hbm = pl.BlockSpec(memory_space=pl.ANY)
     return call(
         functools.partial(late_kernel, turned),
         [shaped(*t.shape)] * 2,
         meta,
         [value, new, res, t, v, row_gap, col_gap],
-        in_specs=[None, block, block, block, block, row, col],
-        out_specs=[block, block],
+        in_specs=[None, hbm, hbm, block, block, row, col],
+        out_specs=[hbm, hbm],
+        scratch=[pltpu.VMEM(block.block_shape, jnp.float32)] * 2 + [pltpu.SemaphoreType.DMA((2,))],
         aliases={2: 0, 3: 1},
     )
 
@@ -507,11 +521,9 @@
         far_own += joined("f", chunks)
         far_back.append(back_far(far_own[-1]))
     fixed = (t, v, row_gap, col_gap)
-    pair = most(meta, t, near_own, near_back, extra, far_own[0], far_back[0], *fixed)
-    for i in (1, 2):
-        pair = late(meta, False, i + 1, far_own[i], *pair, *fixed)
-        pair = late(meta, True, i + 1, far_back[i], *pair, *fixed)
-    return pair
+    pair = most(meta, t, near_own, near_back, extra, *far_own[:2], *far_back[:2], *fixed)
+    pair = late(meta, False, far_own[2], *pair, *fixed)
+    return late(meta, True, far_back[2], *pair, *fixed)
 
 
 NEAR_GROUPS = ((1, (1, 2, 3)), (0, (0,)), (0, (1, 2, 3)))

time: 284 us -> 289 us (1.018)
  starting transfers between devices: 53.2 us -> 63.6 us
  Pallas kernels: 61.3 us -> 53.8 us
    ppermute x40, starting transfers between devices: 53.2 us -> 63.6 us  [routed(): return lax.ppermute(block, ('row', 'col'), route)]
    pallas_call x41 -> x39, Pallas kernels: 61.3 us -> 53.8 us  [call(): pl.pallas_call(kernel, out_shape=list(shapes), grid_spec=pltpu.PrefetchSc...]
  transfers between devices with their start and end apart: 40 -> 40, of which waited for: 18 -> 16; matrix products, arithmetic and copies ran while one was open for 0% -> 0% of each run, Pallas kernels for 21% -> 18%
where the time goes in v3:
time: 289 us; the launch traced here: 283 us
  waiting for transfers between devices  160 us (55%)
  starting transfers between devices  63.6 us (22%)
  Pallas kernels  53.8 us (19%)
  local copies, waits for them, and re-layouts  5.02 us (2%)
    ppermute x40, waiting for transfers between devices, routed(): return lax.ppermute(block, ('row', 'col'), route)  160 us
    ppermute x40, starting transfers between devices, routed(): return lax.ppermute(block, ('row', 'col'), route)  63.6 us
    pallas_call x39, Pallas kernels, call(): pl.pallas_call(kernel, out_shape=list(shapes), grid_spec=pltpu.PrefetchSc...  53.8 us
  transfers between devices with their start and end apart: 40, of which 16 were waited for; matrix products, arithmetic and copies ran while one was open for 0% of the time, Pallas kernels for 18%

profile of v3, /device:TPU:29, one launch (start us, length us, event | category | flops | bytes accessed | tf_op | source)
XLA Modules:
  0.0 283.3 jit_solution(543617796671666240)
XLA Ops:
  1.5 1.6 copy-done
  3.1 1.6 copy-done.2
  9.4 54.0 %collective-permute-done.33.a_ref = f32[2,512,128]{2,1,0:T(8,128)S(1)} collective-permute-done((f32[2,512,128]{2,1,0:T(8,128)S(1)}, f32[2,512,128]{2,1,0:T(8,128)S(1)}, u32[]{:S(2)}, u32[]{:S(2)}) %collective-permute-start.33) | collective-permute-done | bytes 524320 | tf_op jit(solution)/shard_map/ppermute | solution.py:84
  68.9 1.6 shard_map.68._
  70.5 2.1 shard_map.69
  72.7 25.4 %collective-permute-done.a_ref = f32[2,512,128]{2,1,0:T(8,128)S(1)} collective-permute-done((f32[2,512,128]{2,1,0:T(8,128)S(1)}, f32[2,512,128]{2,1,0:T(8,128)S(1)}, u32[]{:S(2)}, u32[]{:S(2)}) %collective-permute-start) | collective-permute-done | bytes 524320 | tf_op jit(solution)/shard_map/ppermute | solution.py:84
  99.3 5.7 %shard_map.73 = (f32[2,136,512]{2,1,0:T(8,128)S(1)}, f32[2,136,512]{2,1,0:T(8,128)S(1)}, f32[2,136,512]{2,1,0:T(8,128)S(1)}) custom-call(s32[8]{0:T(128)S(1)} %compare_select_fusion.6.m._, f32[512,1024]{1,0:T(8,128)S(1)} %collective-permute-done.8.at_ref, f32[512,1024]{1,0:T(8,128)} %collective-permute-done.9.av_ref, bf16[4,512,1024]{2,1,0:T(8,128)(2,1)S(1)} %shard_map.60.own_ref), custom_call_target="tpu_custom_call" | custom-call | tf_op jit(solution)/shard_map/pallas_call | solution.py:129
  105.4 2.7 collective-permute-start.24
  111.4 3.2 %shard_map.67.keep_pass.keep_stay = f32[2,136,512]{2,1,0:T(8,128)S(1)} custom-call(s32[8]{0:T(128)S(1)} %compare_select_fusion.6.m._, f32[512,1024]{1,0:T(8,128)S(1)} %collective-permute-done.8.at_ref, f32[512,1024]{1,0:T(8,128)} %collective-permute-done.9.av_ref, bf16[4,512,1024]{2,1,0:T(8,128)(2,1)S(1)} %shard_map.60.own_ref), custom_call_target="tpu_custom_call" | custom-call | tf_op jit(solution)/shard_map/pallas_call | solution.py:129
  115.5 2.4 shard_map.84
  117.8 4.2 %collective-permute-done.12.come_pass.come_stay = f32[2,136,512]{2,1,0:T(8,128)S(1)} collective-permute-done((f32[2,136,512]{2,1,0:T(8,128)S(1)}, f32[2,136,512]{2,1,0:T(8,128)S(1)}, u32[]{:S(2)}, u32[]{:S(2)}) %collective-permute-start.12) | collective-permute-done | bytes 557088 | tf_op jit(solution)/shard_map/ppermute | solution.py:84
  123.3 5.7 %shard_map.72 = (f32[2,136,512]{2,1,0:T(8,128)S(1)}, f32[2,136,512]{2,1,0:T(8,128)S(1)}, f32[2,136,512]{2,1,0:T(8,128)S(1)}) custom-call(s32[8]{0:T(128)S(1)} %compare_select_fusion.6.m._, f32[512,1024]{1,0:T(8,128)S(1)} %collective-permute-done.8.at_ref, f32[512,1024]{1,0:T(8,128)} %collective-permute-done.9.av_ref, bf16[4,512,1024]{2,1,0:T(8,128)(2,1)S(1)} %shard_map.60.own_ref), custom_call_target="tpu_custom_call" | custom-call | tf_op jit(solution)/shard_map/pallas_call | solution.py:129
  129.6 4.4 %collective-permute-done.14.come_pass.come_stay = f32[2,136,512]{2,1,0:T(8,128)S(1)} collective-permute-done((f32[2,136,512]{2,1,0:T(8,128)S(1)}, f32[2,136,512]{2,1,0:T(8,128)S(1)}, u32[]{:S(2)}, u32[]{:S(2)}) %collective-permute-start.14) | collective-permute-done | bytes 557088 | tf_op jit(solution)/shard_map/ppermute | solution.py:84
  134.2 11.8 %collective-permute-done.16.come_pass.come_stay = f32[2,136,512]{2,1,0:T(8,128)S(1)} collective-permute-done((f32[2,136,512]{2,1,0:T(8,128)S(1)}, f32[2,136,512]{2,1,0:T(8,128)S(1)}, u32[]{:S(2)}, u32[]{:S(2)}) %collective-permute-start.16) | collective-permute-done | bytes 557088 | tf_op jit(solution)/shard_map/ppermute | solution.py:84
  152.6 4.5 %collective-permute-done.27.come_pass.come_stay = f32[2,128,512]{2,1,0:T(8,128)S(1)} collective-permute-done((f32[2,128,512]{2,1,0:T(8,128)S(1)}, f32[2,128,512]{2,1,0:T(8,128)S(1)}, u32[]{:S(2)}, u32[]{:S(2)}) %collective-permute-start.27) | collective-permute-done | bytes 524320 | tf_op jit(solution)/shard_map/ppermute | solution.py:84
  158.5 2.4 shard_map.63
  164.6 3.8 %collective-permute-done.29.come_pass.come_stay = f32[2,128,512]{2,1,0:T(8,128)S(1)} collective-permute-done((f32[2,128,512]{2,1,0:T(8,128)S(1)}, f32[2,128,512]{2,1,0:T(8,128)S(1)}, u32[]{:S(2)}, u32[]{:S(2)}) %collective-permute-start.29) | collective-permute-done | bytes 524320 | tf_op jit(solution)/shard_map/ppermute | solution.py:84
  169.7 20.8 %collective-permute-start.1 = (f32[2,512,128]{2,1,0:T(8,128)S(1)}, f32[2,512,128]{2,1,0:T(8,128)S(1)}, u32[]{:S(2)}, u32[]{:S(2)}) collective-permute-start(f32[2,512,128]{2,1,0:T(8,128)S(1)} %collective-permute-done.a_ref), channel_id=1, source_target_pairs={{0,1},{1,0},{2,3},{3,2},{4,5},{5,4},{6,7},{7,6},{8,9},{9,8},{10,11... | collective-permute-start | bytes 1572872 | tf_op jit(solution)/shard_map/ppermute | solution.py:84
  191.1 2.4 shard_map.82
  195.7 5.4 %collective-permute-done.21.refs_7_ = f32[136,512]{1,0:T(8,128)S(1)} collective-permute-done((f32[136,512]{1,0:T(8,128)S(1)}, f32[136,512]{1,0:T(8,128)S(1)}, u32[]{:S(2)}, u32[]{:S(2)}) %collective-permute-start.21) | collective-permute-done | bytes 278560 | tf_op jit(solution)/shard_map/ppermute | solution.py:84
  201.1 1.7 shard_map.80
  202.8 3.4 %collective-permute-start.22 = (f32[512,512]{1,0:T(8,128)}, f32[512,512]{1,0:T(8,128)}, u32[]{:S(2)}, u32[]{:S(2)}) collective-permute-start(f32[512,512]{1,0:T(8,128)} %get-tuple-element.53.refs_0_), channel_id=1, source_target_pairs={{0,4},{1,8},{4,0},{5,12},{8,5},{9,13},{12,1},{13,9},{18,22},{19,26... | collective-permute-start | bytes 3145736 | tf_op jit(solution)/shard_map/ppermute | solution.py:84
  209.5 2.8 collective-permute-start.36
  212.8 2.3 collective-permute-done.30.b_ref
  215.7 2.4 collective-permute-start.32
  220.4 28.8 %collective-permute-done.36.b_ref = f32[128,512]{1,0:T(8,128)S(1)} collective-permute-done((f32[128,512]{1,0:T(8,128)S(1)}, f32[128,512]{1,0:T(8,128)S(1)}, u32[]{:S(2)}, u32[]{:S(2)}) %collective-permute-start.36) | collective-permute-done | bytes 262176 | tf_op jit(solution)/shard_map/ppermute | solution.py:84
  250.5 2.1 collective-permute-start.38
  254.8 11.0 %collective-permute-done.37.refs_1_ = f32[128,512]{1,0:T(8,128)S(1)} collective-permute-done((f32[128,512]{1,0:T(8,128)S(1)}, f32[128,512]{1,0:T(8,128)S(1)}, u32[]{:S(2)}, u32[]{:S(2)}) %collective-permute-start.37) | collective-permute-done | bytes 262176 | tf_op jit(solution)/shard_map/ppermute | solution.py:84
  266.4 2.0 collective-permute-start.39
  269.2 4.5 %collective-permute-start.7 = (f32[128,512]{1,0:T(8,128)S(1)}, f32[128,512]{1,0:T(8,128)}, u32[]{:S(2)}, u32[]{:S(2)}) collective-permute-start(f32[128,512]{1,0:T(8,128)S(1)} %shard_map.66.value_ref), channel_id=1, source_target_pairs={{0,6},{1,14},{4,2},{5,10},{8,7},{9,15},{12,3},{13,11},{18,16},{19,... | collective-permute-start | bytes 786440 | tf_op jit(solution)/shard_map/ppermute | solution.py:84
  274.1 1.6 copy-done.3
  275.7 5.4 %shard_map.95 = (f32[512,1024]{1,0:T(8,128)}, f32[512,1024]{1,0:T(8,128)}) custom-call(s32[8]{0:T(128)S(1)} %compare_select_fusion.6.m._, f32[512,512]{1,0:T(8,128)} %get-tuple-element.53.refs_0_, f32[512,512]{1,0:T(8,128)} %collective-permute-done.22.refs_1_, f32[8,512]{1,0:T(8,128)S(1)} %get-tuple-element.54.refs_2_, f32[256,512]{1,0:T(8,128)S(1)} %shard_map.89.refs_3_, ...), custom_call_target="tpu_custom_call" | custom-call | tf_op jit(solution)/shard_map/pallas_call | solution.py:129
  (105 shorter events, 48.3 us)
Async XLA Ops:
  0.6 66.6 %collective-permute-start.8 = (f32[512,1024]{1,0:T(8,128)}, f32[512,1024]{1,0:T(8,128)S(1)}, u32[]{:S(2)}, u32[]{:S(2)}) collective-permute-start(f32[512,1024]{1,0:T(8,128)} %t_ref.15), channel_id=1, source_target_pairs={{0,1},{1,0},{2,3},{3,2},{4,5},{5,4},{6,7},{7,6},{8,9},{9,8},{10,11... | collective-permute-start | bytes 6291464 | tf_op jit(solution)/shard_map/ppermute | solution.py:84
  1.4 66.1 %collective-permute-start.9 = (f32[512,1024]{1,0:T(8,128)}, f32[512,1024]{1,0:T(8,128)}, u32[]{:S(2)}, u32[]{:S(2)}) collective-permute-start(f32[512,1024]{1,0:T(8,128)} %v_ref.15), channel_id=1, source_target_pairs={{0,1},{1,0},{2,3},{3,2},{4,5},{5,4},{6,7},{7,6},{8,9},{9,8},{10,11... | collective-permute-start | bytes 6291464 | tf_op jit(solution)/shard_map/ppermute | solution.py:84
  5.4 58.3 %collective-permute-start.2 = (f32[2,512,256]{2,1,0:T(8,128)S(1)}, f32[2,512,256]{2,1,0:T(8,128)S(1)}, u32[]{:S(2)}, u32[]{:S(2)}) collective-permute-start(f32[2,512,256]{2,1,0:T(8,128)S(1)} %shard_map.62), channel_id=1, source_target_pairs={{0,2},{1,3},{2,0},{3,1},{4,6},{5,7},{6,4},{7,5},{8,10},{9,11},{10,... | collective-permute-start | bytes 3145736 | tf_op jit(solution)/shard_map/ppermute | solution.py:84
  6.4 59.5 %collective-permute-start.25 = (f32[2,512,256]{2,1,0:T(8,128)S(1)}, f32[2,512,256]{2,1,0:T(8,128)S(1)}, u32[]{:S(2)}, u32[]{:S(2)}) collective-permute-start(f32[2,512,256]{2,1,0:T(8,128)S(1)} %shard_map.83), channel_id=1, source_target_pairs={{0,2},{1,3},{2,0},{3,1},{4,6},{5,7},{6,4},{7,5},{8,10},{9,11},{10,... | collective-permute-start | bytes 3145736 | tf_op jit(solution)/shard_map/ppermute | solution.py:84
  8.4 55.1 %collective-permute-start.33 = (f32[2,512,128]{2,1,0:T(8,128)S(1)}, f32[2,512,128]{2,1,0:T(8,128)S(1)}, u32[]{:S(2)}, u32[]{:S(2)}) collective-permute-start(f32[2,512,128]{2,1,0:T(8,128)S(1)} %shard_map.90), channel_id=1, source_target_pairs={{0,2},{1,3},{2,0},{3,1},{4,6},{5,7},{6,4},{7,5},{8,10},{9,11},{10,... | collective-permute-start | bytes 1572872 | tf_op jit(solution)/shard_map/ppermute | solution.py:84
  63.4 41.6 %collective-permute-start.23 = (f32[2,512,256]{2,1,0:T(8,128)S(1)}, f32[2,512,256]{2,1,0:T(8,128)S(1)}, u32[]{:S(2)}, u32[]{:S(2)}) collective-permute-start(f32[2,512,256]{2,1,0:T(8,128)S(1)} %shard_map.81), channel_id=1, source_target_pairs={{0,2},{1,3},{2,0},{3,1},{4,6},{5,7},{6,4},{7,5},{8,10},{9,11},{10,... | collective-permute-start | bytes 3145736 | tf_op jit(solution)/shard_map/ppermute | solution.py:84
  63.7 44.4 %collective-permute-start.3 = (f32[2,512,256]{2,1,0:T(8,128)S(1)}, f32[2,512,256]{2,1,0:T(8,128)S(1)}, u32[]{:S(2)}, u32[]{:S(2)}) collective-permute-start(f32[2,512,256]{2,1,0:T(8,128)S(1)} %collective-permute-done.2.a_ref), channel_id=1, source_target_pairs={{0,1},{1,0},{2,3},{3,2},{4,5},{5,4},{6,7},{7,6},{8,9},{9,8},{10,11... | collective-permute-start | bytes 3145736 | tf_op jit(solution)/shard_map/ppermute | solution.py:84
  65.9 32.2 %collective-permute-start = (f32[2,512,128]{2,1,0:T(8,128)S(1)}, f32[2,512,128]{2,1,0:T(8,128)S(1)}, u32[]{:S(2)}, u32[]{:S(2)}) collective-permute-start(f32[2,512,128]{2,1,0:T(8,128)S(1)} %shard_map.59), channel_id=1, source_target_pairs={{0,2},{1,3},{2,0},{3,1},{4,6},{5,7},{6,4},{7,5},{8,10},{9,11},{10,... | collective-permute-start | bytes 1572872 | tf_op jit(solution)/shard_map/ppermute | solution.py:84
  67.2 48.0 %collective-permute-start.26 = (f32[2,512,256]{2,1,0:T(8,128)S(1)}, f32[2,512,256]{2,1,0:T(8,128)S(1)}, u32[]{:S(2)}, u32[]{:S(2)}) collective-permute-start(f32[2,512,256]{2,1,0:T(8,128)S(1)} %collective-permute-done.25.a_ref), channel_id=1, source_target_pairs={{0,1},{1,0},{2,3},{3,2},{4,5},{5,4},{6,7},{7,6},{8,9},{9,8},{10,11... | collective-permute-start | bytes 3145736 | tf_op jit(solution)/shard_map/ppermute | solution.py:84
  67.5 37.9 %collective-permute-start.34 = (f32[2,512,128]{2,1,0:T(8,128)S(1)}, f32[2,512,128]{2,1,0:T(8,128)S(1)}, u32[]{:S(2)}, u32[]{:S(2)}) collective-permute-start(f32[2,512,128]{2,1,0:T(8,128)S(1)} %collective-permute-done.33.a_ref), channel_id=1, source_target_pairs={{0,1},{1,0},{2,3},{3,2},{4,5},{5,4},{6,7},{7,6},{8,9},{9,8},{10,11... | collective-permute-start | bytes 1572872 | tf_op jit(solution)/shard_map/ppermute | solution.py:84
  105.0 17.0 %collective-permute-start.12 = (f32[2,136,512]{2,1,0:T(8,128)S(1)}, f32[2,136,512]{2,1,0:T(8,128)S(1)}, u32[]{:S(2)}, u32[]{:S(2)}) collective-permute-start(f32[2,136,512]{2,1,0:T(8,128)S(1)} %get-tuple-element.42), channel_id=1, source_target_pairs={{0,4},{1,5},{2,6},{3,7},{4,0},{5,1},{6,2},{7,3},{8,12},{9,13},{10,... | collective-permute-start | bytes 1671176 | tf_op jit(solution)/shard_map/ppermute | solution.py:84
  105.4 46.0 %collective-permute-start.24 = (f32[2,512,256]{2,1,0:T(8,128)S(1)}, f32[2,512,256]{2,1,0:T(8,128)S(1)}, u32[]{:S(2)}, u32[]{:S(2)}) collective-permute-start(f32[2,512,256]{2,1,0:T(8,128)S(1)} %collective-permute-done.23.a_ref), channel_id=1, source_target_pairs={{0,1},{1,0},{2,3},{3,2},{4,5},{5,4},{6,7},{7,6},{8,9},{9,8},{10,11... | collective-permute-start | bytes 3145736 | tf_op jit(solution)/shard_map/ppermute | solution.py:84
  108.1 25.9 %collective-permute-start.14 = (f32[2,136,512]{2,1,0:T(8,128)S(1)}, f32[2,136,512]{2,1,0:T(8,128)S(1)}, u32[]{:S(2)}, u32[]{:S(2)}) collective-permute-start(f32[2,136,512]{2,1,0:T(8,128)S(1)} %get-tuple-element.46), channel_id=1, source_target_pairs={{0,4},{1,5},{2,6},{3,7},{4,0},{5,1},{6,2},{7,3},{8,12},{9,13},{10,... | collective-permute-start | bytes 1671176 | tf_op jit(solution)/shard_map/ppermute | solution.py:84
  110.1 35.8 %collective-permute-start.16 = (f32[2,136,512]{2,1,0:T(8,128)S(1)}, f32[2,136,512]{2,1,0:T(8,128)S(1)}, u32[]{:S(2)}, u32[]{:S(2)}) collective-permute-start(f32[2,136,512]{2,1,0:T(8,128)S(1)} %get-tuple-element.50), channel_id=1, source_target_pairs={{0,4},{1,5},{2,6},{3,7},{4,0},{5,1},{6,2},{7,3},{8,12},{9,13},{10,... | collective-permute-start | bytes 1671176 | tf_op jit(solution)/shard_map/ppermute | solution.py:84
  115.2 32.6 %collective-permute-start.11 = (f32[136,512]{1,0:T(8,128)S(1)}, f32[136,512]{1,0:T(8,128)S(1)}, u32[]{:S(2)}, u32[]{:S(2)}) collective-permute-start(f32[136,512]{1,0:T(8,128)S(1)} %get-tuple-element.40), channel_id=1, source_target_pairs={{0,8},{1,9},{2,10},{3,11},{4,12},{5,13},{6,14},{7,15},{8,0},{9,1},... | collective-permute-start | bytes 835592 | tf_op jit(solution)/shard_map/ppermute | solution.py:84
  122.1 35.1 %collective-permute-start.27 = (f32[2,128,512]{2,1,0:T(8,128)S(1)}, f32[2,128,512]{2,1,0:T(8,128)S(1)}, u32[]{:S(2)}, u32[]{:S(2)}) collective-permute-start(f32[2,128,512]{2,1,0:T(8,128)S(1)} %get-tuple-element.56), channel_id=1, source_target_pairs={{0,4},{1,5},{2,6},{3,7},{4,0},{5,1},{6,2},{7,3},{8,12},{9,13},{10,... | collective-permute-start | bytes 1572872 | tf_op jit(solution)/shard_map/ppermute | solution.py:84
  146.0 22.5 %collective-permute-start.29 = (f32[2,128,512]{2,1,0:T(8,128)S(1)}, f32[2,128,512]{2,1,0:T(8,128)S(1)}, u32[]{:S(2)}, u32[]{:S(2)}) collective-permute-start(f32[2,128,512]{2,1,0:T(8,128)S(1)} %get-tuple-element.60), channel_id=1, source_target_pairs={{0,4},{1,5},{2,6},{3,7},{4,0},{5,1},{6,2},{7,3},{8,12},{9,13},{10,... | collective-permute-start | bytes 1572872 | tf_op jit(solution)/shard_map/ppermute | solution.py:84
  151.3 18.4 %collective-permute-start.18 = (f32[136,512]{1,0:T(8,128)S(1)}, f32[136,512]{1,0:T(8,128)S(1)}, u32[]{:S(2)}, u32[]{:S(2)}) collective-permute-start(f32[136,512]{1,0:T(8,128)S(1)} %shard_map.71.refs_0_), channel_id=1, source_target_pairs={{2,18},{3,19},{6,22},{7,23},{10,26},{11,27},{14,30},{15,31},{16,0}... | collective-permute-start | bytes 835592 | tf_op jit(solution)/shard_map/ppermute | solution.py:84
  157.2 33.3 %collective-permute-start.19 = (f32[136,512]{1,0:T(8,128)S(1)}, f32[136,512]{1,0:T(8,128)S(1)}, u32[]{:S(2)}, u32[]{:S(2)}) collective-permute-start(f32[136,512]{1,0:T(8,128)S(1)} %shard_map.75.refs_1_), channel_id=1, source_target_pairs={{2,18},{3,19},{6,22},{7,23},{10,26},{11,27},{14,30},{15,31},{16,0}... | collective-permute-start | bytes 835592 | tf_op jit(solution)/shard_map/ppermute | solution.py:84
  160.9 41.9 %collective-permute-start.35 = (f32[2,128,512]{2,1,0:T(8,128)S(1)}, f32[2,128,512]{2,1,0:T(8,128)S(1)}, u32[]{:S(2)}, u32[]{:S(2)}) collective-permute-start(f32[2,128,512]{2,1,0:T(8,128)S(1)} %get-tuple-element.63), channel_id=1, source_target_pairs={{0,4},{1,5},{2,6},{3,7},{4,0},{5,1},{6,2},{7,3},{8,12},{9,13},{10,... | collective-permute-start | bytes 1572872 | tf_op jit(solution)/shard_map/ppermute | solution.py:84
  162.7 32.4 %collective-permute-start.20 = (f32[136,512]{1,0:T(8,128)S(1)}, f32[136,512]{1,0:T(8,128)S(1)}, u32[]{:S(2)}, u32[]{:S(2)}) collective-permute-start(f32[136,512]{1,0:T(8,128)S(1)} %shard_map.77.refs_2_), channel_id=1, source_target_pairs={{2,18},{3,19},{6,22},{7,23},{10,26},{11,27},{14,30},{15,31},{16,0}... | collective-permute-start | bytes 835592 | tf_op jit(solution)/shard_map/ppermute | solution.py:84
  168.4 32.7 %collective-permute-start.21 = (f32[136,512]{1,0:T(8,128)S(1)}, f32[136,512]{1,0:T(8,128)S(1)}, u32[]{:S(2)}, u32[]{:S(2)}) collective-permute-start(f32[136,512]{1,0:T(8,128)S(1)} %shard_map.79.refs_3_), channel_id=1, source_target_pairs={{2,18},{3,19},{6,22},{7,23},{10,26},{11,27},{14,30},{15,31},{16,0}... | collective-permute-start | bytes 835592 | tf_op jit(solution)/shard_map/ppermute | solution.py:84
  169.7 46.0 %collective-permute-start.1 = (f32[2,512,128]{2,1,0:T(8,128)S(1)}, f32[2,512,128]{2,1,0:T(8,128)S(1)}, u32[]{:S(2)}, u32[]{:S(2)}) collective-permute-start(f32[2,512,128]{2,1,0:T(8,128)S(1)} %collective-permute-done.a_ref), channel_id=1, source_target_pairs={{0,1},{1,0},{2,3},{3,2},{4,5},{5,4},{6,7},{7,6},{8,9},{9,8},{10,11... | collective-permute-start | bytes 1572872 | tf_op jit(solution)/shard_map/ppermute | solution.py:84
  190.5 29.2 %collective-permute-start.4 = (f32[2,128,512]{2,1,0:T(8,128)S(1)}, f32[2,128,512]{2,1,0:T(8,128)S(1)}, u32[]{:S(2)}, u32[]{:S(2)}) collective-permute-start(f32[2,128,512]{2,1,0:T(8,128)S(1)} %get-tuple-element.36), channel_id=1, source_target_pairs={{0,4},{1,5},{2,6},{3,7},{4,0},{5,1},{6,2},{7,3},{8,12},{9,13},{10,... | collective-permute-start | bytes 1572872 | tf_op jit(solution)/shard_map/ppermute | solution.py:84
  202.8 71.2 %collective-permute-start.22 = (f32[512,512]{1,0:T(8,128)}, f32[512,512]{1,0:T(8,128)}, u32[]{:S(2)}, u32[]{:S(2)}) collective-permute-start(f32[512,512]{1,0:T(8,128)} %get-tuple-element.53.refs_0_), channel_id=1, source_target_pairs={{0,4},{1,8},{4,0},{5,12},{8,5},{9,13},{12,1},{13,9},{18,22},{19,26... | collective-permute-start | bytes 3145736 | tf_op jit(solution)/shard_map/ppermute | solution.py:84
  209.5 39.7 %collective-permute-start.36 = (f32[128,512]{1,0:T(8,128)S(1)}, f32[128,512]{1,0:T(8,128)S(1)}, u32[]{:S(2)}, u32[]{:S(2)}) collective-permute-start(f32[128,512]{1,0:T(8,128)S(1)} %get-tuple-element.65), channel_id=1, source_target_pairs={{0,8},{1,9},{2,10},{3,11},{4,12},{5,13},{6,14},{7,15},{8,0},{9,1},... | collective-permute-start | bytes 786440 | tf_op jit(solution)/shard_map/ppermute | solution.py:84
  215.1 34.8 %collective-permute-start.31 = (f32[128,512]{1,0:T(8,128)S(1)}, f32[128,512]{1,0:T(8,128)S(1)}, u32[]{:S(2)}, u32[]{:S(2)}) collective-permute-start(f32[128,512]{1,0:T(8,128)S(1)} %shard_map.86.refs_0_), channel_id=1, source_target_pairs={{0,16},{1,17},{2,18},{3,19},{4,20},{5,21},{6,22},{7,23},{8,24},{9,... | collective-permute-start | bytes 786440 | tf_op jit(solution)/shard_map/ppermute | solution.py:84
  215.7 34.2 %collective-permute-start.32 = (f32[128,512]{1,0:T(8,128)S(1)}, f32[128,512]{1,0:T(8,128)S(1)}, u32[]{:S(2)}, u32[]{:S(2)}) collective-permute-start(f32[128,512]{1,0:T(8,128)S(1)} %shard_map.88.refs_1_), channel_id=1, source_target_pairs={{0,16},{1,17},{2,18},{3,19},{4,20},{5,21},{6,22},{7,23},{8,24},{9,... | collective-permute-start | bytes 786440 | tf_op jit(solution)/shard_map/ppermute | solution.py:84
  220.3 32.9 %collective-permute-start.5 = (f32[128,512]{1,0:T(8,128)S(1)}, f32[128,512]{1,0:T(8,128)S(1)}, u32[]{:S(2)}, u32[]{:S(2)}) collective-permute-start(f32[128,512]{1,0:T(8,128)S(1)} %get-tuple-element.38), channel_id=1, source_target_pairs={{0,8},{1,9},{2,10},{3,11},{4,12},{5,13},{6,14},{7,15},{8,0},{9,1},... | collective-permute-start | bytes 786440 | tf_op jit(solution)/shard_map/ppermute | solution.py:84
  249.8 16.0 %collective-permute-start.37 = (f32[128,512]{1,0:T(8,128)S(1)}, f32[128,512]{1,0:T(8,128)S(1)}, u32[]{:S(2)}, u32[]{:S(2)}) collective-permute-start(f32[128,512]{1,0:T(8,128)S(1)} %shard_map.93.refs_0_), channel_id=1, source_target_pairs={{0,16},{1,17},{2,18},{3,19},{4,20},{5,21},{6,22},{7,23},{8,24},{9,... | collective-permute-start | bytes 786440 | tf_op jit(solution)/shard_map/ppermute | solution.py:84
  250.5 23.5 %collective-permute-start.38 = (f32[256,512]{1,0:T(8,128)S(1)}, f32[256,512]{1,0:T(8,128)}, u32[]{:S(2)}, u32[]{:S(2)}) collective-permute-start(f32[256,512]{1,0:T(8,128)S(1)} %shard_map.89.refs_3_), channel_id=1, source_target_pairs={{0,6},{1,14},{4,2},{5,10},{8,7},{9,15},{12,3},{13,11},{18,16},{19,... | collective-permute-start | bytes 1572872 | tf_op jit(solution)/shard_map/ppermute | solution.py:84
  253.8 14.9 %collective-permute-start.6 = (f32[128,512]{1,0:T(8,128)S(1)}, f32[128,512]{1,0:T(8,128)S(1)}, u32[]{:S(2)}, u32[]{:S(2)}) collective-permute-start(f32[128,512]{1,0:T(8,128)S(1)} %shard_map.65.refs_0_), channel_id=1, source_target_pairs={{0,16},{1,17},{2,18},{3,19},{4,20},{5,21},{6,22},{7,23},{8,24},{9,... | collective-permute-start | bytes 786440 | tf_op jit(solution)/shard_map/ppermute | solution.py:84
  (14 other events, 179.1 us)

commit v4 on v3

--- a/solution.py
+++ b/solution.py
@@ -88,8 +88,12 @@
     return r >> 2 == c >> 1
 
 
+def flips(z, c):
+    return (z > c) ^ ((z ^ c) == 3)
+
+
 def flipped(z, x, c):
-    return x if z < c else 1 - x
+    return x ^ flips(z, c)
 
 
 def near_target(r, c):
@@ -108,7 +112,7 @@
     return (2 * c + flipped(z ^ 2, x, c), z ^ 2)
 
 
-X_PLACE, ODD, TURN_1, TURN_2, NEAR, MIDDLE, PLACE = range(7)
+X_PLACE, ODD, TURN_1, TURN_2, TURN_3, NEAR, MIDDLE, PLACE = range(8)
 VMEM = 40 * 2**20
 
 
@@ -295,14 +299,11 @@
 def far_kernel(side, m, a_ref, b_ref, own_ref, *outs):
     n = own_ref.shape[1]
     w = outs[0].shape[1]
-    count = len(outs)
-    right = own_right(own_ref, placed(m[TURN_2] ^ side, n))
-    left = jnp.concatenate([left_of(ref[0], ref[1]) for ref in (a_ref, b_ref)], axis=0)
-    block = crossed(left, right)
-    for d in range(2):
+    for d, (ref, turn) in enumerate(((a_ref, TURN_2), (b_ref, TURN_3))):
+        right = own_right(own_ref, placed(m[turn] ^ side, n))
+        block = crossed(left_of(ref[0], ref[1]), right)
         for i, out_ref in enumerate(outs):
-            first = (d * count + i) * w
-            out_ref[d] = block[first : first + w]
+            out_ref[d] = block[i * w : (i + 1) * w]
 
 
 def far_parts(meta, a, b, own, side):
@@ -465,11 +466,12 @@
     values = {
         X_PLACE: x,
         ODD: (z + c) % 2,
-        TURN_1: jnp.where(c % 2 == 1, x, 1 - x),
-        TURN_2: jnp.where(c // 2 == 1, x, 1 - x),
+        TURN_1: x ^ flips(c ^ 1, c),
+        TURN_2: x ^ flips(c ^ 2, c),
+        TURN_3: x ^ flips(c ^ 3, c),
         NEAR: r // 4 == c // 2,
         MIDDLE: z == c,
-        PLACE: jnp.where(z <= c, x, 1 - x),
+        PLACE: x ^ flips(z, c),
     }
     meta = jnp.zeros((8,), jnp.int32)
     for index, value in values.items():
@@ -527,7 +529,7 @@
 
 
 NEAR_GROUPS = ((1, (1, 2, 3)), (0, (0,)), (0, (1, 2, 3)))
-FAR_GROUPS = (("s0", 1, 0, 2), ("k0", 0, 0, 2), ("s1", 1, 2, 2), ("k1", 0, 2, 1), ("k2", 0, 3, 1))
+FAR_GROUPS = (("s0", 1, 0, 2), ("k0", 0, 0, 2), ("s1", 1, 2, 2), ("k1", 0, 2, 2))
 
 
 def gap_slices(shape, occ_energy, vir_energy):

time: 289 us -> 285 us (0.986)
  starting transfers between devices: 63.6 us -> 41 us
  waiting for transfers between devices: 160 us -> 180 us
    ppermute x40 -> x38, starting transfers between devices: 63.6 us -> 41 us  [routed(): return lax.ppermute(block, ('row', 'col'), route)]
    ppermute x40 -> x38, waiting for transfers between devices: 160 us -> 180 us  [routed(): return lax.ppermute(block, ('row', 'col'), route)]
    pallas_call x39 -> x37, Pallas kernels: 53.8 us -> 52.4 us  [call(): pl.pallas_call(kernel, out_shape=list(shapes), grid_spec=pltpu.PrefetchSc...]
  transfers between devices with their start and end apart: 40 -> 38, of which waited for: 16 -> 17; matrix products, arithmetic and copies ran while one was open for 0% -> 0% of each run, Pallas kernels for 18% -> 18%
where the time goes in v4:
time: 285 us; the launch traced here: 280 us
  waiting for transfers between devices  180 us (63%)
  Pallas kernels  52.4 us (18%)
  starting transfers between devices  41 us (14%)
  local copies, waits for them, and re-layouts  5.02 us (2%)
    ppermute x38, waiting for transfers between devices, routed(): return lax.ppermute(block, ('row', 'col'), route)  180 us
    pallas_call x37, Pallas kernels, call(): pl.pallas_call(kernel, out_shape=list(shapes), grid_spec=pltpu.PrefetchSc...  52.4 us
    ppermute x38, starting transfers between devices, routed(): return lax.ppermute(block, ('row', 'col'), route)  41 us
  transfers between devices with their start and end apart: 38, of which 17 were waited for; matrix products, arithmetic and copies ran while one was open for 0% of the time, Pallas kernels for 18%

profile of v4, /device:TPU:29, one launch (start us, length us, event | category | flops | bytes accessed | tf_op | source)
XLA Modules:
  0.0 280.3 jit_solution(8244642174056672122)
XLA Ops:
  9.5 20.3 %collective-permute-done.2.a_ref = f32[2,512,256]{2,1,0:T(8,128)S(1)} collective-permute-done((f32[2,512,256]{2,1,0:T(8,128)S(1)}, f32[2,512,256]{2,1,0:T(8,128)S(1)}, u32[]{:S(2)}, u32[]{:S(2)}) %collective-permute-start.2) | collective-permute-done | bytes 1048608 | tf_op jit(solution)/shard_map/ppermute | solution.py:84
  30.0 22.2 %collective-permute-done.23.a_ref = f32[2,512,256]{2,1,0:T(8,128)S(1)} collective-permute-done((f32[2,512,256]{2,1,0:T(8,128)S(1)}, f32[2,512,256]{2,1,0:T(8,128)S(1)}, u32[]{:S(2)}, u32[]{:S(2)}) %collective-permute-start.23) | collective-permute-done | bytes 1048608 | tf_op jit(solution)/shard_map/ppermute | solution.py:84
  52.2 2.2 collective-permute-start.3
  54.4 20.3 %collective-permute-done.25.a_ref = f32[2,512,256]{2,1,0:T(8,128)S(1)} collective-permute-done((f32[2,512,256]{2,1,0:T(8,128)S(1)}, f32[2,512,256]{2,1,0:T(8,128)S(1)}, u32[]{:S(2)}, u32[]{:S(2)}) %collective-permute-start.25) | collective-permute-done | bytes 1048608 | tf_op jit(solution)/shard_map/ppermute | solution.py:84
  74.7 2.2 collective-permute-start.26
  78.1 1.6 shard_map.68._
  79.7 2.1 shard_map.69
  83.1 5.7 %shard_map.73 = (f32[2,136,512]{2,1,0:T(8,128)S(1)}, f32[2,136,512]{2,1,0:T(8,128)S(1)}, f32[2,136,512]{2,1,0:T(8,128)S(1)}) custom-call(s32[8]{0:T(128)S(1)} %compare_select_fusion.7.m._, f32[512,1024]{1,0:T(8,128)S(1)} %collective-permute-done.8.at_ref, f32[512,1024]{1,0:T(8,128)} %collective-permute-done.9.av_ref, bf16[4,512,1024]{2,1,0:T(8,128)(2,1)S(1)} %shard_map.60.own_ref), custom_call_target="tpu_custom_call" | custom-call | tf_op jit(solution)/shard_map/pallas_call | solution.py:133
  88.8 8.3 %collective-permute-done.a_ref = f32[2,512,256]{2,1,0:T(8,128)S(1)} collective-permute-done((f32[2,512,256]{2,1,0:T(8,128)S(1)}, f32[2,512,256]{2,1,0:T(8,128)S(1)}, u32[]{:S(2)}, u32[]{:S(2)}) %collective-permute-start) | collective-permute-done | bytes 1048608 | tf_op jit(solution)/shard_map/ppermute | solution.py:84
  99.8 2.4 shard_map.84
  102.6 2.4 collective-permute-start.1
  105.0 3.2 %shard_map.67.keep_pass.keep_stay = f32[2,136,512]{2,1,0:T(8,128)S(1)} custom-call(s32[8]{0:T(128)S(1)} %compare_select_fusion.7.m._, f32[512,1024]{1,0:T(8,128)S(1)} %collective-permute-done.8.at_ref, f32[512,1024]{1,0:T(8,128)} %collective-permute-done.9.av_ref, bf16[4,512,1024]{2,1,0:T(8,128)(2,1)S(1)} %shard_map.60.own_ref), custom_call_target="tpu_custom_call" | custom-call | tf_op jit(solution)/shard_map/pallas_call | solution.py:133
  110.2 5.7 %shard_map.72 = (f32[2,136,512]{2,1,0:T(8,128)S(1)}, f32[2,136,512]{2,1,0:T(8,128)S(1)}, f32[2,136,512]{2,1,0:T(8,128)S(1)}) custom-call(s32[8]{0:T(128)S(1)} %compare_select_fusion.7.m._, f32[512,1024]{1,0:T(8,128)S(1)} %collective-permute-done.8.at_ref, f32[512,1024]{1,0:T(8,128)} %collective-permute-done.9.av_ref, bf16[4,512,1024]{2,1,0:T(8,128)(2,1)S(1)} %shard_map.60.own_ref), custom_call_target="tpu_custom_call" | custom-call | tf_op jit(solution)/shard_map/pallas_call | solution.py:133
  116.6 5.4 %collective-permute-done.14.come_pass.come_stay = f32[2,136,512]{2,1,0:T(8,128)S(1)} collective-permute-done((f32[2,136,512]{2,1,0:T(8,128)S(1)}, f32[2,136,512]{2,1,0:T(8,128)S(1)}, u32[]{:S(2)}, u32[]{:S(2)}) %collective-permute-start.14) | collective-permute-done | bytes 557088 | tf_op jit(solution)/shard_map/ppermute | solution.py:84
  122.8 22.4 %collective-permute-done.27.come_pass.come_stay = f32[2,128,512]{2,1,0:T(8,128)S(1)} collective-permute-done((f32[2,128,512]{2,1,0:T(8,128)S(1)}, f32[2,128,512]{2,1,0:T(8,128)S(1)}, u32[]{:S(2)}, u32[]{:S(2)}) %collective-permute-start.27) | collective-permute-done | bytes 524320 | tf_op jit(solution)/shard_map/ppermute | solution.py:84
  153.1 9.0 %collective-permute-done.17.b_ref = f32[136,512]{1,0:T(8,128)S(1)} collective-permute-done((f32[136,512]{1,0:T(8,128)S(1)}, f32[136,512]{1,0:T(8,128)S(1)}, u32[]{:S(2)}, u32[]{:S(2)}) %collective-permute-start.17) | collective-permute-done | bytes 278560 | tf_op jit(solution)/shard_map/ppermute | solution.py:84
  165.2 2.4 shard_map.63
  167.6 2.4 collective-permute-start.33
  170.0 17.6 %collective-permute-done.19.refs_5_ = f32[136,512]{1,0:T(8,128)S(1)} collective-permute-done((f32[136,512]{1,0:T(8,128)S(1)}, f32[136,512]{1,0:T(8,128)S(1)}, u32[]{:S(2)}, u32[]{:S(2)}) %collective-permute-start.19) | collective-permute-done | bytes 278560 | tf_op jit(solution)/shard_map/ppermute | solution.py:84
  187.6 2.4 shard_map.82
  190.6 3.0 %collective-permute-done.20.refs_6_ = f32[136,512]{1,0:T(8,128)S(1)} collective-permute-done((f32[136,512]{1,0:T(8,128)S(1)}, f32[136,512]{1,0:T(8,128)S(1)}, u32[]{:S(2)}, u32[]{:S(2)}) %collective-permute-start.20) | collective-permute-done | bytes 278560 | tf_op jit(solution)/shard_map/ppermute | solution.py:84
  194.2 5.4 %collective-permute-done.21.refs_7_ = f32[136,512]{1,0:T(8,128)S(1)} collective-permute-done((f32[136,512]{1,0:T(8,128)S(1)}, f32[136,512]{1,0:T(8,128)S(1)}, u32[]{:S(2)}, u32[]{:S(2)}) %collective-permute-start.21) | collective-permute-done | bytes 278560 | tf_op jit(solution)/shard_map/ppermute | solution.py:84
  199.6 1.7 shard_map.80
  201.3 1.9 collective-permute-start.22
  203.2 2.4 shard_map.61
  206.2 4.7 %collective-permute-start.34 = (f32[128,512]{1,0:T(8,128)S(1)}, f32[128,512]{1,0:T(8,128)S(1)}, u32[]{:S(2)}, u32[]{:S(2)}) collective-permute-start(f32[128,512]{1,0:T(8,128)S(1)} %get-tuple-element.69), channel_id=1, source_target_pairs={{0,8},{1,9},{2,10},{3,11},{4,12},{5,13},{6,14},{7,15},{8,0},{9,1},... | collective-permute-start | bytes 786440 | tf_op jit(solution)/shard_map/ppermute | solution.py:84
  215.3 31.8 %collective-permute-done.34.b_ref = f32[128,512]{1,0:T(8,128)S(1)} collective-permute-done((f32[128,512]{1,0:T(8,128)S(1)}, f32[128,512]{1,0:T(8,128)S(1)}, u32[]{:S(2)}, u32[]{:S(2)}) %collective-permute-start.34) | collective-permute-done | bytes 262176 | tf_op jit(solution)/shard_map/ppermute | solution.py:84
  248.4 2.1 collective-permute-start.36
  252.6 10.4 %collective-permute-done.35.refs_1_ = f32[128,512]{1,0:T(8,128)S(1)} collective-permute-done((f32[128,512]{1,0:T(8,128)S(1)}, f32[128,512]{1,0:T(8,128)S(1)}, u32[]{:S(2)}, u32[]{:S(2)}) %collective-permute-start.35) | collective-permute-done | bytes 262176 | tf_op jit(solution)/shard_map/ppermute | solution.py:84
  263.7 2.0 collective-permute-start.37
  266.5 4.2 %collective-permute-start.7 = (f32[128,512]{1,0:T(8,128)S(1)}, f32[128,512]{1,0:T(8,128)}, u32[]{:S(2)}, u32[]{:S(2)}) collective-permute-start(f32[128,512]{1,0:T(8,128)S(1)} %shard_map.66.value_ref), channel_id=1, source_target_pairs={{0,6},{1,10},{4,2},{5,14},{8,3},{9,15},{12,7},{13,11},{18,16},{19,... | collective-permute-start | bytes 786440 | tf_op jit(solution)/shard_map/ppermute | solution.py:84
  272.6 5.4 %shard_map.93 = (f32[512,1024]{1,0:T(8,128)}, f32[512,1024]{1,0:T(8,128)}) custom-call(s32[8]{0:T(128)S(1)} %compare_select_fusion.7.m._, f32[512,512]{1,0:T(8,128)} %get-tuple-element.56.refs_0_, f32[512,512]{1,0:T(8,128)} %collective-permute-done.22.refs_1_, f32[8,512]{1,0:T(8,128)S(1)} %get-tuple-element.57.refs_2_, f32[256,512]{1,0:T(8,128)S(1)} %shard_map.89.refs_3_, ...), custom_call_target="tpu_custom_call" | custom-call | tf_op jit(solution)/shard_map/pallas_call | solution.py:133
  (99 shorter events, 43.8 us)
Async XLA Ops:
  0.6 76.2 %collective-permute-start.8 = (f32[512,1024]{1,0:T(8,128)}, f32[512,1024]{1,0:T(8,128)S(1)}, u32[]{:S(2)}, u32[]{:S(2)}) collective-permute-start(f32[512,1024]{1,0:T(8,128)} %t_ref.13), channel_id=1, source_target_pairs={{0,1},{1,0},{2,3},{3,2},{4,5},{5,4},{6,7},{7,6},{8,9},{9,8},{10,11... | collective-permute-start | bytes 6291464 | tf_op jit(solution)/shard_map/ppermute | solution.py:84
  1.4 78.3 %collective-permute-start.9 = (f32[512,1024]{1,0:T(8,128)}, f32[512,1024]{1,0:T(8,128)}, u32[]{:S(2)}, u32[]{:S(2)}) collective-permute-start(f32[512,1024]{1,0:T(8,128)} %v_ref.13), channel_id=1, source_target_pairs={{0,1},{1,0},{2,3},{3,2},{4,5},{5,4},{6,7},{7,6},{8,9},{9,8},{10,11... | collective-permute-start | bytes 6291464 | tf_op jit(solution)/shard_map/ppermute | solution.py:84
  5.4 24.4 %collective-permute-start.2 = (f32[2,512,256]{2,1,0:T(8,128)S(1)}, f32[2,512,256]{2,1,0:T(8,128)S(1)}, u32[]{:S(2)}, u32[]{:S(2)}) collective-permute-start(f32[2,512,256]{2,1,0:T(8,128)S(1)} %shard_map.62), channel_id=1, source_target_pairs={{0,2},{1,3},{2,0},{3,1},{4,6},{5,7},{6,4},{7,5},{8,10},{9,11},{10,... | collective-permute-start | bytes 3145736 | tf_op jit(solution)/shard_map/ppermute | solution.py:84
  6.4 45.8 %collective-permute-start.23 = (f32[2,512,256]{2,1,0:T(8,128)S(1)}, f32[2,512,256]{2,1,0:T(8,128)S(1)}, u32[]{:S(2)}, u32[]{:S(2)}) collective-permute-start(f32[2,512,256]{2,1,0:T(8,128)S(1)} %shard_map.81), channel_id=1, source_target_pairs={{0,2},{1,3},{2,0},{3,1},{4,6},{5,7},{6,4},{7,5},{8,10},{9,11},{10,... | collective-permute-start | bytes 3145736 | tf_op jit(solution)/shard_map/ppermute | solution.py:84
  8.4 66.2 %collective-permute-start.25 = (f32[2,512,256]{2,1,0:T(8,128)S(1)}, f32[2,512,256]{2,1,0:T(8,128)S(1)}, u32[]{:S(2)}, u32[]{:S(2)}) collective-permute-start(f32[2,512,256]{2,1,0:T(8,128)S(1)} %shard_map.83), channel_id=1, source_target_pairs={{0,2},{1,3},{2,0},{3,1},{4,6},{5,7},{6,4},{7,5},{8,10},{9,11},{10,... | collective-permute-start | bytes 3145736 | tf_op jit(solution)/shard_map/ppermute | solution.py:84
  29.7 67.4 %collective-permute-start = (f32[2,512,256]{2,1,0:T(8,128)S(1)}, f32[2,512,256]{2,1,0:T(8,128)S(1)}, u32[]{:S(2)}, u32[]{:S(2)}) collective-permute-start(f32[2,512,256]{2,1,0:T(8,128)S(1)} %shard_map.59), channel_id=1, source_target_pairs={{0,2},{1,3},{2,0},{3,1},{4,6},{5,7},{6,4},{7,5},{8,10},{9,11},{10,... | collective-permute-start | bytes 3145736 | tf_op jit(solution)/shard_map/ppermute | solution.py:84
  52.2 46.2 %collective-permute-start.3 = (f32[2,512,256]{2,1,0:T(8,128)S(1)}, f32[2,512,256]{2,1,0:T(8,128)S(1)}, u32[]{:S(2)}, u32[]{:S(2)}) collective-permute-start(f32[2,512,256]{2,1,0:T(8,128)S(1)} %collective-permute-done.2.a_ref), channel_id=1, source_target_pairs={{0,1},{1,0},{2,3},{3,2},{4,5},{5,4},{6,7},{7,6},{8,9},{9,8},{10,11... | collective-permute-start | bytes 3145736 | tf_op jit(solution)/shard_map/ppermute | solution.py:84
  74.7 23.9 %collective-permute-start.26 = (f32[2,512,256]{2,1,0:T(8,128)S(1)}, f32[2,512,256]{2,1,0:T(8,128)S(1)}, u32[]{:S(2)}, u32[]{:S(2)}) collective-permute-start(f32[2,512,256]{2,1,0:T(8,128)S(1)} %collective-permute-done.25.a_ref), channel_id=1, source_target_pairs={{0,1},{1,0},{2,3},{3,2},{4,5},{5,4},{6,7},{7,6},{8,9},{9,8},{10,11... | collective-permute-start | bytes 3145736 | tf_op jit(solution)/shard_map/ppermute | solution.py:84
  76.8 25.4 %collective-permute-start.24 = (f32[2,512,256]{2,1,0:T(8,128)S(1)}, f32[2,512,256]{2,1,0:T(8,128)S(1)}, u32[]{:S(2)}, u32[]{:S(2)}) collective-permute-start(f32[2,512,256]{2,1,0:T(8,128)S(1)} %collective-permute-done.23.a_ref), channel_id=1, source_target_pairs={{0,1},{1,0},{2,3},{3,2},{4,5},{5,4},{6,7},{7,6},{8,9},{9,8},{10,11... | collective-permute-start | bytes 3145736 | tf_op jit(solution)/shard_map/ppermute | solution.py:84
  81.8 20.7 %collective-permute-start.10 = (f32[2,136,512]{2,1,0:T(8,128)S(1)}, f32[2,136,512]{2,1,0:T(8,128)S(1)}, u32[]{:S(2)}, u32[]{:S(2)}) collective-permute-start(f32[2,136,512]{2,1,0:T(8,128)S(1)} %shard_map.69), channel_id=1, source_target_pairs={{0,4},{1,5},{2,6},{3,7},{4,0},{5,1},{6,2},{7,3},{8,12},{9,13},{10,... | collective-permute-start | bytes 1671176 | tf_op jit(solution)/shard_map/ppermute | solution.py:84
  98.4 23.6 %collective-permute-start.14 = (f32[2,136,512]{2,1,0:T(8,128)S(1)}, f32[2,136,512]{2,1,0:T(8,128)S(1)}, u32[]{:S(2)}, u32[]{:S(2)}) collective-permute-start(f32[2,136,512]{2,1,0:T(8,128)S(1)} %get-tuple-element.49), channel_id=1, source_target_pairs={{0,4},{1,5},{2,6},{3,7},{4,0},{5,1},{6,2},{7,3},{8,12},{9,13},{10,... | collective-permute-start | bytes 1671176 | tf_op jit(solution)/shard_map/ppermute | solution.py:84
  98.6 46.7 %collective-permute-start.16 = (f32[2,136,512]{2,1,0:T(8,128)S(1)}, f32[2,136,512]{2,1,0:T(8,128)S(1)}, u32[]{:S(2)}, u32[]{:S(2)}) collective-permute-start(f32[2,136,512]{2,1,0:T(8,128)S(1)} %get-tuple-element.53), channel_id=1, source_target_pairs={{0,4},{1,5},{2,6},{3,7},{4,0},{5,1},{6,2},{7,3},{8,12},{9,13},{10,... | collective-permute-start | bytes 1671176 | tf_op jit(solution)/shard_map/ppermute | solution.py:84
  102.2 42.9 %collective-permute-start.27 = (f32[2,128,512]{2,1,0:T(8,128)S(1)}, f32[2,128,512]{2,1,0:T(8,128)S(1)}, u32[]{:S(2)}, u32[]{:S(2)}) collective-permute-start(f32[2,128,512]{2,1,0:T(8,128)S(1)} %get-tuple-element.59), channel_id=1, source_target_pairs={{0,4},{1,5},{2,6},{3,7},{4,0},{5,1},{6,2},{7,3},{8,12},{9,13},{10,... | collective-permute-start | bytes 1572872 | tf_op jit(solution)/shard_map/ppermute | solution.py:84
  102.6 98.7 %collective-permute-start.1 = (f32[2,512,256]{2,1,0:T(8,128)S(1)}, f32[2,512,256]{2,1,0:T(8,128)S(1)}, u32[]{:S(2)}, u32[]{:S(2)}) collective-permute-start(f32[2,512,256]{2,1,0:T(8,128)S(1)} %collective-permute-done.a_ref), channel_id=1, source_target_pairs={{0,1},{1,0},{2,3},{3,2},{4,5},{5,4},{6,7},{7,6},{8,9},{9,8},{10,11... | collective-permute-start | bytes 3145736 | tf_op jit(solution)/shard_map/ppermute | solution.py:84
  110.0 37.1 %collective-permute-start.11 = (f32[136,512]{1,0:T(8,128)S(1)}, f32[136,512]{1,0:T(8,128)S(1)}, u32[]{:S(2)}, u32[]{:S(2)}) collective-permute-start(f32[136,512]{1,0:T(8,128)S(1)} %get-tuple-element.43), channel_id=1, source_target_pairs={{0,8},{1,9},{2,10},{3,11},{4,12},{5,13},{6,14},{7,15},{8,0},{9,1},... | collective-permute-start | bytes 835592 | tf_op jit(solution)/shard_map/ppermute | solution.py:84
  122.0 27.1 %collective-permute-start.13 = (f32[136,512]{1,0:T(8,128)S(1)}, f32[136,512]{1,0:T(8,128)S(1)}, u32[]{:S(2)}, u32[]{:S(2)}) collective-permute-start(f32[136,512]{1,0:T(8,128)S(1)} %get-tuple-element.47), channel_id=1, source_target_pairs={{0,8},{1,9},{2,10},{3,11},{4,12},{5,13},{6,14},{7,15},{8,0},{9,1},... | collective-permute-start | bytes 835592 | tf_op jit(solution)/shard_map/ppermute | solution.py:84
  145.3 18.6 %collective-permute-start.29 = (f32[2,128,512]{2,1,0:T(8,128)S(1)}, f32[2,128,512]{2,1,0:T(8,128)S(1)}, u32[]{:S(2)}, u32[]{:S(2)}) collective-permute-start(f32[2,128,512]{2,1,0:T(8,128)S(1)} %get-tuple-element.63), channel_id=1, source_target_pairs={{0,4},{1,5},{2,6},{3,7},{4,0},{5,1},{6,2},{7,3},{8,12},{9,13},{10,... | collective-permute-start | bytes 1572872 | tf_op jit(solution)/shard_map/ppermute | solution.py:84
  147.2 14.9 %collective-permute-start.17 = (f32[136,512]{1,0:T(8,128)S(1)}, f32[136,512]{1,0:T(8,128)S(1)}, u32[]{:S(2)}, u32[]{:S(2)}) collective-permute-start(f32[136,512]{1,0:T(8,128)S(1)} %get-tuple-element.55), channel_id=1, source_target_pairs={{0,8},{1,9},{2,10},{3,11},{4,12},{5,13},{6,14},{7,15},{8,0},{9,1},... | collective-permute-start | bytes 835592 | tf_op jit(solution)/shard_map/ppermute | solution.py:84
  149.1 18.5 %collective-permute-start.18 = (f32[136,512]{1,0:T(8,128)S(1)}, f32[136,512]{1,0:T(8,128)S(1)}, u32[]{:S(2)}, u32[]{:S(2)}) collective-permute-start(f32[136,512]{1,0:T(8,128)S(1)} %shard_map.71.refs_0_), channel_id=1, source_target_pairs={{2,18},{3,19},{6,22},{7,23},{10,26},{11,27},{14,30},{15,31},{16,0}... | collective-permute-start | bytes 835592 | tf_op jit(solution)/shard_map/ppermute | solution.py:84
  151.2 36.4 %collective-permute-start.19 = (f32[136,512]{1,0:T(8,128)S(1)}, f32[136,512]{1,0:T(8,128)S(1)}, u32[]{:S(2)}, u32[]{:S(2)}) collective-permute-start(f32[136,512]{1,0:T(8,128)S(1)} %shard_map.75.refs_1_), channel_id=1, source_target_pairs={{2,18},{3,19},{6,22},{7,23},{10,26},{11,27},{14,30},{15,31},{16,0}... | collective-permute-start | bytes 835592 | tf_op jit(solution)/shard_map/ppermute | solution.py:84
  162.0 31.5 %collective-permute-start.20 = (f32[136,512]{1,0:T(8,128)S(1)}, f32[136,512]{1,0:T(8,128)S(1)}, u32[]{:S(2)}, u32[]{:S(2)}) collective-permute-start(f32[136,512]{1,0:T(8,128)S(1)} %shard_map.77.refs_2_), channel_id=1, source_target_pairs={{2,18},{3,19},{6,22},{7,23},{10,26},{11,27},{14,30},{15,31},{16,0}... | collective-permute-start | bytes 835592 | tf_op jit(solution)/shard_map/ppermute | solution.py:84
  163.9 35.7 %collective-permute-start.21 = (f32[136,512]{1,0:T(8,128)S(1)}, f32[136,512]{1,0:T(8,128)S(1)}, u32[]{:S(2)}, u32[]{:S(2)}) collective-permute-start(f32[136,512]{1,0:T(8,128)S(1)} %shard_map.79.refs_3_), channel_id=1, source_target_pairs={{2,18},{3,19},{6,22},{7,23},{10,26},{11,27},{14,30},{15,31},{16,0}... | collective-permute-start | bytes 835592 | tf_op jit(solution)/shard_map/ppermute | solution.py:84
  167.6 37.9 %collective-permute-start.33 = (f32[2,128,512]{2,1,0:T(8,128)S(1)}, f32[2,128,512]{2,1,0:T(8,128)S(1)}, u32[]{:S(2)}, u32[]{:S(2)}) collective-permute-start(f32[2,128,512]{2,1,0:T(8,128)S(1)} %get-tuple-element.67), channel_id=1, source_target_pairs={{0,4},{1,5},{2,6},{3,7},{4,0},{5,1},{6,2},{7,3},{8,12},{9,13},{10,... | collective-permute-start | bytes 1572872 | tf_op jit(solution)/shard_map/ppermute | solution.py:84
  187.6 27.0 %collective-permute-start.4 = (f32[2,128,512]{2,1,0:T(8,128)S(1)}, f32[2,128,512]{2,1,0:T(8,128)S(1)}, u32[]{:S(2)}, u32[]{:S(2)}) collective-permute-start(f32[2,128,512]{2,1,0:T(8,128)S(1)} %get-tuple-element.39), channel_id=1, source_target_pairs={{0,4},{1,5},{2,6},{3,7},{4,0},{5,1},{6,2},{7,3},{8,12},{9,13},{10,... | collective-permute-start | bytes 1572872 | tf_op jit(solution)/shard_map/ppermute | solution.py:84
  193.6 17.3 %collective-permute-start.28 = (f32[128,512]{1,0:T(8,128)S(1)}, f32[128,512]{1,0:T(8,128)S(1)}, u32[]{:S(2)}, u32[]{:S(2)}) collective-permute-start(f32[128,512]{1,0:T(8,128)S(1)} %get-tuple-element.61), channel_id=1, source_target_pairs={{0,8},{1,9},{2,10},{3,11},{4,12},{5,13},{6,14},{7,15},{8,0},{9,1},... | collective-permute-start | bytes 786440 | tf_op jit(solution)/shard_map/ppermute | solution.py:84
  201.3 69.8 %collective-permute-start.22 = (f32[512,512]{1,0:T(8,128)}, f32[512,512]{1,0:T(8,128)}, u32[]{:S(2)}, u32[]{:S(2)}) collective-permute-start(f32[512,512]{1,0:T(8,128)} %get-tuple-element.56.refs_0_), channel_id=1, source_target_pairs={{0,4},{1,8},{4,0},{5,12},{8,5},{9,13},{12,1},{13,9},{18,22},{19,26... | collective-permute-start | bytes 3145736 | tf_op jit(solution)/shard_map/ppermute | solution.py:84
  206.2 40.8 %collective-permute-start.34 = (f32[128,512]{1,0:T(8,128)S(1)}, f32[128,512]{1,0:T(8,128)S(1)}, u32[]{:S(2)}, u32[]{:S(2)}) collective-permute-start(f32[128,512]{1,0:T(8,128)S(1)} %get-tuple-element.69), channel_id=1, source_target_pairs={{0,8},{1,9},{2,10},{3,11},{4,12},{5,13},{6,14},{7,15},{8,0},{9,1},... | collective-permute-start | bytes 786440 | tf_op jit(solution)/shard_map/ppermute | solution.py:84
  211.5 36.3 %collective-permute-start.31 = (f32[128,512]{1,0:T(8,128)S(1)}, f32[128,512]{1,0:T(8,128)S(1)}, u32[]{:S(2)}, u32[]{:S(2)}) collective-permute-start(f32[128,512]{1,0:T(8,128)S(1)} %shard_map.86.refs_0_), channel_id=1, source_target_pairs={{0,16},{1,17},{2,18},{3,19},{4,20},{5,21},{6,22},{7,23},{8,24},{9,... | collective-permute-start | bytes 786440 | tf_op jit(solution)/shard_map/ppermute | solution.py:84
  213.7 34.1 %collective-permute-start.32 = (f32[128,512]{1,0:T(8,128)S(1)}, f32[128,512]{1,0:T(8,128)S(1)}, u32[]{:S(2)}, u32[]{:S(2)}) collective-permute-start(f32[128,512]{1,0:T(8,128)S(1)} %shard_map.88.refs_1_), channel_id=1, source_target_pairs={{0,16},{1,17},{2,18},{3,19},{4,20},{5,21},{6,22},{7,23},{8,24},{9,... | collective-permute-start | bytes 786440 | tf_op jit(solution)/shard_map/ppermute | solution.py:84
  215.2 36.5 %collective-permute-start.5 = (f32[128,512]{1,0:T(8,128)S(1)}, f32[128,512]{1,0:T(8,128)S(1)}, u32[]{:S(2)}, u32[]{:S(2)}) collective-permute-start(f32[128,512]{1,0:T(8,128)S(1)} %get-tuple-element.41), channel_id=1, source_target_pairs={{0,8},{1,9},{2,10},{3,11},{4,12},{5,13},{6,14},{7,15},{8,0},{9,1},... | collective-permute-start | bytes 786440 | tf_op jit(solution)/shard_map/ppermute | solution.py:84
  247.7 15.4 %collective-permute-start.35 = (f32[128,512]{1,0:T(8,128)S(1)}, f32[128,512]{1,0:T(8,128)S(1)}, u32[]{:S(2)}, u32[]{:S(2)}) collective-permute-start(f32[128,512]{1,0:T(8,128)S(1)} %shard_map.91.refs_0_), channel_id=1, source_target_pairs={{0,16},{1,17},{2,18},{3,19},{4,20},{5,21},{6,22},{7,23},{8,24},{9,... | collective-permute-start | bytes 786440 | tf_op jit(solution)/shard_map/ppermute | solution.py:84
  248.4 22.7 %collective-permute-start.36 = (f32[256,512]{1,0:T(8,128)S(1)}, f32[256,512]{1,0:T(8,128)}, u32[]{:S(2)}, u32[]{:S(2)}) collective-permute-start(f32[256,512]{1,0:T(8,128)S(1)} %shard_map.89.refs_3_), channel_id=1, source_target_pairs={{0,6},{1,10},{4,2},{5,14},{8,3},{9,15},{12,7},{13,11},{18,16},{19,... | collective-permute-start | bytes 1572872 | tf_op jit(solution)/shard_map/ppermute | solution.py:84
  (12 other events, 139.9 us)

commit v5 on v4

--- a/solution.py
+++ b/solution.py
@@ -373,8 +373,8 @@
 
 def most_kernel(m, *refs):
     near_own, near_back, extra_ref = refs[:3]
-    far_own, far_back = refs[3:5], refs[5:7]
-    t_ref, v_ref, row_ref, col_ref, new_ref, res_ref = refs[7:]
+    far_own, far_back = refs[3:4], refs[4:5]
+    t_ref, v_ref, row_ref, col_ref, new_ref, res_ref = refs[5:]
     n = t_ref.shape[0]
     place = m[PLACE]
 
@@ -412,19 +412,23 @@
     return call(most_kernel, [shaped(*t.shape)] * 2, meta, args)
 
 
-def late_kernel(turned, m, value_ref, _, __, t_ref, v_ref, row_ref, col_ref, new_ref, res_ref, new, res, sems):
-    n, w = max(value_ref.shape), min(value_ref.shape)
+def late_kernel(turned, chunk, count, m, *refs):
+    values = refs[:count]
+    t_ref, v_ref, row_ref, col_ref, new_ref, res_ref, new, res, sems = refs[count + 2 :]
+    w = min(values[0].shape)
+    n = max(values[0].shape)
 
     @pl.when(m[NEAR] == 0)
     def _():
-        value = value_ref[...].T if turned else value_ref[...]
+        parts = [ref[...].T if turned else ref[...] for ref in values]
+        value = parts[0] if count == 1 else jnp.concatenate(parts, axis=int(turned))
         new[...], res[...] = closing(
             t_ref[...], v_ref[...], row_ref[...], col_ref[...], value
         )
         if turned:
-            rows, cols = pl.ds(0, n), placed(1 - m[PLACE], n, n - w, w)
+            rows, cols = pl.ds(0, n), placed(1 - m[PLACE], n, chunk * w, count * w)
         else:
-            rows, cols = pl.ds(n - w, w), placed(m[PLACE], n)
+            rows, cols = pl.ds(chunk * w, count * w), placed(m[PLACE], n)
         copies = [
             pltpu.make_async_copy(source, target.at[rows, cols], sems.at[i])
             for i, (source, target) in enumerate(((new, new_ref), (res, res_ref)))
@@ -435,26 +439,27 @@
             copy.wait()
 
 
-def late(meta, turned, value, new, res, t, v, row_gap, col_gap):
-    w, n = value.shape
+def late(meta, turned, chunk, values, new, res, t, v, row_gap, col_gap):
+    w, n = values[0].shape
+    count = len(values)
     if turned:
-        at = lambda i, m: (0, (2 - m[PLACE]) * CHUNKS - 1)
-        block = pl.BlockSpec((n, w), at)
-        row, col = None, pl.BlockSpec((1, w), at)
+        at = lambda i, m: (0, ((1 - m[PLACE]) * CHUNKS + chunk) // count)
+        block = pl.BlockSpec((n, count * w), at)
+        row, col = None, pl.BlockSpec((1, count * w), at)
     else:
-        block = pl.BlockSpec((w, n), lambda i, m: (CHUNKS - 1, m[PLACE]))
-        row = pl.BlockSpec((w, 1), lambda i, m: (CHUNKS - 1, 0))
+        block = pl.BlockSpec((count * w, n), lambda i, m: (chunk // count, m[PLACE]))
+        row = pl.BlockSpec((count * w, 1), lambda i, m: (chunk // count, 0))
         col = pl.BlockSpec((1, n), lambda i, m: (0, m[PLACE]))
     hbm = pl.BlockSpec(memory_space=pl.ANY)
     return call(
-        functools.partial(late_kernel, turned),
+        functools.partial(late_kernel, turned, chunk, count),
         [shaped(*t.shape)] * 2,
         meta,
-        [value, new, res, t, v, row_gap, col_gap],
-        in_specs=[None, hbm, hbm, block, block, row, col],
+        [*values, new, res, t, v, row_gap, col_gap],
+        in_specs=[*[None] * count, hbm, hbm, block, block, row, col],
         out_specs=[hbm, hbm],
         scratch=[pltpu.VMEM(block.block_shape, jnp.float32)] * 2 + [pltpu.SemaphoreType.DMA((2,))],
-        aliases={2: 0, 3: 1},
+        aliases={count + 1: 0, count + 2: 1},
     )
 
 
@@ -523,9 +528,10 @@
         far_own += joined("f", chunks)
         far_back.append(back_far(far_own[-1]))
     fixed = (t, v, row_gap, col_gap)
-    pair = most(meta, t, near_own, near_back, extra, *far_own[:2], *far_back[:2], *fixed)
-    pair = late(meta, False, far_own[2], *pair, *fixed)
-    return late(meta, True, far_back[2], *pair, *fixed)
+    pair = most(meta, t, near_own, near_back, extra, far_own[0], far_back[0], *fixed)
+    pair = late(meta, False, 2, far_own[1:], *pair, *fixed)
+    pair = late(meta, True, 2, far_back[1:2], *pair, *fixed)
+    return late(meta, True, 3, far_back[2:], *pair, *fixed)
 
 
 NEAR_GROUPS = ((1, (1, 2, 3)), (0, (0,)), (0, (1, 2, 3)))

time: 285 us -> 286 us (level)
  waiting for transfers between devices: 180 us -> 188 us
  starting transfers between devices: 41 us -> 34.6 us
    ppermute x38, waiting for transfers between devices: 180 us -> 188 us  [routed(): return lax.ppermute(block, ('row', 'col'), route)]
    ppermute x38, starting transfers between devices: 41 us -> 34.6 us  [routed(): return lax.ppermute(block, ('row', 'col'), route)]
    pallas_call x37 -> x38, Pallas kernels: 52.4 us -> 53.9 us  [call(): pl.pallas_call(kernel, out_shape=list(shapes), grid_spec=pltpu.PrefetchSc...]
  transfers between devices with their start and end apart: 38 -> 38, of which waited for: 17 -> 20; matrix products, arithmetic and copies ran while one was open for 0% -> 0% of each run, Pallas kernels for 18% -> 19%
where the time goes in v5:
time: 286 us; the launch traced here: 282 us
  waiting for transfers between devices  188 us (66%)
  Pallas kernels  53.9 us (19%)
  starting transfers between devices  34.6 us (12%)
  local copies, waits for them, and re-layouts  5.02 us (2%)
    ppermute x38, waiting for transfers between devices, routed(): return lax.ppermute(block, ('row', 'col'), route)  188 us
    pallas_call x38, Pallas kernels, call(): pl.pallas_call(kernel, out_shape=list(shapes), grid_spec=pltpu.PrefetchSc...  53.9 us
    ppermute x38, starting transfers between devices, routed(): return lax.ppermute(block, ('row', 'col'), route)  34.6 us
  transfers between devices with their start and end apart: 38, of which 20 were waited for; matrix products, arithmetic and copies ran while one was open for 0% of the time, Pallas kernels for 19%

profile of v5, /device:TPU:29, one launch (start us, length us, event | category | flops | bytes accessed | tf_op | source)
XLA Modules:
  0.0 282.4 jit_solution(16647051966095784488)
XLA Ops:
  9.5 20.3 %collective-permute-done.2.a_ref = f32[2,512,256]{2,1,0:T(8,128)S(1)} collective-permute-done((f32[2,512,256]{2,1,0:T(8,128)S(1)}, f32[2,512,256]{2,1,0:T(8,128)S(1)}, u32[]{:S(2)}, u32[]{:S(2)}) %collective-permute-start.2) | collective-permute-done | bytes 1048608 | tf_op jit(solution)/shard_map/ppermute | solution.py:84
  30.0 22.2 %collective-permute-done.27.a_ref = f32[2,512,256]{2,1,0:T(8,128)S(1)} collective-permute-done((f32[2,512,256]{2,1,0:T(8,128)S(1)}, f32[2,512,256]{2,1,0:T(8,128)S(1)}, u32[]{:S(2)}, u32[]{:S(2)}) %collective-permute-start.27) | collective-permute-done | bytes 1048608 | tf_op jit(solution)/shard_map/ppermute | solution.py:84
  52.2 2.2 collective-permute-start.3
  54.4 20.3 %collective-permute-done.29.a_ref = f32[2,512,256]{2,1,0:T(8,128)S(1)} collective-permute-done((f32[2,512,256]{2,1,0:T(8,128)S(1)}, f32[2,512,256]{2,1,0:T(8,128)S(1)}, u32[]{:S(2)}, u32[]{:S(2)}) %collective-permute-start.29) | collective-permute-done | bytes 1048608 | tf_op jit(solution)/shard_map/ppermute | solution.py:84
  74.7 2.2 collective-permute-start.30
  79.7 2.1 shard_map.72
  83.1 5.7 %shard_map.76 = (f32[2,136,512]{2,1,0:T(8,128)S(1)}, f32[2,136,512]{2,1,0:T(8,128)S(1)}, f32[2,136,512]{2,1,0:T(8,128)S(1)}) custom-call(s32[8]{0:T(128)S(1)} %compare_select_fusion.7.m._, f32[512,1024]{1,0:T(8,128)S(1)} %collective-permute-done.12.at_ref, f32[512,1024]{1,0:T(8,128)} %collective-permute-done.13.av_ref, ...), custom_call_target="tpu_custom_call" | custom-call | tf_op jit(solution)/shard_map/pallas_call | solution.py:133
  88.8 8.3 %collective-permute-done.a_ref = f32[2,512,256]{2,1,0:T(8,128)S(1)} collective-permute-done((f32[2,512,256]{2,1,0:T(8,128)S(1)}, f32[2,512,256]{2,1,0:T(8,128)S(1)}, u32[]{:S(2)}, u32[]{:S(2)}) %collective-permute-start) | collective-permute-done | bytes 1048608 | tf_op jit(solution)/shard_map/ppermute | solution.py:84
  99.8 2.4 shard_map.87
  102.6 2.4 collective-permute-start.1
  105.0 3.2 %shard_map.70.keep_pass.keep_stay = f32[2,136,512]{2,1,0:T(8,128)S(1)} custom-call(s32[8]{0:T(128)S(1)} %compare_select_fusion.7.m._, f32[512,1024]{1,0:T(8,128)S(1)} %collective-permute-done.12.at_ref, f32[512,1024]{1,0:T(8,128)} %collective-permute-done.13.av_ref, bf16[4,512,1024]{2,1,0:T(8,128)(2,1)S(1)} %shard_map.60.own_ref), custom_call_target="tpu_custom_call" | custom-call | tf_op jit(solution)/shard_map/pallas_call | solution.py:133
  110.2 5.7 %shard_map.75 = (f32[2,136,512]{2,1,0:T(8,128)S(1)}, f32[2,136,512]{2,1,0:T(8,128)S(1)}, f32[2,136,512]{2,1,0:T(8,128)S(1)}) custom-call(s32[8]{0:T(128)S(1)} %compare_select_fusion.7.m._, f32[512,1024]{1,0:T(8,128)S(1)} %collective-permute-done.12.at_ref, f32[512,1024]{1,0:T(8,128)} %collective-permute-done.13.av_ref, ...), custom_call_target="tpu_custom_call" | custom-call | tf_op jit(solution)/shard_map/pallas_call | solution.py:133
  116.6 5.4 %collective-permute-done.18.come_pass.come_stay = f32[2,136,512]{2,1,0:T(8,128)S(1)} collective-permute-done((f32[2,136,512]{2,1,0:T(8,128)S(1)}, f32[2,136,512]{2,1,0:T(8,128)S(1)}, u32[]{:S(2)}, u32[]{:S(2)}) %collective-permute-start.18) | collective-permute-done | bytes 557088 | tf_op jit(solution)/shard_map/ppermute | solution.py:84
  122.8 22.4 %collective-permute-done.31.come_pass.come_stay = f32[2,128,512]{2,1,0:T(8,128)S(1)} collective-permute-done((f32[2,128,512]{2,1,0:T(8,128)S(1)}, f32[2,128,512]{2,1,0:T(8,128)S(1)}, u32[]{:S(2)}, u32[]{:S(2)}) %collective-permute-start.31) | collective-permute-done | bytes 524320 | tf_op jit(solution)/shard_map/ppermute | solution.py:84
  153.1 9.0 %collective-permute-done.21.b_ref = f32[136,512]{1,0:T(8,128)S(1)} collective-permute-done((f32[136,512]{1,0:T(8,128)S(1)}, f32[136,512]{1,0:T(8,128)S(1)}, u32[]{:S(2)}, u32[]{:S(2)}) %collective-permute-start.21) | collective-permute-done | bytes 278560 | tf_op jit(solution)/shard_map/ppermute | solution.py:84
  165.2 2.4 shard_map.63
  167.6 2.4 collective-permute-start.8
  170.0 17.6 %collective-permute-done.23.refs_5_ = f32[136,512]{1,0:T(8,128)S(1)} collective-permute-done((f32[136,512]{1,0:T(8,128)S(1)}, f32[136,512]{1,0:T(8,128)S(1)}, u32[]{:S(2)}, u32[]{:S(2)}) %collective-permute-start.23) | collective-permute-done | bytes 278560 | tf_op jit(solution)/shard_map/ppermute | solution.py:84
  187.6 2.4 shard_map.85
  190.6 3.0 %collective-permute-done.24.refs_6_ = f32[136,512]{1,0:T(8,128)S(1)} collective-permute-done((f32[136,512]{1,0:T(8,128)S(1)}, f32[136,512]{1,0:T(8,128)S(1)}, u32[]{:S(2)}, u32[]{:S(2)}) %collective-permute-start.24) | collective-permute-done | bytes 278560 | tf_op jit(solution)/shard_map/ppermute | solution.py:84
  194.2 5.4 %collective-permute-done.25.refs_7_ = f32[136,512]{1,0:T(8,128)S(1)} collective-permute-done((f32[136,512]{1,0:T(8,128)S(1)}, f32[136,512]{1,0:T(8,128)S(1)}, u32[]{:S(2)}, u32[]{:S(2)}) %collective-permute-start.25) | collective-permute-done | bytes 278560 | tf_op jit(solution)/shard_map/ppermute | solution.py:84
  203.2 2.4 shard_map.61
  208.1 7.5 %collective-permute-done.34.b_ref = f32[128,512]{1,0:T(8,128)S(1)} collective-permute-done((f32[128,512]{1,0:T(8,128)S(1)}, f32[128,512]{1,0:T(8,128)S(1)}, u32[]{:S(2)}, u32[]{:S(2)}) %collective-permute-start.34) | collective-permute-done | bytes 262176 | tf_op jit(solution)/shard_map/ppermute | solution.py:84
  219.1 7.6 %collective-permute-done.35.refs_2_ = f32[128,512]{1,0:T(8,128)S(1)} collective-permute-done((f32[128,512]{1,0:T(8,128)S(1)}, f32[128,512]{1,0:T(8,128)S(1)}, u32[]{:S(2)}, u32[]{:S(2)}) %collective-permute-start.35) | collective-permute-done | bytes 262176 | tf_op jit(solution)/shard_map/ppermute | solution.py:84
  226.7 5.7 %collective-permute-done.36.refs_3_ = f32[128,512]{1,0:T(8,128)S(1)} collective-permute-done((f32[128,512]{1,0:T(8,128)S(1)}, f32[128,512]{1,0:T(8,128)S(1)}, u32[]{:S(2)}, u32[]{:S(2)}) %collective-permute-start.36) | collective-permute-done | bytes 262176 | tf_op jit(solution)/shard_map/ppermute | solution.py:84
  233.0 2.2 collective-permute-start.37
  235.2 9.0 %collective-permute-done.9.b_ref = f32[128,512]{1,0:T(8,128)S(1)} collective-permute-done((f32[128,512]{1,0:T(8,128)S(1)}, f32[128,512]{1,0:T(8,128)S(1)}, u32[]{:S(2)}, u32[]{:S(2)}) %collective-permute-start.9) | collective-permute-done | bytes 262176 | tf_op jit(solution)/shard_map/ppermute | solution.py:84
  244.9 2.6 collective-permute-done.5.b_ref
  248.2 15.2 %collective-permute-done.10.refs_1_ = f32[128,512]{1,0:T(8,128)S(1)} collective-permute-done((f32[128,512]{1,0:T(8,128)S(1)}, f32[128,512]{1,0:T(8,128)S(1)}, u32[]{:S(2)}, u32[]{:S(2)}) %collective-permute-start.10) | collective-permute-done | bytes 262176 | tf_op jit(solution)/shard_map/ppermute | solution.py:84
  264.0 2.0 collective-permute-start.11
  266.0 2.7 collective-permute-done.6.refs_1_
  273.3 5.3 %shard_map.93 = (f32[512,1024]{1,0:T(8,128)}, f32[512,1024]{1,0:T(8,128)}) custom-call(s32[8]{0:T(128)S(1)} %compare_select_fusion.7.m._, f32[512,512]{1,0:T(8,128)} %get-tuple-element.62.refs_0_, f32[512,512]{1,0:T(8,128)} %collective-permute-done.26.refs_1_, f32[8,512]{1,0:T(8,128)S(1)} %get-tuple-element.63.refs_2_, f32[256,512]{1,0:T(8,128)S(1)} %shard_map.92.refs_3_, ...), custom_call_target="tpu_custom_call" | custom-call | tf_op jit(solution)/shard_map/pallas_call | solution.py:133
  (100 shorter events, 51.8 us)
Async XLA Ops:
  0.6 76.2 %collective-permute-start.12 = (f32[512,1024]{1,0:T(8,128)}, f32[512,1024]{1,0:T(8,128)S(1)}, u32[]{:S(2)}, u32[]{:S(2)}) collective-permute-start(f32[512,1024]{1,0:T(8,128)} %refs_3_.3), channel_id=1, source_target_pairs={{0,1},{1,0},{2,3},{3,2},{4,5},{5,4},{6,7},{7,6},{8,9},{9,8},{10,11... | collective-permute-start | bytes 6291464 | tf_op jit(solution)/shard_map/ppermute | solution.py:84
  1.4 78.3 %collective-permute-start.13 = (f32[512,1024]{1,0:T(8,128)}, f32[512,1024]{1,0:T(8,128)}, u32[]{:S(2)}, u32[]{:S(2)}) collective-permute-start(f32[512,1024]{1,0:T(8,128)} %refs_4_.5), channel_id=1, source_target_pairs={{0,1},{1,0},{2,3},{3,2},{4,5},{5,4},{6,7},{7,6},{8,9},{9,8},{10,11... | collective-permute-start | bytes 6291464 | tf_op jit(solution)/shard_map/ppermute | solution.py:84
  5.4 24.4 %collective-permute-start.2 = (f32[2,512,256]{2,1,0:T(8,128)S(1)}, f32[2,512,256]{2,1,0:T(8,128)S(1)}, u32[]{:S(2)}, u32[]{:S(2)}) collective-permute-start(f32[2,512,256]{2,1,0:T(8,128)S(1)} %shard_map.62), channel_id=1, source_target_pairs={{0,2},{1,3},{2,0},{3,1},{4,6},{5,7},{6,4},{7,5},{8,10},{9,11},{10,... | collective-permute-start | bytes 3145736 | tf_op jit(solution)/shard_map/ppermute | solution.py:84
  6.4 45.8 %collective-permute-start.27 = (f32[2,512,256]{2,1,0:T(8,128)S(1)}, f32[2,512,256]{2,1,0:T(8,128)S(1)}, u32[]{:S(2)}, u32[]{:S(2)}) collective-permute-start(f32[2,512,256]{2,1,0:T(8,128)S(1)} %shard_map.84), channel_id=1, source_target_pairs={{0,2},{1,3},{2,0},{3,1},{4,6},{5,7},{6,4},{7,5},{8,10},{9,11},{10,... | collective-permute-start | bytes 3145736 | tf_op jit(solution)/shard_map/ppermute | solution.py:84
  8.4 66.2 %collective-permute-start.29 = (f32[2,512,256]{2,1,0:T(8,128)S(1)}, f32[2,512,256]{2,1,0:T(8,128)S(1)}, u32[]{:S(2)}, u32[]{:S(2)}) collective-permute-start(f32[2,512,256]{2,1,0:T(8,128)S(1)} %shard_map.86), channel_id=1, source_target_pairs={{0,2},{1,3},{2,0},{3,1},{4,6},{5,7},{6,4},{7,5},{8,10},{9,11},{10,... | collective-permute-start | bytes 3145736 | tf_op jit(solution)/shard_map/ppermute | solution.py:84
  29.7 67.4 %collective-permute-start = (f32[2,512,256]{2,1,0:T(8,128)S(1)}, f32[2,512,256]{2,1,0:T(8,128)S(1)}, u32[]{:S(2)}, u32[]{:S(2)}) collective-permute-start(f32[2,512,256]{2,1,0:T(8,128)S(1)} %shard_map.59), channel_id=1, source_target_pairs={{0,2},{1,3},{2,0},{3,1},{4,6},{5,7},{6,4},{7,5},{8,10},{9,11},{10,... | collective-permute-start | bytes 3145736 | tf_op jit(solution)/shard_map/ppermute | solution.py:84
  52.2 46.2 %collective-permute-start.3 = (f32[2,512,256]{2,1,0:T(8,128)S(1)}, f32[2,512,256]{2,1,0:T(8,128)S(1)}, u32[]{:S(2)}, u32[]{:S(2)}) collective-permute-start(f32[2,512,256]{2,1,0:T(8,128)S(1)} %collective-permute-done.2.a_ref), channel_id=1, source_target_pairs={{0,1},{1,0},{2,3},{3,2},{4,5},{5,4},{6,7},{7,6},{8,9},{9,8},{10,11... | collective-permute-start | bytes 3145736 | tf_op jit(solution)/shard_map/ppermute | solution.py:84
  74.7 23.9 %collective-permute-start.30 = (f32[2,512,256]{2,1,0:T(8,128)S(1)}, f32[2,512,256]{2,1,0:T(8,128)S(1)}, u32[]{:S(2)}, u32[]{:S(2)}) collective-permute-start(f32[2,512,256]{2,1,0:T(8,128)S(1)} %collective-permute-done.29.a_ref), channel_id=1, source_target_pairs={{0,1},{1,0},{2,3},{3,2},{4,5},{5,4},{6,7},{7,6},{8,9},{9,8},{10,11... | collective-permute-start | bytes 3145736 | tf_op jit(solution)/shard_map/ppermute | solution.py:84
  76.8 25.4 %collective-permute-start.28 = (f32[2,512,256]{2,1,0:T(8,128)S(1)}, f32[2,512,256]{2,1,0:T(8,128)S(1)}, u32[]{:S(2)}, u32[]{:S(2)}) collective-permute-start(f32[2,512,256]{2,1,0:T(8,128)S(1)} %collective-permute-done.27.a_ref), channel_id=1, source_target_pairs={{0,1},{1,0},{2,3},{3,2},{4,5},{5,4},{6,7},{7,6},{8,9},{9,8},{10,11... | collective-permute-start | bytes 3145736 | tf_op jit(solution)/shard_map/ppermute | solution.py:84
  81.8 20.7 %collective-permute-start.14 = (f32[2,136,512]{2,1,0:T(8,128)S(1)}, f32[2,136,512]{2,1,0:T(8,128)S(1)}, u32[]{:S(2)}, u32[]{:S(2)}) collective-permute-start(f32[2,136,512]{2,1,0:T(8,128)S(1)} %shard_map.72), channel_id=1, source_target_pairs={{0,4},{1,5},{2,6},{3,7},{4,0},{5,1},{6,2},{7,3},{8,12},{9,13},{10,... | collective-permute-start | bytes 1671176 | tf_op jit(solution)/shard_map/ppermute | solution.py:84
  98.4 23.6 %collective-permute-start.18 = (f32[2,136,512]{2,1,0:T(8,128)S(1)}, f32[2,136,512]{2,1,0:T(8,128)S(1)}, u32[]{:S(2)}, u32[]{:S(2)}) collective-permute-start(f32[2,136,512]{2,1,0:T(8,128)S(1)} %get-tuple-element.55), channel_id=1, source_target_pairs={{0,4},{1,5},{2,6},{3,7},{4,0},{5,1},{6,2},{7,3},{8,12},{9,13},{10,... | collective-permute-start | bytes 1671176 | tf_op jit(solution)/shard_map/ppermute | solution.py:84
  98.6 46.7 %collective-permute-start.20 = (f32[2,136,512]{2,1,0:T(8,128)S(1)}, f32[2,136,512]{2,1,0:T(8,128)S(1)}, u32[]{:S(2)}, u32[]{:S(2)}) collective-permute-start(f32[2,136,512]{2,1,0:T(8,128)S(1)} %get-tuple-element.59), channel_id=1, source_target_pairs={{0,4},{1,5},{2,6},{3,7},{4,0},{5,1},{6,2},{7,3},{8,12},{9,13},{10,... | collective-permute-start | bytes 1671176 | tf_op jit(solution)/shard_map/ppermute | solution.py:84
  102.2 42.9 %collective-permute-start.31 = (f32[2,128,512]{2,1,0:T(8,128)S(1)}, f32[2,128,512]{2,1,0:T(8,128)S(1)}, u32[]{:S(2)}, u32[]{:S(2)}) collective-permute-start(f32[2,128,512]{2,1,0:T(8,128)S(1)} %get-tuple-element.65), channel_id=1, source_target_pairs={{0,4},{1,5},{2,6},{3,7},{4,0},{5,1},{6,2},{7,3},{8,12},{9,13},{10,... | collective-permute-start | bytes 1572872 | tf_op jit(solution)/shard_map/ppermute | solution.py:84
  102.6 98.7 %collective-permute-start.1 = (f32[2,512,256]{2,1,0:T(8,128)S(1)}, f32[2,512,256]{2,1,0:T(8,128)S(1)}, u32[]{:S(2)}, u32[]{:S(2)}) collective-permute-start(f32[2,512,256]{2,1,0:T(8,128)S(1)} %collective-permute-done.a_ref), channel_id=1, source_target_pairs={{0,1},{1,0},{2,3},{3,2},{4,5},{5,4},{6,7},{7,6},{8,9},{9,8},{10,11... | collective-permute-start | bytes 3145736 | tf_op jit(solution)/shard_map/ppermute | solution.py:84
  110.0 37.1 %collective-permute-start.15 = (f32[136,512]{1,0:T(8,128)S(1)}, f32[136,512]{1,0:T(8,128)S(1)}, u32[]{:S(2)}, u32[]{:S(2)}) collective-permute-start(f32[136,512]{1,0:T(8,128)S(1)} %get-tuple-element.49), channel_id=1, source_target_pairs={{0,8},{1,9},{2,10},{3,11},{4,12},{5,13},{6,14},{7,15},{8,0},{9,1},... | collective-permute-start | bytes 835592 | tf_op jit(solution)/shard_map/ppermute | solution.py:84
  122.0 27.1 %collective-permute-start.17 = (f32[136,512]{1,0:T(8,128)S(1)}, f32[136,512]{1,0:T(8,128)S(1)}, u32[]{:S(2)}, u32[]{:S(2)}) collective-permute-start(f32[136,512]{1,0:T(8,128)S(1)} %get-tuple-element.53), channel_id=1, source_target_pairs={{0,8},{1,9},{2,10},{3,11},{4,12},{5,13},{6,14},{7,15},{8,0},{9,1},... | collective-permute-start | bytes 835592 | tf_op jit(solution)/shard_map/ppermute | solution.py:84
  145.3 18.6 %collective-permute-start.33 = (f32[2,128,512]{2,1,0:T(8,128)S(1)}, f32[2,128,512]{2,1,0:T(8,128)S(1)}, u32[]{:S(2)}, u32[]{:S(2)}) collective-permute-start(f32[2,128,512]{2,1,0:T(8,128)S(1)} %get-tuple-element.69), channel_id=1, source_target_pairs={{0,4},{1,5},{2,6},{3,7},{4,0},{5,1},{6,2},{7,3},{8,12},{9,13},{10,... | collective-permute-start | bytes 1572872 | tf_op jit(solution)/shard_map/ppermute | solution.py:84
  149.1 18.5 %collective-permute-start.22 = (f32[136,512]{1,0:T(8,128)S(1)}, f32[136,512]{1,0:T(8,128)S(1)}, u32[]{:S(2)}, u32[]{:S(2)}) collective-permute-start(f32[136,512]{1,0:T(8,128)S(1)} %shard_map.74.refs_0_), channel_id=1, source_target_pairs={{2,18},{3,19},{6,22},{7,23},{10,26},{11,27},{14,30},{15,31},{16,0}... | collective-permute-start | bytes 835592 | tf_op jit(solution)/shard_map/ppermute | solution.py:84
  151.2 36.4 %collective-permute-start.23 = (f32[136,512]{1,0:T(8,128)S(1)}, f32[136,512]{1,0:T(8,128)S(1)}, u32[]{:S(2)}, u32[]{:S(2)}) collective-permute-start(f32[136,512]{1,0:T(8,128)S(1)} %shard_map.78.refs_1_), channel_id=1, source_target_pairs={{2,18},{3,19},{6,22},{7,23},{10,26},{11,27},{14,30},{15,31},{16,0}... | collective-permute-start | bytes 835592 | tf_op jit(solution)/shard_map/ppermute | solution.py:84
  162.0 31.5 %collective-permute-start.24 = (f32[136,512]{1,0:T(8,128)S(1)}, f32[136,512]{1,0:T(8,128)S(1)}, u32[]{:S(2)}, u32[]{:S(2)}) collective-permute-start(f32[136,512]{1,0:T(8,128)S(1)} %shard_map.80.refs_2_), channel_id=1, source_target_pairs={{2,18},{3,19},{6,22},{7,23},{10,26},{11,27},{14,30},{15,31},{16,0}... | collective-permute-start | bytes 835592 | tf_op jit(solution)/shard_map/ppermute | solution.py:84
  163.9 35.7 %collective-permute-start.25 = (f32[136,512]{1,0:T(8,128)S(1)}, f32[136,512]{1,0:T(8,128)S(1)}, u32[]{:S(2)}, u32[]{:S(2)}) collective-permute-start(f32[136,512]{1,0:T(8,128)S(1)} %shard_map.82.refs_3_), channel_id=1, source_target_pairs={{2,18},{3,19},{6,22},{7,23},{10,26},{11,27},{14,30},{15,31},{16,0}... | collective-permute-start | bytes 835592 | tf_op jit(solution)/shard_map/ppermute | solution.py:84
  167.6 48.7 %collective-permute-start.8 = (f32[2,128,512]{2,1,0:T(8,128)S(1)}, f32[2,128,512]{2,1,0:T(8,128)S(1)}, u32[]{:S(2)}, u32[]{:S(2)}) collective-permute-start(f32[2,128,512]{2,1,0:T(8,128)S(1)} %get-tuple-element.45), channel_id=1, source_target_pairs={{0,4},{1,5},{2,6},{3,7},{4,0},{5,1},{6,2},{7,3},{8,12},{9,13},{10,... | collective-permute-start | bytes 1572872 | tf_op jit(solution)/shard_map/ppermute | solution.py:84
  187.6 29.4 %collective-permute-start.4 = (f32[2,128,512]{2,1,0:T(8,128)S(1)}, f32[2,128,512]{2,1,0:T(8,128)S(1)}, u32[]{:S(2)}, u32[]{:S(2)}) collective-permute-start(f32[2,128,512]{2,1,0:T(8,128)S(1)} %get-tuple-element.41), channel_id=1, source_target_pairs={{0,4},{1,5},{2,6},{3,7},{4,0},{5,1},{6,2},{7,3},{8,12},{9,13},{10,... | collective-permute-start | bytes 1572872 | tf_op jit(solution)/shard_map/ppermute | solution.py:84
  199.6 16.1 %collective-permute-start.34 = (f32[128,512]{1,0:T(8,128)S(1)}, f32[128,512]{1,0:T(8,128)S(1)}, u32[]{:S(2)}, u32[]{:S(2)}) collective-permute-start(f32[128,512]{1,0:T(8,128)S(1)} %get-tuple-element.71), channel_id=1, source_target_pairs={{0,8},{1,9},{2,10},{3,11},{4,12},{5,13},{6,14},{7,15},{8,0},{9,1},... | collective-permute-start | bytes 786440 | tf_op jit(solution)/shard_map/ppermute | solution.py:84
  201.3 70.4 %collective-permute-start.26 = (f32[512,512]{1,0:T(8,128)}, f32[512,512]{1,0:T(8,128)}, u32[]{:S(2)}, u32[]{:S(2)}) collective-permute-start(f32[512,512]{1,0:T(8,128)} %get-tuple-element.62.refs_0_), channel_id=1, source_target_pairs={{0,4},{1,8},{4,0},{5,12},{8,5},{9,13},{12,1},{13,9},{18,22},{19,26... | collective-permute-start | bytes 3145736 | tf_op jit(solution)/shard_map/ppermute | solution.py:84
  208.0 18.7 %collective-permute-start.35 = (f32[128,512]{1,0:T(8,128)S(1)}, f32[128,512]{1,0:T(8,128)S(1)}, u32[]{:S(2)}, u32[]{:S(2)}) collective-permute-start(f32[128,512]{1,0:T(8,128)S(1)} %shard_map.89.refs_0_), channel_id=1, source_target_pairs={{0,16},{1,17},{2,18},{3,19},{4,20},{5,21},{6,22},{7,23},{8,24},{9,... | collective-permute-start | bytes 786440 | tf_op jit(solution)/shard_map/ppermute | solution.py:84
  216.2 16.2 %collective-permute-start.36 = (f32[128,512]{1,0:T(8,128)S(1)}, f32[128,512]{1,0:T(8,128)S(1)}, u32[]{:S(2)}, u32[]{:S(2)}) collective-permute-start(f32[128,512]{1,0:T(8,128)S(1)} %shard_map.91.refs_1_), channel_id=1, source_target_pairs={{0,16},{1,17},{2,18},{3,19},{4,20},{5,21},{6,22},{7,23},{8,24},{9,... | collective-permute-start | bytes 786440 | tf_op jit(solution)/shard_map/ppermute | solution.py:84
  216.9 27.3 %collective-permute-start.9 = (f32[128,512]{1,0:T(8,128)S(1)}, f32[128,512]{1,0:T(8,128)S(1)}, u32[]{:S(2)}, u32[]{:S(2)}) collective-permute-start(f32[128,512]{1,0:T(8,128)S(1)} %get-tuple-element.47), channel_id=1, source_target_pairs={{0,8},{1,9},{2,10},{3,11},{4,12},{5,13},{6,14},{7,15},{8,0},{9,1},... | collective-permute-start | bytes 786440 | tf_op jit(solution)/shard_map/ppermute | solution.py:84
  217.6 29.9 %collective-permute-start.5 = (f32[128,512]{1,0:T(8,128)S(1)}, f32[128,512]{1,0:T(8,128)S(1)}, u32[]{:S(2)}, u32[]{:S(2)}) collective-permute-start(f32[128,512]{1,0:T(8,128)S(1)} %get-tuple-element.43), channel_id=1, source_target_pairs={{0,8},{1,9},{2,10},{3,11},{4,12},{5,13},{6,14},{7,15},{8,0},{9,1},... | collective-permute-start | bytes 786440 | tf_op jit(solution)/shard_map/ppermute | solution.py:84
  233.0 38.7 %collective-permute-start.37 = (f32[256,512]{1,0:T(8,128)S(1)}, f32[256,512]{1,0:T(8,128)}, u32[]{:S(2)}, u32[]{:S(2)}) collective-permute-start(f32[256,512]{1,0:T(8,128)S(1)} %shard_map.92.refs_3_), channel_id=1, source_target_pairs={{0,6},{1,10},{4,2},{5,14},{8,3},{9,15},{12,7},{13,11},{18,16},{19,... | collective-permute-start | bytes 1572872 | tf_op jit(solution)/shard_map/ppermute | solution.py:84
  244.8 18.6 %collective-permute-start.10 = (f32[128,512]{1,0:T(8,128)S(1)}, f32[128,512]{1,0:T(8,128)S(1)}, u32[]{:S(2)}, u32[]{:S(2)}) collective-permute-start(f32[128,512]{1,0:T(8,128)S(1)} %shard_map.68.refs_0_), channel_id=1, source_target_pairs={{0,16},{1,17},{2,18},{3,19},{4,20},{5,21},{6,22},{7,23},{8,24},{9,... | collective-permute-start | bytes 786440 | tf_op jit(solution)/shard_map/ppermute | solution.py:84
  248.1 20.6 %collective-permute-start.6 = (f32[128,512]{1,0:T(8,128)S(1)}, f32[128,512]{1,0:T(8,128)S(1)}, u32[]{:S(2)}, u32[]{:S(2)}) collective-permute-start(f32[128,512]{1,0:T(8,128)S(1)} %shard_map.65.refs_0_), channel_id=1, source_target_pairs={{0,16},{1,17},{2,18},{3,19},{4,20},{5,21},{6,22},{7,23},{8,24},{9,... | collective-permute-start | bytes 786440 | tf_op jit(solution)/shard_map/ppermute | solution.py:84
  (12 other events, 225.3 us)

commit v6 on v5

--- a/solution.py
+++ b/solution.py
@@ -96,12 +96,14 @@
     return x ^ flips(z, c)
 
 
+def swap_target(r, c):
+    return (r ^ 1, c) if r >> 1 == c else None
+
+
 def near_target(r, c):
     z, x = r >> 1, r & 1
-    if not is_near(r, c):
+    if not is_near(r, c) or z == c:
         return None
-    if z == c:
-        return (r ^ 1, c)
     return (2 * c + flipped(z, x, c), z)
 
 
@@ -110,6 +112,14 @@
     if not is_near(r, c):
         return None
     return (2 * c + flipped(z ^ 2, x, c), z ^ 2)
+
+
+def hop_of(target):
+    return lambda r, c: target(r, c) and (r, c ^ 2)
+
+
+def after_hop(target):
+    return lambda r, c: target(r, c ^ 2)
 
 
 X_PLACE, ODD, TURN_1, TURN_2, TURN_3, NEAR, MIDDLE, PLACE = range(8)
@@ -372,9 +382,9 @@
 
 
 def most_kernel(m, *refs):
-    near_own, near_back, extra_ref = refs[:3]
-    far_own, far_back = refs[3:4], refs[4:5]
-    t_ref, v_ref, row_ref, col_ref, new_ref, res_ref = refs[5:]
+    near_own, near_swap, near_back, extra_ref = refs[:4]
+    far_own, far_back = refs[4:5], refs[5:6]
+    t_ref, v_ref, row_ref, col_ref, new_ref, res_ref = refs[6:]
     n = t_ref.shape[0]
     place = m[PLACE]
 
@@ -404,7 +414,7 @@
         lane = lax.broadcasted_iota(jnp.int32, (n, n), 1)
         own = near_own[...]
         write(0, n, placed(place, n), jnp.where(line >= lane, own, own.T))
-        lower = jnp.where(line > lane, near_back[...].T, extra_ref[:1, :])
+        lower = jnp.where(line > lane, near_swap[...].T, extra_ref[:1, :])
         write(0, n, placed(1 - place, n), jnp.where(line < lane, own, lower))
 
 
@@ -488,8 +498,7 @@
     over_z = lambda block: routed(block, lambda r, c: (r ^ 2, c))
     over_far = lambda block: routed(block, lambda r, c: (r ^ 4, c))
     to_near = lambda block: routed(block, lambda r, c: None if is_near(r, c) else (r ^ 4, c))
-    back_near = lambda block: routed(block, near_target)
-    back_far = lambda block: routed(block, far_target)
+    over = lambda target: lambda block: routed(block, target)
 
     next_t = beside(t)
     next_v = beside(v)
@@ -522,19 +531,26 @@
         return join(meta, [total[tag, k] for k in chunks], [come[tag, k] for k in chunks])
 
     near_own, extra = joined("n", range(CHUNKS))
-    near_back = back_near(near_own)
+    near_swap = over(swap_target)(near_own)
+    near_back = over(hop_of(near_target))(near_own)
+    near_back = over(after_hop(near_target))(near_back)
     far_own, far_back = [], []
-    for chunks in ((0, 1), (2,), (3,)):
+    for i, chunks in enumerate(((0, 1), (2,), (3,))):
         far_own += joined("f", chunks)
-        far_back.append(back_far(far_own[-1]))
+        if i in HOPS:
+            back = over(hop_of(far_target))(far_own[-1])
+            far_back.append(over(after_hop(far_target))(back))
+        else:
+            far_back.append(over(far_target)(far_own[-1]))
     fixed = (t, v, row_gap, col_gap)
-    pair = most(meta, t, near_own, near_back, extra, far_own[0], far_back[0], *fixed)
+    pair = most(meta, t, near_own, near_swap, near_back, extra, far_own[0], far_back[0], *fixed)
     pair = late(meta, False, 2, far_own[1:], *pair, *fixed)
     pair = late(meta, True, 2, far_back[1:2], *pair, *fixed)
     return late(meta, True, 3, far_back[2:], *pair, *fixed)
 
 
 NEAR_GROUPS = ((1, (1, 2, 3)), (0, (0,)), (0, (1, 2, 3)))
+HOPS = (0,)
 FAR_GROUPS = (("s0", 1, 0, 2), ("k0", 0, 0, 2), ("s1", 1, 2, 2), ("k1", 0, 2, 2))
 
 

time: 286 us -> 288 us (level)
  starting transfers between devices: 34.6 us -> 78.3 us
  waiting for transfers between devices: 188 us -> 146 us
    ppermute x38 -> x41, starting transfers between devices: 34.6 us -> 78.3 us  [routed(): return lax.ppermute(block, ('row', 'col'), route)]
    ppermute x38 -> x41, waiting for transfers between devices: 188 us -> 146 us  [routed(): return lax.ppermute(block, ('row', 'col'), route)]
  transfers between devices with their start and end apart: 38 -> 41, of which waited for: 20 -> 16; matrix products, arithmetic and copies ran while one was open for 0% -> 0% of each run, Pallas kernels for 19% -> 18%
where the time goes in v6:
time: 288 us; the launch traced here: 285 us
  waiting for transfers between devices  146 us (51%)
  starting transfers between devices  78.3 us (27%)
  Pallas kernels  54.2 us (19%)
  local copies, waits for them, and re-layouts  5.02 us (2%)
    ppermute x41, waiting for transfers between devices, routed(): return lax.ppermute(block, ('row', 'col'), route)  146 us
    ppermute x41, starting transfers between devices, routed(): return lax.ppermute(block, ('row', 'col'), route)  78.3 us
    pallas_call x38, Pallas kernels, call(): pl.pallas_call(kernel, out_shape=list(shapes), grid_spec=pltpu.PrefetchSc...  54.2 us
  transfers between devices with their start and end apart: 41, of which 16 were waited for; matrix products, arithmetic and copies ran while one was open for 0% of the time, Pallas kernels for 18%

profile of v6, /device:TPU:29, one launch (start us, length us, event | category | flops | bytes accessed | tf_op | source)
XLA Modules:
  0.0 285.2 jit_solution(15788291615426706956)
XLA Ops:
  13.6 2.1 shard_map.72
  17.0 5.7 %shard_map.76 = (f32[2,136,512]{2,1,0:T(8,128)S(1)}, f32[2,136,512]{2,1,0:T(8,128)S(1)}, f32[2,136,512]{2,1,0:T(8,128)S(1)}) custom-call(s32[8]{0:T(128)S(1)} %compare_select_fusion.7.m._, f32[512,1024]{1,0:T(8,128)S(1)} %collective-permute-done.12.at_ref, f32[512,1024]{1,0:T(8,128)} %collective-permute-done.13.av_ref, ...), custom_call_target="tpu_custom_call" | custom-call | tf_op jit(solution)/shard_map/pallas_call | solution.py:143
  22.7 7.0 %collective-permute-done.a_ref = f32[2,512,256]{2,1,0:T(8,128)S(1)} collective-permute-done((f32[2,512,256]{2,1,0:T(8,128)S(1)}, f32[2,512,256]{2,1,0:T(8,128)S(1)}, u32[]{:S(2)}, u32[]{:S(2)}) %collective-permute-start) | collective-permute-done | bytes 1048608 | tf_op jit(solution)/shard_map/ppermute | solution.py:84
  30.9 21.3 %collective-permute-done.2.a_ref = f32[2,512,256]{2,1,0:T(8,128)S(1)} collective-permute-done((f32[2,512,256]{2,1,0:T(8,128)S(1)}, f32[2,512,256]{2,1,0:T(8,128)S(1)}, u32[]{:S(2)}, u32[]{:S(2)}) %collective-permute-start.2) | collective-permute-done | bytes 1048608 | tf_op jit(solution)/shard_map/ppermute | solution.py:84
  53.4 21.3 %collective-permute-done.29.a_ref = f32[2,512,256]{2,1,0:T(8,128)S(1)} collective-permute-done((f32[2,512,256]{2,1,0:T(8,128)S(1)}, f32[2,512,256]{2,1,0:T(8,128)S(1)}, u32[]{:S(2)}, u32[]{:S(2)}) %collective-permute-start.29) | collective-permute-done | bytes 1048608 | tf_op jit(solution)/shard_map/ppermute | solution.py:84
  75.9 21.3 %collective-permute-done.31.a_ref = f32[2,512,256]{2,1,0:T(8,128)S(1)} collective-permute-done((f32[2,512,256]{2,1,0:T(8,128)S(1)}, f32[2,512,256]{2,1,0:T(8,128)S(1)}, u32[]{:S(2)}, u32[]{:S(2)}) %collective-permute-start.31) | collective-permute-done | bytes 1048608 | tf_op jit(solution)/shard_map/ppermute | solution.py:84
  98.4 3.2 %shard_map.70.keep_pass.keep_stay = f32[2,136,512]{2,1,0:T(8,128)S(1)} custom-call(s32[8]{0:T(128)S(1)} %compare_select_fusion.7.m._, f32[512,1024]{1,0:T(8,128)S(1)} %collective-permute-done.12.at_ref, f32[512,1024]{1,0:T(8,128)} %collective-permute-done.13.av_ref, bf16[4,512,1024]{2,1,0:T(8,128)(2,1)S(1)} %shard_map.60.own_ref), custom_call_target="tpu_custom_call" | custom-call | tf_op jit(solution)/shard_map/pallas_call | solution.py:143
  102.5 5.7 %shard_map.75 = (f32[2,136,512]{2,1,0:T(8,128)S(1)}, f32[2,136,512]{2,1,0:T(8,128)S(1)}, f32[2,136,512]{2,1,0:T(8,128)S(1)}) custom-call(s32[8]{0:T(128)S(1)} %compare_select_fusion.7.m._, f32[512,1024]{1,0:T(8,128)S(1)} %collective-permute-done.12.at_ref, f32[512,1024]{1,0:T(8,128)} %collective-permute-done.13.av_ref, ...), custom_call_target="tpu_custom_call" | custom-call | tf_op jit(solution)/shard_map/pallas_call | solution.py:143
  113.7 2.7 collective-permute-done.17.b_ref
  118.3 10.1 %collective-permute-done.19.b_ref = f32[136,512]{1,0:T(8,128)S(1)} collective-permute-done((f32[136,512]{1,0:T(8,128)S(1)}, f32[136,512]{1,0:T(8,128)S(1)}, u32[]{:S(2)}, u32[]{:S(2)}) %collective-permute-start.19) | collective-permute-done | bytes 278560 | tf_op jit(solution)/shard_map/ppermute | solution.py:84
  130.2 4.1 %collective-permute-done.21.b_ref = f32[136,512]{1,0:T(8,128)S(1)} collective-permute-done((f32[136,512]{1,0:T(8,128)S(1)}, f32[136,512]{1,0:T(8,128)S(1)}, u32[]{:S(2)}, u32[]{:S(2)}) %collective-permute-start.21) | collective-permute-done | bytes 278560 | tf_op jit(solution)/shard_map/ppermute | solution.py:84
  137.7 2.4 shard_map.87
  141.4 17.7 %collective-permute-done.23.refs_5_ = f32[136,512]{1,0:T(8,128)S(1)} collective-permute-done((f32[136,512]{1,0:T(8,128)S(1)}, f32[136,512]{1,0:T(8,128)S(1)}, u32[]{:S(2)}, u32[]{:S(2)}) %collective-permute-start.23) | collective-permute-done | bytes 278560 | tf_op jit(solution)/shard_map/ppermute | solution.py:84
  159.7 5.4 %collective-permute-done.24.refs_6_ = f32[136,512]{1,0:T(8,128)S(1)} collective-permute-done((f32[136,512]{1,0:T(8,128)S(1)}, f32[136,512]{1,0:T(8,128)S(1)}, u32[]{:S(2)}, u32[]{:S(2)}) %collective-permute-start.24) | collective-permute-done | bytes 278560 | tf_op jit(solution)/shard_map/ppermute | solution.py:84
  166.3 4.8 %collective-permute-done.25.refs_7_ = f32[136,512]{1,0:T(8,128)S(1)} collective-permute-done((f32[136,512]{1,0:T(8,128)S(1)}, f32[136,512]{1,0:T(8,128)S(1)}, u32[]{:S(2)}, u32[]{:S(2)}) %collective-permute-start.25) | collective-permute-done | bytes 278560 | tf_op jit(solution)/shard_map/ppermute | solution.py:84
  171.5 1.7 shard_map.83
  174.9 2.4 shard_map.85
  177.9 2.0 collective-permute-start.34
  180.6 5.6 %collective-permute-done.34.b_ref = f32[128,512]{1,0:T(8,128)S(1)} collective-permute-done((f32[128,512]{1,0:T(8,128)S(1)}, f32[128,512]{1,0:T(8,128)S(1)}, u32[]{:S(2)}, u32[]{:S(2)}) %collective-permute-start.34) | collective-permute-done | bytes 262176 | tf_op jit(solution)/shard_map/ppermute | solution.py:84
  186.8 6.0 %collective-permute-done.36.b_ref = f32[128,512]{1,0:T(8,128)S(1)} collective-permute-done((f32[128,512]{1,0:T(8,128)S(1)}, f32[128,512]{1,0:T(8,128)S(1)}, u32[]{:S(2)}, u32[]{:S(2)}) %collective-permute-start.36) | collective-permute-done | bytes 262176 | tf_op jit(solution)/shard_map/ppermute | solution.py:84
  193.6 2.4 shard_map.63
  197.2 9.0 %collective-permute-done.37.refs_2_ = f32[128,512]{1,0:T(8,128)S(1)} collective-permute-done((f32[128,512]{1,0:T(8,128)S(1)}, f32[128,512]{1,0:T(8,128)S(1)}, u32[]{:S(2)}, u32[]{:S(2)}) %collective-permute-start.37) | collective-permute-done | bytes 262176 | tf_op jit(solution)/shard_map/ppermute | solution.py:84
  207.5 4.4 %collective-permute-done.38.refs_3_ = f32[128,512]{1,0:T(8,128)S(1)} collective-permute-done((f32[128,512]{1,0:T(8,128)S(1)}, f32[128,512]{1,0:T(8,128)S(1)}, u32[]{:S(2)}, u32[]{:S(2)}) %collective-permute-start.38) | collective-permute-done | bytes 262176 | tf_op jit(solution)/shard_map/ppermute | solution.py:84
  212.5 4.4 %collective-permute-start.39 = (f32[256,512]{1,0:T(8,128)S(1)}, f32[256,512]{1,0:T(8,128)}, u32[]{:S(2)}, u32[]{:S(2)}) collective-permute-start(f32[256,512]{1,0:T(8,128)S(1)} %shard_map.92.refs_4_), channel_id=1, source_target_pairs={{0,2},{1,3},{4,6},{5,7},{8,10},{9,11},{12,14},{13,15},{18,16},{19,... | collective-permute-start | bytes 1572872 | tf_op jit(solution)/shard_map/ppermute | solution.py:84
  216.9 3.2 %collective-permute-start.26 = (f32[512,512]{1,0:T(8,128)}, f32[512,512]{1,0:T(8,128)}, u32[]{:S(2)}, u32[]{:S(2)}) collective-permute-start(f32[512,512]{1,0:T(8,128)} %get-tuple-element.62.refs_0_), channel_id=1, source_target_pairs={{0,4},{4,0},{9,13},{13,9},{18,22},{22,18},{27,31},{31,27}} | collective-permute-start | bytes 3145736 | tf_op jit(solution)/shard_map/ppermute | solution.py:84
  221.7 2.4 shard_map.61
  228.4 4.6 %collective-permute-done.9.b_ref = f32[128,512]{1,0:T(8,128)S(1)} collective-permute-done((f32[128,512]{1,0:T(8,128)S(1)}, f32[128,512]{1,0:T(8,128)S(1)}, u32[]{:S(2)}, u32[]{:S(2)}) %collective-permute-start.9) | collective-permute-done | bytes 262176 | tf_op jit(solution)/shard_map/ppermute | solution.py:84
  233.7 10.1 %collective-permute-start.10 = (f32[128,512]{1,0:T(8,128)S(1)}, f32[128,512]{1,0:T(8,128)S(1)}, u32[]{:S(2)}, u32[]{:S(2)}) collective-permute-start(f32[128,512]{1,0:T(8,128)S(1)} %shard_map.68.refs_0_), channel_id=1, source_target_pairs={{0,16},{1,17},{2,18},{3,19},{4,20},{5,21},{6,22},{7,23},{8,24},{9,... | collective-permute-start | bytes 786440 | tf_op jit(solution)/shard_map/ppermute | solution.py:84
  244.3 2.2 collective-permute-start.6
  248.1 20.0 %collective-permute-start.11 = (f32[128,512]{1,0:T(8,128)S(1)}, f32[128,512]{1,0:T(8,128)}, u32[]{:S(2)}, u32[]{:S(2)}) collective-permute-start(f32[128,512]{1,0:T(8,128)S(1)} %shard_map.69.refs_0_), channel_id=1, source_target_pairs={{0,6},{1,10},{4,2},{5,14},{8,3},{9,15},{12,7},{13,11},{18,16},{19,... | collective-permute-start | bytes 786440 | tf_op jit(solution)/shard_map/ppermute | solution.py:84
  268.6 5.1 %collective-permute-start.7 = (f32[128,512]{1,0:T(8,128)S(1)}, f32[128,512]{1,0:T(8,128)}, u32[]{:S(2)}, u32[]{:S(2)}) collective-permute-start(f32[128,512]{1,0:T(8,128)S(1)} %shard_map.66.refs_1_), channel_id=1, source_target_pairs={{0,6},{1,10},{4,2},{5,14},{8,3},{9,15},{12,7},{13,11},{18,16},{19,... | collective-permute-start | bytes 786440 | tf_op jit(solution)/shard_map/ppermute | solution.py:84
  275.7 5.6 %shard_map.93 = (f32[512,1024]{1,0:T(8,128)}, f32[512,1024]{1,0:T(8,128)}) custom-call(s32[8]{0:T(128)S(1)} %compare_select_fusion.7.m._, f32[512,512]{1,0:T(8,128)} %get-tuple-element.62.refs_0_, f32[512,512]{1,0:T(8,128)} %collective-permute-done.26.refs_1_, f32[512,512]{1,0:T(8,128)} %collective-permute-done.28.refs_2_, ...), custom_call_target="tpu_custom_call" | custom-call | tf_op jit(solution)/shard_map/pallas_call | solution.py:143
  (106 shorter events, 58.0 us)
Async XLA Ops:
  5.4 24.4 %collective-permute-start = (f32[2,512,256]{2,1,0:T(8,128)S(1)}, f32[2,512,256]{2,1,0:T(8,128)S(1)}, u32[]{:S(2)}, u32[]{:S(2)}) collective-permute-start(f32[2,512,256]{2,1,0:T(8,128)S(1)} %shard_map.59), channel_id=1, source_target_pairs={{0,2},{1,3},{2,0},{3,1},{4,6},{5,7},{6,4},{7,5},{8,10},{9,11},{10,... | collective-permute-start | bytes 3145736 | tf_op jit(solution)/shard_map/ppermute | solution.py:84
  6.4 45.8 %collective-permute-start.2 = (f32[2,512,256]{2,1,0:T(8,128)S(1)}, f32[2,512,256]{2,1,0:T(8,128)S(1)}, u32[]{:S(2)}, u32[]{:S(2)}) collective-permute-start(f32[2,512,256]{2,1,0:T(8,128)S(1)} %shard_map.62), channel_id=1, source_target_pairs={{0,2},{1,3},{2,0},{3,1},{4,6},{5,7},{6,4},{7,5},{8,10},{9,11},{10,... | collective-permute-start | bytes 3145736 | tf_op jit(solution)/shard_map/ppermute | solution.py:84
  8.4 66.2 %collective-permute-start.29 = (f32[2,512,256]{2,1,0:T(8,128)S(1)}, f32[2,512,256]{2,1,0:T(8,128)S(1)}, u32[]{:S(2)}, u32[]{:S(2)}) collective-permute-start(f32[2,512,256]{2,1,0:T(8,128)S(1)} %shard_map.84), channel_id=1, source_target_pairs={{0,2},{1,3},{2,0},{3,1},{4,6},{5,7},{6,4},{7,5},{8,10},{9,11},{10,... | collective-permute-start | bytes 3145736 | tf_op jit(solution)/shard_map/ppermute | solution.py:84
  9.5 87.7 %collective-permute-start.31 = (f32[2,512,256]{2,1,0:T(8,128)S(1)}, f32[2,512,256]{2,1,0:T(8,128)S(1)}, u32[]{:S(2)}, u32[]{:S(2)}) collective-permute-start(f32[2,512,256]{2,1,0:T(8,128)S(1)} %shard_map.86), channel_id=1, source_target_pairs={{0,2},{1,3},{2,0},{3,1},{4,6},{5,7},{6,4},{7,5},{8,10},{9,11},{10,... | collective-permute-start | bytes 3145736 | tf_op jit(solution)/shard_map/ppermute | solution.py:84
  15.7 82.7 %collective-permute-start.14 = (f32[2,136,512]{2,1,0:T(8,128)S(1)}, f32[2,136,512]{2,1,0:T(8,128)S(1)}, u32[]{:S(2)}, u32[]{:S(2)}) collective-permute-start(f32[2,136,512]{2,1,0:T(8,128)S(1)} %shard_map.72), channel_id=1, source_target_pairs={{0,4},{1,5},{2,6},{3,7},{4,0},{5,1},{6,2},{7,3},{8,12},{9,13},{10,... | collective-permute-start | bytes 1671176 | tf_op jit(solution)/shard_map/ppermute | solution.py:84
  29.7 72.6 %collective-permute-start.16 = (f32[2,136,512]{2,1,0:T(8,128)S(1)}, f32[2,136,512]{2,1,0:T(8,128)S(1)}, u32[]{:S(2)}, u32[]{:S(2)}) collective-permute-start(f32[2,136,512]{2,1,0:T(8,128)S(1)} %get-tuple-element.51), channel_id=1, source_target_pairs={{0,4},{1,5},{2,6},{3,7},{4,0},{5,1},{6,2},{7,3},{8,12},{9,13},{10,... | collective-permute-start | bytes 1671176 | tf_op jit(solution)/shard_map/ppermute | solution.py:84
  52.2 56.7 %collective-permute-start.18 = (f32[2,136,512]{2,1,0:T(8,128)S(1)}, f32[2,136,512]{2,1,0:T(8,128)S(1)}, u32[]{:S(2)}, u32[]{:S(2)}) collective-permute-start(f32[2,136,512]{2,1,0:T(8,128)S(1)} %get-tuple-element.55), channel_id=1, source_target_pairs={{0,4},{1,5},{2,6},{3,7},{4,0},{5,1},{6,2},{7,3},{8,12},{9,13},{10,... | collective-permute-start | bytes 1671176 | tf_op jit(solution)/shard_map/ppermute | solution.py:84
  74.7 36.2 %collective-permute-start.20 = (f32[2,136,512]{2,1,0:T(8,128)S(1)}, f32[2,136,512]{2,1,0:T(8,128)S(1)}, u32[]{:S(2)}, u32[]{:S(2)}) collective-permute-start(f32[2,136,512]{2,1,0:T(8,128)S(1)} %get-tuple-element.59), channel_id=1, source_target_pairs={{0,4},{1,5},{2,6},{3,7},{4,0},{5,1},{6,2},{7,3},{8,12},{9,13},{10,... | collective-permute-start | bytes 1671176 | tf_op jit(solution)/shard_map/ppermute | solution.py:84
  97.1 39.3 %collective-permute-start.32 = (f32[2,512,256]{2,1,0:T(8,128)S(1)}, f32[2,512,256]{2,1,0:T(8,128)S(1)}, u32[]{:S(2)}, u32[]{:S(2)}) collective-permute-start(f32[2,512,256]{2,1,0:T(8,128)S(1)} %collective-permute-done.31.a_ref), channel_id=1, source_target_pairs={{0,1},{1,0},{2,3},{3,2},{4,5},{5,4},{6,7},{7,6},{8,9},{9,8},{10,11... | collective-permute-start | bytes 3145736 | tf_op jit(solution)/shard_map/ppermute | solution.py:84
  98.4 74.8 %collective-permute-start.30 = (f32[2,512,256]{2,1,0:T(8,128)S(1)}, f32[2,512,256]{2,1,0:T(8,128)S(1)}, u32[]{:S(2)}, u32[]{:S(2)}) collective-permute-start(f32[2,512,256]{2,1,0:T(8,128)S(1)} %collective-permute-done.29.a_ref), channel_id=1, source_target_pairs={{0,1},{1,0},{2,3},{3,2},{4,5},{5,4},{6,7},{7,6},{8,9},{9,8},{10,11... | collective-permute-start | bytes 3145736 | tf_op jit(solution)/shard_map/ppermute | solution.py:84
  110.9 17.4 %collective-permute-start.19 = (f32[136,512]{1,0:T(8,128)S(1)}, f32[136,512]{1,0:T(8,128)S(1)}, u32[]{:S(2)}, u32[]{:S(2)}) collective-permute-start(f32[136,512]{1,0:T(8,128)S(1)} %get-tuple-element.57), channel_id=1, source_target_pairs={{0,8},{1,9},{2,10},{3,11},{4,12},{5,13},{6,14},{7,15},{8,0},{9,1},... | collective-permute-start | bytes 835592 | tf_op jit(solution)/shard_map/ppermute | solution.py:84
  111.7 22.6 %collective-permute-start.21 = (f32[136,512]{1,0:T(8,128)S(1)}, f32[136,512]{1,0:T(8,128)S(1)}, u32[]{:S(2)}, u32[]{:S(2)}) collective-permute-start(f32[136,512]{1,0:T(8,128)S(1)} %get-tuple-element.61), channel_id=1, source_target_pairs={{0,8},{1,9},{2,10},{3,11},{4,12},{5,13},{6,14},{7,15},{8,0},{9,1},... | collective-permute-start | bytes 835592 | tf_op jit(solution)/shard_map/ppermute | solution.py:84
  116.4 23.7 %collective-permute-start.22 = (f32[136,512]{1,0:T(8,128)S(1)}, f32[136,512]{1,0:T(8,128)S(1)}, u32[]{:S(2)}, u32[]{:S(2)}) collective-permute-start(f32[136,512]{1,0:T(8,128)S(1)} %shard_map.74.refs_0_), channel_id=1, source_target_pairs={{2,18},{3,19},{6,22},{7,23},{10,26},{11,27},{14,30},{15,31},{16,0}... | collective-permute-start | bytes 835592 | tf_op jit(solution)/shard_map/ppermute | solution.py:84
  128.3 30.8 %collective-permute-start.23 = (f32[136,512]{1,0:T(8,128)S(1)}, f32[136,512]{1,0:T(8,128)S(1)}, u32[]{:S(2)}, u32[]{:S(2)}) collective-permute-start(f32[136,512]{1,0:T(8,128)S(1)} %shard_map.78.refs_1_), channel_id=1, source_target_pairs={{2,18},{3,19},{6,22},{7,23},{10,26},{11,27},{14,30},{15,31},{16,0}... | collective-permute-start | bytes 835592 | tf_op jit(solution)/shard_map/ppermute | solution.py:84
  134.3 30.7 %collective-permute-start.24 = (f32[136,512]{1,0:T(8,128)S(1)}, f32[136,512]{1,0:T(8,128)S(1)}, u32[]{:S(2)}, u32[]{:S(2)}) collective-permute-start(f32[136,512]{1,0:T(8,128)S(1)} %shard_map.80.refs_2_), channel_id=1, source_target_pairs={{2,18},{3,19},{6,22},{7,23},{10,26},{11,27},{14,30},{15,31},{16,0}... | collective-permute-start | bytes 835592 | tf_op jit(solution)/shard_map/ppermute | solution.py:84
  136.4 34.6 %collective-permute-start.25 = (f32[136,512]{1,0:T(8,128)S(1)}, f32[136,512]{1,0:T(8,128)S(1)}, u32[]{:S(2)}, u32[]{:S(2)}) collective-permute-start(f32[136,512]{1,0:T(8,128)S(1)} %shard_map.82.refs_3_), channel_id=1, source_target_pairs={{2,18},{3,19},{6,22},{7,23},{10,26},{11,27},{14,30},{15,31},{16,0}... | collective-permute-start | bytes 835592 | tf_op jit(solution)/shard_map/ppermute | solution.py:84
  140.1 37.2 %collective-permute-start.33 = (f32[2,128,512]{2,1,0:T(8,128)S(1)}, f32[2,128,512]{2,1,0:T(8,128)S(1)}, u32[]{:S(2)}, u32[]{:S(2)}) collective-permute-start(f32[2,128,512]{2,1,0:T(8,128)S(1)} %get-tuple-element.65), channel_id=1, source_target_pairs={{0,4},{1,5},{2,6},{3,7},{4,0},{5,1},{6,2},{7,3},{8,12},{9,13},{10,... | collective-permute-start | bytes 1572872 | tf_op jit(solution)/shard_map/ppermute | solution.py:84
  159.1 34.4 %collective-permute-start.3 = (f32[2,512,256]{2,1,0:T(8,128)S(1)}, f32[2,512,256]{2,1,0:T(8,128)S(1)}, u32[]{:S(2)}, u32[]{:S(2)}) collective-permute-start(f32[2,512,256]{2,1,0:T(8,128)S(1)} %collective-permute-done.2.a_ref), channel_id=1, source_target_pairs={{0,1},{1,0},{2,3},{3,2},{4,5},{5,4},{6,7},{7,6},{8,9},{9,8},{10,11... | collective-permute-start | bytes 3145736 | tf_op jit(solution)/shard_map/ppermute | solution.py:84
  165.1 14.8 %collective-permute-start.35 = (f32[2,128,512]{2,1,0:T(8,128)S(1)}, f32[2,128,512]{2,1,0:T(8,128)S(1)}, u32[]{:S(2)}, u32[]{:S(2)}) collective-permute-start(f32[2,128,512]{2,1,0:T(8,128)S(1)} %get-tuple-element.69), channel_id=1, source_target_pairs={{0,4},{1,5},{2,6},{3,7},{4,0},{5,1},{6,2},{7,3},{8,12},{9,13},{10,... | collective-permute-start | bytes 1572872 | tf_op jit(solution)/shard_map/ppermute | solution.py:84
  171.0 45.8 %collective-permute-start.1 = (f32[2,512,256]{2,1,0:T(8,128)S(1)}, f32[2,512,256]{2,1,0:T(8,128)S(1)}, u32[]{:S(2)}, u32[]{:S(2)}) collective-permute-start(f32[2,512,256]{2,1,0:T(8,128)S(1)} %collective-permute-done.a_ref), channel_id=1, source_target_pairs={{0,1},{1,0},{2,3},{3,2},{4,5},{5,4},{6,7},{7,6},{8,9},{9,8},{10,11... | collective-permute-start | bytes 3145736 | tf_op jit(solution)/shard_map/ppermute | solution.py:84
  173.2 46.8 %collective-permute-start.27 = (f32[512,512]{1,0:T(8,128)}, f32[512,512]{1,0:T(8,128)}, u32[]{:S(2)}, u32[]{:S(2)}) collective-permute-start(f32[512,512]{1,0:T(8,128)} %get-tuple-element.62.refs_0_), channel_id=1, source_target_pairs={{1,3},{5,7},{8,10},{12,14},{19,17},{23,21},{26,24},{30,28}} | collective-permute-start | bytes 3145736 | tf_op jit(solution)/shard_map/ppermute | solution.py:84
  186.8 19.5 %collective-permute-start.37 = (f32[128,512]{1,0:T(8,128)S(1)}, f32[128,512]{1,0:T(8,128)S(1)}, u32[]{:S(2)}, u32[]{:S(2)}) collective-permute-start(f32[128,512]{1,0:T(8,128)S(1)} %shard_map.89.refs_0_), channel_id=1, source_target_pairs={{0,16},{1,17},{2,18},{3,19},{4,20},{5,21},{6,22},{7,23},{8,24},{9,... | collective-permute-start | bytes 786440 | tf_op jit(solution)/shard_map/ppermute | solution.py:84
  193.5 18.4 %collective-permute-start.38 = (f32[128,512]{1,0:T(8,128)S(1)}, f32[128,512]{1,0:T(8,128)S(1)}, u32[]{:S(2)}, u32[]{:S(2)}) collective-permute-start(f32[128,512]{1,0:T(8,128)S(1)} %shard_map.91.refs_1_), channel_id=1, source_target_pairs={{0,16},{1,17},{2,18},{3,19},{4,20},{5,21},{6,22},{7,23},{8,24},{9,... | collective-permute-start | bytes 786440 | tf_op jit(solution)/shard_map/ppermute | solution.py:84
  196.0 28.1 %collective-permute-start.8 = (f32[2,128,512]{2,1,0:T(8,128)S(1)}, f32[2,128,512]{2,1,0:T(8,128)S(1)}, u32[]{:S(2)}, u32[]{:S(2)}) collective-permute-start(f32[2,128,512]{2,1,0:T(8,128)S(1)} %get-tuple-element.45), channel_id=1, source_target_pairs={{0,4},{1,5},{2,6},{3,7},{4,0},{5,1},{6,2},{7,3},{8,12},{9,13},{10,... | collective-permute-start | bytes 1572872 | tf_op jit(solution)/shard_map/ppermute | solution.py:84
  206.3 18.5 %collective-permute-start.4 = (f32[2,128,512]{2,1,0:T(8,128)S(1)}, f32[2,128,512]{2,1,0:T(8,128)S(1)}, u32[]{:S(2)}, u32[]{:S(2)}) collective-permute-start(f32[2,128,512]{2,1,0:T(8,128)S(1)} %get-tuple-element.41), channel_id=1, source_target_pairs={{0,4},{1,5},{2,6},{3,7},{4,0},{5,1},{6,2},{7,3},{8,12},{9,13},{10,... | collective-permute-start | bytes 1572872 | tf_op jit(solution)/shard_map/ppermute | solution.py:84
  216.9 57.2 %collective-permute-start.26 = (f32[512,512]{1,0:T(8,128)}, f32[512,512]{1,0:T(8,128)}, u32[]{:S(2)}, u32[]{:S(2)}) collective-permute-start(f32[512,512]{1,0:T(8,128)} %get-tuple-element.62.refs_0_), channel_id=1, source_target_pairs={{0,4},{4,0},{9,13},{13,9},{18,22},{22,18},{27,31},{31,27}} | collective-permute-start | bytes 3145736 | tf_op jit(solution)/shard_map/ppermute | solution.py:84
  220.1 54.0 %collective-permute-start.28 = (f32[512,512]{1,0:T(8,128)}, f32[512,512]{1,0:T(8,128)}, u32[]{:S(2)}, u32[]{:S(2)}) collective-permute-start(f32[512,512]{1,0:T(8,128)} %collective-permute-done.27), channel_id=1, source_target_pairs={{3,8},{7,12},{10,5},{14,1},{17,26},{21,30},{24,23},{28,19}} | collective-permute-start | bytes 3145736 | tf_op jit(solution)/shard_map/ppermute | solution.py:84
  225.5 18.3 %collective-permute-start.5 = (f32[128,512]{1,0:T(8,128)S(1)}, f32[128,512]{1,0:T(8,128)S(1)}, u32[]{:S(2)}, u32[]{:S(2)}) collective-permute-start(f32[128,512]{1,0:T(8,128)S(1)} %get-tuple-element.43), channel_id=1, source_target_pairs={{0,8},{1,9},{2,10},{3,11},{4,12},{5,13},{6,14},{7,15},{8,0},{9,1},... | collective-permute-start | bytes 786440 | tf_op jit(solution)/shard_map/ppermute | solution.py:84
  227.0 47.1 %collective-permute-start.40 = (f32[256,512]{1,0:T(8,128)}, f32[256,512]{1,0:T(8,128)}, u32[]{:S(2)}, u32[]{:S(2)}) collective-permute-start(f32[256,512]{1,0:T(8,128)} %collective-permute-done.39), channel_id=1, source_target_pairs={{2,6},{3,10},{6,2},{7,14},{10,3},{11,15},{14,7},{15,11},{16,16},{1... | collective-permute-start | bytes 1572872 | tf_op jit(solution)/shard_map/ppermute | solution.py:84
  244.3 23.7 %collective-permute-start.6 = (f32[128,512]{1,0:T(8,128)S(1)}, f32[128,512]{1,0:T(8,128)S(1)}, u32[]{:S(2)}, u32[]{:S(2)}) collective-permute-start(f32[128,512]{1,0:T(8,128)S(1)} %shard_map.65.refs_0_), channel_id=1, source_target_pairs={{0,16},{1,17},{2,18},{3,19},{4,20},{5,21},{6,22},{7,23},{8,24},{9,... | collective-permute-start | bytes 786440 | tf_op jit(solution)/shard_map/ppermute | solution.py:84
  248.1 33.9 %collective-permute-start.11 = (f32[128,512]{1,0:T(8,128)S(1)}, f32[128,512]{1,0:T(8,128)}, u32[]{:S(2)}, u32[]{:S(2)}) collective-permute-start(f32[128,512]{1,0:T(8,128)S(1)} %shard_map.69.refs_0_), channel_id=1, source_target_pairs={{0,6},{1,10},{4,2},{5,14},{8,3},{9,15},{12,7},{13,11},{18,16},{19,... | collective-permute-start | bytes 786440 | tf_op jit(solution)/shard_map/ppermute | solution.py:84
  268.6 14.8 %collective-permute-start.7 = (f32[128,512]{1,0:T(8,128)S(1)}, f32[128,512]{1,0:T(8,128)}, u32[]{:S(2)}, u32[]{:S(2)}) collective-permute-start(f32[128,512]{1,0:T(8,128)S(1)} %shard_map.66.refs_1_), channel_id=1, source_target_pairs={{0,6},{1,10},{4,2},{5,14},{8,3},{9,15},{12,7},{13,11},{18,16},{19,... | collective-permute-start | bytes 786440 | tf_op jit(solution)/shard_map/ppermute | solution.py:84
  (15 other events, 245.3 us)

commit v7 on v6

--- a/solution.py
+++ b/solution.py
@@ -535,13 +535,9 @@
     near_back = over(hop_of(near_target))(near_own)
     near_back = over(after_hop(near_target))(near_back)
     far_own, far_back = [], []
-    for i, chunks in enumerate(((0, 1), (2,), (3,))):
+    for chunks in ((0, 1), (2,), (3,)):
         far_own += joined("f", chunks)
-        if i in HOPS:
-            back = over(hop_of(far_target))(far_own[-1])
-            far_back.append(over(after_hop(far_target))(back))
-        else:
-            far_back.append(over(far_target)(far_own[-1]))
+        far_back.append(over(far_target)(far_own[-1]))
     fixed = (t, v, row_gap, col_gap)
     pair = most(meta, t, near_own, near_swap, near_back, extra, far_own[0], far_back[0], *fixed)
     pair = late(meta, False, 2, far_own[1:], *pair, *fixed)
@@ -550,7 +546,6 @@
 
 
 NEAR_GROUPS = ((1, (1, 2, 3)), (0, (0,)), (0, (1, 2, 3)))
-HOPS = (0,)
 FAR_GROUPS = (("s0", 1, 0, 2), ("k0", 0, 0, 2), ("s1", 1, 2, 2), ("k1", 0, 2, 2))
 
 

time: 288 us -> 266 us (0.924)
  the two profiles are of different devices: /device:TPU:29 before, /device:TPU:0 now
where the time goes in v7:
time: 266 us
  waiting for transfers between devices  135 us (51%)
  starting transfers between devices  69.2 us (26%)
  Pallas kernels  55 us (21%)
  local copies, waits for them, and re-layouts  5.02 us (2%)
    ppermute x40, waiting for transfers between devices, routed(): return lax.ppermute(block, ('row', 'col'), route)  135 us
    ppermute x40, starting transfers between devices, routed(): return lax.ppermute(block, ('row', 'col'), route)  69.2 us
    pallas_call x38, Pallas kernels, call(): pl.pallas_call(kernel, out_shape=list(shapes), grid_spec=pltpu.PrefetchSc...  55 us
  transfers between devices with their start and end apart: 40, of which 15 were waited for; matrix products, arithmetic and copies ran while one was open for 0% of the time, Pallas kernels for 20%

profile of v7, /device:TPU:0, one launch (start us, length us, event | category | flops | bytes accessed | tf_op | source)
XLA Modules:
  0.0 265.8 jit_solution(4915589666607493125)
XLA Ops:
  5.2 3.0 %collective-permute-start = (f32[2,512,256]{2,1,0:T(8,128)S(1)}, f32[2,512,256]{2,1,0:T(8,128)S(1)}, u32[]{:S(2)}, u32[]{:S(2)}) collective-permute-start(f32[2,512,256]{2,1,0:T(8,128)S(1)} %shard_map.59), channel_id=1, source_target_pairs={{0,2},{1,3},{2,0},{3,1},{4,6},{5,7},{6,4},{7,5},{8,10},{9,11},{10,... | collective-permute-start | bytes 3145736 | tf_op jit(solution)/shard_map/ppermute | solution.py:84
  11.8 2.1 shard_map.72
  19.6 6.5 %shard_map.76 = (f32[2,136,512]{2,1,0:T(8,128)S(1)}, f32[2,136,512]{2,1,0:T(8,128)}, f32[2,136,512]{2,1,0:T(8,128)S(1)}) custom-call(s32[8]{0:T(128)S(1)} %compare_select_fusion.7.m._, f32[512,1024]{1,0:T(8,128)S(1)} %collective-permute-done.12.at_ref, f32[512,1024]{1,0:T(8,128)} %collective-permute-done.13.av_ref, bf16[4,512,1024]{2,1,0:T(8,128)(2,1)S(1)} %shard_map.60.own_ref), custom_call_target="tpu_custom_call" | custom-call | tf_op jit(solution)/shard_map/pallas_call | solution.py:143
  26.1 6.1 %collective-permute-done.a_ref = f32[2,512,256]{2,1,0:T(8,128)S(1)} collective-permute-done((f32[2,512,256]{2,1,0:T(8,128)S(1)}, f32[2,512,256]{2,1,0:T(8,128)S(1)}, u32[]{:S(2)}, u32[]{:S(2)}) %collective-permute-start) | collective-permute-done | bytes 1048608 | tf_op jit(solution)/shard_map/ppermute | solution.py:84
  34.2 20.5 %collective-permute-done.2.a_ref = f32[2,512,256]{2,1,0:T(8,128)S(1)} collective-permute-done((f32[2,512,256]{2,1,0:T(8,128)S(1)}, f32[2,512,256]{2,1,0:T(8,128)S(1)}, u32[]{:S(2)}, u32[]{:S(2)}) %collective-permute-start.2) | collective-permute-done | bytes 1048608 | tf_op jit(solution)/shard_map/ppermute | solution.py:84
  56.7 3.3 %shard_map.70.keep_pass.keep_stay = f32[2,136,512]{2,1,0:T(8,128)S(1)} custom-call(s32[8]{0:T(128)S(1)} %compare_select_fusion.7.m._, f32[512,1024]{1,0:T(8,128)S(1)} %collective-permute-done.12.at_ref, f32[512,1024]{1,0:T(8,128)} %collective-permute-done.13.av_ref, bf16[4,512,1024]{2,1,0:T(8,128)(2,1)S(1)} %shard_map.60.own_ref), custom_call_target="tpu_custom_call" | custom-call | tf_op jit(solution)/shard_map/pallas_call | solution.py:143
  60.6 2.1 collective-permute-start.15
  62.7 5.7 %shard_map.75 = (f32[2,136,512]{2,1,0:T(8,128)S(1)}, f32[2,136,512]{2,1,0:T(8,128)S(1)}, f32[2,136,512]{2,1,0:T(8,128)S(1)}) custom-call(s32[8]{0:T(128)S(1)} %compare_select_fusion.7.m._, f32[512,1024]{1,0:T(8,128)S(1)} %collective-permute-done.12.at_ref, f32[512,1024]{1,0:T(8,128)} %collective-permute-done.13.av_ref, ...), custom_call_target="tpu_custom_call" | custom-call | tf_op jit(solution)/shard_map/pallas_call | solution.py:143
  70.4 2.1 collective-permute-start.17
  73.0 7.2 %collective-permute-done.20.come_pass.come_stay = f32[2,136,512]{2,1,0:T(8,128)S(1)} collective-permute-done((f32[2,136,512]{2,1,0:T(8,128)S(1)}, f32[2,136,512]{2,1,0:T(8,128)S(1)}, u32[]{:S(2)}, u32[]{:S(2)}) %collective-permute-start.20) | collective-permute-done | bytes 557088 | tf_op jit(solution)/shard_map/ppermute | solution.py:84
  82.9 16.0 %collective-permute-done.31.a_ref = f32[2,512,256]{2,1,0:T(8,128)S(1)} collective-permute-done((f32[2,512,256]{2,1,0:T(8,128)S(1)}, f32[2,512,256]{2,1,0:T(8,128)S(1)}, u32[]{:S(2)}, u32[]{:S(2)}) %collective-permute-start.31) | collective-permute-done | bytes 1048608 | tf_op jit(solution)/shard_map/ppermute | solution.py:84
  105.9 30.4 %collective-permute-done.22.refs_4_ = f32[136,512]{1,0:T(8,128)S(1)} collective-permute-done((f32[136,512]{1,0:T(8,128)S(1)}, f32[136,512]{1,0:T(8,128)S(1)}, u32[]{:S(2)}, u32[]{:S(2)}) %collective-permute-start.22) | collective-permute-done | bytes 278560 | tf_op jit(solution)/shard_map/ppermute | solution.py:84
  137.6 4.7 %collective-permute-done.23.refs_5_ = f32[136,512]{1,0:T(8,128)S(1)} collective-permute-done((f32[136,512]{1,0:T(8,128)S(1)}, f32[136,512]{1,0:T(8,128)S(1)}, u32[]{:S(2)}, u32[]{:S(2)}) %collective-permute-start.23) | collective-permute-done | bytes 278560 | tf_op jit(solution)/shard_map/ppermute | solution.py:84
  142.3 6.0 %collective-permute-done.24.refs_6_ = f32[136,512]{1,0:T(8,128)S(1)} collective-permute-done((f32[136,512]{1,0:T(8,128)S(1)}, f32[136,512]{1,0:T(8,128)S(1)}, u32[]{:S(2)}, u32[]{:S(2)}) %collective-permute-start.24) | collective-permute-done | bytes 278560 | tf_op jit(solution)/shard_map/ppermute | solution.py:84
  148.2 5.0 %collective-permute-done.25.refs_7_ = f32[136,512]{1,0:T(8,128)S(1)} collective-permute-done((f32[136,512]{1,0:T(8,128)S(1)}, f32[136,512]{1,0:T(8,128)S(1)}, u32[]{:S(2)}, u32[]{:S(2)}) %collective-permute-start.25) | collective-permute-done | bytes 278560 | tf_op jit(solution)/shard_map/ppermute | solution.py:84
  156.5 2.4 shard_map.87
  161.0 2.4 shard_map.63
  165.2 2.4 shard_map.85
  167.6 6.2 %collective-permute-done.33.come_pass.come_stay = f32[2,128,512]{2,1,0:T(8,128)S(1)} collective-permute-done((f32[2,128,512]{2,1,0:T(8,128)S(1)}, f32[2,128,512]{2,1,0:T(8,128)S(1)}, u32[]{:S(2)}, u32[]{:S(2)}) %collective-permute-start.33) | collective-permute-done | bytes 524320 | tf_op jit(solution)/shard_map/ppermute | solution.py:84
  174.5 10.5 %collective-permute-done.35.come_pass.come_stay = f32[2,128,512]{2,1,0:T(8,128)S(1)} collective-permute-done((f32[2,128,512]{2,1,0:T(8,128)S(1)}, f32[2,128,512]{2,1,0:T(8,128)S(1)}, u32[]{:S(2)}, u32[]{:S(2)}) %collective-permute-start.35) | collective-permute-done | bytes 524320 | tf_op jit(solution)/shard_map/ppermute | solution.py:84
  187.5 2.2 collective-permute-start.26
  193.8 2.4 shard_map.61
  196.8 3.0 %collective-permute-start.38 = (f32[128,512]{1,0:T(8,128)S(1)}, f32[128,512]{1,0:T(8,128)S(1)}, u32[]{:S(2)}, u32[]{:S(2)}) collective-permute-start(f32[128,512]{1,0:T(8,128)S(1)} %shard_map.91.refs_1_), channel_id=1, source_target_pairs={{0,16},{1,17},{2,18},{3,19},{4,20},{5,21},{6,22},{7,23},{8,24},{9,... | collective-permute-start | bytes 786440 | tf_op jit(solution)/shard_map/ppermute | solution.py:84
  200.4 5.9 %collective-permute-done.4.come_pass.come_stay = f32[2,128,512]{2,1,0:T(8,128)S(1)} collective-permute-done((f32[2,128,512]{2,1,0:T(8,128)S(1)}, f32[2,128,512]{2,1,0:T(8,128)S(1)}, u32[]{:S(2)}, u32[]{:S(2)}) %collective-permute-start.4) | collective-permute-done | bytes 524320 | tf_op jit(solution)/shard_map/ppermute | solution.py:84
  207.0 7.2 %collective-permute-start.5 = (f32[128,512]{1,0:T(8,128)S(1)}, f32[128,512]{1,0:T(8,128)S(1)}, u32[]{:S(2)}, u32[]{:S(2)}) collective-permute-start(f32[128,512]{1,0:T(8,128)S(1)} %get-tuple-element.43), channel_id=1, source_target_pairs={{0,8},{1,9},{2,10},{3,11},{4,12},{5,13},{6,14},{7,15},{8,0},{9,1},... | collective-permute-start | bytes 786440 | tf_op jit(solution)/shard_map/ppermute | solution.py:84
  214.2 3.0 %collective-permute-done.38.refs_3_ = f32[128,512]{1,0:T(8,128)S(1)} collective-permute-done((f32[128,512]{1,0:T(8,128)S(1)}, f32[128,512]{1,0:T(8,128)S(1)}, u32[]{:S(2)}, u32[]{:S(2)}) %collective-permute-start.38) | collective-permute-done | bytes 262176 | tf_op jit(solution)/shard_map/ppermute | solution.py:84
  217.8 5.7 %collective-permute-start.39 = (f32[256,512]{1,0:T(8,128)S(1)}, f32[256,512]{1,0:T(8,128)}, u32[]{:S(2)}, u32[]{:S(2)}) collective-permute-start(f32[256,512]{1,0:T(8,128)S(1)} %shard_map.92.refs_4_), channel_id=1, source_target_pairs={{0,6},{1,10},{4,2},{5,14},{8,3},{9,15},{12,7},{13,11},{18,16},{19,... | collective-permute-start | bytes 1572872 | tf_op jit(solution)/shard_map/ppermute | solution.py:84
  226.5 6.2 %collective-permute-start.6 = (f32[128,512]{1,0:T(8,128)S(1)}, f32[128,512]{1,0:T(8,128)S(1)}, u32[]{:S(2)}, u32[]{:S(2)}) collective-permute-start(f32[128,512]{1,0:T(8,128)S(1)} %shard_map.65.refs_0_), channel_id=1, source_target_pairs={{0,16},{1,17},{2,18},{3,19},{4,20},{5,21},{6,22},{7,23},{8,24},{9,... | collective-permute-start | bytes 786440 | tf_op jit(solution)/shard_map/ppermute | solution.py:84
  232.7 10.7 %collective-permute-done.10.refs_1_ = f32[128,512]{1,0:T(8,128)S(1)} collective-permute-done((f32[128,512]{1,0:T(8,128)S(1)}, f32[128,512]{1,0:T(8,128)S(1)}, u32[]{:S(2)}, u32[]{:S(2)}) %collective-permute-start.10) | collective-permute-done | bytes 262176 | tf_op jit(solution)/shard_map/ppermute | solution.py:84
  244.0 4.8 %collective-permute-start.11 = (f32[128,512]{1,0:T(8,128)S(1)}, f32[128,512]{1,0:T(8,128)}, u32[]{:S(2)}, u32[]{:S(2)}) collective-permute-start(f32[128,512]{1,0:T(8,128)S(1)} %shard_map.69.refs_0_), channel_id=1, source_target_pairs={{0,6},{1,10},{4,2},{5,14},{8,3},{9,15},{12,7},{13,11},{18,16},{19,... | collective-permute-start | bytes 786440 | tf_op jit(solution)/shard_map/ppermute | solution.py:84
  249.3 5.0 %collective-permute-start.7 = (f32[128,512]{1,0:T(8,128)S(1)}, f32[128,512]{1,0:T(8,128)}, u32[]{:S(2)}, u32[]{:S(2)}) collective-permute-start(f32[128,512]{1,0:T(8,128)S(1)} %shard_map.66.refs_1_), channel_id=1, source_target_pairs={{0,6},{1,10},{4,2},{5,14},{8,3},{9,15},{12,7},{13,11},{18,16},{19,... | collective-permute-start | bytes 786440 | tf_op jit(solution)/shard_map/ppermute | solution.py:84
  256.4 5.6 %shard_map.93 = (f32[512,1024]{1,0:T(8,128)}, f32[512,1024]{1,0:T(8,128)}) custom-call(s32[8]{0:T(128)S(1)} %compare_select_fusion.7.m._, f32[512,512]{1,0:T(8,128)} %get-tuple-element.62.refs_0_, f32[512,512]{1,0:T(8,128)} %collective-permute-done.26.refs_1_, f32[512,512]{1,0:T(8,128)} %collective-permute-done.28.refs_2_, ...), custom_call_target="tpu_custom_call" | custom-call | tf_op jit(solution)/shard_map/pallas_call | solution.py:143
  (104 shorter events, 58.2 us)
Async XLA Ops:
  5.2 27.0 %collective-permute-start = (f32[2,512,256]{2,1,0:T(8,128)S(1)}, f32[2,512,256]{2,1,0:T(8,128)S(1)}, u32[]{:S(2)}, u32[]{:S(2)}) collective-permute-start(f32[2,512,256]{2,1,0:T(8,128)S(1)} %shard_map.59), channel_id=1, source_target_pairs={{0,2},{1,3},{2,0},{3,1},{4,6},{5,7},{6,4},{7,5},{8,10},{9,11},{10,... | collective-permute-start | bytes 3145736 | tf_op jit(solution)/shard_map/ppermute | solution.py:84
  8.9 45.7 %collective-permute-start.2 = (f32[2,512,256]{2,1,0:T(8,128)S(1)}, f32[2,512,256]{2,1,0:T(8,128)S(1)}, u32[]{:S(2)}, u32[]{:S(2)}) collective-permute-start(f32[2,512,256]{2,1,0:T(8,128)S(1)} %shard_map.62), channel_id=1, source_target_pairs={{0,2},{1,3},{2,0},{3,1},{4,6},{5,7},{6,4},{7,5},{8,10},{9,11},{10,... | collective-permute-start | bytes 3145736 | tf_op jit(solution)/shard_map/ppermute | solution.py:84
  14.0 42.7 %collective-permute-start.14 = (f32[2,136,512]{2,1,0:T(8,128)S(1)}, f32[2,136,512]{2,1,0:T(8,128)S(1)}, u32[]{:S(2)}, u32[]{:S(2)}) collective-permute-start(f32[2,136,512]{2,1,0:T(8,128)S(1)} %shard_map.72), channel_id=1, source_target_pairs={{0,4},{1,5},{2,6},{3,7},{4,0},{5,1},{6,2},{7,3},{8,12},{9,13},{10,... | collective-permute-start | bytes 1671176 | tf_op jit(solution)/shard_map/ppermute | solution.py:84
  16.7 65.6 %collective-permute-start.29 = (f32[2,512,256]{2,1,0:T(8,128)S(1)}, f32[2,512,256]{2,1,0:T(8,128)S(1)}, u32[]{:S(2)}, u32[]{:S(2)}) collective-permute-start(f32[2,512,256]{2,1,0:T(8,128)S(1)} %shard_map.84), channel_id=1, source_target_pairs={{0,2},{1,3},{2,0},{3,1},{4,6},{5,7},{6,4},{7,5},{8,10},{9,11},{10,... | collective-permute-start | bytes 3145736 | tf_op jit(solution)/shard_map/ppermute | solution.py:84
  19.1 79.9 %collective-permute-start.31 = (f32[2,512,256]{2,1,0:T(8,128)S(1)}, f32[2,512,256]{2,1,0:T(8,128)S(1)}, u32[]{:S(2)}, u32[]{:S(2)}) collective-permute-start(f32[2,512,256]{2,1,0:T(8,128)S(1)} %shard_map.86), channel_id=1, source_target_pairs={{0,2},{1,3},{2,0},{3,1},{4,6},{5,7},{6,4},{7,5},{8,10},{9,11},{10,... | collective-permute-start | bytes 3145736 | tf_op jit(solution)/shard_map/ppermute | solution.py:84
  32.2 28.4 %collective-permute-start.16 = (f32[2,136,512]{2,1,0:T(8,128)S(1)}, f32[2,136,512]{2,1,0:T(8,128)S(1)}, u32[]{:S(2)}, u32[]{:S(2)}) collective-permute-start(f32[2,136,512]{2,1,0:T(8,128)S(1)} %get-tuple-element.51), channel_id=1, source_target_pairs={{0,4},{1,5},{2,6},{3,7},{4,0},{5,1},{6,2},{7,3},{8,12},{9,13},{10,... | collective-permute-start | bytes 1671176 | tf_op jit(solution)/shard_map/ppermute | solution.py:84
  56.6 23.6 %collective-permute-start.20 = (f32[2,136,512]{2,1,0:T(8,128)S(1)}, f32[2,136,512]{2,1,0:T(8,128)S(1)}, u32[]{:S(2)}, u32[]{:S(2)}) collective-permute-start(f32[2,136,512]{2,1,0:T(8,128)S(1)} %get-tuple-element.59), channel_id=1, source_target_pairs={{0,4},{1,5},{2,6},{3,7},{4,0},{5,1},{6,2},{7,3},{8,12},{9,13},{10,... | collective-permute-start | bytes 1671176 | tf_op jit(solution)/shard_map/ppermute | solution.py:84
  60.6 38.4 %collective-permute-start.15 = (f32[136,512]{1,0:T(8,128)S(1)}, f32[136,512]{1,0:T(8,128)S(1)}, u32[]{:S(2)}, u32[]{:S(2)}) collective-permute-start(f32[136,512]{1,0:T(8,128)S(1)} %get-tuple-element.49), channel_id=1, source_target_pairs={{0,8},{1,9},{2,10},{3,11},{4,12},{5,13},{6,14},{7,15},{8,0},{9,1},... | collective-permute-start | bytes 835592 | tf_op jit(solution)/shard_map/ppermute | solution.py:84
  70.4 29.7 %collective-permute-start.17 = (f32[136,512]{1,0:T(8,128)S(1)}, f32[136,512]{1,0:T(8,128)S(1)}, u32[]{:S(2)}, u32[]{:S(2)}) collective-permute-start(f32[136,512]{1,0:T(8,128)S(1)} %get-tuple-element.53), channel_id=1, source_target_pairs={{0,8},{1,9},{2,10},{3,11},{4,12},{5,13},{6,14},{7,15},{8,0},{9,1},... | collective-permute-start | bytes 835592 | tf_op jit(solution)/shard_map/ppermute | solution.py:84
  80.2 21.7 %collective-permute-start.19 = (f32[136,512]{1,0:T(8,128)S(1)}, f32[136,512]{1,0:T(8,128)S(1)}, u32[]{:S(2)}, u32[]{:S(2)}) collective-permute-start(f32[136,512]{1,0:T(8,128)S(1)} %get-tuple-element.57), channel_id=1, source_target_pairs={{0,8},{1,9},{2,10},{3,11},{4,12},{5,13},{6,14},{7,15},{8,0},{9,1},... | collective-permute-start | bytes 835592 | tf_op jit(solution)/shard_map/ppermute | solution.py:84
  82.4 21.5 %collective-permute-start.21 = (f32[136,512]{1,0:T(8,128)S(1)}, f32[136,512]{1,0:T(8,128)S(1)}, u32[]{:S(2)}, u32[]{:S(2)}) collective-permute-start(f32[136,512]{1,0:T(8,128)S(1)} %get-tuple-element.61), channel_id=1, source_target_pairs={{0,8},{1,9},{2,10},{3,11},{4,12},{5,13},{6,14},{7,15},{8,0},{9,1},... | collective-permute-start | bytes 835592 | tf_op jit(solution)/shard_map/ppermute | solution.py:84
  99.0 57.6 %collective-permute-start.32 = (f32[2,512,256]{2,1,0:T(8,128)S(1)}, f32[2,512,256]{2,1,0:T(8,128)S(1)}, u32[]{:S(2)}, u32[]{:S(2)}) collective-permute-start(f32[2,512,256]{2,1,0:T(8,128)S(1)} %collective-permute-done.31.a_ref), channel_id=1, source_target_pairs={{0,1},{1,0},{2,3},{3,2},{4,5},{5,4},{6,7},{7,6},{8,9},{9,8},{10,11... | collective-permute-start | bytes 3145736 | tf_op jit(solution)/shard_map/ppermute | solution.py:84
  99.0 61.7 %collective-permute-start.3 = (f32[2,512,256]{2,1,0:T(8,128)S(1)}, f32[2,512,256]{2,1,0:T(8,128)S(1)}, u32[]{:S(2)}, u32[]{:S(2)}) collective-permute-start(f32[2,512,256]{2,1,0:T(8,128)S(1)} %collective-permute-done.2.a_ref), channel_id=1, source_target_pairs={{0,1},{1,0},{2,3},{3,2},{4,5},{5,4},{6,7},{7,6},{8,9},{9,8},{10,11... | collective-permute-start | bytes 3145736 | tf_op jit(solution)/shard_map/ppermute | solution.py:84
  100.1 36.2 %collective-permute-start.22 = (f32[136,512]{1,0:T(8,128)S(1)}, f32[136,512]{1,0:T(8,128)S(1)}, u32[]{:S(2)}, u32[]{:S(2)}) collective-permute-start(f32[136,512]{1,0:T(8,128)S(1)} %shard_map.74.refs_0_), channel_id=1, source_target_pairs={{2,18},{3,19},{6,22},{7,23},{10,26},{11,27},{14,30},{15,31},{16,0}... | collective-permute-start | bytes 835592 | tf_op jit(solution)/shard_map/ppermute | solution.py:84
  102.0 40.3 %collective-permute-start.23 = (f32[136,512]{1,0:T(8,128)S(1)}, f32[136,512]{1,0:T(8,128)S(1)}, u32[]{:S(2)}, u32[]{:S(2)}) collective-permute-start(f32[136,512]{1,0:T(8,128)S(1)} %shard_map.78.refs_1_), channel_id=1, source_target_pairs={{2,18},{3,19},{6,22},{7,23},{10,26},{11,27},{14,30},{15,31},{16,0}... | collective-permute-start | bytes 835592 | tf_op jit(solution)/shard_map/ppermute | solution.py:84
  103.9 44.4 %collective-permute-start.24 = (f32[136,512]{1,0:T(8,128)S(1)}, f32[136,512]{1,0:T(8,128)S(1)}, u32[]{:S(2)}, u32[]{:S(2)}) collective-permute-start(f32[136,512]{1,0:T(8,128)S(1)} %shard_map.80.refs_2_), channel_id=1, source_target_pairs={{2,18},{3,19},{6,22},{7,23},{10,26},{11,27},{14,30},{15,31},{16,0}... | collective-permute-start | bytes 835592 | tf_op jit(solution)/shard_map/ppermute | solution.py:84
  136.3 16.9 %collective-permute-start.25 = (f32[136,512]{1,0:T(8,128)S(1)}, f32[136,512]{1,0:T(8,128)S(1)}, u32[]{:S(2)}, u32[]{:S(2)}) collective-permute-start(f32[136,512]{1,0:T(8,128)S(1)} %shard_map.82.refs_3_), channel_id=1, source_target_pairs={{2,18},{3,19},{6,22},{7,23},{10,26},{11,27},{14,30},{15,31},{16,0}... | collective-permute-start | bytes 835592 | tf_op jit(solution)/shard_map/ppermute | solution.py:84
  142.3 21.2 %collective-permute-start.30 = (f32[2,512,256]{2,1,0:T(8,128)S(1)}, f32[2,512,256]{2,1,0:T(8,128)S(1)}, u32[]{:S(2)}, u32[]{:S(2)}) collective-permute-start(f32[2,512,256]{2,1,0:T(8,128)S(1)} %collective-permute-done.29.a_ref), channel_id=1, source_target_pairs={{0,1},{1,0},{2,3},{3,2},{4,5},{5,4},{6,7},{7,6},{8,9},{9,8},{10,11... | collective-permute-start | bytes 3145736 | tf_op jit(solution)/shard_map/ppermute | solution.py:84
  148.2 39.1 %collective-permute-start.1 = (f32[2,512,256]{2,1,0:T(8,128)S(1)}, f32[2,512,256]{2,1,0:T(8,128)S(1)}, u32[]{:S(2)}, u32[]{:S(2)}) collective-permute-start(f32[2,512,256]{2,1,0:T(8,128)S(1)} %collective-permute-done.a_ref), channel_id=1, source_target_pairs={{0,1},{1,0},{2,3},{3,2},{4,5},{5,4},{6,7},{7,6},{8,9},{9,8},{10,11... | collective-permute-start | bytes 3145736 | tf_op jit(solution)/shard_map/ppermute | solution.py:84
  154.9 34.8 %collective-permute-start.27 = (f32[512,512]{1,0:T(8,128)}, f32[512,512]{1,0:T(8,128)}, u32[]{:S(2)}, u32[]{:S(2)}) collective-permute-start(f32[512,512]{1,0:T(8,128)} %get-tuple-element.62.refs_0_), channel_id=1, source_target_pairs={{1,3},{5,7},{8,10},{12,14},{19,17},{23,21},{26,24},{30,28}} | collective-permute-start | bytes 3145736 | tf_op jit(solution)/shard_map/ppermute | solution.py:84
  160.7 24.3 %collective-permute-start.35 = (f32[2,128,512]{2,1,0:T(8,128)S(1)}, f32[2,128,512]{2,1,0:T(8,128)S(1)}, u32[]{:S(2)}, u32[]{:S(2)}) collective-permute-start(f32[2,128,512]{2,1,0:T(8,128)S(1)} %get-tuple-element.69), channel_id=1, source_target_pairs={{0,4},{1,5},{2,6},{3,7},{4,0},{5,1},{6,2},{7,3},{8,12},{9,13},{10,... | collective-permute-start | bytes 1572872 | tf_op jit(solution)/shard_map/ppermute | solution.py:84
  163.5 33.3 %collective-permute-start.8 = (f32[2,128,512]{2,1,0:T(8,128)S(1)}, f32[2,128,512]{2,1,0:T(8,128)S(1)}, u32[]{:S(2)}, u32[]{:S(2)}) collective-permute-start(f32[2,128,512]{2,1,0:T(8,128)S(1)} %get-tuple-element.45), channel_id=1, source_target_pairs={{0,4},{1,5},{2,6},{3,7},{4,0},{5,1},{6,2},{7,3},{8,12},{9,13},{10,... | collective-permute-start | bytes 1572872 | tf_op jit(solution)/shard_map/ppermute | solution.py:84
  185.0 21.3 %collective-permute-start.4 = (f32[2,128,512]{2,1,0:T(8,128)S(1)}, f32[2,128,512]{2,1,0:T(8,128)S(1)}, u32[]{:S(2)}, u32[]{:S(2)}) collective-permute-start(f32[2,128,512]{2,1,0:T(8,128)S(1)} %get-tuple-element.41), channel_id=1, source_target_pairs={{0,4},{1,5},{2,6},{3,7},{4,0},{5,1},{6,2},{7,3},{8,12},{9,13},{10,... | collective-permute-start | bytes 1572872 | tf_op jit(solution)/shard_map/ppermute | solution.py:84
  187.5 67.3 %collective-permute-start.26 = (f32[512,512]{1,0:T(8,128)}, f32[512,512]{1,0:T(8,128)}, u32[]{:S(2)}, u32[]{:S(2)}) collective-permute-start(f32[512,512]{1,0:T(8,128)} %get-tuple-element.62.refs_0_), channel_id=1, source_target_pairs={{0,4},{4,0},{9,13},{13,9},{18,22},{22,18},{27,31},{31,27}} | collective-permute-start | bytes 3145736 | tf_op jit(solution)/shard_map/ppermute | solution.py:84
  189.7 65.0 %collective-permute-start.28 = (f32[512,512]{1,0:T(8,128)}, f32[512,512]{1,0:T(8,128)}, u32[]{:S(2)}, u32[]{:S(2)}) collective-permute-start(f32[512,512]{1,0:T(8,128)} %collective-permute-done.27), channel_id=1, source_target_pairs={{3,8},{7,12},{10,5},{14,1},{17,26},{21,30},{24,23},{28,19}} | collective-permute-start | bytes 3145736 | tf_op jit(solution)/shard_map/ppermute | solution.py:84
  196.8 20.4 %collective-permute-start.38 = (f32[128,512]{1,0:T(8,128)S(1)}, f32[128,512]{1,0:T(8,128)S(1)}, u32[]{:S(2)}, u32[]{:S(2)}) collective-permute-start(f32[128,512]{1,0:T(8,128)S(1)} %shard_map.91.refs_1_), channel_id=1, source_target_pairs={{0,16},{1,17},{2,18},{3,19},{4,20},{5,21},{6,22},{7,23},{8,24},{9,... | collective-permute-start | bytes 786440 | tf_op jit(solution)/shard_map/ppermute | solution.py:84
  206.3 17.2 %collective-permute-start.9 = (f32[128,512]{1,0:T(8,128)S(1)}, f32[128,512]{1,0:T(8,128)S(1)}, u32[]{:S(2)}, u32[]{:S(2)}) collective-permute-start(f32[128,512]{1,0:T(8,128)S(1)} %get-tuple-element.47), channel_id=1, source_target_pairs={{0,8},{1,9},{2,10},{3,11},{4,12},{5,13},{6,14},{7,15},{8,0},{9,1},... | collective-permute-start | bytes 786440 | tf_op jit(solution)/shard_map/ppermute | solution.py:84
  207.0 19.0 %collective-permute-start.5 = (f32[128,512]{1,0:T(8,128)S(1)}, f32[128,512]{1,0:T(8,128)S(1)}, u32[]{:S(2)}, u32[]{:S(2)}) collective-permute-start(f32[128,512]{1,0:T(8,128)S(1)} %get-tuple-element.43), channel_id=1, source_target_pairs={{0,8},{1,9},{2,10},{3,11},{4,12},{5,13},{6,14},{7,15},{8,0},{9,1},... | collective-permute-start | bytes 786440 | tf_op jit(solution)/shard_map/ppermute | solution.py:84
  217.8 36.9 %collective-permute-start.39 = (f32[256,512]{1,0:T(8,128)S(1)}, f32[256,512]{1,0:T(8,128)}, u32[]{:S(2)}, u32[]{:S(2)}) collective-permute-start(f32[256,512]{1,0:T(8,128)S(1)} %shard_map.92.refs_4_), channel_id=1, source_target_pairs={{0,6},{1,10},{4,2},{5,14},{8,3},{9,15},{12,7},{13,11},{18,16},{19,... | collective-permute-start | bytes 1572872 | tf_op jit(solution)/shard_map/ppermute | solution.py:84
  224.1 19.3 %collective-permute-start.10 = (f32[128,512]{1,0:T(8,128)S(1)}, f32[128,512]{1,0:T(8,128)S(1)}, u32[]{:S(2)}, u32[]{:S(2)}) collective-permute-start(f32[128,512]{1,0:T(8,128)S(1)} %shard_map.68.refs_0_), channel_id=1, source_target_pairs={{0,16},{1,17},{2,18},{3,19},{4,20},{5,21},{6,22},{7,23},{8,24},{9,... | collective-permute-start | bytes 786440 | tf_op jit(solution)/shard_map/ppermute | solution.py:84
  226.5 22.2 %collective-permute-start.6 = (f32[128,512]{1,0:T(8,128)S(1)}, f32[128,512]{1,0:T(8,128)S(1)}, u32[]{:S(2)}, u32[]{:S(2)}) collective-permute-start(f32[128,512]{1,0:T(8,128)S(1)} %shard_map.65.refs_0_), channel_id=1, source_target_pairs={{0,16},{1,17},{2,18},{3,19},{4,20},{5,21},{6,22},{7,23},{8,24},{9,... | collective-permute-start | bytes 786440 | tf_op jit(solution)/shard_map/ppermute | solution.py:84
  244.0 18.7 %collective-permute-start.11 = (f32[128,512]{1,0:T(8,128)S(1)}, f32[128,512]{1,0:T(8,128)}, u32[]{:S(2)}, u32[]{:S(2)}) collective-permute-start(f32[128,512]{1,0:T(8,128)S(1)} %shard_map.69.refs_0_), channel_id=1, source_target_pairs={{0,6},{1,10},{4,2},{5,14},{8,3},{9,15},{12,7},{13,11},{18,16},{19,... | collective-permute-start | bytes 786440 | tf_op jit(solution)/shard_map/ppermute | solution.py:84
  (14 other events, 236.4 us)

commit v8 on v7

--- a/solution.py
+++ b/solution.py
@@ -226,20 +226,30 @@
     return call(prep_kernel, [jax.ShapeDtypeStruct((4, *t.shape), jnp.bfloat16)], meta, [t, v])[0]
 
 
+def lines(k, w):
+    return w + PAD if k == CHUNKS - 1 else w
+
+
 def middle_block(m, side, chunks, own_ref, outs):
     n = own_ref.shape[1]
     w = n // CHUNKS
     half = m[X_PLACE] ^ side
+    same, cross = placed(half, n), placed(1 - half, n)
     left = own_left(own_ref, placed(half, n, chunks[0] * w, len(chunks) * w))
-    diagonal = crossed(left, own_right(own_ref, placed(half, n)))
-    aside = crossed(left, own_right(own_ref, placed(1 - half, n)))
+    diagonal = crossed(left, own_right(own_ref, same))
+    aside = crossed(left, own_right(own_ref, cross))
     lane = lax.broadcasted_iota(jnp.int32, (w, n), 1)
     for i, (k, out_ref) in enumerate(zip(chunks, outs)):
         line = lax.broadcasted_iota(jnp.int32, (w, n), 0) + k * w
         rows = slice(i * w, (i + 1) * w)
         out_ref[0, :w, :] = jnp.where(line >= lane, diagonal[rows], aside[rows])
-        extra = jnp.sum(jnp.where(line == lane, aside[rows], 0.0), axis=0, keepdims=True)
-        out_ref[0, w:, :] = jnp.broadcast_to(extra, (PAD, n))
+        if out_ref.shape[1] > w:
+            whole = lambda i, cols: own_ref[i, :, cols].astype(jnp.float32) + own_ref[
+                i + 1, :, cols
+            ].astype(jnp.float32)
+            products = whole(0, same) * whole(2, cross) + whole(2, same) * whole(0, cross)
+            extra = jnp.sum(products, axis=0, keepdims=True)
+            out_ref[0, w:, :] = jnp.broadcast_to(extra, (PAD, n))
 
 
 def middle_kernel(side, k, m, own_ref, out_ref):
@@ -248,13 +258,13 @@
 
 def middle_part(meta, own, side, k):
     n = own.shape[1]
-    w = n // CHUNKS
+    w = lines(k, n // CHUNKS)
     return call(
         functools.partial(middle_kernel, side, k),
-        [shaped(2, w + PAD, n)],
+        [shaped(2, w, n)],
         meta,
         [own],
-        out_specs=[pl.BlockSpec((1, w + PAD, n), lambda i, m: (0, 0, 0))],
+        out_specs=[pl.BlockSpec((1, w, n), lambda i, m: (0, 0, 0))],
     )[0]
 
 
@@ -263,22 +273,21 @@
     w = n // CHUNKS
     block = pl.BlockSpec((n, w), lambda i, m: (0, (m[X_PLACE] ^ side) * CHUNKS + k))
     return call(
-        functools.partial(next_kernel_blocked, side),
+        functools.partial(next_kernel, side),
         [shaped(*base.shape)],
         meta,
         [base, at, av, own],
         in_specs=[pl.BlockSpec(memory_space=pl.ANY), block, block, None],
-        out_specs=[pl.BlockSpec((1, w + PAD, n), lambda i, m: (1, 0, 0))],
+        out_specs=[pl.BlockSpec((1, *base.shape[1:]), lambda i, m: (1, 0, 0))],
         aliases={1: 0},
     )[0]
 
 
-def next_kernel_blocked(side, m, _, at_ref, av_ref, own_ref, out_ref):
+def next_kernel(side, m, _, at_ref, av_ref, own_ref, out_ref):
     n = own_ref.shape[1]
     w = at_ref.shape[1]
     right = own_right(own_ref, placed(m[TURN_1] ^ side, n))
     out_ref[0, :w, :] = crossed(left_of(at_ref[...], av_ref[...]), right)
-    out_ref[0, w:, :] = jnp.zeros((PAD, n), jnp.float32)
 
 
 def near_parts(meta, at, av, own, side, chunks):
@@ -286,15 +295,15 @@
     w = n // CHUNKS
     half = pl.BlockSpec((n, n), lambda i, m: (0, m[X_PLACE] ^ side))
     return call(
-        functools.partial(near_half_kernel, side, chunks),
-        [shaped(2, w + PAD, n) for _ in chunks],
+        functools.partial(near_kernel, side, chunks),
+        [shaped(2, lines(k, w), n) for k in chunks],
         meta,
         [at, av, own],
         in_specs=[half, half, None],
     )
 
 
-def near_half_kernel(side, chunks, m, at_ref, av_ref, own_ref, *outs):
+def near_kernel(side, chunks, m, at_ref, av_ref, own_ref, *outs):
     n = own_ref.shape[1]
     w = n // CHUNKS
     middle_block(m, side, chunks, own_ref, outs)
@@ -303,7 +312,8 @@
     block = crossed(left_of(at_ref[:, cols], av_ref[:, cols]), right)
     for i, out_ref in enumerate(outs):
         out_ref[1, :w, :] = block[i * w : (i + 1) * w]
-        out_ref[1, w:, :] = jnp.zeros((PAD, n), jnp.float32)
+        if out_ref.shape[1] > w:
+            out_ref[1, w:, :] = jnp.zeros((PAD, n), jnp.float32)
 
 
 def far_kernel(side, m, a_ref, b_ref, own_ref, *outs):
@@ -355,22 +365,18 @@
 
 def join_kernel(w, count, _, *refs):
     out_ref = refs[2 * count]
-    extra = None
     for k in range(count):
         a_ref, b_ref = refs[k], refs[count + k]
         out_ref[k * w : (k + 1) * w, :] = a_ref[:w, :] + b_ref[:w, :]
         if a_ref.shape[0] > w:
-            pad = a_ref[w:, :] + b_ref[w:, :]
-            extra = pad if extra is None else extra + pad
-    if extra is not None:
-        refs[2 * count + 1][...] = extra
+            refs[2 * count + 1][...] = a_ref[w:, :] + b_ref[w:, :]
 
 
 def join(meta, parts, comes):
     n = parts[0].shape[1]
     w = n // CHUNKS
     shapes = [shaped(len(parts) * w, n)]
-    if parts[0].shape[0] > w:
+    if parts[-1].shape[0] > w:
         shapes.append(shaped(PAD, n))
     return call(functools.partial(join_kernel, w, len(parts)), shapes, meta, [*parts, *comes])
 

time: 266 us -> 264 us (level)
  waiting for transfers between devices: 135 us -> 132 us
    ppermute x40, waiting for transfers between devices: 135 us -> 132 us  [routed(): return lax.ppermute(block, ('row', 'col'), route)]
  transfers between devices with their start and end apart: 40 -> 40, of which waited for: 15 -> 14; matrix products, arithmetic and copies ran while one was open for 0% -> 0% of each run, Pallas kernels for 20% -> 21%
where the time goes in v8:
time: 264 us
  waiting for transfers between devices  132 us (50%)
  starting transfers between devices  69.2 us (26%)
  Pallas kernels  56.5 us (21%)
  local copies, waits for them, and re-layouts  5.02 us (2%)
    ppermute x40, waiting for transfers between devices, routed(): return lax.ppermute(block, ('row', 'col'), route)  132 us
    ppermute x40, starting transfers between devices, routed(): return lax.ppermute(block, ('row', 'col'), route)  69.2 us
    pallas_call x38, Pallas kernels, call(): pl.pallas_call(kernel, out_shape=list(shapes), grid_spec=pltpu.PrefetchSc...  56.5 us
  transfers between devices with their start and end apart: 40, of which 14 were waited for; matrix products, arithmetic and copies ran while one was open for 0% of the time, Pallas kernels for 21%

profile of v8, /device:TPU:0, one launch (start us, length us, event | category | flops | bytes accessed | tf_op | source)
XLA Modules:
  0.0 263.8 jit_solution(3197492717751259688)
XLA Ops:
  5.2 3.0 %collective-permute-start = (f32[2,512,256]{2,1,0:T(8,128)S(1)}, f32[2,512,256]{2,1,0:T(8,128)S(1)}, u32[]{:S(2)}, u32[]{:S(2)}) collective-permute-start(f32[2,512,256]{2,1,0:T(8,128)S(1)} %shard_map.59), channel_id=1, source_target_pairs={{0,2},{1,3},{2,0},{3,1},{4,6},{5,7},{6,4},{7,5},{8,10},{9,11},{10,... | collective-permute-start | bytes 3145736 | tf_op jit(solution)/shard_map/ppermute | solution.py:84
  11.8 2.1 shard_map.72
  19.8 6.8 %shard_map.76 = (f32[2,128,512]{2,1,0:T(8,128)S(1)}, f32[2,128,512]{2,1,0:T(8,128)S(1)}, f32[2,136,512]{2,1,0:T(8,128)S(1)}) custom-call(s32[8]{0:T(128)S(1)} %compare_select_fusion.7.m._, f32[512,1024]{1,0:T(8,128)S(1)} %collective-permute-done.12.at_ref, f32[512,1024]{1,0:T(8,128)} %collective-permute-done.13.av_ref, ...), custom_call_target="tpu_custom_call" | custom-call | tf_op jit(solution)/shard_map/pallas_call | solution.py:143
  26.6 5.6 %collective-permute-done.a_ref = f32[2,512,256]{2,1,0:T(8,128)S(1)} collective-permute-done((f32[2,512,256]{2,1,0:T(8,128)S(1)}, f32[2,512,256]{2,1,0:T(8,128)S(1)}, u32[]{:S(2)}, u32[]{:S(2)}) %collective-permute-start) | collective-permute-done | bytes 1048608 | tf_op jit(solution)/shard_map/ppermute | solution.py:84
  34.2 20.5 %collective-permute-done.2.a_ref = f32[2,512,256]{2,1,0:T(8,128)S(1)} collective-permute-done((f32[2,512,256]{2,1,0:T(8,128)S(1)}, f32[2,512,256]{2,1,0:T(8,128)S(1)}, u32[]{:S(2)}, u32[]{:S(2)}) %collective-permute-start.2) | collective-permute-done | bytes 1048608 | tf_op jit(solution)/shard_map/ppermute | solution.py:84
  56.7 3.3 %shard_map.70.keep_pass.keep_stay = f32[2,128,512]{2,1,0:T(8,128)S(1)} custom-call(s32[8]{0:T(128)S(1)} %compare_select_fusion.7.m._, f32[512,1024]{1,0:T(8,128)S(1)} %collective-permute-done.12.at_ref, f32[512,1024]{1,0:T(8,128)} %collective-permute-done.13.av_ref, bf16[4,512,1024]{2,1,0:T(8,128)(2,1)S(1)} %shard_map.60.own_ref), custom_call_target="tpu_custom_call" | custom-call | tf_op jit(solution)/shard_map/pallas_call | solution.py:143
  60.6 2.1 collective-permute-start.15
  62.7 6.8 %shard_map.75 = (f32[2,128,512]{2,1,0:T(8,128)S(1)}, f32[2,128,512]{2,1,0:T(8,128)S(1)}, f32[2,136,512]{2,1,0:T(8,128)S(1)}) custom-call(s32[8]{0:T(128)S(1)} %compare_select_fusion.7.m._, f32[512,1024]{1,0:T(8,128)S(1)} %collective-permute-done.12.at_ref, f32[512,1024]{1,0:T(8,128)} %collective-permute-done.13.av_ref, ...), custom_call_target="tpu_custom_call" | custom-call | tf_op jit(solution)/shard_map/pallas_call | solution.py:143
  70.2 2.1 collective-permute-start.17
  72.8 6.5 %collective-permute-done.18.come_pass.come_stay = f32[2,128,512]{2,1,0:T(8,128)S(1)} collective-permute-done((f32[2,128,512]{2,1,0:T(8,128)S(1)}, f32[2,128,512]{2,1,0:T(8,128)S(1)}, u32[]{:S(2)}, u32[]{:S(2)}) %collective-permute-start.18) | collective-permute-done | bytes 524320 | tf_op jit(solution)/shard_map/ppermute | solution.py:84
  82.0 17.0 %collective-permute-done.31.a_ref = f32[2,512,256]{2,1,0:T(8,128)S(1)} collective-permute-done((f32[2,512,256]{2,1,0:T(8,128)S(1)}, f32[2,512,256]{2,1,0:T(8,128)S(1)}, u32[]{:S(2)}, u32[]{:S(2)}) %collective-permute-start.31) | collective-permute-done | bytes 1048608 | tf_op jit(solution)/shard_map/ppermute | solution.py:84
  105.7 29.1 %collective-permute-done.22.refs_4_ = f32[128,512]{1,0:T(8,128)S(1)} collective-permute-done((f32[128,512]{1,0:T(8,128)S(1)}, f32[128,512]{1,0:T(8,128)S(1)}, u32[]{:S(2)}, u32[]{:S(2)}) %collective-permute-start.22) | collective-permute-done | bytes 262176 | tf_op jit(solution)/shard_map/ppermute | solution.py:84
  136.4 4.1 %collective-permute-done.23.refs_5_ = f32[128,512]{1,0:T(8,128)S(1)} collective-permute-done((f32[128,512]{1,0:T(8,128)S(1)}, f32[128,512]{1,0:T(8,128)S(1)}, u32[]{:S(2)}, u32[]{:S(2)}) %collective-permute-start.23) | collective-permute-done | bytes 262176 | tf_op jit(solution)/shard_map/ppermute | solution.py:84
  140.5 5.6 %collective-permute-done.24.refs_6_ = f32[128,512]{1,0:T(8,128)S(1)} collective-permute-done((f32[128,512]{1,0:T(8,128)S(1)}, f32[128,512]{1,0:T(8,128)S(1)}, u32[]{:S(2)}, u32[]{:S(2)}) %collective-permute-start.24) | collective-permute-done | bytes 262176 | tf_op jit(solution)/shard_map/ppermute | solution.py:84
  146.1 5.0 %collective-permute-done.25.refs_7_ = f32[136,512]{1,0:T(8,128)S(1)} collective-permute-done((f32[136,512]{1,0:T(8,128)S(1)}, f32[136,512]{1,0:T(8,128)S(1)}, u32[]{:S(2)}, u32[]{:S(2)}) %collective-permute-start.25) | collective-permute-done | bytes 278560 | tf_op jit(solution)/shard_map/ppermute | solution.py:84
  154.4 2.4 shard_map.87
  158.9 2.4 shard_map.63
  163.1 2.4 shard_map.85
  165.5 6.2 %collective-permute-done.33.come_pass.come_stay = f32[2,128,512]{2,1,0:T(8,128)S(1)} collective-permute-done((f32[2,128,512]{2,1,0:T(8,128)S(1)}, f32[2,128,512]{2,1,0:T(8,128)S(1)}, u32[]{:S(2)}, u32[]{:S(2)}) %collective-permute-start.33) | collective-permute-done | bytes 524320 | tf_op jit(solution)/shard_map/ppermute | solution.py:84
  172.4 10.5 %collective-permute-done.35.come_pass.come_stay = f32[2,128,512]{2,1,0:T(8,128)S(1)} collective-permute-done((f32[2,128,512]{2,1,0:T(8,128)S(1)}, f32[2,128,512]{2,1,0:T(8,128)S(1)}, u32[]{:S(2)}, u32[]{:S(2)}) %collective-permute-start.35) | collective-permute-done | bytes 524320 | tf_op jit(solution)/shard_map/ppermute | solution.py:84
  185.4 2.2 collective-permute-start.26
  191.7 2.4 shard_map.61
  194.7 3.0 %collective-permute-start.38 = (f32[128,512]{1,0:T(8,128)S(1)}, f32[128,512]{1,0:T(8,128)S(1)}, u32[]{:S(2)}, u32[]{:S(2)}) collective-permute-start(f32[128,512]{1,0:T(8,128)S(1)} %shard_map.91.refs_1_), channel_id=1, source_target_pairs={{0,16},{1,17},{2,18},{3,19},{4,20},{5,21},{6,22},{7,23},{8,24},{9,... | collective-permute-start | bytes 786440 | tf_op jit(solution)/shard_map/ppermute | solution.py:84
  198.3 5.9 %collective-permute-done.4.come_pass.come_stay = f32[2,128,512]{2,1,0:T(8,128)S(1)} collective-permute-done((f32[2,128,512]{2,1,0:T(8,128)S(1)}, f32[2,128,512]{2,1,0:T(8,128)S(1)}, u32[]{:S(2)}, u32[]{:S(2)}) %collective-permute-start.4) | collective-permute-done | bytes 524320 | tf_op jit(solution)/shard_map/ppermute | solution.py:84
  204.9 7.2 %collective-permute-start.5 = (f32[128,512]{1,0:T(8,128)S(1)}, f32[128,512]{1,0:T(8,128)S(1)}, u32[]{:S(2)}, u32[]{:S(2)}) collective-permute-start(f32[128,512]{1,0:T(8,128)S(1)} %get-tuple-element.43), channel_id=1, source_target_pairs={{0,8},{1,9},{2,10},{3,11},{4,12},{5,13},{6,14},{7,15},{8,0},{9,1},... | collective-permute-start | bytes 786440 | tf_op jit(solution)/shard_map/ppermute | solution.py:84
  212.1 3.0 %collective-permute-done.38.refs_3_ = f32[128,512]{1,0:T(8,128)S(1)} collective-permute-done((f32[128,512]{1,0:T(8,128)S(1)}, f32[128,512]{1,0:T(8,128)S(1)}, u32[]{:S(2)}, u32[]{:S(2)}) %collective-permute-start.38) | collective-permute-done | bytes 262176 | tf_op jit(solution)/shard_map/ppermute | solution.py:84
  215.7 5.7 %collective-permute-start.39 = (f32[256,512]{1,0:T(8,128)S(1)}, f32[256,512]{1,0:T(8,128)}, u32[]{:S(2)}, u32[]{:S(2)}) collective-permute-start(f32[256,512]{1,0:T(8,128)S(1)} %shard_map.92.refs_4_), channel_id=1, source_target_pairs={{0,6},{1,10},{4,2},{5,14},{8,3},{9,15},{12,7},{13,11},{18,16},{19,... | collective-permute-start | bytes 1572872 | tf_op jit(solution)/shard_map/ppermute | solution.py:84
  224.4 6.2 %collective-permute-start.6 = (f32[128,512]{1,0:T(8,128)S(1)}, f32[128,512]{1,0:T(8,128)S(1)}, u32[]{:S(2)}, u32[]{:S(2)}) collective-permute-start(f32[128,512]{1,0:T(8,128)S(1)} %shard_map.65.refs_0_), channel_id=1, source_target_pairs={{0,16},{1,17},{2,18},{3,19},{4,20},{5,21},{6,22},{7,23},{8,24},{9,... | collective-permute-start | bytes 786440 | tf_op jit(solution)/shard_map/ppermute | solution.py:84
  230.6 10.6 %collective-permute-done.10.refs_1_ = f32[128,512]{1,0:T(8,128)S(1)} collective-permute-done((f32[128,512]{1,0:T(8,128)S(1)}, f32[128,512]{1,0:T(8,128)S(1)}, u32[]{:S(2)}, u32[]{:S(2)}) %collective-permute-start.10) | collective-permute-done | bytes 262176 | tf_op jit(solution)/shard_map/ppermute | solution.py:84
  241.8 4.9 %collective-permute-start.11 = (f32[128,512]{1,0:T(8,128)S(1)}, f32[128,512]{1,0:T(8,128)}, u32[]{:S(2)}, u32[]{:S(2)}) collective-permute-start(f32[128,512]{1,0:T(8,128)S(1)} %shard_map.69.refs_0_), channel_id=1, source_target_pairs={{0,6},{1,10},{4,2},{5,14},{8,3},{9,15},{12,7},{13,11},{18,16},{19,... | collective-permute-start | bytes 786440 | tf_op jit(solution)/shard_map/ppermute | solution.py:84
  247.3 5.0 %collective-permute-start.7 = (f32[128,512]{1,0:T(8,128)S(1)}, f32[128,512]{1,0:T(8,128)}, u32[]{:S(2)}, u32[]{:S(2)}) collective-permute-start(f32[128,512]{1,0:T(8,128)S(1)} %shard_map.66.refs_1_), channel_id=1, source_target_pairs={{0,6},{1,10},{4,2},{5,14},{8,3},{9,15},{12,7},{13,11},{18,16},{19,... | collective-permute-start | bytes 786440 | tf_op jit(solution)/shard_map/ppermute | solution.py:84
  254.3 5.6 %shard_map.93 = (f32[512,1024]{1,0:T(8,128)}, f32[512,1024]{1,0:T(8,128)}) custom-call(s32[8]{0:T(128)S(1)} %compare_select_fusion.7.m._, f32[512,512]{1,0:T(8,128)} %get-tuple-element.62.refs_0_, f32[512,512]{1,0:T(8,128)} %collective-permute-done.26.refs_1_, f32[512,512]{1,0:T(8,128)} %collective-permute-done.28.refs_2_, ...), custom_call_target="tpu_custom_call" | custom-call | tf_op jit(solution)/shard_map/pallas_call | solution.py:143
  (104 shorter events, 57.2 us)
Async XLA Ops:
  5.2 27.0 %collective-permute-start = (f32[2,512,256]{2,1,0:T(8,128)S(1)}, f32[2,512,256]{2,1,0:T(8,128)S(1)}, u32[]{:S(2)}, u32[]{:S(2)}) collective-permute-start(f32[2,512,256]{2,1,0:T(8,128)S(1)} %shard_map.59), channel_id=1, source_target_pairs={{0,2},{1,3},{2,0},{3,1},{4,6},{5,7},{6,4},{7,5},{8,10},{9,11},{10,... | collective-permute-start | bytes 3145736 | tf_op jit(solution)/shard_map/ppermute | solution.py:84
  8.9 45.7 %collective-permute-start.2 = (f32[2,512,256]{2,1,0:T(8,128)S(1)}, f32[2,512,256]{2,1,0:T(8,128)S(1)}, u32[]{:S(2)}, u32[]{:S(2)}) collective-permute-start(f32[2,512,256]{2,1,0:T(8,128)S(1)} %shard_map.62), channel_id=1, source_target_pairs={{0,2},{1,3},{2,0},{3,1},{4,6},{5,7},{6,4},{7,5},{8,10},{9,11},{10,... | collective-permute-start | bytes 3145736 | tf_op jit(solution)/shard_map/ppermute | solution.py:84
  14.0 42.7 %collective-permute-start.14 = (f32[2,128,512]{2,1,0:T(8,128)S(1)}, f32[2,128,512]{2,1,0:T(8,128)S(1)}, u32[]{:S(2)}, u32[]{:S(2)}) collective-permute-start(f32[2,128,512]{2,1,0:T(8,128)S(1)} %shard_map.72), channel_id=1, source_target_pairs={{0,4},{1,5},{2,6},{3,7},{4,0},{5,1},{6,2},{7,3},{8,12},{9,13},{10,... | collective-permute-start | bytes 1572872 | tf_op jit(solution)/shard_map/ppermute | solution.py:84
  16.7 64.7 %collective-permute-start.29 = (f32[2,512,256]{2,1,0:T(8,128)S(1)}, f32[2,512,256]{2,1,0:T(8,128)S(1)}, u32[]{:S(2)}, u32[]{:S(2)}) collective-permute-start(f32[2,512,256]{2,1,0:T(8,128)S(1)} %shard_map.84), channel_id=1, source_target_pairs={{0,2},{1,3},{2,0},{3,1},{4,6},{5,7},{6,4},{7,5},{8,10},{9,11},{10,... | collective-permute-start | bytes 3145736 | tf_op jit(solution)/shard_map/ppermute | solution.py:84
  19.2 79.8 %collective-permute-start.31 = (f32[2,512,256]{2,1,0:T(8,128)S(1)}, f32[2,512,256]{2,1,0:T(8,128)S(1)}, u32[]{:S(2)}, u32[]{:S(2)}) collective-permute-start(f32[2,512,256]{2,1,0:T(8,128)S(1)} %shard_map.86), channel_id=1, source_target_pairs={{0,2},{1,3},{2,0},{3,1},{4,6},{5,7},{6,4},{7,5},{8,10},{9,11},{10,... | collective-permute-start | bytes 3145736 | tf_op jit(solution)/shard_map/ppermute | solution.py:84
  32.2 28.4 %collective-permute-start.16 = (f32[2,128,512]{2,1,0:T(8,128)S(1)}, f32[2,128,512]{2,1,0:T(8,128)S(1)}, u32[]{:S(2)}, u32[]{:S(2)}) collective-permute-start(f32[2,128,512]{2,1,0:T(8,128)S(1)} %get-tuple-element.51), channel_id=1, source_target_pairs={{0,4},{1,5},{2,6},{3,7},{4,0},{5,1},{6,2},{7,3},{8,12},{9,13},{10,... | collective-permute-start | bytes 1572872 | tf_op jit(solution)/shard_map/ppermute | solution.py:84
  56.6 22.7 %collective-permute-start.18 = (f32[2,128,512]{2,1,0:T(8,128)S(1)}, f32[2,128,512]{2,1,0:T(8,128)S(1)}, u32[]{:S(2)}, u32[]{:S(2)}) collective-permute-start(f32[2,128,512]{2,1,0:T(8,128)S(1)} %get-tuple-element.55), channel_id=1, source_target_pairs={{0,4},{1,5},{2,6},{3,7},{4,0},{5,1},{6,2},{7,3},{8,12},{9,13},{10,... | collective-permute-start | bytes 1572872 | tf_op jit(solution)/shard_map/ppermute | solution.py:84
  60.6 38.4 %collective-permute-start.15 = (f32[128,512]{1,0:T(8,128)S(1)}, f32[128,512]{1,0:T(8,128)S(1)}, u32[]{:S(2)}, u32[]{:S(2)}) collective-permute-start(f32[128,512]{1,0:T(8,128)S(1)} %get-tuple-element.49), channel_id=1, source_target_pairs={{0,8},{1,9},{2,10},{3,11},{4,12},{5,13},{6,14},{7,15},{8,0},{9,1},... | collective-permute-start | bytes 786440 | tf_op jit(solution)/shard_map/ppermute | solution.py:84
  70.2 29.9 %collective-permute-start.17 = (f32[128,512]{1,0:T(8,128)S(1)}, f32[128,512]{1,0:T(8,128)S(1)}, u32[]{:S(2)}, u32[]{:S(2)}) collective-permute-start(f32[128,512]{1,0:T(8,128)S(1)} %get-tuple-element.53), channel_id=1, source_target_pairs={{0,8},{1,9},{2,10},{3,11},{4,12},{5,13},{6,14},{7,15},{8,0},{9,1},... | collective-permute-start | bytes 786440 | tf_op jit(solution)/shard_map/ppermute | solution.py:84
  79.3 24.5 %collective-permute-start.21 = (f32[136,512]{1,0:T(8,128)S(1)}, f32[136,512]{1,0:T(8,128)S(1)}, u32[]{:S(2)}, u32[]{:S(2)}) collective-permute-start(f32[136,512]{1,0:T(8,128)S(1)} %get-tuple-element.61), channel_id=1, source_target_pairs={{0,8},{1,9},{2,10},{3,11},{4,12},{5,13},{6,14},{7,15},{8,0},{9,1},... | collective-permute-start | bytes 835592 | tf_op jit(solution)/shard_map/ppermute | solution.py:84
  81.4 20.5 %collective-permute-start.19 = (f32[128,512]{1,0:T(8,128)S(1)}, f32[128,512]{1,0:T(8,128)S(1)}, u32[]{:S(2)}, u32[]{:S(2)}) collective-permute-start(f32[128,512]{1,0:T(8,128)S(1)} %get-tuple-element.57), channel_id=1, source_target_pairs={{0,8},{1,9},{2,10},{3,11},{4,12},{5,13},{6,14},{7,15},{8,0},{9,1},... | collective-permute-start | bytes 786440 | tf_op jit(solution)/shard_map/ppermute | solution.py:84
  99.0 55.5 %collective-permute-start.32 = (f32[2,512,256]{2,1,0:T(8,128)S(1)}, f32[2,512,256]{2,1,0:T(8,128)S(1)}, u32[]{:S(2)}, u32[]{:S(2)}) collective-permute-start(f32[2,512,256]{2,1,0:T(8,128)S(1)} %collective-permute-done.31.a_ref), channel_id=1, source_target_pairs={{0,1},{1,0},{2,3},{3,2},{4,5},{5,4},{6,7},{7,6},{8,9},{9,8},{10,11... | collective-permute-start | bytes 3145736 | tf_op jit(solution)/shard_map/ppermute | solution.py:84
  99.0 59.6 %collective-permute-start.3 = (f32[2,512,256]{2,1,0:T(8,128)S(1)}, f32[2,512,256]{2,1,0:T(8,128)S(1)}, u32[]{:S(2)}, u32[]{:S(2)}) collective-permute-start(f32[2,512,256]{2,1,0:T(8,128)S(1)} %collective-permute-done.2.a_ref), channel_id=1, source_target_pairs={{0,1},{1,0},{2,3},{3,2},{4,5},{5,4},{6,7},{7,6},{8,9},{9,8},{10,11... | collective-permute-start | bytes 3145736 | tf_op jit(solution)/shard_map/ppermute | solution.py:84
  100.1 34.8 %collective-permute-start.22 = (f32[128,512]{1,0:T(8,128)S(1)}, f32[128,512]{1,0:T(8,128)S(1)}, u32[]{:S(2)}, u32[]{:S(2)}) collective-permute-start(f32[128,512]{1,0:T(8,128)S(1)} %shard_map.74.refs_0_), channel_id=1, source_target_pairs={{2,18},{3,19},{6,22},{7,23},{10,26},{11,27},{14,30},{15,31},{16,0}... | collective-permute-start | bytes 786440 | tf_op jit(solution)/shard_map/ppermute | solution.py:84
  102.0 38.5 %collective-permute-start.23 = (f32[128,512]{1,0:T(8,128)S(1)}, f32[128,512]{1,0:T(8,128)S(1)}, u32[]{:S(2)}, u32[]{:S(2)}) collective-permute-start(f32[128,512]{1,0:T(8,128)S(1)} %shard_map.78.refs_1_), channel_id=1, source_target_pairs={{2,18},{3,19},{6,22},{7,23},{10,26},{11,27},{14,30},{15,31},{16,0}... | collective-permute-start | bytes 786440 | tf_op jit(solution)/shard_map/ppermute | solution.py:84
  103.9 42.3 %collective-permute-start.24 = (f32[128,512]{1,0:T(8,128)S(1)}, f32[128,512]{1,0:T(8,128)S(1)}, u32[]{:S(2)}, u32[]{:S(2)}) collective-permute-start(f32[128,512]{1,0:T(8,128)S(1)} %shard_map.80.refs_2_), channel_id=1, source_target_pairs={{2,18},{3,19},{6,22},{7,23},{10,26},{11,27},{14,30},{15,31},{16,0}... | collective-permute-start | bytes 786440 | tf_op jit(solution)/shard_map/ppermute | solution.py:84
  134.9 16.2 %collective-permute-start.25 = (f32[136,512]{1,0:T(8,128)S(1)}, f32[136,512]{1,0:T(8,128)S(1)}, u32[]{:S(2)}, u32[]{:S(2)}) collective-permute-start(f32[136,512]{1,0:T(8,128)S(1)} %shard_map.82.refs_3_), channel_id=1, source_target_pairs={{2,18},{3,19},{6,22},{7,23},{10,26},{11,27},{14,30},{15,31},{16,0}... | collective-permute-start | bytes 835592 | tf_op jit(solution)/shard_map/ppermute | solution.py:84
  140.5 20.8 %collective-permute-start.30 = (f32[2,512,256]{2,1,0:T(8,128)S(1)}, f32[2,512,256]{2,1,0:T(8,128)S(1)}, u32[]{:S(2)}, u32[]{:S(2)}) collective-permute-start(f32[2,512,256]{2,1,0:T(8,128)S(1)} %collective-permute-done.29.a_ref), channel_id=1, source_target_pairs={{0,1},{1,0},{2,3},{3,2},{4,5},{5,4},{6,7},{7,6},{8,9},{9,8},{10,11... | collective-permute-start | bytes 3145736 | tf_op jit(solution)/shard_map/ppermute | solution.py:84
  146.1 39.1 %collective-permute-start.1 = (f32[2,512,256]{2,1,0:T(8,128)S(1)}, f32[2,512,256]{2,1,0:T(8,128)S(1)}, u32[]{:S(2)}, u32[]{:S(2)}) collective-permute-start(f32[2,512,256]{2,1,0:T(8,128)S(1)} %collective-permute-done.a_ref), channel_id=1, source_target_pairs={{0,1},{1,0},{2,3},{3,2},{4,5},{5,4},{6,7},{7,6},{8,9},{9,8},{10,11... | collective-permute-start | bytes 3145736 | tf_op jit(solution)/shard_map/ppermute | solution.py:84
  152.8 34.8 %collective-permute-start.27 = (f32[512,512]{1,0:T(8,128)}, f32[512,512]{1,0:T(8,128)}, u32[]{:S(2)}, u32[]{:S(2)}) collective-permute-start(f32[512,512]{1,0:T(8,128)} %get-tuple-element.62.refs_0_), channel_id=1, source_target_pairs={{1,3},{5,7},{8,10},{12,14},{19,17},{23,21},{26,24},{30,28}} | collective-permute-start | bytes 3145736 | tf_op jit(solution)/shard_map/ppermute | solution.py:84
  158.6 24.3 %collective-permute-start.35 = (f32[2,128,512]{2,1,0:T(8,128)S(1)}, f32[2,128,512]{2,1,0:T(8,128)S(1)}, u32[]{:S(2)}, u32[]{:S(2)}) collective-permute-start(f32[2,128,512]{2,1,0:T(8,128)S(1)} %get-tuple-element.69), channel_id=1, source_target_pairs={{0,4},{1,5},{2,6},{3,7},{4,0},{5,1},{6,2},{7,3},{8,12},{9,13},{10,... | collective-permute-start | bytes 1572872 | tf_op jit(solution)/shard_map/ppermute | solution.py:84
  161.3 33.3 %collective-permute-start.8 = (f32[2,128,512]{2,1,0:T(8,128)S(1)}, f32[2,128,512]{2,1,0:T(8,128)S(1)}, u32[]{:S(2)}, u32[]{:S(2)}) collective-permute-start(f32[2,128,512]{2,1,0:T(8,128)S(1)} %get-tuple-element.45), channel_id=1, source_target_pairs={{0,4},{1,5},{2,6},{3,7},{4,0},{5,1},{6,2},{7,3},{8,12},{9,13},{10,... | collective-permute-start | bytes 1572872 | tf_op jit(solution)/shard_map/ppermute | solution.py:84
  182.9 21.3 %collective-permute-start.4 = (f32[2,128,512]{2,1,0:T(8,128)S(1)}, f32[2,128,512]{2,1,0:T(8,128)S(1)}, u32[]{:S(2)}, u32[]{:S(2)}) collective-permute-start(f32[2,128,512]{2,1,0:T(8,128)S(1)} %get-tuple-element.41), channel_id=1, source_target_pairs={{0,4},{1,5},{2,6},{3,7},{4,0},{5,1},{6,2},{7,3},{8,12},{9,13},{10,... | collective-permute-start | bytes 1572872 | tf_op jit(solution)/shard_map/ppermute | solution.py:84
  185.4 67.3 %collective-permute-start.26 = (f32[512,512]{1,0:T(8,128)}, f32[512,512]{1,0:T(8,128)}, u32[]{:S(2)}, u32[]{:S(2)}) collective-permute-start(f32[512,512]{1,0:T(8,128)} %get-tuple-element.62.refs_0_), channel_id=1, source_target_pairs={{0,4},{4,0},{9,13},{13,9},{18,22},{22,18},{27,31},{31,27}} | collective-permute-start | bytes 3145736 | tf_op jit(solution)/shard_map/ppermute | solution.py:84
  187.6 65.1 %collective-permute-start.28 = (f32[512,512]{1,0:T(8,128)}, f32[512,512]{1,0:T(8,128)}, u32[]{:S(2)}, u32[]{:S(2)}) collective-permute-start(f32[512,512]{1,0:T(8,128)} %collective-permute-done.27), channel_id=1, source_target_pairs={{3,8},{7,12},{10,5},{14,1},{17,26},{21,30},{24,23},{28,19}} | collective-permute-start | bytes 3145736 | tf_op jit(solution)/shard_map/ppermute | solution.py:84
  194.7 20.4 %collective-permute-start.38 = (f32[128,512]{1,0:T(8,128)S(1)}, f32[128,512]{1,0:T(8,128)S(1)}, u32[]{:S(2)}, u32[]{:S(2)}) collective-permute-start(f32[128,512]{1,0:T(8,128)S(1)} %shard_map.91.refs_1_), channel_id=1, source_target_pairs={{0,16},{1,17},{2,18},{3,19},{4,20},{5,21},{6,22},{7,23},{8,24},{9,... | collective-permute-start | bytes 786440 | tf_op jit(solution)/shard_map/ppermute | solution.py:84
  204.2 17.2 %collective-permute-start.9 = (f32[128,512]{1,0:T(8,128)S(1)}, f32[128,512]{1,0:T(8,128)S(1)}, u32[]{:S(2)}, u32[]{:S(2)}) collective-permute-start(f32[128,512]{1,0:T(8,128)S(1)} %get-tuple-element.47), channel_id=1, source_target_pairs={{0,8},{1,9},{2,10},{3,11},{4,12},{5,13},{6,14},{7,15},{8,0},{9,1},... | collective-permute-start | bytes 786440 | tf_op jit(solution)/shard_map/ppermute | solution.py:84
  204.9 19.0 %collective-permute-start.5 = (f32[128,512]{1,0:T(8,128)S(1)}, f32[128,512]{1,0:T(8,128)S(1)}, u32[]{:S(2)}, u32[]{:S(2)}) collective-permute-start(f32[128,512]{1,0:T(8,128)S(1)} %get-tuple-element.43), channel_id=1, source_target_pairs={{0,8},{1,9},{2,10},{3,11},{4,12},{5,13},{6,14},{7,15},{8,0},{9,1},... | collective-permute-start | bytes 786440 | tf_op jit(solution)/shard_map/ppermute | solution.py:84
  215.7 36.9 %collective-permute-start.39 = (f32[256,512]{1,0:T(8,128)S(1)}, f32[256,512]{1,0:T(8,128)}, u32[]{:S(2)}, u32[]{:S(2)}) collective-permute-start(f32[256,512]{1,0:T(8,128)S(1)} %shard_map.92.refs_4_), channel_id=1, source_target_pairs={{0,6},{1,10},{4,2},{5,14},{8,3},{9,15},{12,7},{13,11},{18,16},{19,... | collective-permute-start | bytes 1572872 | tf_op jit(solution)/shard_map/ppermute | solution.py:84
  222.0 19.3 %collective-permute-start.10 = (f32[128,512]{1,0:T(8,128)S(1)}, f32[128,512]{1,0:T(8,128)S(1)}, u32[]{:S(2)}, u32[]{:S(2)}) collective-permute-start(f32[128,512]{1,0:T(8,128)S(1)} %shard_map.68.refs_0_), channel_id=1, source_target_pairs={{0,16},{1,17},{2,18},{3,19},{4,20},{5,21},{6,22},{7,23},{8,24},{9,... | collective-permute-start | bytes 786440 | tf_op jit(solution)/shard_map/ppermute | solution.py:84
  224.4 22.2 %collective-permute-start.6 = (f32[128,512]{1,0:T(8,128)S(1)}, f32[128,512]{1,0:T(8,128)S(1)}, u32[]{:S(2)}, u32[]{:S(2)}) collective-permute-start(f32[128,512]{1,0:T(8,128)S(1)} %shard_map.65.refs_0_), channel_id=1, source_target_pairs={{0,16},{1,17},{2,18},{3,19},{4,20},{5,21},{6,22},{7,23},{8,24},{9,... | collective-permute-start | bytes 786440 | tf_op jit(solution)/shard_map/ppermute | solution.py:84
  241.8 18.7 %collective-permute-start.11 = (f32[128,512]{1,0:T(8,128)S(1)}, f32[128,512]{1,0:T(8,128)}, u32[]{:S(2)}, u32[]{:S(2)}) collective-permute-start(f32[128,512]{1,0:T(8,128)S(1)} %shard_map.69.refs_0_), channel_id=1, source_target_pairs={{0,6},{1,10},{4,2},{5,14},{8,3},{9,15},{12,7},{13,11},{18,16},{19,... | collective-permute-start | bytes 786440 | tf_op jit(solution)/shard_map/ppermute | solution.py:84
  (14 other events, 236.2 us)

commit v9 on v8

--- a/solution.py
+++ b/solution.py
@@ -387,64 +387,107 @@
     return t - residual / denom, residual
 
 
-def most_kernel(m, *refs):
-    near_own, near_swap, near_back, extra_ref = refs[:4]
-    far_own, far_back = refs[4:5], refs[5:6]
-    t_ref, v_ref, row_ref, col_ref, new_ref, res_ref = refs[6:]
+def grid_of(n):
+    line = lax.broadcasted_iota(jnp.int32, (n, n), 0)
+    return line, lax.broadcasted_iota(jnp.int32, (n, n), 1)
+
+
+def most_kernel(m, near_ref, far_ref, t_ref, v_ref, row_ref, col_ref, new_ref, res_ref):
     n = t_ref.shape[0]
-    place = m[PLACE]
-
-    def write(first, count, half, value):
-        rows = pl.ds(first, count)
-        new_ref[rows, half], res_ref[rows, half] = closing(
-            t_ref[rows, half], v_ref[rows, half], row_ref[rows, :], col_ref[:, half], value
+
+    def write(value):
+        rows = slice(0, value.shape[0])
+        new_ref[rows], res_ref[rows] = closing(
+            t_ref[rows], v_ref[rows], row_ref[rows], col_ref[...], value
+        )
+
+    @pl.when(m[NEAR] == 0)
+    def _():
+        write(far_ref[...])
+
+    @pl.when((m[NEAR] == 1) & (m[MIDDLE] == 0))
+    def _():
+        write(near_ref[...])
+
+    @pl.when(m[MIDDLE] == 1)
+    def _():
+        line, lane = grid_of(n)
+        own = near_ref[...]
+        write(jnp.where(line >= lane, own, own.T))
+
+
+def half_specs(n, at):
+    block = pl.BlockSpec((n, n), lambda i, m: (0, at(m)))
+    return [block, block, None, pl.BlockSpec((1, n), lambda i, m: (0, at(m)))], [block, block]
+
+
+def most(meta, near_own, far_own, t, *args):
+    ins, outs = half_specs(t.shape[0], lambda m: m[PLACE])
+    return call(
+        most_kernel,
+        [shaped(*t.shape)] * 2,
+        meta,
+        [near_own, far_own, t, *args],
+        in_specs=[None, None, *ins],
+        out_specs=outs,
+    )
+
+
+def back_kernel(m, near_ref, swap_ref, back_ref, extra_ref, *refs):
+    far = refs[:3]
+    t_ref, v_ref, row_ref, col_ref, _, _, new_ref, res_ref = refs[3:]
+    n = t_ref.shape[0]
+
+    def write(value, cols=slice(None)):
+        new_ref[:, cols], res_ref[:, cols] = closing(
+            t_ref[:, cols], v_ref[:, cols], row_ref[...], col_ref[:, cols], value
         )
 
     @pl.when(m[NEAR] == 0)
     def _():
         first = 0
-        for own_ref, back_ref in zip(far_own, far_back):
-            count = own_ref.shape[0]
-            write(first, count, placed(place, n), own_ref[...])
-            write(0, n, placed(1 - place, n, first, count), back_ref[...].T)
-            first += count
+        for ref in far:
+            write(ref[...].T, slice(first, first + ref.shape[0]))
+            first += ref.shape[0]
 
     @pl.when((m[NEAR] == 1) & (m[MIDDLE] == 0))
     def _():
-        write(0, n, placed(place, n), near_own[...])
-        write(0, n, placed(1 - place, n), near_back[...].T)
+        write(back_ref[...].T)
 
     @pl.when(m[MIDDLE] == 1)
     def _():
-        line = lax.broadcasted_iota(jnp.int32, (n, n), 0)
-        lane = lax.broadcasted_iota(jnp.int32, (n, n), 1)
-        own = near_own[...]
-        write(0, n, placed(place, n), jnp.where(line >= lane, own, own.T))
-        lower = jnp.where(line > lane, near_swap[...].T, extra_ref[:1, :])
-        write(0, n, placed(1 - place, n), jnp.where(line < lane, own, lower))
-
-
-def most(meta, t, *args):
-    return call(most_kernel, [shaped(*t.shape)] * 2, meta, args)
-
-
-def late_kernel(turned, chunk, count, m, *refs):
+        line, lane = grid_of(n)
+        lower = jnp.where(line > lane, swap_ref[...].T, extra_ref[:1, :])
+        write(jnp.where(line < lane, near_ref[...], lower))
+
+
+def back_half(meta, values, new, res, t, *args):
+    ins, outs = half_specs(t.shape[0], lambda m: 1 - m[PLACE])
+    hbm = pl.BlockSpec(memory_space=pl.ANY)
+    count = len(values) + 4
+    return call(
+        back_kernel,
+        [shaped(*t.shape)] * 2,
+        meta,
+        [*values, t, *args, new, res],
+        in_specs=[*[None] * len(values), *ins, hbm, hbm],
+        out_specs=outs,
+        aliases={count + 1: 0, count + 2: 1},
+    )
+
+
+def late_kernel(chunk, count, m, *refs):
     values = refs[:count]
     t_ref, v_ref, row_ref, col_ref, new_ref, res_ref, new, res, sems = refs[count + 2 :]
-    w = min(values[0].shape)
-    n = max(values[0].shape)
+    w, n = values[0].shape
 
     @pl.when(m[NEAR] == 0)
     def _():
-        parts = [ref[...].T if turned else ref[...] for ref in values]
-        value = parts[0] if count == 1 else jnp.concatenate(parts, axis=int(turned))
+        value = jnp.concatenate([ref[...] for ref in values], axis=0)
         new[...], res[...] = closing(
             t_ref[...], v_ref[...], row_ref[...], col_ref[...], value
         )
-        if turned:
-            rows, cols = pl.ds(0, n), placed(1 - m[PLACE], n, chunk * w, count * w)
-        else:
-            rows, cols = pl.ds(chunk * w, count * w), placed(m[PLACE], n)
+        rows, cols = pl.ds(chunk * w, count * w), placed(m[PLACE], n)
         copies = [
             pltpu.make_async_copy(source, target.at[rows, cols], sems.at[i])
             for i, (source, target) in enumerate(((new, new_ref), (res, res_ref)))
@@ -455,20 +498,15 @@
             copy.wait()
 
 
-def late(meta, turned, chunk, values, new, res, t, v, row_gap, col_gap):
+def late(meta, chunk, values, new, res, t, v, row_gap, col_gap):
     w, n = values[0].shape
     count = len(values)
-    if turned:
-        at = lambda i, m: (0, ((1 - m[PLACE]) * CHUNKS + chunk) // count)
-        block = pl.BlockSpec((n, count * w), at)
-        row, col = None, pl.BlockSpec((1, count * w), at)
-    else:
-        block = pl.BlockSpec((count * w, n), lambda i, m: (chunk // count, m[PLACE]))
-        row = pl.BlockSpec((count * w, 1), lambda i, m: (chunk // count, 0))
-        col = pl.BlockSpec((1, n), lambda i, m: (0, m[PLACE]))
+    block = pl.BlockSpec((count * w, n), lambda i, m: (chunk // count, m[PLACE]))
+    row = pl.BlockSpec((count * w, 1), lambda i, m: (chunk // count, 0))
+    col = pl.BlockSpec((1, n), lambda i, m: (0, m[PLACE]))
     hbm = pl.BlockSpec(memory_space=pl.ANY)
     return call(
-        functools.partial(late_kernel, turned, chunk, count),
+        functools.partial(late_kernel, chunk, count),
         [shaped(*t.shape)] * 2,
         meta,
         [*values, new, res, t, v, row_gap, col_gap],
@@ -545,10 +583,10 @@
         far_own += joined("f", chunks)
         far_back.append(over(far_target)(far_own[-1]))
     fixed = (t, v, row_gap, col_gap)
-    pair = most(meta, t, near_own, near_swap, near_back, extra, far_own[0], far_back[0], *fixed)
-    pair = late(meta, False, 2, far_own[1:], *pair, *fixed)
-    pair = late(meta, True, 2, far_back[1:2], *pair, *fixed)
-    return late(meta, True, 3, far_back[2:], *pair, *fixed)
+    pair = most(meta, near_own, far_own[0], *fixed)
+    pair = late(meta, 2, far_own[1:], *pair, *fixed)
+    values = [near_own, near_swap, near_back, extra, *far_back]
+    return back_half(meta, values, *pair, *fixed)
 
 
 NEAR_GROUPS = ((1, (1, 2, 3)), (0, (0,)), (0, (1, 2, 3)))

time: 264 us -> 259 us (0.981)
  the two profiles are of different devices: /device:TPU:0 before, /device:TPU:7 now
where the time goes in v9:
time: 259 us; the launch traced here: 258 us
  waiting for transfers between devices  102 us (39%)
  starting transfers between devices  91.1 us (35%)
  Pallas kernels  58.7 us (23%)
  local copies, waits for them, and re-layouts  5.02 us (2%)
    ppermute x40, waiting for transfers between devices, routed(): return lax.ppermute(block, ('row', 'col'), route)  102 us
    ppermute x40, starting transfers between devices, routed(): return lax.ppermute(block, ('row', 'col'), route)  91.1 us
    pallas_call x37, Pallas kernels, call(): pl.pallas_call(kernel, out_shape=list(shapes), grid_spec=pltpu.PrefetchSc...  58.7 us
  transfers between devices with their start and end apart: 40, of which 13 were waited for; matrix products, arithmetic and copies ran while one was open for 0% of the time, Pallas kernels for 21%

profile of v9, /device:TPU:7, one launch (start us, length us, event | category | flops | bytes accessed | tf_op | source)
XLA Modules:
  0.0 258.1 jit_solution(7042518162064675356)
XLA Ops:
  10.5 2.1 shard_map.62
  13.0 6.8 %shard_map.66 = (f32[2,128,512]{2,1,0:T(8,128)S(1)}, f32[2,128,512]{2,1,0:T(8,128)S(1)}, f32[2,136,512]{2,1,0:T(8,128)S(1)}) custom-call(s32[8]{0:T(128)S(1)} %compare_select_fusion.7._.m, f32[512,1024]{1,0:T(8,128)S(1)} %collective-permute-done.at_ref, f32[512,1024]{1,0:T(8,128)} %collective-permute-done.1.av_ref, bf16[4,512,1024]{2,1,0:T(8,128)(2,1)S(1)} %shard_map.59.own_ref), custom_call_target="tpu_custom_call" | custom-call | tf_op jit(solution)/shard_map/pallas_call | solution.py:143
  22.1 7.7 %collective-permute-done.17.a_ref = f32[2,512,256]{2,1,0:T(8,128)S(1)} collective-permute-done((f32[2,512,256]{2,1,0:T(8,128)S(1)}, f32[2,512,256]{2,1,0:T(8,128)S(1)}, u32[]{:S(2)}, u32[]{:S(2)}) %collective-permute-start.17) | collective-permute-done | bytes 1048608 | tf_op jit(solution)/shard_map/ppermute | solution.py:84
  30.9 21.3 %collective-permute-done.19.a_ref = f32[2,512,256]{2,1,0:T(8,128)S(1)} collective-permute-done((f32[2,512,256]{2,1,0:T(8,128)S(1)}, f32[2,512,256]{2,1,0:T(8,128)S(1)}, u32[]{:S(2)}, u32[]{:S(2)}) %collective-permute-start.19) | collective-permute-done | bytes 1048608 | tf_op jit(solution)/shard_map/ppermute | solution.py:84
  52.7 3.2 %shard_map.60.keep_pass.keep_stay = f32[2,128,512]{2,1,0:T(8,128)S(1)} custom-call(s32[8]{0:T(128)S(1)} %compare_select_fusion.7._.m, f32[512,1024]{1,0:T(8,128)S(1)} %collective-permute-done.at_ref, f32[512,1024]{1,0:T(8,128)} %collective-permute-done.1.av_ref, bf16[4,512,1024]{2,1,0:T(8,128)(2,1)S(1)} %shard_map.59.own_ref), custom_call_target="tpu_custom_call" | custom-call | tf_op jit(solution)/shard_map/pallas_call | solution.py:143
  57.9 6.8 %shard_map.65 = (f32[2,128,512]{2,1,0:T(8,128)S(1)}, f32[2,128,512]{2,1,0:T(8,128)S(1)}, f32[2,136,512]{2,1,0:T(8,128)S(1)}) custom-call(s32[8]{0:T(128)S(1)} %compare_select_fusion.7._.m, f32[512,1024]{1,0:T(8,128)S(1)} %collective-permute-done.at_ref, f32[512,1024]{1,0:T(8,128)} %collective-permute-done.1.av_ref, bf16[4,512,1024]{2,1,0:T(8,128)(2,1)S(1)} %shard_map.59.own_ref), custom_call_target="tpu_custom_call" | custom-call | tf_op jit(solution)/shard_map/pallas_call | solution.py:143
  69.1 1.9 collective-permute-done.5.b_ref
  70.9 4.2 %collective-permute-start.10 = (f32[128,512]{1,0:T(8,128)S(1)}, f32[128,512]{1,0:T(8,128)S(1)}, u32[]{:S(2)}, u32[]{:S(2)}) collective-permute-start(f32[128,512]{1,0:T(8,128)S(1)} %shard_map.64.refs_0_), channel_id=1, source_target_pairs={{2,18},{3,19},{6,22},{7,23},{10,26},{11,27},{14,30},{15,31},{16,0}... | collective-permute-start | bytes 786440 | tf_op jit(solution)/shard_map/ppermute | solution.py:84
  75.9 4.2 %collective-permute-start.11 = (f32[128,512]{1,0:T(8,128)S(1)}, f32[128,512]{1,0:T(8,128)S(1)}, u32[]{:S(2)}, u32[]{:S(2)}) collective-permute-start(f32[128,512]{1,0:T(8,128)S(1)} %shard_map.68.refs_1_), channel_id=1, source_target_pairs={{2,18},{3,19},{6,22},{7,23},{10,26},{11,27},{14,30},{15,31},{16,0}... | collective-permute-start | bytes 786440 | tf_op jit(solution)/shard_map/ppermute | solution.py:84
  82.0 15.1 %collective-permute-done.30.a_ref = f32[2,512,256]{2,1,0:T(8,128)S(1)} collective-permute-done((f32[2,512,256]{2,1,0:T(8,128)S(1)}, f32[2,512,256]{2,1,0:T(8,128)S(1)}, u32[]{:S(2)}, u32[]{:S(2)}) %collective-permute-start.30) | collective-permute-done | bytes 1048608 | tf_op jit(solution)/shard_map/ppermute | solution.py:84
  99.6 4.2 %collective-permute-start.13 = (f32[136,512]{1,0:T(8,128)S(1)}, f32[136,512]{1,0:T(8,128)S(1)}, u32[]{:S(2)}, u32[]{:S(2)}) collective-permute-start(f32[136,512]{1,0:T(8,128)S(1)} %shard_map.72.refs_3_), channel_id=1, source_target_pairs={{2,18},{3,19},{6,22},{7,23},{10,26},{11,27},{14,30},{15,31},{16,0}... | collective-permute-start | bytes 835592 | tf_op jit(solution)/shard_map/ppermute | solution.py:84
  103.8 4.2 %collective-permute-done.13.refs_7_ = f32[136,512]{1,0:T(8,128)S(1)} collective-permute-done((f32[136,512]{1,0:T(8,128)S(1)}, f32[136,512]{1,0:T(8,128)S(1)}, u32[]{:S(2)}, u32[]{:S(2)}) %collective-permute-start.13) | collective-permute-done | bytes 278560 | tf_op jit(solution)/shard_map/ppermute | solution.py:84
  110.2 2.4 shard_map.77
  114.2 2.4 shard_map.86
  118.1 2.4 shard_map.75
  120.5 2.4 shard_map.84
  124.0 16.7 %collective-permute-start.22 = (f32[128,512]{1,0:T(8,128)S(1)}, f32[128,512]{1,0:T(8,128)S(1)}, u32[]{:S(2)}, u32[]{:S(2)}) collective-permute-start(f32[128,512]{1,0:T(8,128)S(1)} %get-tuple-element.57), channel_id=1, source_target_pairs={{0,8},{1,9},{2,10},{3,11},{4,12},{5,13},{6,14},{7,15},{8,0},{9,1},... | collective-permute-start | bytes 786440 | tf_op jit(solution)/shard_map/ppermute | solution.py:84
  141.3 10.5 %collective-permute-start.24 = (f32[128,512]{1,0:T(8,128)S(1)}, f32[128,512]{1,0:T(8,128)S(1)}, u32[]{:S(2)}, u32[]{:S(2)}) collective-permute-start(f32[128,512]{1,0:T(8,128)S(1)} %get-tuple-element.61), channel_id=1, source_target_pairs={{0,8},{1,9},{2,10},{3,11},{4,12},{5,13},{6,14},{7,15},{8,0},{9,1},... | collective-permute-start | bytes 786440 | tf_op jit(solution)/shard_map/ppermute | solution.py:84
  152.4 10.6 %collective-permute-start.33 = (f32[128,512]{1,0:T(8,128)S(1)}, f32[128,512]{1,0:T(8,128)S(1)}, u32[]{:S(2)}, u32[]{:S(2)}) collective-permute-start(f32[128,512]{1,0:T(8,128)S(1)} %get-tuple-element.65), channel_id=1, source_target_pairs={{0,8},{1,9},{2,10},{3,11},{4,12},{5,13},{6,14},{7,15},{8,0},{9,1},... | collective-permute-start | bytes 786440 | tf_op jit(solution)/shard_map/ppermute | solution.py:84
  163.1 1.7 collective-permute-start.14
  164.8 13.4 %collective-permute-start.16 = (f32[512,512]{1,0:T(8,128)}, f32[512,512]{1,0:T(8,128)}, u32[]{:S(2)}, u32[]{:S(2)}) collective-permute-start(f32[512,512]{1,0:T(8,128)} %collective-permute-done.15), channel_id=1, source_target_pairs={{3,8},{7,12},{10,5},{14,1},{17,26},{21,30},{24,23},{28,19}} | collective-permute-start | bytes 3145736 | tf_op jit(solution)/shard_map/ppermute | solution.py:84
  179.5 2.6 collective-permute-start.25
  183.3 15.2 %collective-permute-done.37.b_ref = f32[128,512]{1,0:T(8,128)S(1)} collective-permute-done((f32[128,512]{1,0:T(8,128)S(1)}, f32[128,512]{1,0:T(8,128)S(1)}, u32[]{:S(2)}, u32[]{:S(2)}) %collective-permute-start.37) | collective-permute-done | bytes 262176 | tf_op jit(solution)/shard_map/ppermute | solution.py:84
  199.1 4.1 %collective-permute-done.25.refs_2_ = f32[128,512]{1,0:T(8,128)S(1)} collective-permute-done((f32[128,512]{1,0:T(8,128)S(1)}, f32[128,512]{1,0:T(8,128)S(1)}, u32[]{:S(2)}, u32[]{:S(2)}) %collective-permute-start.25) | collective-permute-done | bytes 262176 | tf_op jit(solution)/shard_map/ppermute | solution.py:84
  203.2 2.9 %collective-permute-start.38 = (f32[128,512]{1,0:T(8,128)S(1)}, f32[128,512]{1,0:T(8,128)S(1)}, u32[]{:S(2)}, u32[]{:S(2)}) collective-permute-start(f32[128,512]{1,0:T(8,128)S(1)} %shard_map.91.refs_0_), channel_id=1, source_target_pairs={{0,16},{1,17},{2,18},{3,19},{4,20},{5,21},{6,22},{7,23},{8,24},{9,... | collective-permute-start | bytes 786440 | tf_op jit(solution)/shard_map/ppermute | solution.py:84
  208.8 10.2 %collective-permute-done.34.refs_1_ = f32[128,512]{1,0:T(8,128)S(1)} collective-permute-done((f32[128,512]{1,0:T(8,128)S(1)}, f32[128,512]{1,0:T(8,128)S(1)}, u32[]{:S(2)}, u32[]{:S(2)}) %collective-permute-start.34) | collective-permute-done | bytes 262176 | tf_op jit(solution)/shard_map/ppermute | solution.py:84
  221.6 3.0 %collective-permute-done.38.refs_1_ = f32[128,512]{1,0:T(8,128)S(1)} collective-permute-done((f32[128,512]{1,0:T(8,128)S(1)}, f32[128,512]{1,0:T(8,128)S(1)}, u32[]{:S(2)}, u32[]{:S(2)}) %collective-permute-start.38) | collective-permute-done | bytes 262176 | tf_op jit(solution)/shard_map/ppermute | solution.py:84
  229.1 3.1 %shard_map.93 = (f32[512,1024]{1,0:T(8,128)}, f32[512,1024]{1,0:T(8,128)}) custom-call(s32[8]{0:T(128)S(1)} %compare_select_fusion.7._.m, f32[512,512]{1,0:T(8,128)S(1)} %get-tuple-element.52.near_ref, f32[256,512]{1,0:T(8,128)} %shard_map.82.far_ref, f32[512,1024]{1,0:T(8,128)S(1)} %copy-done.1, f32[512,1024]{1,0:T(8,128)S(1)} %copy-done.3, ...), custom_call_target="tpu_custom_call" | custom-call | tf_op jit(solution)/shard_map/pallas_call | solution.py:143
  232.2 2.7 %shard_map.94 = (f32[512,1024]{1,0:T(8,128)}, f32[512,1024]{1,0:T(8,128)}) custom-call(s32[8]{0:T(128)S(1)} %compare_select_fusion.7._.m, f32[128,512]{1,0:T(8,128)} %shard_map.89.refs_0_, f32[128,512]{1,0:T(8,128)} %shard_map.92.refs_1_, f32[512,1024]{1,0:T(8,128)} %get-tuple-element.70.refs_2_, ...), custom_call_target="tpu_custom_call", output_to_operand_aliasing={{0}: (3, {}), {1}: (4, {})} | custom-call | tf_op jit(solution)/shard_map/pallas_call | solution.py:143
  235.0 15.1 %collective-permute-done.35.refs_1_ = f32[128,512]{1,0:T(8,128)} collective-permute-done((f32[128,512]{1,0:T(8,128)}, f32[128,512]{1,0:T(8,128)}, u32[]{:S(2)}, u32[]{:S(2)}) %collective-permute-start.35) | collective-permute-done | bytes 262176 | tf_op jit(solution)/shard_map/ppermute | solution.py:84
  250.0 3.7 %collective-permute-done.39.refs_2_ = f32[128,512]{1,0:T(8,128)} collective-permute-done((f32[128,512]{1,0:T(8,128)}, f32[128,512]{1,0:T(8,128)}, u32[]{:S(2)}, u32[]{:S(2)}) %collective-permute-start.39) | collective-permute-done | bytes 262176 | tf_op jit(solution)/shard_map/ppermute | solution.py:84
  253.7 4.4 %shard_map.95 = (f32[512,1024]{1,0:T(8,128)}, f32[512,1024]{1,0:T(8,128)}) custom-call(s32[8]{0:T(128)S(1)} %compare_select_fusion.7._.m, f32[512,512]{1,0:T(8,128)S(1)} %get-tuple-element.52.near_ref, f32[512,512]{1,0:T(8,128)} %collective-permute-done.14.swap_ref, ...), custom_call_target="tpu_custom_call", output_to_operand_aliasing={{0}: (12, {}), {1}: (13, {})} | custom-call | tf_op jit(solution)/shard_map/pallas_call | solution.py:143
  (103 shorter events, 45.6 us)
Async XLA Ops:
  5.4 24.4 %collective-permute-start.17 = (f32[2,512,256]{2,1,0:T(8,128)S(1)}, f32[2,512,256]{2,1,0:T(8,128)S(1)}, u32[]{:S(2)}, u32[]{:S(2)}) collective-permute-start(f32[2,512,256]{2,1,0:T(8,128)S(1)} %shard_map.74), channel_id=1, source_target_pairs={{0,2},{1,3},{2,0},{3,1},{4,6},{5,7},{6,4},{7,5},{8,10},{9,11},{10,... | collective-permute-start | bytes 3145736 | tf_op jit(solution)/shard_map/ppermute | solution.py:84
  6.4 45.8 %collective-permute-start.19 = (f32[2,512,256]{2,1,0:T(8,128)S(1)}, f32[2,512,256]{2,1,0:T(8,128)S(1)}, u32[]{:S(2)}, u32[]{:S(2)}) collective-permute-start(f32[2,512,256]{2,1,0:T(8,128)S(1)} %shard_map.76), channel_id=1, source_target_pairs={{0,2},{1,3},{2,0},{3,1},{4,6},{5,7},{6,4},{7,5},{8,10},{9,11},{10,... | collective-permute-start | bytes 3145736 | tf_op jit(solution)/shard_map/ppermute | solution.py:84
  12.7 39.8 %collective-permute-start.2 = (f32[2,128,512]{2,1,0:T(8,128)S(1)}, f32[2,128,512]{2,1,0:T(8,128)S(1)}, u32[]{:S(2)}, u32[]{:S(2)}) collective-permute-start(f32[2,128,512]{2,1,0:T(8,128)S(1)} %shard_map.62), channel_id=1, source_target_pairs={{0,4},{1,5},{2,6},{3,7},{4,0},{5,1},{6,2},{7,3},{8,12},{9,13},{10,... | collective-permute-start | bytes 1572872 | tf_op jit(solution)/shard_map/ppermute | solution.py:84
  19.8 46.5 %collective-permute-start.8 = (f32[2,136,512]{2,1,0:T(8,128)S(1)}, f32[2,136,512]{2,1,0:T(8,128)S(1)}, u32[]{:S(2)}, u32[]{:S(2)}) collective-permute-start(f32[2,136,512]{2,1,0:T(8,128)S(1)} %get-tuple-element.49), channel_id=1, source_target_pairs={{0,4},{1,5},{2,6},{3,7},{4,0},{5,1},{6,2},{7,3},{8,12},{9,13},{10,... | collective-permute-start | bytes 1671176 | tf_op jit(solution)/shard_map/ppermute | solution.py:84
  21.1 35.5 %collective-permute-start.4 = (f32[2,128,512]{2,1,0:T(8,128)S(1)}, f32[2,128,512]{2,1,0:T(8,128)S(1)}, u32[]{:S(2)}, u32[]{:S(2)}) collective-permute-start(f32[2,128,512]{2,1,0:T(8,128)S(1)} %get-tuple-element.41), channel_id=1, source_target_pairs={{0,4},{1,5},{2,6},{3,7},{4,0},{5,1},{6,2},{7,3},{8,12},{9,13},{10,... | collective-permute-start | bytes 1572872 | tf_op jit(solution)/shard_map/ppermute | solution.py:84
  29.7 51.0 %collective-permute-start.28 = (f32[2,512,256]{2,1,0:T(8,128)S(1)}, f32[2,512,256]{2,1,0:T(8,128)S(1)}, u32[]{:S(2)}, u32[]{:S(2)}) collective-permute-start(f32[2,512,256]{2,1,0:T(8,128)S(1)} %shard_map.83), channel_id=1, source_target_pairs={{0,2},{1,3},{2,0},{3,1},{4,6},{5,7},{6,4},{7,5},{8,10},{9,11},{10,... | collective-permute-start | bytes 3145736 | tf_op jit(solution)/shard_map/ppermute | solution.py:84
  52.2 44.9 %collective-permute-start.30 = (f32[2,512,256]{2,1,0:T(8,128)S(1)}, f32[2,512,256]{2,1,0:T(8,128)S(1)}, u32[]{:S(2)}, u32[]{:S(2)}) collective-permute-start(f32[2,512,256]{2,1,0:T(8,128)S(1)} %shard_map.85), channel_id=1, source_target_pairs={{0,2},{1,3},{2,0},{3,1},{4,6},{5,7},{6,4},{7,5},{8,10},{9,11},{10,... | collective-permute-start | bytes 3145736 | tf_op jit(solution)/shard_map/ppermute | solution.py:84
  68.2 30.2 %collective-permute-start.9 = (f32[136,512]{1,0:T(8,128)S(1)}, f32[136,512]{1,0:T(8,128)S(1)}, u32[]{:S(2)}, u32[]{:S(2)}) collective-permute-start(f32[136,512]{1,0:T(8,128)S(1)} %get-tuple-element.51), channel_id=1, source_target_pairs={{0,8},{1,9},{2,10},{3,11},{4,12},{5,13},{6,14},{7,15},{8,0},{9,1},... | collective-permute-start | bytes 835592 | tf_op jit(solution)/shard_map/ppermute | solution.py:84
  70.9 27.5 %collective-permute-start.10 = (f32[128,512]{1,0:T(8,128)S(1)}, f32[128,512]{1,0:T(8,128)S(1)}, u32[]{:S(2)}, u32[]{:S(2)}) collective-permute-start(f32[128,512]{1,0:T(8,128)S(1)} %shard_map.64.refs_0_), channel_id=1, source_target_pairs={{2,18},{3,19},{6,22},{7,23},{10,26},{11,27},{14,30},{15,31},{16,0}... | collective-permute-start | bytes 786440 | tf_op jit(solution)/shard_map/ppermute | solution.py:84
  75.9 23.1 %collective-permute-start.11 = (f32[128,512]{1,0:T(8,128)S(1)}, f32[128,512]{1,0:T(8,128)S(1)}, u32[]{:S(2)}, u32[]{:S(2)}) collective-permute-start(f32[128,512]{1,0:T(8,128)S(1)} %shard_map.68.refs_1_), channel_id=1, source_target_pairs={{2,18},{3,19},{6,22},{7,23},{10,26},{11,27},{14,30},{15,31},{16,0}... | collective-permute-start | bytes 786440 | tf_op jit(solution)/shard_map/ppermute | solution.py:84
  80.7 18.9 %collective-permute-start.12 = (f32[128,512]{1,0:T(8,128)S(1)}, f32[128,512]{1,0:T(8,128)S(1)}, u32[]{:S(2)}, u32[]{:S(2)}) collective-permute-start(f32[128,512]{1,0:T(8,128)S(1)} %shard_map.70.refs_2_), channel_id=1, source_target_pairs={{2,18},{3,19},{6,22},{7,23},{10,26},{11,27},{14,30},{15,31},{16,0}... | collective-permute-start | bytes 786440 | tf_op jit(solution)/shard_map/ppermute | solution.py:84
  97.1 13.1 %collective-permute-start.20 = (f32[2,512,256]{2,1,0:T(8,128)S(1)}, f32[2,512,256]{2,1,0:T(8,128)S(1)}, u32[]{:S(2)}, u32[]{:S(2)}) collective-permute-start(f32[2,512,256]{2,1,0:T(8,128)S(1)} %collective-permute-done.19.a_ref), channel_id=1, source_target_pairs={{0,1},{1,0},{2,3},{3,2},{4,5},{5,4},{6,7},{7,6},{8,9},{9,8},{10,11... | collective-permute-start | bytes 3145736 | tf_op jit(solution)/shard_map/ppermute | solution.py:84
  98.4 14.8 %collective-permute-start.31 = (f32[2,512,256]{2,1,0:T(8,128)S(1)}, f32[2,512,256]{2,1,0:T(8,128)S(1)}, u32[]{:S(2)}, u32[]{:S(2)}) collective-permute-start(f32[2,512,256]{2,1,0:T(8,128)S(1)} %collective-permute-done.30.a_ref), channel_id=1, source_target_pairs={{0,1},{1,0},{2,3},{3,2},{4,5},{5,4},{6,7},{7,6},{8,9},{9,8},{10,11... | collective-permute-start | bytes 3145736 | tf_op jit(solution)/shard_map/ppermute | solution.py:84
  98.4 18.1 %collective-permute-start.18 = (f32[2,512,256]{2,1,0:T(8,128)S(1)}, f32[2,512,256]{2,1,0:T(8,128)S(1)}, u32[]{:S(2)}, u32[]{:S(2)}) collective-permute-start(f32[2,512,256]{2,1,0:T(8,128)S(1)} %collective-permute-done.17.a_ref), channel_id=1, source_target_pairs={{0,1},{1,0},{2,3},{3,2},{4,5},{5,4},{6,7},{7,6},{8,9},{9,8},{10,11... | collective-permute-start | bytes 3145736 | tf_op jit(solution)/shard_map/ppermute | solution.py:84
  98.9 18.2 %collective-permute-start.29 = (f32[2,512,256]{2,1,0:T(8,128)S(1)}, f32[2,512,256]{2,1,0:T(8,128)S(1)}, u32[]{:S(2)}, u32[]{:S(2)}) collective-permute-start(f32[2,512,256]{2,1,0:T(8,128)S(1)} %collective-permute-done.28.a_ref), channel_id=1, source_target_pairs={{0,1},{1,0},{2,3},{3,2},{4,5},{5,4},{6,7},{7,6},{8,9},{9,8},{10,11... | collective-permute-start | bytes 3145736 | tf_op jit(solution)/shard_map/ppermute | solution.py:84
  108.7 56.1 %collective-permute-start.15 = (f32[512,512]{1,0:T(8,128)S(1)}, f32[512,512]{1,0:T(8,128)}, u32[]{:S(2)}, u32[]{:S(2)}) collective-permute-start(f32[512,512]{1,0:T(8,128)S(1)} %get-tuple-element.52.near_ref), channel_id=1, source_target_pairs={{1,3},{5,7},{8,10},{12,14},{19,17},{23,21},{26,24},{30,28}} | collective-permute-start | bytes 3145736 | tf_op jit(solution)/shard_map/ppermute | solution.py:84
  113.2 27.5 %collective-permute-start.23 = (f32[2,128,512]{2,1,0:T(8,128)S(1)}, f32[2,128,512]{2,1,0:T(8,128)S(1)}, u32[]{:S(2)}, u32[]{:S(2)}) collective-permute-start(f32[2,128,512]{2,1,0:T(8,128)S(1)} %get-tuple-element.59), channel_id=1, source_target_pairs={{0,4},{1,5},{2,6},{3,7},{4,0},{5,1},{6,2},{7,3},{8,12},{9,13},{10,... | collective-permute-start | bytes 1572872 | tf_op jit(solution)/shard_map/ppermute | solution.py:84
  116.6 35.3 %collective-permute-start.32 = (f32[2,128,512]{2,1,0:T(8,128)S(1)}, f32[2,128,512]{2,1,0:T(8,128)S(1)}, u32[]{:S(2)}, u32[]{:S(2)}) collective-permute-start(f32[2,128,512]{2,1,0:T(8,128)S(1)} %get-tuple-element.63), channel_id=1, source_target_pairs={{0,4},{1,5},{2,6},{3,7},{4,0},{5,1},{6,2},{7,3},{8,12},{9,13},{10,... | collective-permute-start | bytes 1572872 | tf_op jit(solution)/shard_map/ppermute | solution.py:84
  117.1 45.9 %collective-permute-start.36 = (f32[2,128,512]{2,1,0:T(8,128)S(1)}, f32[2,128,512]{2,1,0:T(8,128)S(1)}, u32[]{:S(2)}, u32[]{:S(2)}) collective-permute-start(f32[2,128,512]{2,1,0:T(8,128)S(1)} %get-tuple-element.67), channel_id=1, source_target_pairs={{0,4},{1,5},{2,6},{3,7},{4,0},{5,1},{6,2},{7,3},{8,12},{9,13},{10,... | collective-permute-start | bytes 1572872 | tf_op jit(solution)/shard_map/ppermute | solution.py:84
  124.0 54.8 %collective-permute-start.22 = (f32[128,512]{1,0:T(8,128)S(1)}, f32[128,512]{1,0:T(8,128)S(1)}, u32[]{:S(2)}, u32[]{:S(2)}) collective-permute-start(f32[128,512]{1,0:T(8,128)S(1)} %get-tuple-element.57), channel_id=1, source_target_pairs={{0,8},{1,9},{2,10},{3,11},{4,12},{5,13},{6,14},{7,15},{8,0},{9,1},... | collective-permute-start | bytes 786440 | tf_op jit(solution)/shard_map/ppermute | solution.py:84
  141.3 38.2 %collective-permute-start.24 = (f32[128,512]{1,0:T(8,128)S(1)}, f32[128,512]{1,0:T(8,128)S(1)}, u32[]{:S(2)}, u32[]{:S(2)}) collective-permute-start(f32[128,512]{1,0:T(8,128)S(1)} %get-tuple-element.61), channel_id=1, source_target_pairs={{0,8},{1,9},{2,10},{3,11},{4,12},{5,13},{6,14},{7,15},{8,0},{9,1},... | collective-permute-start | bytes 786440 | tf_op jit(solution)/shard_map/ppermute | solution.py:84
  152.4 30.2 %collective-permute-start.33 = (f32[128,512]{1,0:T(8,128)S(1)}, f32[128,512]{1,0:T(8,128)S(1)}, u32[]{:S(2)}, u32[]{:S(2)}) collective-permute-start(f32[128,512]{1,0:T(8,128)S(1)} %get-tuple-element.65), channel_id=1, source_target_pairs={{0,8},{1,9},{2,10},{3,11},{4,12},{5,13},{6,14},{7,15},{8,0},{9,1},... | collective-permute-start | bytes 786440 | tf_op jit(solution)/shard_map/ppermute | solution.py:84
  163.1 90.6 %collective-permute-start.14 = (f32[512,512]{1,0:T(8,128)S(1)}, f32[512,512]{1,0:T(8,128)}, u32[]{:S(2)}, u32[]{:S(2)}) collective-permute-start(f32[512,512]{1,0:T(8,128)S(1)} %get-tuple-element.52.near_ref), channel_id=1, source_target_pairs={{0,4},{4,0},{9,13},{13,9},{18,22},{22,18},{27,31},{31,27}} | collective-permute-start | bytes 3145736 | tf_op jit(solution)/shard_map/ppermute | solution.py:84
  164.8 88.9 %collective-permute-start.16 = (f32[512,512]{1,0:T(8,128)}, f32[512,512]{1,0:T(8,128)}, u32[]{:S(2)}, u32[]{:S(2)}) collective-permute-start(f32[512,512]{1,0:T(8,128)} %collective-permute-done.15), channel_id=1, source_target_pairs={{3,8},{7,12},{10,5},{14,1},{17,26},{21,30},{24,23},{28,19}} | collective-permute-start | bytes 3145736 | tf_op jit(solution)/shard_map/ppermute | solution.py:84
  178.8 19.7 %collective-permute-start.37 = (f32[128,512]{1,0:T(8,128)S(1)}, f32[128,512]{1,0:T(8,128)S(1)}, u32[]{:S(2)}, u32[]{:S(2)}) collective-permute-start(f32[128,512]{1,0:T(8,128)S(1)} %get-tuple-element.69), channel_id=1, source_target_pairs={{0,8},{1,9},{2,10},{3,11},{4,12},{5,13},{6,14},{7,15},{8,0},{9,1},... | collective-permute-start | bytes 786440 | tf_op jit(solution)/shard_map/ppermute | solution.py:84
  179.5 23.8 %collective-permute-start.25 = (f32[128,512]{1,0:T(8,128)S(1)}, f32[128,512]{1,0:T(8,128)S(1)}, u32[]{:S(2)}, u32[]{:S(2)}) collective-permute-start(f32[128,512]{1,0:T(8,128)S(1)} %shard_map.79.refs_0_), channel_id=1, source_target_pairs={{0,16},{1,17},{2,18},{3,19},{4,20},{5,21},{6,22},{7,23},{8,24},{9,... | collective-permute-start | bytes 786440 | tf_op jit(solution)/shard_map/ppermute | solution.py:84
  182.6 23.5 %collective-permute-start.26 = (f32[128,512]{1,0:T(8,128)S(1)}, f32[128,512]{1,0:T(8,128)S(1)}, u32[]{:S(2)}, u32[]{:S(2)}) collective-permute-start(f32[128,512]{1,0:T(8,128)S(1)} %shard_map.81.refs_1_), channel_id=1, source_target_pairs={{0,16},{1,17},{2,18},{3,19},{4,20},{5,21},{6,22},{7,23},{8,24},{9,... | collective-permute-start | bytes 786440 | tf_op jit(solution)/shard_map/ppermute | solution.py:84
  198.5 20.5 %collective-permute-start.34 = (f32[128,512]{1,0:T(8,128)S(1)}, f32[128,512]{1,0:T(8,128)S(1)}, u32[]{:S(2)}, u32[]{:S(2)}) collective-permute-start(f32[128,512]{1,0:T(8,128)S(1)} %shard_map.88.refs_0_), channel_id=1, source_target_pairs={{0,16},{1,17},{2,18},{3,19},{4,20},{5,21},{6,22},{7,23},{8,24},{9,... | collective-permute-start | bytes 786440 | tf_op jit(solution)/shard_map/ppermute | solution.py:84
  203.2 21.4 %collective-permute-start.38 = (f32[128,512]{1,0:T(8,128)S(1)}, f32[128,512]{1,0:T(8,128)S(1)}, u32[]{:S(2)}, u32[]{:S(2)}) collective-permute-start(f32[128,512]{1,0:T(8,128)S(1)} %shard_map.91.refs_0_), channel_id=1, source_target_pairs={{0,16},{1,17},{2,18},{3,19},{4,20},{5,21},{6,22},{7,23},{8,24},{9,... | collective-permute-start | bytes 786440 | tf_op jit(solution)/shard_map/ppermute | solution.py:84
  207.5 46.2 %collective-permute-start.27 = (f32[256,512]{1,0:T(8,128)}, f32[256,512]{1,0:T(8,128)}, u32[]{:S(2)}, u32[]{:S(2)}) collective-permute-start(f32[256,512]{1,0:T(8,128)} %shard_map.82.far_ref), channel_id=1, source_target_pairs={{0,6},{1,10},{4,2},{5,14},{8,3},{9,15},{12,7},{13,11},{18,16},{19,... | collective-permute-start | bytes 1572872 | tf_op jit(solution)/shard_map/ppermute | solution.py:84
  220.3 29.8 %collective-permute-start.35 = (f32[128,512]{1,0:T(8,128)}, f32[128,512]{1,0:T(8,128)}, u32[]{:S(2)}, u32[]{:S(2)}) collective-permute-start(f32[128,512]{1,0:T(8,128)} %shard_map.89.refs_0_), channel_id=1, source_target_pairs={{0,6},{1,10},{4,2},{5,14},{8,3},{9,15},{12,7},{13,11},{18,16},{19,... | collective-permute-start | bytes 786440 | tf_op jit(solution)/shard_map/ppermute | solution.py:84
  225.9 27.8 %collective-permute-start.39 = (f32[128,512]{1,0:T(8,128)}, f32[128,512]{1,0:T(8,128)}, u32[]{:S(2)}, u32[]{:S(2)}) collective-permute-start(f32[128,512]{1,0:T(8,128)} %shard_map.92.refs_1_), channel_id=1, source_target_pairs={{0,6},{1,10},{4,2},{5,14},{8,3},{9,15},{12,7},{13,11},{18,16},{19,... | collective-permute-start | bytes 786440 | tf_op jit(solution)/shard_map/ppermute | solution.py:84
  (14 other events, 199.4 us)

commit v10 on v9

--- a/solution.py
+++ b/solution.py
@@ -123,18 +123,14 @@
 
 
 X_PLACE, ODD, TURN_1, TURN_2, TURN_3, NEAR, MIDDLE, PLACE = range(8)
-VMEM = 40 * 2**20
-
-
-def params():
-    return pltpu.CompilerParams(vmem_limit_bytes=VMEM)
+SMALL, MEDIUM, LARGE, WHOLE = 8 * 2**20, 24 * 2**20, 40 * 2**20, 60 * 2**20
 
 
 def zeros(count):
     return (0,) * count
 
 
-def call(kernel, shapes, meta, args, in_specs=None, out_specs=None, scratch=(), aliases=None):
+def call(kernel, shapes, meta, args, in_specs=None, out_specs=None, scratch=(), aliases=None, vmem=LARGE):
     if in_specs is None:
         in_specs = [None] * len(args)
     if out_specs is None:
@@ -151,7 +147,7 @@
             scratch_shapes=list(scratch),
         ),
         input_output_aliases=aliases or {},
-        compiler_params=params(),
+        compiler_params=pltpu.CompilerParams(vmem_limit_bytes=vmem),
     )(meta, *args)
 
 
@@ -214,6 +210,7 @@
         [t, v],
         in_specs=[hbm, hbm],
         scratch=[pltpu.SemaphoreType.DMA((2,))],
+        vmem=LARGE if first or not side else WHOLE,
     )[0]
 
 
@@ -268,48 +265,50 @@
     )[0]
 
 
-def next_part(meta, base, at, av, own, side, k):
+def next_part(meta, base, piece, own, side):
     n = own.shape[1]
     w = n // CHUNKS
-    block = pl.BlockSpec((n, w), lambda i, m: (0, (m[X_PLACE] ^ side) * CHUNKS + k))
     return call(
         functools.partial(next_kernel, side),
         [shaped(*base.shape)],
         meta,
-        [base, at, av, own],
-        in_specs=[pl.BlockSpec(memory_space=pl.ANY), block, block, None],
+        [base, piece, own],
+        in_specs=[
+            pl.BlockSpec(memory_space=pl.ANY),
+            pl.BlockSpec((2, n, w), lambda i, m: (0, 0, 0)),
+            None,
+        ],
         out_specs=[pl.BlockSpec((1, *base.shape[1:]), lambda i, m: (1, 0, 0))],
         aliases={1: 0},
     )[0]
 
 
-def next_kernel(side, m, _, at_ref, av_ref, own_ref, out_ref):
+def next_kernel(side, m, _, piece_ref, own_ref, out_ref):
     n = own_ref.shape[1]
-    w = at_ref.shape[1]
     right = own_right(own_ref, placed(m[TURN_1] ^ side, n))
-    out_ref[0, :w, :] = crossed(left_of(at_ref[...], av_ref[...]), right)
-
-
-def near_parts(meta, at, av, own, side, chunks):
+    out_ref[0] = crossed(left_of(piece_ref[0], piece_ref[1]), right)
+
+
+def near_parts(meta, pieces, own, side, chunks):
     n = own.shape[1]
     w = n // CHUNKS
-    half = pl.BlockSpec((n, n), lambda i, m: (0, m[X_PLACE] ^ side))
     return call(
         functools.partial(near_kernel, side, chunks),
         [shaped(2, lines(k, w), n) for k in chunks],
         meta,
-        [at, av, own],
-        in_specs=[half, half, None],
-    )
-
-
-def near_kernel(side, chunks, m, at_ref, av_ref, own_ref, *outs):
+        [*pieces, own],
+    )
+
+
+def near_kernel(side, chunks, m, *refs):
+    pieces, own_ref, outs = refs[: -1 - len(chunks)], refs[-1 - len(chunks)], refs[-len(chunks) :]
     n = own_ref.shape[1]
     w = n // CHUNKS
     middle_block(m, side, chunks, own_ref, outs)
-    cols = slice(chunks[0] * w, (chunks[-1] + 1) * w)
-    right = own_right(own_ref, placed(m[TURN_1] ^ side, n))
-    block = crossed(left_of(at_ref[:, cols], av_ref[:, cols]), right)
+    left = jnp.concatenate([left_of(ref[0], ref[1]) for ref in pieces], axis=0)
+    first = chunks[0] * w
+    left = left[first : first + len(chunks) * w]
+    block = crossed(left, own_right(own_ref, placed(m[TURN_1] ^ side, n)))
     for i, out_ref in enumerate(outs):
         out_ref[1, :w, :] = block[i * w : (i + 1) * w]
         if out_ref.shape[1] > w:
@@ -352,6 +351,7 @@
         meta,
         [keep, come, keep, come],
         in_specs=[leave, leave, stay, stay],
+        vmem=SMALL,
     )
 
 
@@ -360,7 +360,7 @@
 
 
 def add(meta, a, b):
-    return call(add_kernel, [shaped(*a.shape)], meta, [a, b])[0]
+    return call(add_kernel, [shaped(*a.shape)], meta, [a, b], vmem=SMALL)[0]
 
 
 def join_kernel(w, count, _, *refs):
@@ -378,7 +378,7 @@
     shapes = [shaped(len(parts) * w, n)]
     if parts[-1].shape[0] > w:
         shapes.append(shaped(PAD, n))
-    return call(functools.partial(join_kernel, w, len(parts)), shapes, meta, [*parts, *comes])
+    return call(functools.partial(join_kernel, w, len(parts)), shapes, meta, [*parts, *comes], vmem=MEDIUM)
 
 
 def closing(t, v, row, col, value):
@@ -430,6 +430,7 @@
         [near_own, far_own, t, *args],
         in_specs=[None, None, *ins],
         out_specs=outs,
+        vmem=MEDIUM,
     )
 
 
@@ -544,19 +545,19 @@
     to_near = lambda block: routed(block, lambda r, c: None if is_near(r, c) else (r ^ 4, c))
     over = lambda target: lambda block: routed(block, target)
 
-    next_t = beside(t)
-    next_v = beside(v)
     own = prep(meta, t, v)
-    send, keep = {}, {}
+    send, keep, pieces, nexts = {}, {}, {}, {}
+    for tag, side, first, count in FAR_GROUPS:
+        pieces[tag] = pick(meta, t, v, side, first, count)
+        nexts[tag] = beside(pieces[tag])
     base = middle_part(meta, own, 1, 0)
-    send["n", 0] = next_part(meta, base, next_t, next_v, own, 1, 0)
-    for side, chunks in NEAR_GROUPS:
-        blocks = near_parts(meta, next_t, next_v, own, side, chunks)
+    send["n", 0] = next_part(meta, base, nexts["s0"], own, 1)
+    for side, tags, chunks in NEAR_GROUPS:
+        blocks = near_parts(meta, [nexts[tag] for tag in tags], own, side, chunks)
         for k, block in zip(chunks, blocks):
             (send if side else keep)["n", k] = block
     for tag, side, first, count in FAR_GROUPS:
-        piece = pick(meta, t, v, side, first, count)
-        piece = across(piece)
+        piece = across(pieces[tag])
         other = beside(piece)
         blocks = far_parts(meta, piece, other, own, side)
         for i, block in enumerate(blocks):
@@ -589,7 +590,7 @@
     return back_half(meta, values, *pair, *fixed)
 
 
-NEAR_GROUPS = ((1, (1, 2, 3)), (0, (0,)), (0, (1, 2, 3)))
+NEAR_GROUPS = ((1, ("s0", "s1"), (1, 2, 3)), (0, ("k0",), (0,)), (0, ("k0", "k1"), (1, 2, 3)))
 FAR_GROUPS = (("s0", 1, 0, 2), ("k0", 0, 0, 2), ("s1", 1, 2, 2), ("k1", 0, 2, 2))
 
 

time: 259 us -> 261 us (level)
  the two profiles are of different devices: /device:TPU:7 before, /device:TPU:5 now
where the time goes in v10:
time: 261 us
  waiting for transfers between devices  112 us (43%)
  starting transfers between devices  87.7 us (34%)
  Pallas kernels  56.1 us (21%)
  local copies, waits for them, and re-layouts  3.45 us (1%)
    ppermute x42, waiting for transfers between devices, routed(): return lax.ppermute(block, ('row', 'col'), route)  112 us
    ppermute x42, starting transfers between devices, routed(): return lax.ppermute(block, ('row', 'col'), route)  87.7 us
    pallas_call x37, Pallas kernels, call(): pl.pallas_call(kernel, out_shape=list(shapes), grid_spec=pltpu.PrefetchSc...  56.1 us
  transfers between devices with their start and end apart: 42, of which 16 were waited for; matrix products, arithmetic and copies ran while one was open for 0% of the time, Pallas kernels for 19%

profile of v10, /device:TPU:5, one launch (start us, length us, event | category | flops | bytes accessed | tf_op | source)
XLA Modules:
  0.0 260.7 jit_solution(13644476259089705849)
XLA Ops:
  1.2 3.0 %shard_map.63 = f32[2,512,256]{2,1,0:T(8,128)} custom-call(s32[8]{0:T(128)} %compare_select_fusion.7.m._, f32[512,1024]{1,0:T(8,128)} %refs_3_.1, f32[512,1024]{1,0:T(8,128)} %refs_4_.3), custom_call_target="tpu_custom_call" | custom-call | tf_op jit(solution)/shard_map/pallas_call | solution.py:139
  16.2 5.5 %shard_map.70 = (f32[2,128,512]{2,1,0:T(8,128)S(1)}, f32[2,128,512]{2,1,0:T(8,128)S(1)}, f32[2,136,512]{2,1,0:T(8,128)S(1)}) custom-call(s32[8]{0:T(128)S(1)} %copy-done.4, f32[2,512,256]{2,1,0:T(8,128)S(1)} %collective-permute-done.1.piece_ref.refs_0_, f32[2,512,256]{2,1,0:T(8,128)S(1)} %collective-permute-done.5.refs_1_, ...), custom_call_target="tpu_custom_call" | custom-call | tf_op jit(solution)/shard_map/pallas_call | solution.py:139
  23.3 10.5 %collective-permute-done.19.a_ref = f32[2,512,256]{2,1,0:T(8,128)S(1)} collective-permute-done((f32[2,512,256]{2,1,0:T(8,128)S(1)}, f32[2,512,256]{2,1,0:T(8,128)S(1)}, u32[]{:S(2)}, u32[]{:S(2)}) %collective-permute-start.19) | collective-permute-done | bytes 1048608 | tf_op jit(solution)/shard_map/ppermute | solution.py:84
  34.1 22.2 %collective-permute-done.21.a_ref = f32[2,512,256]{2,1,0:T(8,128)S(1)} collective-permute-done((f32[2,512,256]{2,1,0:T(8,128)S(1)}, f32[2,512,256]{2,1,0:T(8,128)S(1)}, u32[]{:S(2)}, u32[]{:S(2)}) %collective-permute-start.21) | collective-permute-done | bytes 1048608 | tf_op jit(solution)/shard_map/ppermute | solution.py:84
  57.7 2.0 shard_map.61.keep_pass.keep_stay
  61.7 5.7 %shard_map.68 = (f32[2,128,512]{2,1,0:T(8,128)S(1)}, f32[2,128,512]{2,1,0:T(8,128)S(1)}, f32[2,136,512]{2,1,0:T(8,128)S(1)}) custom-call(s32[8]{0:T(128)S(1)} %copy-done.4, f32[2,512,256]{2,1,0:T(8,128)S(1)} %collective-permute-done.refs_0_, f32[2,512,256]{2,1,0:T(8,128)S(1)} %collective-permute-done.4.refs_1_, ...), custom_call_target="tpu_custom_call" | custom-call | tf_op jit(solution)/shard_map/pallas_call | solution.py:139
  73.7 4.2 %collective-permute-start.12 = (f32[128,512]{1,0:T(8,128)S(1)}, f32[128,512]{1,0:T(8,128)S(1)}, u32[]{:S(2)}, u32[]{:S(2)}) collective-permute-start(f32[128,512]{1,0:T(8,128)S(1)} %shard_map.66.refs_0_), channel_id=1, source_target_pairs={{2,18},{3,19},{6,22},{7,23},{10,26},{11,27},{14,30},{15,31},{16,0}... | collective-permute-start | bytes 786440 | tf_op jit(solution)/shard_map/ppermute | solution.py:84
  78.7 4.1 %collective-permute-start.13 = (f32[128,512]{1,0:T(8,128)S(1)}, f32[128,512]{1,0:T(8,128)S(1)}, u32[]{:S(2)}, u32[]{:S(2)}) collective-permute-start(f32[128,512]{1,0:T(8,128)S(1)} %shard_map.72.refs_1_), channel_id=1, source_target_pairs={{2,18},{3,19},{6,22},{7,23},{10,26},{11,27},{14,30},{15,31},{16,0}... | collective-permute-start | bytes 786440 | tf_op jit(solution)/shard_map/ppermute | solution.py:84
  84.7 16.5 %collective-permute-done.32.a_ref = f32[2,512,256]{2,1,0:T(8,128)S(1)} collective-permute-done((f32[2,512,256]{2,1,0:T(8,128)S(1)}, f32[2,512,256]{2,1,0:T(8,128)S(1)}, u32[]{:S(2)}, u32[]{:S(2)}) %collective-permute-start.32) | collective-permute-done | bytes 1048608 | tf_op jit(solution)/shard_map/ppermute | solution.py:84
  103.7 4.2 %collective-permute-start.15 = (f32[136,512]{1,0:T(8,128)S(1)}, f32[136,512]{1,0:T(8,128)S(1)}, u32[]{:S(2)}, u32[]{:S(2)}) collective-permute-start(f32[136,512]{1,0:T(8,128)S(1)} %shard_map.76.refs_3_), channel_id=1, source_target_pairs={{2,18},{3,19},{6,22},{7,23},{10,26},{11,27},{14,30},{15,31},{16,0}... | collective-permute-start | bytes 835592 | tf_op jit(solution)/shard_map/ppermute | solution.py:84
  107.9 5.1 %collective-permute-done.15.refs_7_ = f32[136,512]{1,0:T(8,128)S(1)} collective-permute-done((f32[136,512]{1,0:T(8,128)S(1)}, f32[136,512]{1,0:T(8,128)S(1)}, u32[]{:S(2)}, u32[]{:S(2)}) %collective-permute-start.15) | collective-permute-done | bytes 278560 | tf_op jit(solution)/shard_map/ppermute | solution.py:84
  115.0 2.4 shard_map.79
  118.9 2.4 shard_map.86
  122.9 2.4 shard_map.78
  125.3 2.4 shard_map.85
  131.1 8.9 %collective-permute-done.25.come_pass.come_stay = f32[2,128,512]{2,1,0:T(8,128)S(1)} collective-permute-done((f32[2,128,512]{2,1,0:T(8,128)S(1)}, f32[2,128,512]{2,1,0:T(8,128)S(1)}, u32[]{:S(2)}, u32[]{:S(2)}) %collective-permute-start.25) | collective-permute-done | bytes 524320 | tf_op jit(solution)/shard_map/ppermute | solution.py:84
  140.0 14.3 %collective-permute-start.24 = (f32[128,512]{1,0:T(8,128)S(1)}, f32[128,512]{1,0:T(8,128)S(1)}, u32[]{:S(2)}, u32[]{:S(2)}) collective-permute-start(f32[128,512]{1,0:T(8,128)S(1)} %get-tuple-element.57), channel_id=1, source_target_pairs={{0,8},{1,9},{2,10},{3,11},{4,12},{5,13},{6,14},{7,15},{8,0},{9,1},... | collective-permute-start | bytes 786440 | tf_op jit(solution)/shard_map/ppermute | solution.py:84
  155.0 10.6 %collective-permute-start.26 = (f32[128,512]{1,0:T(8,128)S(1)}, f32[128,512]{1,0:T(8,128)S(1)}, u32[]{:S(2)}, u32[]{:S(2)}) collective-permute-start(f32[128,512]{1,0:T(8,128)S(1)} %get-tuple-element.61), channel_id=1, source_target_pairs={{0,8},{1,9},{2,10},{3,11},{4,12},{5,13},{6,14},{7,15},{8,0},{9,1},... | collective-permute-start | bytes 786440 | tf_op jit(solution)/shard_map/ppermute | solution.py:84
  166.2 10.6 %collective-permute-start.35 = (f32[128,512]{1,0:T(8,128)S(1)}, f32[128,512]{1,0:T(8,128)S(1)}, u32[]{:S(2)}, u32[]{:S(2)}) collective-permute-start(f32[128,512]{1,0:T(8,128)S(1)} %get-tuple-element.65), channel_id=1, source_target_pairs={{0,8},{1,9},{2,10},{3,11},{4,12},{5,13},{6,14},{7,15},{8,0},{9,1},... | collective-permute-start | bytes 786440 | tf_op jit(solution)/shard_map/ppermute | solution.py:84
  176.8 10.0 %collective-permute-start.18 = (f32[512,512]{1,0:T(8,128)}, f32[512,512]{1,0:T(8,128)}, u32[]{:S(2)}, u32[]{:S(2)}) collective-permute-start(f32[512,512]{1,0:T(8,128)} %collective-permute-done.17), channel_id=1, source_target_pairs={{3,8},{7,12},{10,5},{14,1},{17,26},{21,30},{24,23},{28,19}} | collective-permute-start | bytes 3145736 | tf_op jit(solution)/shard_map/ppermute | solution.py:84
  188.8 2.4 collective-permute-start.28
  191.8 17.5 %collective-permute-done.39.b_ref = f32[128,512]{1,0:T(8,128)S(1)} collective-permute-done((f32[128,512]{1,0:T(8,128)S(1)}, f32[128,512]{1,0:T(8,128)S(1)}, u32[]{:S(2)}, u32[]{:S(2)}) %collective-permute-start.39) | collective-permute-done | bytes 262176 | tf_op jit(solution)/shard_map/ppermute | solution.py:84
  209.9 3.8 %collective-permute-done.27.refs_2_ = f32[128,512]{1,0:T(8,128)S(1)} collective-permute-done((f32[128,512]{1,0:T(8,128)S(1)}, f32[128,512]{1,0:T(8,128)S(1)}, u32[]{:S(2)}, u32[]{:S(2)}) %collective-permute-start.27) | collective-permute-done | bytes 262176 | tf_op jit(solution)/shard_map/ppermute | solution.py:84
  213.7 2.9 %collective-permute-start.40 = (f32[128,512]{1,0:T(8,128)S(1)}, f32[128,512]{1,0:T(8,128)S(1)}, u32[]{:S(2)}, u32[]{:S(2)}) collective-permute-start(f32[128,512]{1,0:T(8,128)S(1)} %shard_map.91.refs_0_), channel_id=1, source_target_pairs={{0,16},{1,17},{2,18},{3,19},{4,20},{5,21},{6,22},{7,23},{8,24},{9,... | collective-permute-start | bytes 786440 | tf_op jit(solution)/shard_map/ppermute | solution.py:84
  216.5 8.5 %collective-permute-done.28.refs_3_ = f32[128,512]{1,0:T(8,128)S(1)} collective-permute-done((f32[128,512]{1,0:T(8,128)S(1)}, f32[128,512]{1,0:T(8,128)S(1)}, u32[]{:S(2)}, u32[]{:S(2)}) %collective-permute-start.28) | collective-permute-done | bytes 262176 | tf_op jit(solution)/shard_map/ppermute | solution.py:84
  227.8 2.9 %collective-permute-done.36.refs_1_ = f32[128,512]{1,0:T(8,128)S(1)} collective-permute-done((f32[128,512]{1,0:T(8,128)S(1)}, f32[128,512]{1,0:T(8,128)S(1)}, u32[]{:S(2)}, u32[]{:S(2)}) %collective-permute-start.36) | collective-permute-done | bytes 262176 | tf_op jit(solution)/shard_map/ppermute | solution.py:84
  233.3 3.2 %collective-permute-done.40.refs_1_ = f32[128,512]{1,0:T(8,128)S(1)} collective-permute-done((f32[128,512]{1,0:T(8,128)S(1)}, f32[128,512]{1,0:T(8,128)S(1)}, u32[]{:S(2)}, u32[]{:S(2)}) %collective-permute-start.40) | collective-permute-done | bytes 262176 | tf_op jit(solution)/shard_map/ppermute | solution.py:84
  240.9 3.2 %shard_map.93 = (f32[512,1024]{1,0:T(8,128)}, f32[512,1024]{1,0:T(8,128)}) custom-call(s32[8]{0:T(128)S(1)} %copy-done.4, f32[512,512]{1,0:T(8,128)S(1)} %get-tuple-element.52.near_ref, f32[256,512]{1,0:T(8,128)} %shard_map.84.far_ref, f32[512,1024]{1,0:T(8,128)S(1)} %copy-done, f32[512,1024]{1,0:T(8,128)S(1)} %copy-done.2, ...), custom_call_target="tpu_custom_call" | custom-call | tf_op jit(solution)/shard_map/pallas_call | solution.py:139
  244.1 2.7 %shard_map.94 = (f32[512,1024]{1,0:T(8,128)}, f32[512,1024]{1,0:T(8,128)}) custom-call(s32[8]{0:T(128)S(1)} %copy-done.4, f32[128,512]{1,0:T(8,128)} %shard_map.89.refs_0_, f32[128,512]{1,0:T(8,128)} %shard_map.92.refs_1_, f32[512,1024]{1,0:T(8,128)} %get-tuple-element.70.refs_2_, ...), custom_call_target="tpu_custom_call", output_to_operand_aliasing={{0}: (3, {}), {1}: (4, {})} | custom-call | tf_op jit(solution)/shard_map/pallas_call | solution.py:139
  246.9 6.6 %collective-permute-done.37.refs_1_ = f32[128,512]{1,0:T(8,128)} collective-permute-done((f32[128,512]{1,0:T(8,128)}, f32[128,512]{1,0:T(8,128)}, u32[]{:S(2)}, u32[]{:S(2)}) %collective-permute-start.37) | collective-permute-done | bytes 262176 | tf_op jit(solution)/shard_map/ppermute | solution.py:84
  253.4 2.8 %collective-permute-done.41.refs_2_ = f32[128,512]{1,0:T(8,128)} collective-permute-done((f32[128,512]{1,0:T(8,128)}, f32[128,512]{1,0:T(8,128)}, u32[]{:S(2)}, u32[]{:S(2)}) %collective-permute-start.41) | collective-permute-done | bytes 262176 | tf_op jit(solution)/shard_map/ppermute | solution.py:84
  256.3 4.4 %shard_map.95 = (f32[512,1024]{1,0:T(8,128)}, f32[512,1024]{1,0:T(8,128)}) custom-call(s32[8]{0:T(128)S(1)} %copy-done.4, f32[512,512]{1,0:T(8,128)S(1)} %get-tuple-element.52.near_ref, f32[512,512]{1,0:T(8,128)} %collective-permute-done.16.swap_ref, f32[512,512]{1,0:T(8,128)} %collective-permute-done.18.back_ref, ...), custom_call_target="tpu_custom_call", output_to_operand_aliasing={{0}: (12, {}), {1}: (13, {})} | custom-call | tf_op jit(solution)/shard_map/pallas_call | solution.py:139
  (111 shorter events, 51.4 us)
Async XLA Ops:
  9.5 24.3 %collective-permute-start.19 = (f32[2,512,256]{2,1,0:T(8,128)S(1)}, f32[2,512,256]{2,1,0:T(8,128)S(1)}, u32[]{:S(2)}, u32[]{:S(2)}) collective-permute-start(f32[2,512,256]{2,1,0:T(8,128)S(1)} %shard_map.59), channel_id=1, source_target_pairs={{0,2},{1,3},{2,0},{3,1},{4,6},{5,7},{6,4},{7,5},{8,10},{9,11},{10,... | collective-permute-start | bytes 3145736 | tf_op jit(solution)/shard_map/ppermute | solution.py:84
  9.6 46.7 %collective-permute-start.21 = (f32[2,512,256]{2,1,0:T(8,128)S(1)}, f32[2,512,256]{2,1,0:T(8,128)S(1)}, u32[]{:S(2)}, u32[]{:S(2)}) collective-permute-start(f32[2,512,256]{2,1,0:T(8,128)S(1)} %copy-done.5), channel_id=1, source_target_pairs={{0,2},{1,3},{2,0},{3,1},{4,6},{5,7},{6,4},{7,5},{8,10},{9,11},{10,... | collective-permute-start | bytes 3145736 | tf_op jit(solution)/shard_map/ppermute | solution.py:84
  14.9 41.6 %collective-permute-start.2 = (f32[2,128,512]{2,1,0:T(8,128)S(1)}, f32[2,128,512]{2,1,0:T(8,128)S(1)}, u32[]{:S(2)}, u32[]{:S(2)}) collective-permute-start(f32[2,128,512]{2,1,0:T(8,128)S(1)} %shard_map.64), channel_id=1, source_target_pairs={{0,4},{1,5},{2,6},{3,7},{4,0},{5,1},{6,2},{7,3},{8,12},{9,13},{10,... | collective-permute-start | bytes 1572872 | tf_op jit(solution)/shard_map/ppermute | solution.py:84
  21.8 47.7 %collective-permute-start.10 = (f32[2,136,512]{2,1,0:T(8,128)S(1)}, f32[2,136,512]{2,1,0:T(8,128)S(1)}, u32[]{:S(2)}, u32[]{:S(2)}) collective-permute-start(f32[2,136,512]{2,1,0:T(8,128)S(1)} %get-tuple-element.49), channel_id=1, source_target_pairs={{0,4},{1,5},{2,6},{3,7},{4,0},{5,1},{6,2},{7,3},{8,12},{9,13},{10,... | collective-permute-start | bytes 1671176 | tf_op jit(solution)/shard_map/ppermute | solution.py:84
  22.1 38.3 %collective-permute-start.6 = (f32[2,128,512]{2,1,0:T(8,128)S(1)}, f32[2,128,512]{2,1,0:T(8,128)S(1)}, u32[]{:S(2)}, u32[]{:S(2)}) collective-permute-start(f32[2,128,512]{2,1,0:T(8,128)S(1)} %get-tuple-element.41), channel_id=1, source_target_pairs={{0,4},{1,5},{2,6},{3,7},{4,0},{5,1},{6,2},{7,3},{8,12},{9,13},{10,... | collective-permute-start | bytes 1572872 | tf_op jit(solution)/shard_map/ppermute | solution.py:84
  33.8 49.6 %collective-permute-start.30 = (f32[2,512,256]{2,1,0:T(8,128)S(1)}, f32[2,512,256]{2,1,0:T(8,128)S(1)}, u32[]{:S(2)}, u32[]{:S(2)}) collective-permute-start(f32[2,512,256]{2,1,0:T(8,128)S(1)} %shard_map.67), channel_id=1, source_target_pairs={{0,2},{1,3},{2,0},{3,1},{4,6},{5,7},{6,4},{7,5},{8,10},{9,11},{10,... | collective-permute-start | bytes 3145736 | tf_op jit(solution)/shard_map/ppermute | solution.py:84
  56.3 44.9 %collective-permute-start.32 = (f32[2,512,256]{2,1,0:T(8,128)S(1)}, f32[2,512,256]{2,1,0:T(8,128)S(1)}, u32[]{:S(2)}, u32[]{:S(2)}) collective-permute-start(f32[2,512,256]{2,1,0:T(8,128)S(1)} %shard_map.69), channel_id=1, source_target_pairs={{0,2},{1,3},{2,0},{3,1},{4,6},{5,7},{6,4},{7,5},{8,10},{9,11},{10,... | collective-permute-start | bytes 3145736 | tf_op jit(solution)/shard_map/ppermute | solution.py:84
  71.0 31.6 %collective-permute-start.11 = (f32[136,512]{1,0:T(8,128)S(1)}, f32[136,512]{1,0:T(8,128)S(1)}, u32[]{:S(2)}, u32[]{:S(2)}) collective-permute-start(f32[136,512]{1,0:T(8,128)S(1)} %get-tuple-element.51), channel_id=1, source_target_pairs={{0,8},{1,9},{2,10},{3,11},{4,12},{5,13},{6,14},{7,15},{8,0},{9,1},... | collective-permute-start | bytes 835592 | tf_op jit(solution)/shard_map/ppermute | solution.py:84
  73.7 28.8 %collective-permute-start.12 = (f32[128,512]{1,0:T(8,128)S(1)}, f32[128,512]{1,0:T(8,128)S(1)}, u32[]{:S(2)}, u32[]{:S(2)}) collective-permute-start(f32[128,512]{1,0:T(8,128)S(1)} %shard_map.66.refs_0_), channel_id=1, source_target_pairs={{2,18},{3,19},{6,22},{7,23},{10,26},{11,27},{14,30},{15,31},{16,0}... | collective-permute-start | bytes 786440 | tf_op jit(solution)/shard_map/ppermute | solution.py:84
  78.7 24.3 %collective-permute-start.13 = (f32[128,512]{1,0:T(8,128)S(1)}, f32[128,512]{1,0:T(8,128)S(1)}, u32[]{:S(2)}, u32[]{:S(2)}) collective-permute-start(f32[128,512]{1,0:T(8,128)S(1)} %shard_map.72.refs_1_), channel_id=1, source_target_pairs={{2,18},{3,19},{6,22},{7,23},{10,26},{11,27},{14,30},{15,31},{16,0}... | collective-permute-start | bytes 786440 | tf_op jit(solution)/shard_map/ppermute | solution.py:84
  83.4 20.3 %collective-permute-start.14 = (f32[128,512]{1,0:T(8,128)S(1)}, f32[128,512]{1,0:T(8,128)S(1)}, u32[]{:S(2)}, u32[]{:S(2)}) collective-permute-start(f32[128,512]{1,0:T(8,128)S(1)} %shard_map.74.refs_2_), channel_id=1, source_target_pairs={{2,18},{3,19},{6,22},{7,23},{10,26},{11,27},{14,30},{15,31},{16,0}... | collective-permute-start | bytes 786440 | tf_op jit(solution)/shard_map/ppermute | solution.py:84
  101.2 13.8 %collective-permute-start.22 = (f32[2,512,256]{2,1,0:T(8,128)S(1)}, f32[2,512,256]{2,1,0:T(8,128)S(1)}, u32[]{:S(2)}, u32[]{:S(2)}) collective-permute-start(f32[2,512,256]{2,1,0:T(8,128)S(1)} %collective-permute-done.21.a_ref), channel_id=1, source_target_pairs={{0,1},{1,0},{2,3},{3,2},{4,5},{5,4},{6,7},{7,6},{8,9},{9,8},{10,11... | collective-permute-start | bytes 3145736 | tf_op jit(solution)/shard_map/ppermute | solution.py:84
  102.5 16.2 %collective-permute-start.33 = (f32[2,512,256]{2,1,0:T(8,128)S(1)}, f32[2,512,256]{2,1,0:T(8,128)S(1)}, u32[]{:S(2)}, u32[]{:S(2)}) collective-permute-start(f32[2,512,256]{2,1,0:T(8,128)S(1)} %collective-permute-done.32.a_ref), channel_id=1, source_target_pairs={{0,1},{1,0},{2,3},{3,2},{4,5},{5,4},{6,7},{7,6},{8,9},{9,8},{10,11... | collective-permute-start | bytes 3145736 | tf_op jit(solution)/shard_map/ppermute | solution.py:84
  102.5 18.8 %collective-permute-start.20 = (f32[2,512,256]{2,1,0:T(8,128)S(1)}, f32[2,512,256]{2,1,0:T(8,128)S(1)}, u32[]{:S(2)}, u32[]{:S(2)}) collective-permute-start(f32[2,512,256]{2,1,0:T(8,128)S(1)} %collective-permute-done.19.a_ref), channel_id=1, source_target_pairs={{0,1},{1,0},{2,3},{3,2},{4,5},{5,4},{6,7},{7,6},{8,9},{9,8},{10,11... | collective-permute-start | bytes 3145736 | tf_op jit(solution)/shard_map/ppermute | solution.py:84
  103.0 19.6 %collective-permute-start.31 = (f32[2,512,256]{2,1,0:T(8,128)S(1)}, f32[2,512,256]{2,1,0:T(8,128)S(1)}, u32[]{:S(2)}, u32[]{:S(2)}) collective-permute-start(f32[2,512,256]{2,1,0:T(8,128)S(1)} %collective-permute-done.30.a_ref), channel_id=1, source_target_pairs={{0,1},{1,0},{2,3},{3,2},{4,5},{5,4},{6,7},{7,6},{8,9},{9,8},{10,11... | collective-permute-start | bytes 3145736 | tf_op jit(solution)/shard_map/ppermute | solution.py:84
  113.7 63.2 %collective-permute-start.17 = (f32[512,512]{1,0:T(8,128)S(1)}, f32[512,512]{1,0:T(8,128)}, u32[]{:S(2)}, u32[]{:S(2)}) collective-permute-start(f32[512,512]{1,0:T(8,128)S(1)} %get-tuple-element.52.near_ref), channel_id=1, source_target_pairs={{1,3},{5,7},{8,10},{12,14},{19,17},{23,21},{26,24},{30,28}} | collective-permute-start | bytes 3145736 | tf_op jit(solution)/shard_map/ppermute | solution.py:84
  118.7 21.3 %collective-permute-start.25 = (f32[2,128,512]{2,1,0:T(8,128)S(1)}, f32[2,128,512]{2,1,0:T(8,128)S(1)}, u32[]{:S(2)}, u32[]{:S(2)}) collective-permute-start(f32[2,128,512]{2,1,0:T(8,128)S(1)} %get-tuple-element.59), channel_id=1, source_target_pairs={{0,4},{1,5},{2,6},{3,7},{4,0},{5,1},{6,2},{7,3},{8,12},{9,13},{10,... | collective-permute-start | bytes 1572872 | tf_op jit(solution)/shard_map/ppermute | solution.py:84
  121.4 33.6 %collective-permute-start.34 = (f32[2,128,512]{2,1,0:T(8,128)S(1)}, f32[2,128,512]{2,1,0:T(8,128)S(1)}, u32[]{:S(2)}, u32[]{:S(2)}) collective-permute-start(f32[2,128,512]{2,1,0:T(8,128)S(1)} %get-tuple-element.63), channel_id=1, source_target_pairs={{0,4},{1,5},{2,6},{3,7},{4,0},{5,1},{6,2},{7,3},{8,12},{9,13},{10,... | collective-permute-start | bytes 1572872 | tf_op jit(solution)/shard_map/ppermute | solution.py:84
  122.6 43.6 %collective-permute-start.38 = (f32[2,128,512]{2,1,0:T(8,128)S(1)}, f32[2,128,512]{2,1,0:T(8,128)S(1)}, u32[]{:S(2)}, u32[]{:S(2)}) collective-permute-start(f32[2,128,512]{2,1,0:T(8,128)S(1)} %get-tuple-element.67), channel_id=1, source_target_pairs={{0,4},{1,5},{2,6},{3,7},{4,0},{5,1},{6,2},{7,3},{8,12},{9,13},{10,... | collective-permute-start | bytes 1572872 | tf_op jit(solution)/shard_map/ppermute | solution.py:84
  128.8 118.1 %collective-permute-start.16 = (f32[512,512]{1,0:T(8,128)S(1)}, f32[512,512]{1,0:T(8,128)}, u32[]{:S(2)}, u32[]{:S(2)}) collective-permute-start(f32[512,512]{1,0:T(8,128)S(1)} %get-tuple-element.52.near_ref), channel_id=1, source_target_pairs={{0,4},{4,0},{9,13},{13,9},{18,22},{22,18},{27,31},{31,27}} | collective-permute-start | bytes 3145736 | tf_op jit(solution)/shard_map/ppermute | solution.py:84
  140.0 47.5 %collective-permute-start.24 = (f32[128,512]{1,0:T(8,128)S(1)}, f32[128,512]{1,0:T(8,128)S(1)}, u32[]{:S(2)}, u32[]{:S(2)}) collective-permute-start(f32[128,512]{1,0:T(8,128)S(1)} %get-tuple-element.57), channel_id=1, source_target_pairs={{0,8},{1,9},{2,10},{3,11},{4,12},{5,13},{6,14},{7,15},{8,0},{9,1},... | collective-permute-start | bytes 786440 | tf_op jit(solution)/shard_map/ppermute | solution.py:84
  155.0 33.2 %collective-permute-start.26 = (f32[128,512]{1,0:T(8,128)S(1)}, f32[128,512]{1,0:T(8,128)S(1)}, u32[]{:S(2)}, u32[]{:S(2)}) collective-permute-start(f32[128,512]{1,0:T(8,128)S(1)} %get-tuple-element.61), channel_id=1, source_target_pairs={{0,8},{1,9},{2,10},{3,11},{4,12},{5,13},{6,14},{7,15},{8,0},{9,1},... | collective-permute-start | bytes 786440 | tf_op jit(solution)/shard_map/ppermute | solution.py:84
  166.2 22.6 %collective-permute-start.35 = (f32[128,512]{1,0:T(8,128)S(1)}, f32[128,512]{1,0:T(8,128)S(1)}, u32[]{:S(2)}, u32[]{:S(2)}) collective-permute-start(f32[128,512]{1,0:T(8,128)S(1)} %get-tuple-element.65), channel_id=1, source_target_pairs={{0,8},{1,9},{2,10},{3,11},{4,12},{5,13},{6,14},{7,15},{8,0},{9,1},... | collective-permute-start | bytes 786440 | tf_op jit(solution)/shard_map/ppermute | solution.py:84
  176.8 79.4 %collective-permute-start.18 = (f32[512,512]{1,0:T(8,128)}, f32[512,512]{1,0:T(8,128)}, u32[]{:S(2)}, u32[]{:S(2)}) collective-permute-start(f32[512,512]{1,0:T(8,128)} %collective-permute-done.17), channel_id=1, source_target_pairs={{3,8},{7,12},{10,5},{14,1},{17,26},{21,30},{24,23},{28,19}} | collective-permute-start | bytes 3145736 | tf_op jit(solution)/shard_map/ppermute | solution.py:84
  187.5 21.8 %collective-permute-start.39 = (f32[128,512]{1,0:T(8,128)S(1)}, f32[128,512]{1,0:T(8,128)S(1)}, u32[]{:S(2)}, u32[]{:S(2)}) collective-permute-start(f32[128,512]{1,0:T(8,128)S(1)} %get-tuple-element.69), channel_id=1, source_target_pairs={{0,8},{1,9},{2,10},{3,11},{4,12},{5,13},{6,14},{7,15},{8,0},{9,1},... | collective-permute-start | bytes 786440 | tf_op jit(solution)/shard_map/ppermute | solution.py:84
  188.2 25.5 %collective-permute-start.27 = (f32[128,512]{1,0:T(8,128)S(1)}, f32[128,512]{1,0:T(8,128)S(1)}, u32[]{:S(2)}, u32[]{:S(2)}) collective-permute-start(f32[128,512]{1,0:T(8,128)S(1)} %shard_map.81.refs_0_), channel_id=1, source_target_pairs={{0,16},{1,17},{2,18},{3,19},{4,20},{5,21},{6,22},{7,23},{8,24},{9,... | collective-permute-start | bytes 786440 | tf_op jit(solution)/shard_map/ppermute | solution.py:84
  188.8 36.2 %collective-permute-start.28 = (f32[128,512]{1,0:T(8,128)S(1)}, f32[128,512]{1,0:T(8,128)S(1)}, u32[]{:S(2)}, u32[]{:S(2)}) collective-permute-start(f32[128,512]{1,0:T(8,128)S(1)} %shard_map.83.refs_1_), channel_id=1, source_target_pairs={{0,16},{1,17},{2,18},{3,19},{4,20},{5,21},{6,22},{7,23},{8,24},{9,... | collective-permute-start | bytes 786440 | tf_op jit(solution)/shard_map/ppermute | solution.py:84
  209.3 21.4 %collective-permute-start.36 = (f32[128,512]{1,0:T(8,128)S(1)}, f32[128,512]{1,0:T(8,128)S(1)}, u32[]{:S(2)}, u32[]{:S(2)}) collective-permute-start(f32[128,512]{1,0:T(8,128)S(1)} %shard_map.88.refs_0_), channel_id=1, source_target_pairs={{0,16},{1,17},{2,18},{3,19},{4,20},{5,21},{6,22},{7,23},{8,24},{9,... | collective-permute-start | bytes 786440 | tf_op jit(solution)/shard_map/ppermute | solution.py:84
  213.7 22.8 %collective-permute-start.40 = (f32[128,512]{1,0:T(8,128)S(1)}, f32[128,512]{1,0:T(8,128)S(1)}, u32[]{:S(2)}, u32[]{:S(2)}) collective-permute-start(f32[128,512]{1,0:T(8,128)S(1)} %shard_map.91.refs_0_), channel_id=1, source_target_pairs={{0,16},{1,17},{2,18},{3,19},{4,20},{5,21},{6,22},{7,23},{8,24},{9,... | collective-permute-start | bytes 786440 | tf_op jit(solution)/shard_map/ppermute | solution.py:84
  226.5 29.8 %collective-permute-start.29 = (f32[256,512]{1,0:T(8,128)}, f32[256,512]{1,0:T(8,128)}, u32[]{:S(2)}, u32[]{:S(2)}) collective-permute-start(f32[256,512]{1,0:T(8,128)} %shard_map.84.far_ref), channel_id=1, source_target_pairs={{0,6},{1,10},{4,2},{5,14},{8,3},{9,15},{12,7},{13,11},{18,16},{19,... | collective-permute-start | bytes 1572872 | tf_op jit(solution)/shard_map/ppermute | solution.py:84
  232.0 21.5 %collective-permute-start.37 = (f32[128,512]{1,0:T(8,128)}, f32[128,512]{1,0:T(8,128)}, u32[]{:S(2)}, u32[]{:S(2)}) collective-permute-start(f32[128,512]{1,0:T(8,128)} %shard_map.89.refs_0_), channel_id=1, source_target_pairs={{0,6},{1,10},{4,2},{5,14},{8,3},{9,15},{12,7},{13,11},{18,16},{19,... | collective-permute-start | bytes 786440 | tf_op jit(solution)/shard_map/ppermute | solution.py:84
  237.7 18.5 %collective-permute-start.41 = (f32[128,512]{1,0:T(8,128)}, f32[128,512]{1,0:T(8,128)}, u32[]{:S(2)}, u32[]{:S(2)}) collective-permute-start(f32[128,512]{1,0:T(8,128)} %shard_map.92.refs_1_), channel_id=1, source_target_pairs={{0,6},{1,10},{4,2},{5,14},{8,3},{9,15},{12,7},{13,11},{18,16},{19,... | collective-permute-start | bytes 786440 | tf_op jit(solution)/shard_map/ppermute | solution.py:84
  (18 other events, 206.6 us)

commit v11 on v10

--- a/solution.py
+++ b/solution.py
@@ -474,6 +474,7 @@
         in_specs=[*[None] * len(values), *ins, hbm, hbm],
         out_specs=outs,
         aliases={count + 1: 0, count + 2: 1},
+        vmem=MEDIUM,
     )
 
 
@@ -515,6 +516,7 @@
         out_specs=[hbm, hbm],
         scratch=[pltpu.VMEM(block.block_shape, jnp.float32)] * 2 + [pltpu.SemaphoreType.DMA((2,))],
         aliases={count + 1: 0, count + 2: 1},
+        vmem=MEDIUM,
     )
 
 
@@ -590,8 +592,8 @@
     return back_half(meta, values, *pair, *fixed)
 
 
-NEAR_GROUPS = ((1, ("s0", "s1"), (1, 2, 3)), (0, ("k0",), (0,)), (0, ("k0", "k1"), (1, 2, 3)))
-FAR_GROUPS = (("s0", 1, 0, 2), ("k0", 0, 0, 2), ("s1", 1, 2, 2), ("k1", 0, 2, 2))
+NEAR_GROUPS = ((1, ("s0", "s1"), (1, 2, 3)), (0, ("k0",), (0,)), (0, ("k0", "k1", "k2"), (1, 2, 3)))
+FAR_GROUPS = (("s0", 1, 0, 2), ("k0", 0, 0, 2), ("s1", 1, 2, 2), ("k1", 0, 2, 1), ("k2", 0, 3, 1))
 
 
 def gap_slices(shape, occ_energy, vir_energy):

time: 261 us -> 269 us (1.031)
  the two profiles are of different devices: /device:TPU:5 before, /device:TPU:29 now
where the time goes in v11:
time: 269 us; the launch traced here: 264 us
  starting transfers between devices  118 us (44%)
  waiting for transfers between devices  85 us (32%)
  Pallas kernels  56.4 us (21%)
  local copies, waits for them, and re-layouts  3.47 us (1%)
    ppermute x45, starting transfers between devices, routed(): return lax.ppermute(block, ('row', 'col'), route)  118 us
    ppermute x45, waiting for transfers between devices, routed(): return lax.ppermute(block, ('row', 'col'), route)  85 us
    pallas_call x39, Pallas kernels, call(): pl.pallas_call(kernel, out_shape=list(shapes), grid_spec=pltpu.PrefetchSc...  56.4 us
  transfers between devices with their start and end apart: 45, of which 12 were waited for; matrix products, arithmetic and copies ran while one was open for 0% of the time, Pallas kernels for 19%

profile of v11, /device:TPU:29, one launch (start us, length us, event | category | flops | bytes accessed | tf_op | source)
XLA Modules:
  0.0 264.5 jit_solution(5672971389036498320)
XLA Ops:
  1.2 3.0 %shard_map.63 = f32[2,512,256]{2,1,0:T(8,128)} custom-call(s32[8]{0:T(128)} %compare_select_fusion.7.m._, f32[512,1024]{1,0:T(8,128)} %refs_3_.1, f32[512,1024]{1,0:T(8,128)} %refs_4_.3), custom_call_target="tpu_custom_call" | custom-call | tf_op jit(solution)/shard_map/pallas_call | solution.py:139
  17.8 5.5 %shard_map.71 = (f32[2,128,512]{2,1,0:T(8,128)S(1)}, f32[2,128,512]{2,1,0:T(8,128)S(1)}, f32[2,136,512]{2,1,0:T(8,128)S(1)}) custom-call(s32[8]{0:T(128)S(1)} %copy-done.3, f32[2,512,256]{2,1,0:T(8,128)S(1)} %collective-permute-done.1.piece_ref.refs_0_, f32[2,512,256]{2,1,0:T(8,128)S(1)} %collective-permute-done.6.refs_1_, ...), custom_call_target="tpu_custom_call" | custom-call | tf_op jit(solution)/shard_map/pallas_call | solution.py:139
  23.3 21.6 %collective-permute-done.31.a_ref = f32[2,512,128]{2,1,0:T(8,128)S(1)} collective-permute-done((f32[2,512,128]{2,1,0:T(8,128)S(1)}, f32[2,512,128]{2,1,0:T(8,128)S(1)}, u32[]{:S(2)}, u32[]{:S(2)}) %collective-permute-start.31) | collective-permute-done | bytes 524320 | tf_op jit(solution)/shard_map/ppermute | solution.py:84
  47.9 2.0 shard_map.61.keep_pass.keep_stay
  50.5 17.7 %collective-permute-done.7.come_pass.come_stay = f32[2,128,512]{2,1,0:T(8,128)S(1)} collective-permute-done((f32[2,128,512]{2,1,0:T(8,128)S(1)}, f32[2,128,512]{2,1,0:T(8,128)S(1)}, u32[]{:S(2)}, u32[]{:S(2)}) %collective-permute-start.7) | collective-permute-done | bytes 524320 | tf_op jit(solution)/shard_map/ppermute | solution.py:84
  68.4 5.7 %shard_map.69 = (f32[2,128,512]{2,1,0:T(8,128)S(1)}, f32[2,128,512]{2,1,0:T(8,128)S(1)}, f32[2,136,512]{2,1,0:T(8,128)S(1)}) custom-call(s32[8]{0:T(128)S(1)} %copy-done.3, f32[2,512,256]{2,1,0:T(8,128)S(1)} %collective-permute-done.refs_0_, f32[2,512,128]{2,1,0:T(8,128)S(1)} %collective-permute-done.4.refs_1_, ...), custom_call_target="tpu_custom_call" | custom-call | tf_op jit(solution)/shard_map/pallas_call | solution.py:139
  74.7 6.0 %collective-permute-start.23 = (f32[2,512,256]{2,1,0:T(8,128)S(1)}, f32[2,512,256]{2,1,0:T(8,128)S(1)}, u32[]{:S(2)}, u32[]{:S(2)}) collective-permute-start(f32[2,512,256]{2,1,0:T(8,128)S(1)} %collective-permute-done.22.a_ref), channel_id=1, source_target_pairs={{0,1},{1,0},{2,3},{3,2},{4,5},{5,4},{6,7},{7,6},{8,9},{9,8},{10,11... | collective-permute-start | bytes 3145736 | tf_op jit(solution)/shard_map/ppermute | solution.py:84
  88.9 3.8 %collective-permute-done.10.b_ref = f32[128,512]{1,0:T(8,128)S(1)} collective-permute-done((f32[128,512]{1,0:T(8,128)S(1)}, f32[128,512]{1,0:T(8,128)S(1)}, u32[]{:S(2)}, u32[]{:S(2)}) %collective-permute-start.10) | collective-permute-done | bytes 262176 | tf_op jit(solution)/shard_map/ppermute | solution.py:84
  95.8 8.3 %collective-permute-done.12.b_ref = f32[136,512]{1,0:T(8,128)S(1)} collective-permute-done((f32[136,512]{1,0:T(8,128)S(1)}, f32[136,512]{1,0:T(8,128)S(1)}, u32[]{:S(2)}, u32[]{:S(2)}) %collective-permute-start.12) | collective-permute-done | bytes 278560 | tf_op jit(solution)/shard_map/ppermute | solution.py:84
  104.1 2.6 collective-permute-start.34
  106.7 13.2 %collective-permute-start.21 = (f32[2,512,256]{2,1,0:T(8,128)S(1)}, f32[2,512,256]{2,1,0:T(8,128)S(1)}, u32[]{:S(2)}, u32[]{:S(2)}) collective-permute-start(f32[2,512,256]{2,1,0:T(8,128)S(1)} %collective-permute-done.20.a_ref), channel_id=1, source_target_pairs={{0,1},{1,0},{2,3},{3,2},{4,5},{5,4},{6,7},{7,6},{8,9},{9,8},{10,11... | collective-permute-start | bytes 3145736 | tf_op jit(solution)/shard_map/ppermute | solution.py:84
  121.2 5.0 %collective-permute-done.15.refs_6_ = f32[128,512]{1,0:T(8,128)S(1)} collective-permute-done((f32[128,512]{1,0:T(8,128)S(1)}, f32[128,512]{1,0:T(8,128)S(1)}, u32[]{:S(2)}, u32[]{:S(2)}) %collective-permute-start.15) | collective-permute-done | bytes 262176 | tf_op jit(solution)/shard_map/ppermute | solution.py:84
  127.5 9.6 %collective-permute-start.32 = (f32[2,512,128]{2,1,0:T(8,128)S(1)}, f32[2,512,128]{2,1,0:T(8,128)S(1)}, u32[]{:S(2)}, u32[]{:S(2)}) collective-permute-start(f32[2,512,128]{2,1,0:T(8,128)S(1)} %collective-permute-done.31.a_ref), channel_id=1, source_target_pairs={{0,1},{1,0},{2,3},{3,2},{4,5},{5,4},{6,7},{7,6},{8,9},{9,8},{10,11... | collective-permute-start | bytes 1572872 | tf_op jit(solution)/shard_map/ppermute | solution.py:84
  137.1 2.4 shard_map.80
  141.4 1.7 collective-permute-start.18
  143.4 2.4 shard_map.87
  147.0 7.0 %collective-permute-start.40 = (f32[2,512,128]{2,1,0:T(8,128)S(1)}, f32[2,512,128]{2,1,0:T(8,128)S(1)}, u32[]{:S(2)}, u32[]{:S(2)}) collective-permute-start(f32[2,512,128]{2,1,0:T(8,128)S(1)} %collective-permute-done.39.a_ref), channel_id=1, source_target_pairs={{0,1},{1,0},{2,3},{3,2},{4,5},{5,4},{6,7},{7,6},{8,9},{9,8},{10,11... | collective-permute-start | bytes 1572872 | tf_op jit(solution)/shard_map/ppermute | solution.py:84
  155.9 2.4 shard_map.79
  159.6 10.4 %collective-permute-done.35.come_pass.come_stay = f32[2,128,512]{2,1,0:T(8,128)S(1)} collective-permute-done((f32[2,128,512]{2,1,0:T(8,128)S(1)}, f32[2,128,512]{2,1,0:T(8,128)S(1)}, u32[]{:S(2)}, u32[]{:S(2)}) %collective-permute-start.35) | collective-permute-done | bytes 524320 | tf_op jit(solution)/shard_map/ppermute | solution.py:84
  170.7 3.1 %collective-permute-start.17 = (f32[512,512]{1,0:T(8,128)S(1)}, f32[512,512]{1,0:T(8,128)}, u32[]{:S(2)}, u32[]{:S(2)}) collective-permute-start(f32[512,512]{1,0:T(8,128)S(1)} %get-tuple-element.50.near_ref), channel_id=1, source_target_pairs={{0,4},{4,0},{9,13},{13,9},{18,22},{22,18},{27,31},{31,27}} | collective-permute-start | bytes 3145736 | tf_op jit(solution)/shard_map/ppermute | solution.py:84
  173.8 7.5 %collective-permute-done.41.come_pass.come_stay = f32[2,128,512]{2,1,0:T(8,128)S(1)} collective-permute-done((f32[2,128,512]{2,1,0:T(8,128)S(1)}, f32[2,128,512]{2,1,0:T(8,128)S(1)}, u32[]{:S(2)}, u32[]{:S(2)}) %collective-permute-start.41) | collective-permute-done | bytes 524320 | tf_op jit(solution)/shard_map/ppermute | solution.py:84
  181.3 1.6 collective-permute-start.19
  186.9 11.0 %collective-permute-start.28 = (f32[128,512]{1,0:T(8,128)S(1)}, f32[128,512]{1,0:T(8,128)S(1)}, u32[]{:S(2)}, u32[]{:S(2)}) collective-permute-start(f32[128,512]{1,0:T(8,128)S(1)} %shard_map.82.refs_0_), channel_id=1, source_target_pairs={{0,16},{1,17},{2,18},{3,19},{4,20},{5,21},{6,22},{7,23},{8,24},{9,... | collective-permute-start | bytes 786440 | tf_op jit(solution)/shard_map/ppermute | solution.py:84
  199.2 19.8 %collective-permute-start.37 = (f32[128,512]{1,0:T(8,128)S(1)}, f32[128,512]{1,0:T(8,128)S(1)}, u32[]{:S(2)}, u32[]{:S(2)}) collective-permute-start(f32[128,512]{1,0:T(8,128)S(1)} %shard_map.89.refs_0_), channel_id=1, source_target_pairs={{0,16},{1,17},{2,18},{3,19},{4,20},{5,21},{6,22},{7,23},{8,24},{9,... | collective-permute-start | bytes 786440 | tf_op jit(solution)/shard_map/ppermute | solution.py:84
  221.2 17.1 %collective-permute-start.30 = (f32[256,512]{1,0:T(8,128)}, f32[256,512]{1,0:T(8,128)}, u32[]{:S(2)}, u32[]{:S(2)}) collective-permute-start(f32[256,512]{1,0:T(8,128)} %shard_map.85.far_ref), channel_id=1, source_target_pairs={{0,6},{1,10},{4,2},{5,14},{8,3},{9,15},{12,7},{13,11},{18,16},{19,... | collective-permute-start | bytes 1572872 | tf_op jit(solution)/shard_map/ppermute | solution.py:84
  238.3 3.2 %collective-permute-done.37.refs_1_ = f32[128,512]{1,0:T(8,128)S(1)} collective-permute-done((f32[128,512]{1,0:T(8,128)S(1)}, f32[128,512]{1,0:T(8,128)S(1)}, u32[]{:S(2)}, u32[]{:S(2)}) %collective-permute-start.37) | collective-permute-done | bytes 262176 | tf_op jit(solution)/shard_map/ppermute | solution.py:84
  242.8 2.0 collective-permute-start.38
  244.8 2.4 collective-permute-done.43.refs_1_
  248.4 2.0 collective-permute-start.44
  252.3 3.5 %shard_map.95 = (f32[512,1024]{1,0:T(8,128)}, f32[512,1024]{1,0:T(8,128)}) custom-call(s32[8]{0:T(128)S(1)} %copy-done.3, f32[512,512]{1,0:T(8,128)S(1)} %get-tuple-element.50.near_ref, f32[256,512]{1,0:T(8,128)} %shard_map.85.far_ref, f32[512,1024]{1,0:T(8,128)S(1)} %copy-done, f32[512,1024]{1,0:T(8,128)S(1)} %copy-done.2, ...), custom_call_target="tpu_custom_call" | custom-call | tf_op jit(solution)/shard_map/pallas_call | solution.py:139
  257.4 2.8 %collective-permute-done.44.refs_2_ = f32[128,512]{1,0:T(8,128)} collective-permute-done((f32[128,512]{1,0:T(8,128)}, f32[128,512]{1,0:T(8,128)}, u32[]{:S(2)}, u32[]{:S(2)}) %collective-permute-start.44) | collective-permute-done | bytes 262176 | tf_op jit(solution)/shard_map/ppermute | solution.py:84
  260.2 4.3 %shard_map.97 = (f32[512,1024]{1,0:T(8,128)}, f32[512,1024]{1,0:T(8,128)}) custom-call(s32[8]{0:T(128)S(1)} %copy-done.3, f32[512,512]{1,0:T(8,128)S(1)} %get-tuple-element.50.near_ref, f32[512,512]{1,0:T(8,128)} %collective-permute-done.17.swap_ref, f32[512,512]{1,0:T(8,128)} %collective-permute-done.19.back_ref, ...), custom_call_target="tpu_custom_call", output_to_operand_aliasing={{0}: (12, {}), {1}: (13, {})} | custom-call | tf_op jit(solution)/shard_map/pallas_call | solution.py:139
  (117 shorter events, 52.5 us)
Async XLA Ops:
  9.3 36.9 %collective-permute-start = (f32[2,512,256]{2,1,0:T(8,128)S(1)}, f32[2,512,256]{2,1,0:T(8,128)S(1)}, u32[]{:S(2)}, u32[]{:S(2)}) collective-permute-start(f32[2,512,256]{2,1,0:T(8,128)S(1)} %shard_map.59), channel_id=1, source_target_pairs={{0,1},{1,0},{2,3},{3,2},{4,5},{5,4},{6,7},{7,6},{8,9},{9,8},{10,11... | collective-permute-start | bytes 3145736 | tf_op jit(solution)/shard_map/ppermute | solution.py:84
  9.4 37.0 %collective-permute-start.20 = (f32[2,512,256]{2,1,0:T(8,128)S(1)}, f32[2,512,256]{2,1,0:T(8,128)S(1)}, u32[]{:S(2)}, u32[]{:S(2)}) collective-permute-start(f32[2,512,256]{2,1,0:T(8,128)S(1)} %shard_map.59), channel_id=1, source_target_pairs={{0,2},{1,3},{2,0},{3,1},{4,6},{5,7},{6,4},{7,5},{8,10},{9,11},{10,... | collective-permute-start | bytes 3145736 | tf_op jit(solution)/shard_map/ppermute | solution.py:84
  11.1 33.9 %collective-permute-start.31 = (f32[2,512,128]{2,1,0:T(8,128)S(1)}, f32[2,512,128]{2,1,0:T(8,128)S(1)}, u32[]{:S(2)}, u32[]{:S(2)}) collective-permute-start(f32[2,512,128]{2,1,0:T(8,128)S(1)} %shard_map.67), channel_id=1, source_target_pairs={{0,2},{1,3},{2,0},{3,1},{4,6},{5,7},{6,4},{7,5},{8,10},{9,11},{10,... | collective-permute-start | bytes 1572872 | tf_op jit(solution)/shard_map/ppermute | solution.py:84
  16.3 58.4 %collective-permute-start.22 = (f32[2,512,256]{2,1,0:T(8,128)S(1)}, f32[2,512,256]{2,1,0:T(8,128)S(1)}, u32[]{:S(2)}, u32[]{:S(2)}) collective-permute-start(f32[2,512,256]{2,1,0:T(8,128)S(1)} %copy-done.4), channel_id=1, source_target_pairs={{0,2},{1,3},{2,0},{3,1},{4,6},{5,7},{6,4},{7,5},{8,10},{9,11},{10,... | collective-permute-start | bytes 3145736 | tf_op jit(solution)/shard_map/ppermute | solution.py:84
  16.6 30.1 %collective-permute-start.2 = (f32[2,128,512]{2,1,0:T(8,128)S(1)}, f32[2,128,512]{2,1,0:T(8,128)S(1)}, u32[]{:S(2)}, u32[]{:S(2)}) collective-permute-start(f32[2,128,512]{2,1,0:T(8,128)S(1)} %shard_map.64), channel_id=1, source_target_pairs={{0,4},{1,5},{2,6},{3,7},{4,0},{5,1},{6,2},{7,3},{8,12},{9,13},{10,... | collective-permute-start | bytes 1572872 | tf_op jit(solution)/shard_map/ppermute | solution.py:84
  45.0 37.6 %collective-permute-start.11 = (f32[2,136,512]{2,1,0:T(8,128)S(1)}, f32[2,136,512]{2,1,0:T(8,128)S(1)}, u32[]{:S(2)}, u32[]{:S(2)}) collective-permute-start(f32[2,136,512]{2,1,0:T(8,128)S(1)} %get-tuple-element.47), channel_id=1, source_target_pairs={{0,4},{1,5},{2,6},{3,7},{4,0},{5,1},{6,2},{7,3},{8,12},{9,13},{10,... | collective-permute-start | bytes 1671176 | tf_op jit(solution)/shard_map/ppermute | solution.py:84
  46.2 22.0 %collective-permute-start.7 = (f32[2,128,512]{2,1,0:T(8,128)S(1)}, f32[2,128,512]{2,1,0:T(8,128)S(1)}, u32[]{:S(2)}, u32[]{:S(2)}) collective-permute-start(f32[2,128,512]{2,1,0:T(8,128)S(1)} %get-tuple-element.39), channel_id=1, source_target_pairs={{0,4},{1,5},{2,6},{3,7},{4,0},{5,1},{6,2},{7,3},{8,12},{9,13},{10,... | collective-permute-start | bytes 1572872 | tf_op jit(solution)/shard_map/ppermute | solution.py:84
  46.4 48.1 %collective-permute-start.33 = (f32[2,512,256]{2,1,0:T(8,128)S(1)}, f32[2,512,256]{2,1,0:T(8,128)S(1)}, u32[]{:S(2)}, u32[]{:S(2)}) collective-permute-start(f32[2,512,256]{2,1,0:T(8,128)S(1)} %shard_map.70), channel_id=1, source_target_pairs={{0,2},{1,3},{2,0},{3,1},{4,6},{5,7},{6,4},{7,5},{8,10},{9,11},{10,... | collective-permute-start | bytes 3145736 | tf_op jit(solution)/shard_map/ppermute | solution.py:84
  46.7 34.0 %collective-permute-start.9 = (f32[2,128,512]{2,1,0:T(8,128)S(1)}, f32[2,128,512]{2,1,0:T(8,128)S(1)}, u32[]{:S(2)}, u32[]{:S(2)}) collective-permute-start(f32[2,128,512]{2,1,0:T(8,128)S(1)} %get-tuple-element.43), channel_id=1, source_target_pairs={{0,4},{1,5},{2,6},{3,7},{4,0},{5,1},{6,2},{7,3},{8,12},{9,13},{10,... | collective-permute-start | bytes 1572872 | tf_op jit(solution)/shard_map/ppermute | solution.py:84
  74.7 52.8 %collective-permute-start.23 = (f32[2,512,256]{2,1,0:T(8,128)S(1)}, f32[2,512,256]{2,1,0:T(8,128)S(1)}, u32[]{:S(2)}, u32[]{:S(2)}) collective-permute-start(f32[2,512,256]{2,1,0:T(8,128)S(1)} %collective-permute-done.22.a_ref), channel_id=1, source_target_pairs={{0,1},{1,0},{2,3},{3,2},{4,5},{5,4},{6,7},{7,6},{8,9},{9,8},{10,11... | collective-permute-start | bytes 3145736 | tf_op jit(solution)/shard_map/ppermute | solution.py:84
  83.5 20.6 %collective-permute-start.12 = (f32[136,512]{1,0:T(8,128)S(1)}, f32[136,512]{1,0:T(8,128)S(1)}, u32[]{:S(2)}, u32[]{:S(2)}) collective-permute-start(f32[136,512]{1,0:T(8,128)S(1)} %get-tuple-element.49), channel_id=1, source_target_pairs={{0,8},{1,9},{2,10},{3,11},{4,12},{5,13},{6,14},{7,15},{8,0},{9,1},... | collective-permute-start | bytes 835592 | tf_op jit(solution)/shard_map/ppermute | solution.py:84
  87.0 19.7 %collective-permute-start.13 = (f32[128,512]{1,0:T(8,128)S(1)}, f32[128,512]{1,0:T(8,128)S(1)}, u32[]{:S(2)}, u32[]{:S(2)}) collective-permute-start(f32[128,512]{1,0:T(8,128)S(1)} %shard_map.66.refs_0_), channel_id=1, source_target_pairs={{2,18},{3,19},{6,22},{7,23},{10,26},{11,27},{14,30},{15,31},{16,0}... | collective-permute-start | bytes 786440 | tf_op jit(solution)/shard_map/ppermute | solution.py:84
  92.6 28.0 %collective-permute-start.14 = (f32[128,512]{1,0:T(8,128)S(1)}, f32[128,512]{1,0:T(8,128)S(1)}, u32[]{:S(2)}, u32[]{:S(2)}) collective-permute-start(f32[128,512]{1,0:T(8,128)S(1)} %shard_map.73.refs_1_), channel_id=1, source_target_pairs={{2,18},{3,19},{6,22},{7,23},{10,26},{11,27},{14,30},{15,31},{16,0}... | collective-permute-start | bytes 786440 | tf_op jit(solution)/shard_map/ppermute | solution.py:84
  94.5 31.7 %collective-permute-start.15 = (f32[128,512]{1,0:T(8,128)S(1)}, f32[128,512]{1,0:T(8,128)S(1)}, u32[]{:S(2)}, u32[]{:S(2)}) collective-permute-start(f32[128,512]{1,0:T(8,128)S(1)} %shard_map.75.refs_2_), channel_id=1, source_target_pairs={{2,18},{3,19},{6,22},{7,23},{10,26},{11,27},{14,30},{15,31},{16,0}... | collective-permute-start | bytes 786440 | tf_op jit(solution)/shard_map/ppermute | solution.py:84
  104.1 39.0 %collective-permute-start.34 = (f32[2,512,256]{2,1,0:T(8,128)S(1)}, f32[2,512,256]{2,1,0:T(8,128)S(1)}, u32[]{:S(2)}, u32[]{:S(2)}) collective-permute-start(f32[2,512,256]{2,1,0:T(8,128)S(1)} %collective-permute-done.33.a_ref), channel_id=1, source_target_pairs={{0,1},{1,0},{2,3},{3,2},{4,5},{5,4},{6,7},{7,6},{8,9},{9,8},{10,11... | collective-permute-start | bytes 3145736 | tf_op jit(solution)/shard_map/ppermute | solution.py:84
  106.7 40.3 %collective-permute-start.21 = (f32[2,512,256]{2,1,0:T(8,128)S(1)}, f32[2,512,256]{2,1,0:T(8,128)S(1)}, u32[]{:S(2)}, u32[]{:S(2)}) collective-permute-start(f32[2,512,256]{2,1,0:T(8,128)S(1)} %collective-permute-done.20.a_ref), channel_id=1, source_target_pairs={{0,1},{1,0},{2,3},{3,2},{4,5},{5,4},{6,7},{7,6},{8,9},{9,8},{10,11... | collective-permute-start | bytes 3145736 | tf_op jit(solution)/shard_map/ppermute | solution.py:84
  120.6 20.8 %collective-permute-start.39 = (f32[2,512,128]{2,1,0:T(8,128)S(1)}, f32[2,512,128]{2,1,0:T(8,128)S(1)}, u32[]{:S(2)}, u32[]{:S(2)}) collective-permute-start(f32[2,512,128]{2,1,0:T(8,128)S(1)} %shard_map.68), channel_id=1, source_target_pairs={{0,2},{1,3},{2,0},{3,1},{4,6},{5,7},{6,4},{7,5},{8,10},{9,11},{10,... | collective-permute-start | bytes 1572872 | tf_op jit(solution)/shard_map/ppermute | solution.py:84
  127.5 18.3 %collective-permute-start.32 = (f32[2,512,128]{2,1,0:T(8,128)S(1)}, f32[2,512,128]{2,1,0:T(8,128)S(1)}, u32[]{:S(2)}, u32[]{:S(2)}) collective-permute-start(f32[2,512,128]{2,1,0:T(8,128)S(1)} %collective-permute-done.31.a_ref), channel_id=1, source_target_pairs={{0,1},{1,0},{2,3},{3,2},{4,5},{5,4},{6,7},{7,6},{8,9},{9,8},{10,11... | collective-permute-start | bytes 1572872 | tf_op jit(solution)/shard_map/ppermute | solution.py:84
  141.4 39.9 %collective-permute-start.18 = (f32[512,512]{1,0:T(8,128)S(1)}, f32[512,512]{1,0:T(8,128)}, u32[]{:S(2)}, u32[]{:S(2)}) collective-permute-start(f32[512,512]{1,0:T(8,128)S(1)} %get-tuple-element.50.near_ref), channel_id=1, source_target_pairs={{1,3},{5,7},{8,10},{12,14},{19,17},{23,21},{26,24},{30,28}} | collective-permute-start | bytes 3145736 | tf_op jit(solution)/shard_map/ppermute | solution.py:84
  145.8 24.2 %collective-permute-start.35 = (f32[2,128,512]{2,1,0:T(8,128)S(1)}, f32[2,128,512]{2,1,0:T(8,128)S(1)}, u32[]{:S(2)}, u32[]{:S(2)}) collective-permute-start(f32[2,128,512]{2,1,0:T(8,128)S(1)} %get-tuple-element.60), channel_id=1, source_target_pairs={{0,4},{1,5},{2,6},{3,7},{4,0},{5,1},{6,2},{7,3},{8,12},{9,13},{10,... | collective-permute-start | bytes 1572872 | tf_op jit(solution)/shard_map/ppermute | solution.py:84
  147.0 23.6 %collective-permute-start.40 = (f32[2,512,128]{2,1,0:T(8,128)S(1)}, f32[2,512,128]{2,1,0:T(8,128)S(1)}, u32[]{:S(2)}, u32[]{:S(2)}) collective-permute-start(f32[2,512,128]{2,1,0:T(8,128)S(1)} %collective-permute-done.39.a_ref), channel_id=1, source_target_pairs={{0,1},{1,0},{2,3},{3,2},{4,5},{5,4},{6,7},{7,6},{8,9},{9,8},{10,11... | collective-permute-start | bytes 1572872 | tf_op jit(solution)/shard_map/ppermute | solution.py:84
  154.0 27.3 %collective-permute-start.41 = (f32[2,128,512]{2,1,0:T(8,128)S(1)}, f32[2,128,512]{2,1,0:T(8,128)S(1)}, u32[]{:S(2)}, u32[]{:S(2)}) collective-permute-start(f32[2,128,512]{2,1,0:T(8,128)S(1)} %get-tuple-element.63), channel_id=1, source_target_pairs={{0,4},{1,5},{2,6},{3,7},{4,0},{5,1},{6,2},{7,3},{8,12},{9,13},{10,... | collective-permute-start | bytes 1572872 | tf_op jit(solution)/shard_map/ppermute | solution.py:84
  158.9 26.2 %collective-permute-start.25 = (f32[128,512]{1,0:T(8,128)S(1)}, f32[128,512]{1,0:T(8,128)S(1)}, u32[]{:S(2)}, u32[]{:S(2)}) collective-permute-start(f32[128,512]{1,0:T(8,128)S(1)} %get-tuple-element.55), channel_id=1, source_target_pairs={{0,8},{1,9},{2,10},{3,11},{4,12},{5,13},{6,14},{7,15},{8,0},{9,1},... | collective-permute-start | bytes 786440 | tf_op jit(solution)/shard_map/ppermute | solution.py:84
  170.0 16.9 %collective-permute-start.27 = (f32[128,512]{1,0:T(8,128)S(1)}, f32[128,512]{1,0:T(8,128)S(1)}, u32[]{:S(2)}, u32[]{:S(2)}) collective-permute-start(f32[128,512]{1,0:T(8,128)S(1)} %get-tuple-element.59), channel_id=1, source_target_pairs={{0,8},{1,9},{2,10},{3,11},{4,12},{5,13},{6,14},{7,15},{8,0},{9,1},... | collective-permute-start | bytes 786440 | tf_op jit(solution)/shard_map/ppermute | solution.py:84
  170.7 86.7 %collective-permute-start.17 = (f32[512,512]{1,0:T(8,128)S(1)}, f32[512,512]{1,0:T(8,128)}, u32[]{:S(2)}, u32[]{:S(2)}) collective-permute-start(f32[512,512]{1,0:T(8,128)S(1)} %get-tuple-element.50.near_ref), channel_id=1, source_target_pairs={{0,4},{4,0},{9,13},{13,9},{18,22},{22,18},{27,31},{31,27}} | collective-permute-start | bytes 3145736 | tf_op jit(solution)/shard_map/ppermute | solution.py:84
  181.3 17.3 %collective-permute-start.36 = (f32[128,512]{1,0:T(8,128)S(1)}, f32[128,512]{1,0:T(8,128)S(1)}, u32[]{:S(2)}, u32[]{:S(2)}) collective-permute-start(f32[128,512]{1,0:T(8,128)S(1)} %get-tuple-element.62), channel_id=1, source_target_pairs={{0,8},{1,9},{2,10},{3,11},{4,12},{5,13},{6,14},{7,15},{8,0},{9,1},... | collective-permute-start | bytes 786440 | tf_op jit(solution)/shard_map/ppermute | solution.py:84
  181.3 78.9 %collective-permute-start.19 = (f32[512,512]{1,0:T(8,128)}, f32[512,512]{1,0:T(8,128)}, u32[]{:S(2)}, u32[]{:S(2)}) collective-permute-start(f32[512,512]{1,0:T(8,128)} %collective-permute-done.18), channel_id=1, source_target_pairs={{3,8},{7,12},{10,5},{14,1},{17,26},{21,30},{24,23},{28,19}} | collective-permute-start | bytes 3145736 | tf_op jit(solution)/shard_map/ppermute | solution.py:84
  186.9 32.8 %collective-permute-start.28 = (f32[128,512]{1,0:T(8,128)S(1)}, f32[128,512]{1,0:T(8,128)S(1)}, u32[]{:S(2)}, u32[]{:S(2)}) collective-permute-start(f32[128,512]{1,0:T(8,128)S(1)} %shard_map.82.refs_0_), channel_id=1, source_target_pairs={{0,16},{1,17},{2,18},{3,19},{4,20},{5,21},{6,22},{7,23},{8,24},{9,... | collective-permute-start | bytes 786440 | tf_op jit(solution)/shard_map/ppermute | solution.py:84
  198.5 21.2 %collective-permute-start.29 = (f32[128,512]{1,0:T(8,128)S(1)}, f32[128,512]{1,0:T(8,128)S(1)}, u32[]{:S(2)}, u32[]{:S(2)}) collective-permute-start(f32[128,512]{1,0:T(8,128)S(1)} %shard_map.84.refs_1_), channel_id=1, source_target_pairs={{0,16},{1,17},{2,18},{3,19},{4,20},{5,21},{6,22},{7,23},{8,24},{9,... | collective-permute-start | bytes 786440 | tf_op jit(solution)/shard_map/ppermute | solution.py:84
  199.2 42.3 %collective-permute-start.37 = (f32[128,512]{1,0:T(8,128)S(1)}, f32[128,512]{1,0:T(8,128)S(1)}, u32[]{:S(2)}, u32[]{:S(2)}) collective-permute-start(f32[128,512]{1,0:T(8,128)S(1)} %shard_map.89.refs_0_), channel_id=1, source_target_pairs={{0,16},{1,17},{2,18},{3,19},{4,20},{5,21},{6,22},{7,23},{8,24},{9,... | collective-permute-start | bytes 786440 | tf_op jit(solution)/shard_map/ppermute | solution.py:84
  219.7 27.5 %collective-permute-start.43 = (f32[128,512]{1,0:T(8,128)S(1)}, f32[128,512]{1,0:T(8,128)S(1)}, u32[]{:S(2)}, u32[]{:S(2)}) collective-permute-start(f32[128,512]{1,0:T(8,128)S(1)} %shard_map.93.refs_0_), channel_id=1, source_target_pairs={{0,16},{1,17},{2,18},{3,19},{4,20},{5,21},{6,22},{7,23},{8,24},{9,... | collective-permute-start | bytes 786440 | tf_op jit(solution)/shard_map/ppermute | solution.py:84
  221.2 39.0 %collective-permute-start.30 = (f32[256,512]{1,0:T(8,128)}, f32[256,512]{1,0:T(8,128)}, u32[]{:S(2)}, u32[]{:S(2)}) collective-permute-start(f32[256,512]{1,0:T(8,128)} %shard_map.85.far_ref), channel_id=1, source_target_pairs={{0,6},{1,10},{4,2},{5,14},{8,3},{9,15},{12,7},{13,11},{18,16},{19,... | collective-permute-start | bytes 1572872 | tf_op jit(solution)/shard_map/ppermute | solution.py:84
  (20 other events, 254.6 us)
